TPU v7x, 256 devices: a whole 4x4x8 slice. The times are simulated.
256 devices in a mesh: graph: 32 (over z, y), feat: 8 (over x, core).
Axes of the slice: x: 4, y: 4, z: 8, core: 2. Of those that a mesh axis runs over, the one named last changes fastest.
Arguments:
- features: bfloat16 [65536, 1024], P('graph', 'feat'), may hold values from -6 to 6
- w_self: bfloat16 [1024, 1024], replicated, may hold values from -0.1875 to 0.1875
- w_neigh: bfloat16 [1024, 1024], replicated, may hold values from -0.1875 to 0.1875
- adjacency: bfloat16 [4096, 128, 128], P('graph'), may hold values from 0 to 1.5, as said below
- block_source: int32 [4096], P('graph'), may hold values from 0 to 15
- block_to_slot: int32 [4096], P('graph'), may hold values from 0 to 63
- send_rows: int32 [32, 32, 256], P('graph'), may hold values from 0 to 2047
- send_counts: int32 [32, 32], P('graph'), may hold values from 64 to 256, as said below
- degree: int32 [65536], P('graph'), may hold values from 8 to 32
- cotangent: bfloat16 [65536, 1024], P('graph', 'feat'), may hold values from -6 to 6
Outputs:
- hidden_out: bfloat16 [65536, 1024], P('graph', 'feat')
- grad_features: bfloat16 [65536, 1024], P('graph', 'feat')
- grad_self: float32 [1024, 1024], P('feat')
- grad_neigh: float32 [1024, 1024], P('feat')
Inputs may be any that keep to these rules, and one draw needn't show every extreme that they name: Slots 0 to send_counts[p, q] - 1 from p to q are live; in every draw some partition receives 256 live slots from every partition. `adjacency`: edge weights; a block is mostly zeros.
All inputs are finite; a program needn't handle non-finite values.
Results may differ from a plain program's by a relative error of at most 0.0066.
Values may be sent and summed in bfloat16 or wider, within the bound.
No kernel may reach another device: no remote copies, remote signals or barrier semaphores. Data moves between devices by JAX's collectives and lax.ppermute only.
A program may use at most 128 MiB of HBM per device.

v0:
```python
import jax
import jax.numpy as jnp
from jax import lax
from jax.sharding import PartitionSpec as P


def silu_slope(values):
    sig = jax.nn.sigmoid(values)
    return sig * (1.0 + values * (1.0 - sig))


def on_device(
    features,
    w_self,
    w_neigh,
    adjacency,
    block_source,
    block_to_slot,
    send_rows,
    send_counts,
    degree,
    cotangent,
):
    node_rows, feat_cols = features.shape
    part_count = lax.axis_size("graph")
    block_size = adjacency.shape[1]
    slot_cap = send_rows.shape[2]
    slot_total = part_count * slot_cap // block_size
    source_count = node_rows // block_size
    column_start = lax.axis_index("feat") * feat_cols
    sources = features.reshape(source_count, block_size, feat_cols)
    picked = jnp.take(sources, block_source, axis=0)
    prods = jnp.einsum("kij,kjd->kid", adjacency, picked, preferred_element_type=jnp.float32)
    slot_sums = jax.ops.segment_sum(prods, block_to_slot, num_segments=slot_total)
    live_counts = send_counts[0]
    is_live = jnp.arange(slot_cap, dtype=jnp.int32)[None, :] < live_counts[:, None]
    outgoing = jnp.where(
        is_live[:, :, None], slot_sums.reshape(part_count, slot_cap, feat_cols), 0.0
    ).astype(jnp.bfloat16)
    row_ids = jnp.where(is_live, send_rows[0], -1)
    incoming, incoming_ids = (
        lax.all_to_all(outgoing, "graph", split_axis=0, concat_axis=0, tiled=True),
        lax.all_to_all(row_ids, "graph", split_axis=0, concat_axis=0, tiled=True),
    )
    valid_slot = incoming_ids >= 0
    target_rows = jnp.where(valid_slot, incoming_ids, node_rows).reshape(-1)
    neighbor_sum = (
        jnp.zeros((node_rows, feat_cols), jnp.float32)
        .at[target_rows]
        .add(incoming.reshape(-1, feat_cols).astype(jnp.float32), mode="drop")
    )
    degrees = degree.astype(jnp.float32)[:, None]
    neighbor_mean = (neighbor_sum / degrees).astype(jnp.bfloat16)
    self_rows = lax.dynamic_slice_in_dim(w_self, column_start, feat_cols, 0)
    neigh_rows = lax.dynamic_slice_in_dim(w_neigh, column_start, feat_cols, 0)
    own_term = lax.dot_general(
        self_rows, features, (((0,), (1,)), ((), ())), preferred_element_type=jnp.float32
    )
    agg_term = lax.dot_general(
        neigh_rows, neighbor_mean, (((0,), (1,)), ((), ())), preferred_element_type=jnp.float32
    )
    pre_act = lax.psum_scatter(own_term + agg_term, "feat", scatter_dimension=0, tiled=True).T
    hidden_out = jax.nn.silu(pre_act).astype(jnp.bfloat16)
    grad_pre = (cotangent.astype(jnp.float32) * silu_slope(pre_act)).astype(jnp.bfloat16)
    grad_full = lax.all_gather(grad_pre, "feat", axis=1, tiled=True)
    local_self = lax.dot_general(
        features, grad_full, (((0,), (0,)), ((), ())), preferred_element_type=jnp.float32
    )
    local_neigh = lax.dot_general(
        neighbor_mean, grad_full, (((0,), (0,)), ((), ())), preferred_element_type=jnp.float32
    )
    grad_self, grad_neigh = lax.psum((local_self, local_neigh), "graph")
    self_grad = lax.dot_general(
        grad_full, self_rows, (((1,), (1,)), ((), ())), preferred_element_type=jnp.float32
    )
    back_rows = (
        lax.dot_general(
            grad_full, neigh_rows, (((1,), (1,)), ((), ())), preferred_element_type=jnp.float32
        )
        / degrees
    ).astype(jnp.bfloat16)
    lookup = jnp.where(valid_slot, incoming_ids, 0)
    sending_back = jnp.where(valid_slot[:, :, None], jnp.take(back_rows, lookup, axis=0), 0.0)
    returned = lax.all_to_all(sending_back, "graph", split_axis=0, concat_axis=0, tiled=True)
    slot_blocks = returned.reshape(slot_total, block_size, feat_cols)
    chosen = jnp.take(slot_blocks, block_to_slot, axis=0)
    contrib = jnp.einsum("kij,kid->kjd", adjacency, chosen, preferred_element_type=jnp.float32)
    neigh_grad = jax.ops.segment_sum(contrib, block_source, num_segments=source_count).reshape(
        node_rows, feat_cols
    )
    grad_features = (self_grad + neigh_grad).astype(jnp.bfloat16)
    return (hidden_out, grad_features, grad_self, grad_neigh)


def solution(mesh):
    placed = (
        P("graph", "feat"),
        P(),
        P(),
        P("graph", None, None),
        P("graph"),
        P("graph"),
        P("graph", None, None),
        P("graph", None),
        P("graph"),
        P("graph", "feat"),
    )
    return jax.shard_map(
        on_device,
        mesh=mesh,
        in_specs=placed,
        out_specs=(P("graph", "feat"), P("graph", "feat"), P("feat", None), P("feat", None)),
        check_vma=False,
    )
```

profile of v0, /device:TPU:32, one launch (start us, length us, event | category | flops | bytes accessed | tf_op | source)
XLA Modules:
  0.0 544.0 jit_solution(14531779473950020415)
XLA Ops:
  7.2 0.0 copy-start
  7.2 1.6 compare_select_fusion.4
  8.8 11.4 %all-to-all-start = ((s32[32,1,256]{2,1,0:T(1,128)}), s32[32,1,256]{2,1,0:T(1,128)S(1)}, u32[]{:S(2)}, u32[]{:S(2)}) async-start(s32[32,1,256]{2,1,0:T(1,128)} %compare_select_fusion.4), calls=%async_computation | async-start | bytes 65536 | tf_op jit(solution)/shard_map/all_to_all | solution.py:43
  20.2 0.7 compare_and_fusion.2
  20.8 0.7 compare_select_fusion.7
  21.5 0.7 iota_compare_fusion
  22.2 4.1 gather_fusion
  26.3 9.9 %fusion.9 = f32[128,128,128]{1,2,0:T(8,128)} fusion(bf16[128,128,128]{2,1,0:T(8,128)(2,1)} %param.13, bf16[128,128,128]{2,1,0:T(8,128)(2,1)} %gather_fusion, pred[128]{0:T(512)(128)(4,1)S(1)} %compare_and_fusion.2), kind=kOutput, calls=%fused_computation.17 | convolution fusion | flops 538968064 | bytes 16777344 | tf_op jit(solution)/shard_map/kij,kjd->kid/dot_general | solution.py:33
  36.2 9.0 %copy.27 = f32[128,128,128]{2,1,0:T(8,128)} copy(f32[128,128,128]{1,2,0:T(8,128)} %fusion.9) | data formatting | bytes 16777216 | tf_op jit(solution)/shard_map/kij,kjd->kid/dot_general | solution.py:33
  45.3 0.0 copy-start.8
  45.3 2.5 broadcast_in_dim.92
  47.7 0.0 copy-done.8
  47.7 26.7 %scatter_fusion = f32[64,128,128]{2,1,0:T(8,128)} fusion(f32[64,128,128]{2,1,0:T(8,128)} %broadcast_in_dim.92, s32[128]{0:T(128)S(1)} %copy-done.8, f32[128,128,128]{2,1,0:T(8,128)} %copy.27), kind=kCustom, calls=%fused_computation.3 | custom fusion | flops 2097152 | bytes 25166336 | tf_op jit(solution)/shard_map/scatter-add | solution.py:34
  74.4 0.0 copy-start.7
  74.4 0.0 copy-start.2
  74.4 4.9 fusion.2
  79.3 0.0 all-to-all-done
  79.3 9.9 %all-to-all-start.1 = ((bf16[32,256,128]{2,1,0:T(8,128)(2,1)}), bf16[32,256,128]{2,1,0:T(8,128)(2,1)}, u32[]{:S(2)}, u32[]{:S(2)}) async-start(bf16[32,256,128]{2,1,0:T(8,128)(2,1)} %fusion.2), calls=%async_computation.1 | async-start | bytes 4194304 | tf_op jit(solution)/shard_map/all_to_all | solution.py:42
  89.2 0.0 reduce-scatter.2.cloned.1.call-start
  89.2 0.0 copy-done.7
  89.3 0.0 copy-done.2
  89.3 5.5 %fusion.31 = f32[1024,2048]{1,0:T(8,128)} fusion(bf16[2048,128]{1,0:T(8,128)(2,1)S(1)} %copy-done.2, bf16[1024,1024]{1,0:T(8,128)(2,1)} %param.11, s32[]{:T(128)S(6)} %select_n.95), kind=kOutput, calls=%fused_computation.43 | convolution fusion | flops 536870912 | bytes 9175044 | tf_op jit(solution)/shard_map/dot_general | solution.py:56
  94.7 0.1 compare_select_fusion.2
  94.8 43.5 %all-to-all-done.1 = bf16[32,256,128]{2,1,0:T(8,128)(2,1)} async-done(((bf16[32,256,128]{2,1,0:T(8,128)(2,1)}), bf16[32,256,128]{2,1,0:T(8,128)(2,1)}, u32[]{:S(2)}, u32[]{:S(2)}) %all-to-all-start.1) | async-done | bytes 2097184 | tf_op jit(solution)/shard_map/all_to_all | solution.py:42
  138.3 45.6 %scatter_custom_fusion.1 = f32[2048,128]{1,0:T(8,128)} fusion(s32[8192]{0:T(1024)S(1)} %bitcast.71, bf16[8192,128]{1,0:T(8,128)(2,1)} %bitcast.15, f32[]{:T(128)} %constant.32.clone.1), kind=kCustom, calls=%fused_computation.7 | custom fusion | flops 2097152 | bytes 3145732 | tf_op jit(solution)/shard_map/scatter-add | solution.py:50
  183.9 0.0 copy-done
  183.9 8.3 %convolution_add_fusion = f32[1024,2048]{1,0:T(8,128)} fusion(f32[1024,2048]{1,0:T(8,128)} %fusion.31, bf16[1024,1024]{1,0:T(8,128)(2,1)S(1)} %copy-done, s32[]{:T(128)S(6)} %select_n.95, f32[2048,128]{1,0:T(8,128)} %scatter_custom_fusion.1, f32[2048]{0:T(1024)S(1)} %convert_element_type.35), kind=kOutput, calls=%fused_computation.6 | convolution fusion | flops 539492352 | bytes 18096132 | tf_op jit(solution)/shard_map/dot_general | solution.py:59
  192.2 0.0 reduce-scatter.2.cloned.1.call-update
  192.2 0.2 all-gather.2.cloned.1.call-start
  192.4 1.2 copy.28
  193.7 51.3 %reduce-scatter.2.cloned.1.call-done = f32[128,2048]{1,0:T(8,128)} async-done(((f32[1024,2048]{1,0:T(8,128)}), f32[128,2048]{1,0:T(8,128)}) %reduce-scatter.2.cloned.1.call-update) | async-done | bytes 1048592 | tf_op jit(solution)/shard_map/reduce_scatter | solution.py:62
  245.0 2.6 fusion.26
  247.7 0.0 all-gather.2.cloned.1.call-update
  247.7 0.1 compare_select_fusion
  247.8 34.3 %all-gather.2.cloned.1.call-done = bf16[2048,1024]{0,1:T(8,128)(2,1)} async-done(((bf16[2048,128]{0,1:T(8,128)(2,1)}), bf16[2048,1024]{0,1:T(8,128)(2,1)}) %all-gather.2.cloned.1.call-update) | async-done | bytes 4194320 | tf_op jit(solution)/shard_map/all_gather | solution.py:65
  282.1 3.6 fusion.16
  285.8 24.0 %gather_fusion.1 = bf16[8192,128]{1,0:T(8,128)(2,1)S(1)} fusion(bf16[2048,128]{1,0:T(8,128)(2,1)S(1)} %fusion.16, s32[8192]{0:T(1024)S(1)} %broadcast_clamp_fusion), kind=kCustom, calls=%fused_computation.1 | custom fusion | bytes 4227072 | tf_op jit(solution)/shard_map/jit(_take)/gather | solution.py:83
  309.8 4.6 select_select_fusion
  314.4 10.1 %all-to-all-start.2 = ((bf16[32,256,128]{2,1,0:T(8,128)(2,1)}), bf16[32,256,128]{2,1,0:T(8,128)(2,1)S(1)}, u32[]{:S(2)}, u32[]{:S(2)}) async-start(bf16[32,256,128]{2,1,0:T(8,128)(2,1)} %select_select_fusion), calls=%async_computation.3 | async-start | bytes 4194304 | tf_op jit(solution)/shard_map/all_to_all | solution.py:84
  324.5 0.0 all-reduce.3.cloned.1.call-start
  324.6 0.0 copy-start.3
  324.6 0.0 copy-start.4
  324.6 4.4 convolution_bitcast_fusion
  329.0 0.0 copy-done.3
  329.0 0.0 copy-done.4
  329.0 2.8 fusion.39
  331.8 0.0 all-reduce.3.cloned.1.call-update
  331.8 0.0 copy-done.5
  331.8 1.0 copy.31
  332.8 159.7 %all-reduce.3.cloned.1.call-done = (f32[128,1024]{0,1:T(8,128)}, f32[128,1024]{1,0:T(8,128)}) async-done(((f32[128,1024]{0,1:T(8,128)}, f32[128,1024]{1,0:T(8,128)}), (f32[128,1024]{0,1:T(8,128)}, f32[128,1024]{1,0:T(8,128)})) %all-reduce.3.cloned.1.call-update) | async-done | bytes 1048592 | tf_op jit(solution)/shard_map/psum | solution.py:72
  492.6 2.0 copy.32
  494.6 0.0 all-to-all-done.2
  494.6 3.0 gather_fusion.2
  497.7 8.4 %fusion.12 = f32[128,128,128]{1,2,0:T(8,128)} fusion(bf16[128,128,128]{2,1,0:T(8,128)(2,1)} %param.13, bf16[128,128,128]{2,1,0:T(8,128)(2,1)} %gather_fusion.2, pred[128]{0:T(512)(128)(4,1)S(1)} %compare_and_fusion.1), kind=kOutput, calls=%fused_computation.18 | convolution fusion | flops 538968064 | bytes 16777344 | tf_op jit(solution)/shard_map/kij,kid->kjd/dot_general | solution.py:87
  506.0 9.0 %copy.30 = f32[128,128,128]{2,1,0:T(8,128)} copy(f32[128,128,128]{1,2,0:T(8,128)} %fusion.12) | data formatting | bytes 16777216 | tf_op jit(solution)/shard_map/kij,kid->kjd/dot_general | solution.py:87
  515.0 0.1 broadcast_in_dim.98
  515.1 0.0 copy-done.9
  515.1 17.0 %scatter_fusion.1 = f32[16,128,128]{2,1,0:T(8,128)S(1)} fusion(f32[16,128,128]{2,1,0:T(8,128)S(1)} %broadcast_in_dim.98, s32[128]{0:T(128)S(1)} %copy-done.9, f32[128,128,128]{2,1,0:T(8,128)} %copy.30), kind=kCustom, calls=%fused_computation.5 | custom fusion | flops 2097152 | bytes 25166336 | tf_op jit(solution)/shard_map/scatter-add | solution.py:88
  532.2 0.0 copy-start.6
  532.2 0.0 copy-start.1
  532.2 4.5 fusion.15
  536.6 0.0 copy-done.6
  536.6 0.8 copy.44
  537.4 0.0 copy-done.1
  (9 shorter events, 0.1 us)
Async XLA Ops:
  7.2 176.7 %copy-start = (bf16[1024,1024]{1,0:T(8,128)(2,1)S(1)}, bf16[1024,1024]{1,0:T(8,128)(2,1)}, u32[]{:S(2)}) copy-start(bf16[1024,1024]{1,0:T(8,128)(2,1)} %param.12) | copy-start | bytes 6291460
  8.8 70.5 %all-to-all-start = ((s32[32,1,256]{2,1,0:T(1,128)}), s32[32,1,256]{2,1,0:T(1,128)S(1)}, u32[]{:S(2)}, u32[]{:S(2)}) async-start(s32[32,1,256]{2,1,0:T(1,128)} %compare_select_fusion.4), calls=%async_computation | async-start | bytes 65536 | tf_op jit(solution)/shard_map/all_to_all | solution.py:43
  45.3 2.5 copy-start.8
  74.4 14.8 %copy-start.7 = (s32[2048]{0:T(1024)S(1)}, s32[2048]{0:T(1024)}, u32[]{:S(2)}) copy-start(s32[2048]{0:T(1024)} %param.18) | copy-start | bytes 24580
  74.4 14.8 %copy-start.2 = (bf16[2048,128]{1,0:T(8,128)(2,1)S(1)}, bf16[2048,128]{1,0:T(8,128)(2,1)}, u32[]{:S(2)}) copy-start(bf16[2048,128]{1,0:T(8,128)(2,1)} %param.10) | copy-start | bytes 1572868
  79.3 59.0 %all-to-all-start.1 = ((bf16[32,256,128]{2,1,0:T(8,128)(2,1)}), bf16[32,256,128]{2,1,0:T(8,128)(2,1)}, u32[]{:S(2)}, u32[]{:S(2)}) async-start(bf16[32,256,128]{2,1,0:T(8,128)(2,1)} %fusion.2), calls=%async_computation.1 | async-start | bytes 4194304 | tf_op jit(solution)/shard_map/all_to_all | solution.py:42
  89.2 155.8 %reduce-scatter.2.cloned.1.call-start = ((), (), s32[]{:S(2)}) async-start(), calls=%async_computation.4 | async-start | bytes 9437184 | tf_op jit(solution)/shard_map/reduce_scatter | solution.py:62
  192.2 89.9 %all-gather.2.cloned.1.call-start = ((), (), s32[]{:S(2)}) async-start(), calls=%async_computation.5 | async-start | bytes 4718592 | tf_op jit(solution)/shard_map/all_gather | solution.py:65
  314.4 180.2 %all-to-all-start.2 = ((bf16[32,256,128]{2,1,0:T(8,128)(2,1)}), bf16[32,256,128]{2,1,0:T(8,128)(2,1)S(1)}, u32[]{:S(2)}, u32[]{:S(2)}) async-start(bf16[32,256,128]{2,1,0:T(8,128)(2,1)} %select_select_fusion), calls=%async_computation.3 | async-start | bytes 4194304 | tf_op jit(solution)/shard_map/all_to_all | solution.py:84
  324.5 168.0 %all-reduce.3.cloned.1.call-start = ((), (), s32[]{:S(2)}) async-start(), calls=%async_computation.6 | async-start | bytes 2097152 | tf_op jit(solution)/shard_map/psum | solution.py:72
  324.6 4.4 copy-start.3
  324.6 4.4 copy-start.4
  329.0 2.9 copy-start.5
  506.0 9.1 %copy-start.9 = (s32[128]{0:T(128)S(1)}, s32[128]{0:T(128)}, u32[]{:S(2)}) copy-start(s32[128]{0:T(128)} %param.14) | copy-start | bytes 1540
  532.2 4.5 copy-start.6
  532.2 5.3 copy-start.1
Sparse Core Ops, SparseCore 0:
  192.3 52.6 reduce-scatter.1
  247.8 34.2 all-gather.1
  331.9 160.5 all-reduce.2
where the time goes:
time: 547 us; the launch traced here: 544 us
  waiting for transfers between devices  289 us (53%)
  other arithmetic  105 us (19%)
  local copies, waits for them, and re-layouts  56.8 us (10%)
  matrix products  47.4 us (9%)
  starting transfers between devices  31.6 us (6%)
  between operations  14 us (3%)
    psum x1, waiting for transfers between devices, on_device(): grad_self, grad_neigh = lax.psum((local_self, local_neigh), 'graph')  160 us
    reduce_scatter x1, waiting for transfers between devices, on_device(): lax.psum_scatter(own_term + agg_term, 'feat', scatter_dimension=0, tiled=...  51.3 us
    scatter-add x1, other arithmetic, on_device(): neighbor_sum = jnp.zeros((node_rows, feat_cols), jnp.float32).at[target_r...  45.6 us
    all_to_all x1, waiting for transfers between devices, on_device(): lax.all_to_all(outgoing, 'graph', split_axis=0, concat_axis=0, tiled=True)  43.5 us
    all_gather x1, waiting for transfers between devices, on_device(): grad_full = lax.all_gather(grad_pre, 'feat', axis=1, tiled=True)  34.3 us
    scatter-add x1, other arithmetic, on_device(): jax.ops.segment_sum(prods, block_to_slot, num_segments=slot_total)  26.7 us
    gather x1, local copies, waits for them, and re-layouts, on_device(): jnp.take(back_rows, lookup, axis=0)  24 us
    scatter-add x1, other arithmetic, on_device(): jax.ops.segment_sum(contrib, block_source, num_segments=source_count)  17 us
  transfers between devices with their start and end apart: 6, of which 4 were waited for; matrix products, arithmetic and copies ran while one was open for 14% of the time, Pallas kernels for 0%

commit v1 on v0

v1 whole, which is shorter than its diff:
```python
import functools

import jax
import jax.numpy as jnp
from jax import lax
from jax.experimental import pallas as pl
from jax.experimental.pallas import tpu as pltpu
from jax.sharding import Mesh, PartitionSpec as P

BF16 = jnp.bfloat16
F32 = jnp.float32
VMEM_BYTES = 48 * 1024 * 1024


def params(axes=0):
    return pltpu.CompilerParams(
        dimension_semantics=("arbitrary",) * axes if axes else None, vmem_limit_bytes=VMEM_BYTES
    )


def full_spec(shape):
    return pl.BlockSpec(shape, lambda *unused: (0,) * len(shape))


def forward_blocks_kernel(
    source_ref, slot_ref, count_ref, rows_ref, feat_ref, adj_ref, low_ref, high_ref, sums_ref
):
    step = pl.program_id(0)
    chunk, blk, _ = adj_ref.shape
    parts = low_ref.shape[0]
    cols = feat_ref.shape[1]

    @pl.when(step == 0)
    def _():
        sums_ref[...] = jnp.zeros(sums_ref.shape, F32)

    for item in range(chunk):
        block = step * chunk + item
        start = pl.multiple_of(source_ref[block] * blk, blk)
        product = jnp.dot(
            adj_ref[item], feat_ref[pl.ds(start, blk), :], preferred_element_type=F32
        )
        sums_ref[slot_ref[block]] += product

    @pl.when(step == pl.num_programs(0) - 1)
    def _():
        slot_row = lax.broadcasted_iota(jnp.int32, (blk, cols), 0)
        lane = lax.broadcasted_iota(jnp.int32, (1, 2 * blk), 1)
        tile_row = lax.broadcasted_iota(jnp.int32, (16, blk), 0)

        def emit(part, carry):
            count = count_ref[part]
            low = jnp.where(slot_row < count, sums_ref[2 * part], 0.0)
            high = jnp.where(slot_row + blk < count, sums_ref[2 * part + 1], 0.0)
            low_ref[part, 0:blk, :] = low.astype(BF16)
            high_ref[part] = high.astype(BF16)
            ids = rows_ref[pl.ds(part, 1), :]
            live = lane < count
            fine = jnp.where(live, ids & (blk - 1), -1).astype(F32)
            coarse = jnp.where(live, ids >> 7, -1).astype(F32)
            tile = jnp.where(tile_row == 0, fine[:, :blk], 0.0)
            tile = jnp.where(tile_row == 1, fine[:, blk:], tile)
            tile = jnp.where(tile_row == 2, coarse[:, :blk], tile)
            tile = jnp.where(tile_row == 3, coarse[:, blk:], tile)
            low_ref[part, blk : blk + 16, :] = tile.astype(BF16)
            return carry

        lax.fori_loop(0, parts, emit, 0)


def forward_blocks(block_source, block_to_slot, counts, rows, features, adjacency):
    blocks, blk, _ = adjacency.shape
    nodes, cols = features.shape
    parts, cap = rows.shape
    chunk = 16
    return pl.pallas_call(
        forward_blocks_kernel,
        grid_spec=pltpu.PrefetchScalarGridSpec(
            num_scalar_prefetch=3,
            grid=(blocks // chunk,),
            in_specs=[
                full_spec((parts, cap)),
                full_spec((nodes, cols)),
                pl.BlockSpec((chunk, blk, blk), lambda i, *unused: (i, 0, 0)),
            ],
            out_specs=[full_spec((parts, blk + 16, cols)), full_spec((parts, blk, cols))],
            scratch_shapes=[pltpu.VMEM((parts * cap // blk, blk, cols), F32)],
        ),
        out_shape=[
            jax.ShapeDtypeStruct((parts, blk + 16, cols), BF16),
            jax.ShapeDtypeStruct((parts, blk, cols), BF16),
        ],
        compiler_params=params(1),
        name="forward_blocks",
    )(block_source, block_to_slot, counts, rows, features, adjacency)


def scatter_body(half, ids_ref, rows_ref, hot_ref, acc_ref, group):
    nodes, cols = acc_ref.shape
    blk = 128
    node_row = lax.broadcasted_iota(jnp.int32, (blk, blk), 0).astype(F32)
    for part in range(group):
        tile = ids_ref[part].astype(F32)
        fine = tile[half : half + 1, :]
        coarse = tile[2 + half : 3 + half, :]
        hot = jnp.where(node_row == fine, 1.0, 0.0).astype(BF16)
        for block in range(nodes // blk):
            keep = jnp.where(coarse == float(block), 1.0, 0.0).astype(BF16)
            hot_ref[block * blk : (block + 1) * blk, part * blk : (part + 1) * blk] = hot * keep
    rows = rows_ref[...].reshape(group * blk, cols)
    acc_ref[...] += jnp.dot(hot_ref[...], rows, preferred_element_type=F32)


def scatter_low_kernel(payload_ids_ref, rows_ref, sum_ref, hot_ref):
    @pl.when(pl.program_id(0) == 0)
    def _():
        sum_ref[...] = jnp.zeros(sum_ref.shape, F32)

    scatter_body(0, payload_ids_ref, rows_ref, hot_ref, sum_ref, rows_ref.shape[0])


def scatter_high_kernel(payload_ids_ref, rows_ref, init_ref, degree_ref, mean_ref, hot_ref, acc_ref):
    @pl.when(pl.program_id(0) == 0)
    def _():
        acc_ref[...] = init_ref[...]

    scatter_body(1, payload_ids_ref, rows_ref, hot_ref, acc_ref, rows_ref.shape[0])

    @pl.when(pl.program_id(0) == pl.num_programs(0) - 1)
    def _():
        mean_ref[...] = (acc_ref[...] / degree_ref[...]).astype(BF16)


def scatter_low(low, nodes):
    parts, height, cols = low.shape
    group, blk = 8, 128
    return pl.pallas_call(
        scatter_low_kernel,
        grid=(parts // group,),
        in_specs=[
            pl.BlockSpec((group, 16, cols), lambda i: (i, blk // 16, 0)),
            pl.BlockSpec((group, blk, cols), lambda i: (i, 0, 0)),
        ],
        out_specs=full_spec((nodes, cols)),
        out_shape=jax.ShapeDtypeStruct((nodes, cols), F32),
        scratch_shapes=[pltpu.VMEM((nodes, group * blk), BF16)],
        compiler_params=params(1),
        name="scatter_low",
    )(low, low)


def scatter_high(low, high, partial_sum, degrees):
    parts, blk, cols = high.shape
    nodes = partial_sum.shape[0]
    group = 8
    return pl.pallas_call(
        scatter_high_kernel,
        grid=(parts // group,),
        in_specs=[
            pl.BlockSpec((group, 16, cols), lambda i: (i, blk // 16, 0)),
            pl.BlockSpec((group, blk, cols), lambda i: (i, 0, 0)),
            full_spec((nodes, cols)),
            full_spec((nodes, 1)),
        ],
        out_specs=full_spec((nodes, cols)),
        out_shape=jax.ShapeDtypeStruct((nodes, cols), BF16),
        scratch_shapes=[
            pltpu.VMEM((nodes, group * blk), BF16),
            pltpu.VMEM((nodes, cols), F32),
        ],
        compiler_params=params(1),
        name="scatter_high",
    )(low, high, partial_sum, degrees)


def gather_kernel(half, fine_ref, coarse_ref, back_ref, out_ref, hot_ref):
    group, blk, cols = out_ref.shape
    nodes = back_ref.shape[0]
    lane = lax.broadcasted_iota(jnp.int32, (blk, blk), 1).astype(F32)
    for part in range(group):
        fine = jnp.broadcast_to(fine_ref[0, :, part : part + 1], (blk, blk))
        coarse = jnp.broadcast_to(coarse_ref[0, :, part : part + 1], (blk, blk))
        hot = jnp.where(lane == fine, 1.0, 0.0)
        for block in range(nodes // blk):
            value = jnp.where(coarse == float(block), hot, 0.0).astype(BF16)
            hot_ref[part * blk : (part + 1) * blk, block * blk : (block + 1) * blk] = value
    picked = jnp.dot(hot_ref[...], back_ref[...], preferred_element_type=F32)
    out_ref[...] = picked.astype(BF16).reshape(group, blk, cols)


def gather_rows(half, fine, coarse, back):
    steps, blk, group = fine.shape
    nodes, cols = back.shape
    return pl.pallas_call(
        functools.partial(gather_kernel, half),
        grid=(steps,),
        in_specs=[
            pl.BlockSpec((1, blk, group), lambda i: (i, 0, 0)),
            pl.BlockSpec((1, blk, group), lambda i: (i, 0, 0)),
            full_spec((nodes, cols)),
        ],
        out_specs=pl.BlockSpec((group, blk, cols), lambda i: (i, 0, 0)),
        out_shape=jax.ShapeDtypeStruct((steps * group, blk, cols), BF16),
        scratch_shapes=[pltpu.VMEM((group * blk, nodes), BF16)],
        compiler_params=params(1),
        name="gather_rows",
    )(fine, coarse, back)


def own_term_kernel(feat_ref, weight_ref, out_ref):
    pieces = feat_ref.shape[0]
    rows = jnp.concatenate([feat_ref[piece] for piece in range(pieces)], axis=1)
    out_ref[...] = jnp.dot(rows, weight_ref[...], preferred_element_type=F32)


def own_term(feat_pieces, w_self):
    pieces, rows, cols = feat_pieces.shape
    wide = w_self.shape[1]
    tile = 256
    return pl.pallas_call(
        own_term_kernel,
        grid=(wide // tile,),
        in_specs=[
            full_spec((pieces, rows, cols)),
            pl.BlockSpec((pieces * cols, tile), lambda i: (0, i)),
        ],
        out_specs=pl.BlockSpec((rows, tile), lambda i: (0, i)),
        out_shape=jax.ShapeDtypeStruct((rows, wide), F32),
        compiler_params=params(1),
        name="own_term",
    )(feat_pieces, w_self)


def dense_kernel(mean_ref, own_ref, cot_ref, weight_ref, degree_ref, back_ref, hidden_ref, grad_ref, acc_ref):
    step = pl.program_id(0)
    pieces, rows, cols = mean_ref.shape
    tile = weight_ref.shape[1]
    mean = jnp.concatenate([mean_ref[piece] for piece in range(pieces)], axis=1)
    pre_act = own_ref[...] + jnp.dot(mean, weight_ref[...], preferred_element_type=F32)
    sig = jax.nn.sigmoid(pre_act)
    cot = jnp.concatenate([cot_ref[piece] for piece in range(cot_ref.shape[0])], axis=1)
    slope = sig * (1.0 + pre_act * (1.0 - sig))
    grad = (cot.astype(F32) * slope).astype(BF16)
    hidden = (pre_act * sig).astype(BF16)
    grad_ref[...] = grad
    for piece in range(tile // cols):
        hidden_ref[piece] = hidden[:, piece * cols : (piece + 1) * cols]
    update = lax.dot_general(
        grad, weight_ref[...], (((1,), (1,)), ((), ())), preferred_element_type=F32
    )

    @pl.when(step == 0)
    def _():
        acc_ref[...] = update

    @pl.when(step > 0)
    def _():
        acc_ref[...] += update

    @pl.when(step == pl.num_programs(0) - 1)
    def _():
        back = (acc_ref[...] / degree_ref[...]).astype(BF16)
        for piece in range(pieces):
            back_ref[piece] = back[:, piece * cols : (piece + 1) * cols]


def dense(mean_pieces, own, cot_pieces, w_neigh, degree_rows):
    pieces, rows, cols = mean_pieces.shape
    wide = w_neigh.shape[1]
    tile = 256
    per = tile // cols
    return pl.pallas_call(
        dense_kernel,
        grid=(wide // tile,),
        in_specs=[
            full_spec((pieces, rows, cols)),
            pl.BlockSpec((rows, tile), lambda i: (0, i)),
            pl.BlockSpec((per, rows, cols), lambda i: (i, 0, 0)),
            pl.BlockSpec((pieces * cols, tile), lambda i: (0, i)),
            full_spec((rows, 1)),
        ],
        out_specs=[
            full_spec((pieces, rows, cols)),
            pl.BlockSpec((per, rows, cols), lambda i: (i, 0, 0)),
            pl.BlockSpec((rows, tile), lambda i: (0, i)),
        ],
        out_shape=[
            jax.ShapeDtypeStruct((pieces, rows, cols), BF16),
            jax.ShapeDtypeStruct((pieces, rows, cols), BF16),
            jax.ShapeDtypeStruct((rows, wide), BF16),
        ],
        scratch_shapes=[pltpu.VMEM((rows, wide), F32)],
        compiler_params=params(1),
        name="dense",
    )(mean_pieces, own, cot_pieces, w_neigh, degree_rows)


def backward_blocks_kernel(
    source_ref, slot_ref, low_ref, high_ref, adj_ref, self_ref, out_ref, both_ref, acc_ref
):
    step = pl.program_id(0)
    chunk, blk, _ = adj_ref.shape
    parts = low_ref.shape[0]

    @pl.when(step == 0)
    def _():
        acc_ref[...] = self_ref[...]
        for part in range(parts):
            both_ref[2 * part] = low_ref[part]
            both_ref[2 * part + 1] = high_ref[part]

    for item in range(chunk):
        block = step * chunk + item
        start = pl.multiple_of(source_ref[block] * blk, blk)
        product = jnp.dot(
            adj_ref[item], both_ref[slot_ref[block]], preferred_element_type=F32
        )
        acc_ref[pl.ds(start, blk), :] += product

    @pl.when(step == pl.num_programs(0) - 1)
    def _():
        out_ref[...] = acc_ref[...].astype(BF16)


def backward_blocks(block_source, block_to_slot, low, high, adjacency_t, self_grad):
    blocks, blk, _ = adjacency_t.shape
    nodes, cols = self_grad.shape
    parts = low.shape[0]
    chunk = 16
    return pl.pallas_call(
        backward_blocks_kernel,
        grid_spec=pltpu.PrefetchScalarGridSpec(
            num_scalar_prefetch=2,
            grid=(blocks // chunk,),
            in_specs=[
                full_spec((parts, blk, cols)),
                full_spec((parts, blk, cols)),
                pl.BlockSpec((chunk, blk, blk), lambda i, *unused: (i, 0, 0)),
                full_spec((nodes, cols)),
            ],
            out_specs=full_spec((nodes, cols)),
            scratch_shapes=[
                pltpu.VMEM((2 * parts, blk, cols), BF16),
                pltpu.VMEM((nodes, cols), F32),
            ],
        ),
        out_shape=jax.ShapeDtypeStruct((nodes, cols), BF16),
        compiler_params=params(1),
        name="backward_blocks",
    )(block_source, block_to_slot, low, high, adjacency_t, self_grad)


def swap(value, axis):
    return lax.all_to_all(value, axis, split_axis=0, concat_axis=0, tiled=True)


def after(value, *others):
    return lax.optimization_barrier((value, *others))[0]


def reduce_over_graph(partial):
    rows, wide = partial.shape
    over_y, over_z = lax.axis_size("y"), lax.axis_size("z")
    chunk = rows // over_y
    part = swap(partial.reshape(over_y, chunk, wide), "y").astype(F32).sum(0).astype(BF16)
    part = swap(part.reshape(over_z, chunk // over_z, wide), "z").astype(F32).sum(0).astype(BF16)
    part = swap(jnp.broadcast_to(part[None], (over_z, *part.shape)), "z").reshape(chunk, wide)
    part = swap(jnp.broadcast_to(part[None], (over_y, *part.shape)), "y").reshape(rows, wide)
    return part.astype(F32)


def on_device(
    features,
    w_self,
    w_neigh,
    adjacency,
    block_source,
    block_to_slot,
    send_rows,
    send_counts,
    degree,
    cotangent,
):
    node_rows, feat_cols = features.shape
    feat_size = lax.axis_size("feat")
    feat_at = lax.axis_index("feat")
    share = node_rows // feat_size
    graph = ("z", "y")
    low, high = forward_blocks(
        block_source, block_to_slot, send_counts[0], send_rows[0], features, adjacency
    )
    low_in = swap(low, graph)
    high_in = swap(high, graph)
    pieces = jnp.stack(
        [features.reshape(feat_size, share, feat_cols), cotangent.reshape(feat_size, share, feat_cols)],
        axis=1,
    )
    pieces = swap(after(pieces, low_in), "feat")
    degrees = degree.astype(F32)[:, None]
    degree_rows = lax.dynamic_slice_in_dim(degrees, feat_at * share, share, 0)
    adjacency_t = after(adjacency, low_in).swapaxes(1, 2)
    self_rows = lax.dynamic_slice_in_dim(w_self, feat_at * feat_cols, feat_cols, 0)

    partial_sum = scatter_low(low_in, node_rows)
    blk = adjacency.shape[1]
    parts = low.shape[0]
    ids = low_in[:, blk : blk + 4, :].astype(F32).reshape(parts // 8, 8, 4, blk).transpose(2, 0, 3, 1)
    own = own_term(pieces[:, 0], w_self)
    neighbor_mean = scatter_high(low_in, high_in, partial_sum, degrees)
    mean_pieces = swap(neighbor_mean.reshape(feat_size, share, feat_cols), "feat")
    back_pieces, hidden_pieces, grad_pre = dense(
        mean_pieces, own, pieces[:, 1], w_neigh, degree_rows
    )
    back_rows = swap(back_pieces, "feat").reshape(node_rows, feat_cols)
    grad_full = lax.all_gather(grad_pre, "feat", axis=0, tiled=True)
    back_low = swap(gather_rows(0, ids[0], ids[2], back_rows), graph)
    back_high = swap(gather_rows(1, ids[1], ids[3], back_rows), graph)
    hidden_out = swap(hidden_pieces, "feat").reshape(node_rows, feat_cols)

    both = jnp.concatenate([features, neighbor_mean], axis=1)
    weight_part = lax.dot_general(
        both, grad_full, (((0,), (0,)), ((), ())), preferred_element_type=F32
    ).astype(BF16)
    weight_grads = reduce_over_graph(weight_part)
    self_grad = lax.dot_general(
        grad_full, self_rows, (((1,), (1,)), ((), ())), preferred_element_type=F32
    )
    grad_features = backward_blocks(
        block_source, block_to_slot, back_low, back_high, adjacency_t, self_grad
    )
    return hidden_out, grad_features, weight_grads[:feat_cols], weight_grads[feat_cols:]


def solution(mesh):
    split = Mesh(mesh.devices.reshape(8, 4, 8), ("z", "y", "feat"))
    graph = ("z", "y")
    placed = (
        P(graph, "feat"),
        P(),
        P(),
        P(graph, None, None),
        P(graph),
        P(graph),
        P(graph, None, None),
        P(graph, None),
        P(graph),
        P(graph, "feat"),
    )
    return jax.shard_map(
        on_device,
        mesh=split,
        in_specs=placed,
        out_specs=(P(graph, "feat"), P(graph, "feat"), P("feat", None), P("feat", None)),
        check_vma=False,
    )
```

time: 547 us -> 317 us (0.58)
  waiting for transfers between devices: 289 us -> 106 us
  other arithmetic: 105 us -> 2.92 us
  blocking collectives: 0 us -> 70.9 us
  Pallas kernels: 0 us -> 44.6 us
  matrix products: 47.4 us -> 7.92 us
  local copies, waits for them, and re-layouts: 56.8 us -> 23.3 us
  starting transfers between devices: 31.6 us -> 43.4 us
    psum x1 -> x0, waiting for transfers between devices: 160 us -> none  [on_device(): grad_self, grad_neigh = lax.psum((local_self, local_neigh), 'graph')]
    scatter-add x3 -> x0, other arithmetic: 89.2 us -> none  [the longest x1 45.6 us: on_device(): neighbor_sum = jnp.zeros((node_rows, feat_cols), jnp.float32).at[target_r...]
    all_to_all x0 -> x3, blocking collectives: none -> 70.9 us  [swap(): return lax.all_to_all(value, axis, split_axis=0, concat_axis=0, tiled=True)]
    reduce_scatter x1 -> x0, waiting for transfers between devices: 51.3 us -> none  [on_device(): lax.psum_scatter(own_term + agg_term, 'feat', scatter_dimension=0, tiled=...]
    all_to_all x3 -> x9, waiting for transfers between devices: 43.5 us -> 88.2 us  [swap(): return lax.all_to_all(value, axis, split_axis=0, concat_axis=0, tiled=True)]
    pallas_call x0 -> x8, Pallas kernels: none -> 44.6 us  [the longest x2 13 us: gather_rows(): pl.pallas_call(functools.partial(gather_kernel, half), grid=(steps,), in_...]
    dot_general x7 -> x1, matrix products: 42.9 us -> 4.43 us  [on_device(): lax.dot_general(both, grad_full, (((0,), (0,)), ((), ())), preferred_elem...]
    gather x3 -> x0, local copies, waits for them, and re-layouts: 31.1 us -> none  [the longest x1 24 us: on_device(): jnp.take(back_rows, lookup, axis=0)]
  transfers between devices with their start and end apart: 6 -> 10, of which waited for: 4 -> 8; matrix products, arithmetic and copies ran while one was open for 14% -> 6% of each run, Pallas kernels for 0% -> 11%
where the time goes in v1:
time: 317 us; the launch traced here: 314 us
  waiting for transfers between devices  106 us (33%)
  blocking collectives  70.9 us (22%)
  Pallas kernels  44.6 us (14%)
  starting transfers between devices  43.4 us (14%)
  local copies, waits for them, and re-layouts  23.3 us (7%)
  between operations  14.3 us (5%)
  matrix products  7.92 us (2%)
    all_to_all x9, waiting for transfers between devices, swap(): return lax.all_to_all(value, axis, split_axis=0, concat_axis=0, tiled=True)  88.2 us
    all_to_all x3, blocking collectives, swap(): return lax.all_to_all(value, axis, split_axis=0, concat_axis=0, tiled=True)  70.9 us
    all_to_all x9, starting transfers between devices, swap(): return lax.all_to_all(value, axis, split_axis=0, concat_axis=0, tiled=True)  43.4 us
    all_gather x1, waiting for transfers between devices, on_device(): grad_full = lax.all_gather(grad_pre, 'feat', axis=0, tiled=True)  18.2 us
    pallas_call x2, Pallas kernels, gather_rows(): pl.pallas_call(functools.partial(gather_kernel, half), grid=(steps,), in_...  13 us
    unnamed x39, local copies, waits for them, and re-layouts  12 us
    pallas_call x1, Pallas kernels, backward_blocks(): pl.pallas_call(backward_blocks_kernel, grid_spec=pltpu.PrefetchScalarGrid...  7.47 us
    pallas_call x1, Pallas kernels, forward_blocks(): pl.pallas_call(forward_blocks_kernel, grid_spec=pltpu.PrefetchScalarGridS...  7.42 us
  transfers between devices with their start and end apart: 10, of which 8 were waited for; matrix products, arithmetic and copies ran while one was open for 6% of the time, Pallas kernels for 11%

profile of v1, /device:TPU:32, one launch (start us, length us, event | category | flops | bytes accessed | tf_op | source)
XLA Modules:
  0.0 313.8 jit_solution(7032050685415176574)
XLA Ops:
  7.2 0.0 copy-start.5
  7.2 1.0 copy-done.5
  8.2 0.8 copy-done.11
  9.0 0.7 copy-done.12
  9.6 0.7 copy-done.14
  10.3 0.7 copy-done.16
  10.9 7.4 %forward_blocks.1 = (bf16[32,144,128]{2,1,0:T(8,128)(2,1)S(1)}, bf16[32,128,128]{2,1,0:T(8,128)(2,1)S(1)}) custom-call(s32[128]{0:T(128)S(1)} %copy-done.12, s32[128]{0:T(128)S(1)} %copy-done.14, s32[32]{0:T(128)S(1)} %bitcast.41, s32[32,256]{1,0:T(8,128)S(1)} %bitcast.40, bf16[2048,128]{1,0:T(8,128)(2,1)S(1)} %copy-done.5, bf16[128,128,128]{2,1,0:T(8,128)(2,1)} %adj_ref.1), custom_call_target="tpu_custom_call" | custom-call | tf_op jit(solution)/shard_map/forward_blocks/pallas_call | solution.py:76
  18.4 0.0 copy-start.7
  18.4 0.0 copy-start.18
  18.4 43.3 %all_to_all.60.payload_ids_ref.rows_ref = bf16[32,144,128]{2,1,0:T(8,128)(2,1)S(1)} all-to-all(bf16[32,144,128]{2,1,0:T(8,128)(2,1)S(1)} %get-tuple-element.11), channel_id=1, replica_groups=mesh['z'=8,'y'=4,'feat'=8] {'z','y'}, dimensions={0} | all-to-all | bytes 2359296 | tf_op jit(solution)/shard_map/all_to_all | solution.py:354
  61.7 4.8 %all-to-all-start.1 = ((bf16[32,128,128]{2,1,0:T(8,128)(2,1)}), bf16[32,128,128]{2,1,0:T(8,128)(2,1)S(1)}, u32[]{:S(2)}, u32[]{:S(2)}) async-start(bf16[32,128,128]{2,1,0:T(8,128)(2,1)} %copy-done.7), calls=%async_computation.1 | async-start | bytes 2097152 | tf_op jit(solution)/shard_map/all_to_all | solution.py:354
  66.5 1.1 pad_maximum_fusion
  67.6 25.2 %all-to-all-done.1.rows_ref = bf16[32,128,128]{2,1,0:T(8,128)(2,1)S(1)} async-done(((bf16[32,128,128]{2,1,0:T(8,128)(2,1)}), bf16[32,128,128]{2,1,0:T(8,128)(2,1)S(1)}, u32[]{:S(2)}, u32[]{:S(2)}) %all-to-all-start.1) | async-done | bytes 1048608 | tf_op jit(solution)/shard_map/all_to_all | solution.py:354
  92.8 4.4 %all-to-all-start.3 = ((bf16[8,2,256,128]{3,2,1,0:T(8,128)(2,1)}), bf16[8,2,256,128]{3,2,1,0:T(8,128)(2,1)}, u32[]{:S(2)}, u32[]{:S(2)}) async-start(bf16[8,2,256,128]{3,2,1,0:T(8,128)(2,1)} %pad_maximum_fusion), calls=%async_computation.3 | async-start | bytes 2097152 | tf_op jit(solution)/shard_map/all_to_all | solution.py:354
  97.2 0.4 copy.34.degree_ref
  97.6 5.4 %scatter_low.1.init_ref = f32[2048,128]{1,0:T(8,128)S(1)} custom-call(bf16[32,144,128]{2,1,0:T(8,128)(2,1)S(1)} %all_to_all.60.payload_ids_ref.rows_ref, bf16[32,144,128]{2,1,0:T(8,128)(2,1)S(1)} %all_to_all.60.payload_ids_ref.rows_ref), custom_call_target="tpu_custom_call" | custom-call | tf_op jit(solution)/shard_map/scatter_low/pallas_call | solution.py:137
  103.0 5.7 %scatter_high.1 = bf16[2048,128]{1,0:T(8,128)(2,1)S(1)} custom-call(bf16[32,144,128]{2,1,0:T(8,128)(2,1)S(1)} %all_to_all.60.payload_ids_ref.rows_ref, bf16[32,128,128]{2,1,0:T(8,128)(2,1)S(1)} %all-to-all-done.1.rows_ref, f32[2048,128]{1,0:T(8,128)S(1)} %scatter_low.1.init_ref, f32[2048,1]{1,0:T(8,128)S(1)} %copy.34.degree_ref), custom_call_target="tpu_custom_call" | custom-call | tf_op jit(solution)/shard_map/scatter_high/pallas_call | solution.py:156
  108.7 0.0 copy-start.1
  108.7 0.8 copy-done.1
  109.5 3.8 %all-to-all-done.3 = bf16[8,2,256,128]{3,2,1,0:T(8,128)(2,1)} async-done(((bf16[8,2,256,128]{3,2,1,0:T(8,128)(2,1)}), bf16[8,2,256,128]{3,2,1,0:T(8,128)(2,1)}, u32[]{:S(2)}, u32[]{:S(2)}) %all-to-all-start.3) | async-done | bytes 1048608 | tf_op jit(solution)/shard_map/all_to_all | solution.py:354
  113.2 3.5 %all-to-all-start.2 = ((bf16[8,256,128]{2,1,0:T(8,128)(2,1)}), bf16[8,256,128]{2,1,0:T(8,128)(2,1)S(1)}, u32[]{:S(2)}, u32[]{:S(2)}) async-start(bf16[8,256,128]{2,1,0:T(8,128)(2,1)} %bitcast.38), calls=%async_computation.2 | async-start | bytes 1048576 | tf_op jit(solution)/shard_map/all_to_all | solution.py:354
  116.7 0.0 all-gather.2.cloned.1.call-start
  116.8 0.1 dynamic-slice.3
  116.9 0.1 copy.37.degree_ref
  117.0 2.1 slice_bitcast_fusion
  119.1 1.6 copy-done
  120.7 1.6 own_term.1.own_ref
  122.3 0.0 copy-start.2
  122.3 4.7 %all-to-all-done.2.mean_ref = bf16[8,256,128]{2,1,0:T(8,128)(2,1)S(1)} async-done(((bf16[8,256,128]{2,1,0:T(8,128)(2,1)}), bf16[8,256,128]{2,1,0:T(8,128)(2,1)S(1)}, u32[]{:S(2)}, u32[]{:S(2)}) %all-to-all-start.2) | async-done | bytes 524320 | tf_op jit(solution)/shard_map/all_to_all | solution.py:354
  127.0 1.6 copy-done.3
  128.6 1.0 copy-done.4
  129.6 4.0 %dense.1 = (bf16[8,256,128]{2,1,0:T(8,128)(2,1)S(1)}, bf16[8,256,128]{2,1,0:T(8,128)(2,1)S(1)}, bf16[256,1024]{1,0:T(8,128)(2,1)S(1)}) custom-call(bf16[8,256,128]{2,1,0:T(8,128)(2,1)S(1)} %all-to-all-done.2.mean_ref, f32[256,1024]{1,0:T(8,128)S(1)} %own_term.1.own_ref, bf16[8,256,128]{2,1,0:T(8,128)(2,1)S(1)} %copy-done.4, ...), custom_call_target="tpu_custom_call" | custom-call | tf_op jit(solution)/shard_map/dense/pallas_call | solution.py:272
  133.7 0.0 copy-start.8
  133.7 0.8 copy-done.8
  134.5 0.8 copy-done.9
  135.3 0.8 copy-done.10
  136.1 0.0 all-gather.2.cloned.1.call-update
  136.1 15.9 %all_to_all.61 = bf16[8,256,128]{2,1,0:T(8,128)(2,1)S(1)} all-to-all(bf16[8,256,128]{2,1,0:T(8,128)(2,1)} %copy-done.10), channel_id=1, replica_groups=mesh['z'=8,'y'=4,'feat'=8] {'feat'}, dimensions={0} | all-to-all | bytes 1048576 | tf_op jit(solution)/shard_map/all_to_all | solution.py:354
  152.0 3.5 %all-to-all-start.5 = ((bf16[8,256,128]{2,1,0:T(8,128)(2,1)}), bf16[8,256,128]{2,1,0:T(8,128)(2,1)S(1)}, u32[]{:S(2)}, u32[]{:S(2)}) async-start(bf16[8,256,128]{2,1,0:T(8,128)(2,1)} %copy-done.8), calls=%async_computation.5 | async-start | bytes 1048576 | tf_op jit(solution)/shard_map/all_to_all | solution.py:354
  155.5 18.2 %all-gather.2.cloned.1.call-done = bf16[2048,1024]{1,0:T(8,128)(2,1)} async-done(((bf16[256,1024]{1,0:T(8,128)(2,1)}), bf16[2048,1024]{1,0:T(8,128)(2,1)}) %all-gather.2.cloned.1.call-update) | async-done | bytes 4194320 | tf_op jit(solution)/shard_map/all_gather | solution.py:415
  173.7 4.4 %convolution_convert_fusion = bf16[256,1024]{1,0:T(8,128)(2,1)} fusion(bf16[2048,1024]{1,0:T(8,128)(2,1)} %all-gather.2.cloned.1.call-done, bf16[2048,128]{1,0:T(8,128)(2,1)S(1)} %copy-done.2, bf16[2048,128]{1,0:T(8,128)(2,1)} %feat_ref.1), kind=kOutput, calls=%fused_computation | convolution fusion | flops 1076101120 | bytes 5767168 | tf_op jit(solution)/shard_map/dot_general | solution.py:421
  178.1 0.0 all-to-all-done.5
  178.1 4.1 %all-to-all-start.8 = ((bf16[4,64,1024]{2,1,0:T(8,128)(2,1)}), bf16[4,64,1024]{2,1,0:T(8,128)(2,1)}, u32[]{:S(2)}, u32[]{:S(2)}) async-start(bf16[4,64,1024]{2,1,0:T(8,128)(2,1)} %bitcast.46), calls=%async_computation.8 | async-start | bytes 1048576 | tf_op jit(solution)/shard_map/all_to_all | solution.py:354
  182.3 0.2 copy.39
  182.5 0.1 slice_bitcast_fusion.2
  182.6 6.5 %gather_rows.2 = bf16[32,128,128]{2,1,0:T(8,128)(2,1)} custom-call(f32[4,128,8]{2,1,0:T(8,128)S(1)} %get-tuple-element.21.fine_ref, f32[4,128,8]{2,1,0:T(8,128)S(1)} %get-tuple-element.20.coarse_ref, bf16[2048,128]{1,0:T(8,128)(2,1)S(1)} %bitcast.36), custom_call_target="tpu_custom_call" | custom-call | tf_op jit(solution)/shard_map/gather_rows/pallas_call | solution.py:194
  189.1 3.4 %all-to-all-done.8 = bf16[4,64,1024]{2,1,0:T(8,128)(2,1)} async-done(((bf16[4,64,1024]{2,1,0:T(8,128)(2,1)}), bf16[4,64,1024]{2,1,0:T(8,128)(2,1)}, u32[]{:S(2)}, u32[]{:S(2)}) %all-to-all-start.8) | async-done | bytes 524320 | tf_op jit(solution)/shard_map/all_to_all | solution.py:354
  192.5 6.5 %all-to-all-start.6 = ((bf16[32,128,128]{2,1,0:T(8,128)(2,1)}), bf16[32,128,128]{2,1,0:T(8,128)(2,1)S(1)}, u32[]{:S(2)}, u32[]{:S(2)}) async-start(bf16[32,128,128]{2,1,0:T(8,128)(2,1)} %gather_rows.2), calls=%async_computation.6 | async-start | bytes 2097152 | tf_op jit(solution)/shard_map/all_to_all | solution.py:354
  199.1 1.8 reduce_sum.24
  200.9 25.2 %all-to-all-done.6.low_ref = bf16[32,128,128]{2,1,0:T(8,128)(2,1)S(1)} async-done(((bf16[32,128,128]{2,1,0:T(8,128)(2,1)}), bf16[32,128,128]{2,1,0:T(8,128)(2,1)S(1)}, u32[]{:S(2)}, u32[]{:S(2)}) %all-to-all-start.6) | async-done | bytes 1048608 | tf_op jit(solution)/shard_map/all_to_all | solution.py:354
  226.1 4.8 %all-to-all-start.9 = ((bf16[8,8,1024]{2,1,0:T(8,128)(2,1)}), bf16[8,8,1024]{2,1,0:T(8,128)(2,1)S(1)}, u32[]{:S(2)}, u32[]{:S(2)}) async-start(bf16[8,8,1024]{2,1,0:T(8,128)(2,1)} %bitcast.20), calls=%async_computation.9 | async-start | bytes 262144 | tf_op jit(solution)/shard_map/all_to_all | solution.py:354
  230.8 6.5 %gather_rows.3 = bf16[32,128,128]{2,1,0:T(8,128)(2,1)} custom-call(f32[4,128,8]{2,1,0:T(8,128)S(1)} %get-tuple-element.19.fine_ref, f32[4,128,8]{2,1,0:T(8,128)S(1)} %get-tuple-element.18.coarse_ref, bf16[2048,128]{1,0:T(8,128)(2,1)S(1)} %bitcast.37), custom_call_target="tpu_custom_call" | custom-call | tf_op jit(solution)/shard_map/gather_rows/pallas_call | solution.py:194
  237.3 1.1 all-to-all-done.9
  238.5 8.2 %all-to-all-start.7 = ((bf16[32,128,128]{2,1,0:T(8,128)(2,1)}), bf16[32,128,128]{2,1,0:T(8,128)(2,1)S(1)}, u32[]{:S(2)}, u32[]{:S(2)}) async-start(bf16[32,128,128]{2,1,0:T(8,128)(2,1)} %gather_rows.3), calls=%async_computation.7 | async-start | bytes 2097152 | tf_op jit(solution)/shard_map/all_to_all | solution.py:354
  246.7 24.8 %all-to-all-done.7.high_ref = bf16[32,128,128]{2,1,0:T(8,128)(2,1)S(1)} async-done(((bf16[32,128,128]{2,1,0:T(8,128)(2,1)}), bf16[32,128,128]{2,1,0:T(8,128)(2,1)S(1)}, u32[]{:S(2)}, u32[]{:S(2)}) %all-to-all-start.7) | async-done | bytes 1048608 | tf_op jit(solution)/shard_map/all_to_all | solution.py:354
  271.5 11.8 %all_to_all.62 = bf16[8,8,1024]{2,1,0:T(8,128)(2,1)S(1)} all-to-all(bf16[8,8,1024]{2,1,0:T(8,128)(2,1)S(1)} %broadcast_in_dim.17), channel_id=1, replica_groups=mesh['z'=8,'y'=4,'feat'=8] {'z'}, dimensions={0} | all-to-all | bytes 262144 | tf_op jit(solution)/shard_map/all_to_all | solution.py:354
  283.2 0.9 broadcast_in_dim.19
  284.1 3.5 %all-to-all-start.11 = ((bf16[4,64,1024]{2,1,0:T(8,128)(2,1)}), bf16[4,64,1024]{2,1,0:T(8,128)(2,1)S(1)}, u32[]{:S(2)}, u32[]{:S(2)}) async-start(bf16[4,64,1024]{2,1,0:T(8,128)(2,1)} %broadcast_in_dim.19), calls=%async_computation.11 | async-start | bytes 1048576 | tf_op jit(solution)/shard_map/all_to_all | solution.py:354
  287.6 6.4 %copy.40 = bf16[128,128,128]{1,2,0:T(8,128)(2,1)} copy(bf16[128,128,128]{2,1,0:T(8,128)(2,1)} %adj_ref.1) | data formatting | bytes 8388608 | tf_op jit(solution)/shard_map/optimization_barrier | solution.py:358
  294.1 3.5 %fusion.3.self_ref = f32[2048,128]{1,0:T(8,128)S(1)} fusion(bf16[2048,1024]{1,0:T(8,128)(2,1)} %all-gather.2.cloned.1.call-done, bf16[1024,1024]{1,0:T(8,128)(2,1)} %weight_ref.2, s32[]{:T(128)S(6)} %select_n.7), kind=kOutput, calls=%fused_computation.11 | convolution fusion | flops 536870912 | bytes 5505028 | tf_op jit(solution)/shard_map/dot_general | solution.py:425
  297.6 7.5 %backward_blocks.1 = bf16[2048,128]{1,0:T(8,128)(2,1)} custom-call(s32[128]{0:T(128)S(1)} %copy-done.13, s32[128]{0:T(128)S(1)} %copy-done.15, bf16[32,128,128]{2,1,0:T(8,128)(2,1)S(1)} %all-to-all-done.6.low_ref, bf16[32,128,128]{2,1,0:T(8,128)(2,1)S(1)} %all-to-all-done.7.high_ref, bf16[128,128,128]{2,1,0:T(8,128)(2,1)} %bitcast.42, ...), custom_call_target="tpu_custom_call" | custom-call | tf_op jit(solution)/shard_map/backward_blocks/pallas_call | solution.py:330
  305.1 0.0 all-to-all-done.11
  305.1 1.1 fusion.7
  306.1 0.8 copy.46
  (24 shorter events, 0.1 us)
Async XLA Ops:
  7.2 1.0 copy-start.5
  8.2 0.8 copy-start.11
  9.0 0.7 copy-start.12
  9.6 0.7 copy-start.14
  10.3 0.7 copy-start.16
  10.9 55.5 %copy-start.6 = (bf16[2048,128]{1,0:T(8,128)(2,1)S(1)}, bf16[2048,128]{1,0:T(8,128)(2,1)}, u32[]{:S(2)}) copy-start(bf16[2048,128]{1,0:T(8,128)(2,1)} %feat_ref.1) | copy-start | bytes 1572868
  10.9 55.5 %copy-start.17 = (bf16[2048,128]{1,0:T(8,128)(2,1)S(1)}, bf16[2048,128]{1,0:T(8,128)(2,1)}, u32[]{:S(2)}) copy-start(bf16[2048,128]{1,0:T(8,128)(2,1)} %param.19) | copy-start | bytes 1572868
  18.4 43.3 %copy-start.7 = (bf16[32,128,128]{2,1,0:T(8,128)(2,1)}, bf16[32,128,128]{2,1,0:T(8,128)(2,1)S(1)}, u32[]{:S(2)}) copy-start(bf16[32,128,128]{2,1,0:T(8,128)(2,1)S(1)} %get-tuple-element.12) | copy-start | bytes 3145732
  18.4 78.8 %copy-start.18 = (s32[2048]{0:T(1024)S(1)}, s32[2048]{0:T(1024)}, u32[]{:S(2)}) copy-start(s32[2048]{0:T(1024)} %param.18) | copy-start | bytes 24580
  61.7 31.1 %all-to-all-start.1 = ((bf16[32,128,128]{2,1,0:T(8,128)(2,1)}), bf16[32,128,128]{2,1,0:T(8,128)(2,1)S(1)}, u32[]{:S(2)}, u32[]{:S(2)}) async-start(bf16[32,128,128]{2,1,0:T(8,128)(2,1)} %copy-done.7), calls=%async_computation.1 | async-start | bytes 2097152 | tf_op jit(solution)/shard_map/all_to_all | solution.py:354
  92.8 20.5 %all-to-all-start.3 = ((bf16[8,2,256,128]{3,2,1,0:T(8,128)(2,1)}), bf16[8,2,256,128]{3,2,1,0:T(8,128)(2,1)}, u32[]{:S(2)}, u32[]{:S(2)}) async-start(bf16[8,2,256,128]{3,2,1,0:T(8,128)(2,1)} %pad_maximum_fusion), calls=%async_computation.3 | async-start | bytes 2097152 | tf_op jit(solution)/shard_map/all_to_all | solution.py:354
  108.7 0.8 copy-start.1
  113.2 13.8 %all-to-all-start.2 = ((bf16[8,256,128]{2,1,0:T(8,128)(2,1)}), bf16[8,256,128]{2,1,0:T(8,128)(2,1)S(1)}, u32[]{:S(2)}, u32[]{:S(2)}) async-start(bf16[8,256,128]{2,1,0:T(8,128)(2,1)} %bitcast.38), calls=%async_computation.2 | async-start | bytes 1048576 | tf_op jit(solution)/shard_map/all_to_all | solution.py:354
  116.7 56.9 %all-gather.2.cloned.1.call-start = ((), (), s32[]{:S(2)}) async-start(), calls=%async_computation.12 | async-start | bytes 4718592 | tf_op jit(solution)/shard_map/all_gather | solution.py:415
  119.1 1.6 copy-start
  122.3 51.4 %copy-start.2 = (bf16[2048,128]{1,0:T(8,128)(2,1)S(1)}, bf16[2048,128]{1,0:T(8,128)(2,1)}, u32[]{:S(2)}) copy-start(bf16[2048,128]{1,0:T(8,128)(2,1)} %copy-done.1) | copy-start | bytes 1572868
  127.0 1.6 copy-start.3
  128.6 1.0 copy-start.4
  133.7 0.8 copy-start.8
  134.5 0.8 copy-start.9
  135.3 0.8 copy-start.10
  152.0 26.1 %all-to-all-start.5 = ((bf16[8,256,128]{2,1,0:T(8,128)(2,1)}), bf16[8,256,128]{2,1,0:T(8,128)(2,1)S(1)}, u32[]{:S(2)}, u32[]{:S(2)}) async-start(bf16[8,256,128]{2,1,0:T(8,128)(2,1)} %copy-done.8), calls=%async_computation.5 | async-start | bytes 1048576 | tf_op jit(solution)/shard_map/all_to_all | solution.py:354
  178.1 14.4 %all-to-all-start.8 = ((bf16[4,64,1024]{2,1,0:T(8,128)(2,1)}), bf16[4,64,1024]{2,1,0:T(8,128)(2,1)}, u32[]{:S(2)}, u32[]{:S(2)}) async-start(bf16[4,64,1024]{2,1,0:T(8,128)(2,1)} %bitcast.46), calls=%async_computation.8 | async-start | bytes 1048576 | tf_op jit(solution)/shard_map/all_to_all | solution.py:354
  192.5 33.5 %all-to-all-start.6 = ((bf16[32,128,128]{2,1,0:T(8,128)(2,1)}), bf16[32,128,128]{2,1,0:T(8,128)(2,1)S(1)}, u32[]{:S(2)}, u32[]{:S(2)}) async-start(bf16[32,128,128]{2,1,0:T(8,128)(2,1)} %gather_rows.2), calls=%async_computation.6 | async-start | bytes 2097152 | tf_op jit(solution)/shard_map/all_to_all | solution.py:354
  226.1 12.4 %all-to-all-start.9 = ((bf16[8,8,1024]{2,1,0:T(8,128)(2,1)}), bf16[8,8,1024]{2,1,0:T(8,128)(2,1)S(1)}, u32[]{:S(2)}, u32[]{:S(2)}) async-start(bf16[8,8,1024]{2,1,0:T(8,128)(2,1)} %bitcast.20), calls=%async_computation.9 | async-start | bytes 262144 | tf_op jit(solution)/shard_map/all_to_all | solution.py:354
  238.5 33.0 %all-to-all-start.7 = ((bf16[32,128,128]{2,1,0:T(8,128)(2,1)}), bf16[32,128,128]{2,1,0:T(8,128)(2,1)S(1)}, u32[]{:S(2)}, u32[]{:S(2)}) async-start(bf16[32,128,128]{2,1,0:T(8,128)(2,1)} %gather_rows.3), calls=%async_computation.7 | async-start | bytes 2097152 | tf_op jit(solution)/shard_map/all_to_all | solution.py:354
  284.1 21.0 %all-to-all-start.11 = ((bf16[4,64,1024]{2,1,0:T(8,128)(2,1)}), bf16[4,64,1024]{2,1,0:T(8,128)(2,1)S(1)}, u32[]{:S(2)}, u32[]{:S(2)}) async-start(bf16[4,64,1024]{2,1,0:T(8,128)(2,1)} %broadcast_in_dim.19), calls=%async_computation.11 | async-start | bytes 1048576 | tf_op jit(solution)/shard_map/all_to_all | solution.py:354
  294.1 3.5 %copy-start.13 = (s32[128]{0:T(128)S(1)}, s32[128]{0:T(128)}, u32[]{:S(2)}) copy-start(s32[128]{0:T(128)} %source_ref.3) | copy-start | bytes 1540
  294.1 3.5 %copy-start.15 = (s32[128]{0:T(128)S(1)}, s32[128]{0:T(128)}, u32[]{:S(2)}) copy-start(s32[128]{0:T(128)} %slot_ref.3) | copy-start | bytes 1540
Sparse Core Ops, SparseCore 0:
  136.2 37.4 all-gather.1

commit v2 on v1

--- a/solution.py
+++ b/solution.py
@@ -207,31 +207,36 @@
     )(fine, coarse, back)
 
 
-def own_term_kernel(feat_ref, weight_ref, out_ref):
+def own_term_kernel(at_ref, feat_ref, weight_ref, out_ref):
     pieces = feat_ref.shape[0]
     rows = jnp.concatenate([feat_ref[piece] for piece in range(pieces)], axis=1)
     out_ref[...] = jnp.dot(rows, weight_ref[...], preferred_element_type=F32)
 
 
-def own_term(feat_pieces, w_self):
-    pieces, rows, cols = feat_pieces.shape
+def own_term(at, feat_all, w_self, share):
+    pieces, _, cols = feat_all.shape
     wide = w_self.shape[1]
     tile = 256
     return pl.pallas_call(
         own_term_kernel,
-        grid=(wide // tile,),
-        in_specs=[
-            full_spec((pieces, rows, cols)),
-            pl.BlockSpec((pieces * cols, tile), lambda i: (0, i)),
-        ],
-        out_specs=pl.BlockSpec((rows, tile), lambda i: (0, i)),
-        out_shape=jax.ShapeDtypeStruct((rows, wide), F32),
+        grid_spec=pltpu.PrefetchScalarGridSpec(
+            num_scalar_prefetch=1,
+            grid=(wide // tile,),
+            in_specs=[
+                pl.BlockSpec((pieces, share, cols), lambda i, at: (0, at[0], 0)),
+                pl.BlockSpec((pieces * cols, tile), lambda i, at: (0, i)),
+            ],
+            out_specs=pl.BlockSpec((share, tile), lambda i, at: (0, i)),
+        ),
+        out_shape=jax.ShapeDtypeStruct((share, wide), F32),
         compiler_params=params(1),
         name="own_term",
-    )(feat_pieces, w_self)
-
-
-def dense_kernel(mean_ref, own_ref, cot_ref, weight_ref, degree_ref, back_ref, hidden_ref, grad_ref, acc_ref):
+    )(at, feat_all, w_self)
+
+
+def dense_kernel(
+    at_ref, mean_ref, own_ref, cot_ref, weight_ref, degree_ref, back_ref, hidden_ref, grad_ref, acc_ref
+):
     step = pl.program_id(0)
     pieces, rows, cols = mean_ref.shape
     tile = weight_ref.shape[1]
@@ -264,35 +269,38 @@
             back_ref[piece] = back[:, piece * cols : (piece + 1) * cols]
 
 
-def dense(mean_pieces, own, cot_pieces, w_neigh, degree_rows):
+def dense(at, mean_pieces, own, cot_all, w_neigh, degrees):
     pieces, rows, cols = mean_pieces.shape
     wide = w_neigh.shape[1]
     tile = 256
     per = tile // cols
     return pl.pallas_call(
         dense_kernel,
-        grid=(wide // tile,),
-        in_specs=[
-            full_spec((pieces, rows, cols)),
-            pl.BlockSpec((rows, tile), lambda i: (0, i)),
-            pl.BlockSpec((per, rows, cols), lambda i: (i, 0, 0)),
-            pl.BlockSpec((pieces * cols, tile), lambda i: (0, i)),
-            full_spec((rows, 1)),
-        ],
-        out_specs=[
-            full_spec((pieces, rows, cols)),
-            pl.BlockSpec((per, rows, cols), lambda i: (i, 0, 0)),
-            pl.BlockSpec((rows, tile), lambda i: (0, i)),
-        ],
+        grid_spec=pltpu.PrefetchScalarGridSpec(
+            num_scalar_prefetch=1,
+            grid=(wide // tile,),
+            in_specs=[
+                full_spec((pieces, rows, cols)),
+                pl.BlockSpec((rows, tile), lambda i, at: (0, i)),
+                pl.BlockSpec((per, rows, cols), lambda i, at: (i, at[0], 0)),
+                pl.BlockSpec((pieces * cols, tile), lambda i, at: (0, i)),
+                pl.BlockSpec((rows, 1), lambda i, at: (at[0], 0)),
+            ],
+            out_specs=[
+                full_spec((pieces, rows, cols)),
+                pl.BlockSpec((per, rows, cols), lambda i, at: (i, 0, 0)),
+                pl.BlockSpec((rows, tile), lambda i, at: (0, i)),
+            ],
+            scratch_shapes=[pltpu.VMEM((rows, wide), F32)],
+        ),
         out_shape=[
             jax.ShapeDtypeStruct((pieces, rows, cols), BF16),
             jax.ShapeDtypeStruct((pieces, rows, cols), BF16),
             jax.ShapeDtypeStruct((rows, wide), BF16),
         ],
-        scratch_shapes=[pltpu.VMEM((rows, wide), F32)],
         compiler_params=params(1),
         name="dense",
-    )(mean_pieces, own, cot_pieces, w_neigh, degree_rows)
+    )(at, mean_pieces, own, cot_all, w_neigh, degrees)
 
 
 def backward_blocks_kernel(
@@ -358,15 +366,76 @@
     return lax.optimization_barrier((value, *others))[0]
 
 
+def rotate(value, axis, distance):
+    size = lax.axis_size(axis)
+    return lax.ppermute(value, axis, [(i, (i + distance) % size) for i in range(size)])
+
+
+def scatter_sum(pieces, axis):
+    size, at = lax.axis_size(axis), lax.axis_index(axis)
+    take = functools.partial(lax.dynamic_index_in_dim, pieces, axis=0, keepdims=False)
+    total = take(at).astype(F32)
+    came = [rotate(take((at + d) % size), axis, d) for d in range(1, size)]
+    for piece in came:
+        total = total + piece.astype(F32)
+    return total.astype(BF16)
+
+
+def around(piece, axis):
+    size = lax.axis_size(axis)
+    return [piece] + [rotate(piece, axis, size - i) for i in range(1, size)]
+
+
+def unroll_pieces(pieces, axis):
+    size, at = lax.axis_size(axis), lax.axis_index(axis)
+    doubled = jnp.stack(pieces + pieces)
+    return lax.dynamic_slice_in_dim(doubled, (size - at) % size, size, 0)
+
+
+def assemble_kernel(at_ref, *refs):
+    *piece_refs, first_ref, second_ref = refs
+    size = len(piece_refs)
+    half = size // 2
+    for i, piece_ref in enumerate(piece_refs):
+        place = (at_ref[0] + i) % size
+        value = piece_ref[...].astype(F32)
+
+        @pl.when(place < half)
+        def _():
+            first_ref[place] = value
+
+        @pl.when(place >= half)
+        def _():
+            second_ref[place - half] = value
+
+
+def assemble(at, pieces):
+    rows, wide = pieces[0].shape
+    half = len(pieces) // 2
+    first, second = pl.pallas_call(
+        assemble_kernel,
+        grid_spec=pltpu.PrefetchScalarGridSpec(
+            num_scalar_prefetch=1,
+            grid=(1,),
+            in_specs=[full_spec((rows, wide))] * len(pieces),
+            out_specs=[full_spec((half, rows, wide))] * 2,
+        ),
+        out_shape=[jax.ShapeDtypeStruct((half, rows, wide), F32)] * 2,
+        compiler_params=params(1),
+        name="assemble",
+    )(at, *pieces)
+    return first.reshape(half * rows, wide), second.reshape(half * rows, wide)
+
+
 def reduce_over_graph(partial):
     rows, wide = partial.shape
     over_y, over_z = lax.axis_size("y"), lax.axis_size("z")
     chunk = rows // over_y
-    part = swap(partial.reshape(over_y, chunk, wide), "y").astype(F32).sum(0).astype(BF16)
-    part = swap(part.reshape(over_z, chunk // over_z, wide), "z").astype(F32).sum(0).astype(BF16)
-    part = swap(jnp.broadcast_to(part[None], (over_z, *part.shape)), "z").reshape(chunk, wide)
-    part = swap(jnp.broadcast_to(part[None], (over_y, *part.shape)), "y").reshape(rows, wide)
-    return part.astype(F32)
+    part = scatter_sum(partial.reshape(over_y, chunk, wide), "y")
+    part = scatter_sum(part.reshape(over_z, chunk // over_z, wide), "z")
+    part = unroll_pieces(around(part, "z"), "z").reshape(chunk, wide)
+    at = jnp.full((1,), lax.axis_index("y"), jnp.int32)
+    return assemble(at, around(part, "y"))
 
 
 def on_device(
@@ -384,6 +453,7 @@
     node_rows, feat_cols = features.shape
     feat_size = lax.axis_size("feat")
     feat_at = lax.axis_index("feat")
+    at = jnp.full((1,), feat_at, jnp.int32)
     share = node_rows // feat_size
     graph = ("z", "y")
     low, high = forward_blocks(
@@ -391,13 +461,9 @@
     )
     low_in = swap(low, graph)
     high_in = swap(high, graph)
-    pieces = jnp.stack(
-        [features.reshape(feat_size, share, feat_cols), cotangent.reshape(feat_size, share, feat_cols)],
-        axis=1,
-    )
-    pieces = swap(after(pieces, low_in), "feat")
+    feat_all = lax.all_gather(features, "feat", axis=0)
+    cot_all = lax.all_gather(cotangent, "feat", axis=0)
     degrees = degree.astype(F32)[:, None]
-    degree_rows = lax.dynamic_slice_in_dim(degrees, feat_at * share, share, 0)
     adjacency_t = after(adjacency, low_in).swapaxes(1, 2)
     self_rows = lax.dynamic_slice_in_dim(w_self, feat_at * feat_cols, feat_cols, 0)
 
@@ -405,30 +471,39 @@
     blk = adjacency.shape[1]
     parts = low.shape[0]
     ids = low_in[:, blk : blk + 4, :].astype(F32).reshape(parts // 8, 8, 4, blk).transpose(2, 0, 3, 1)
-    own = own_term(pieces[:, 0], w_self)
+    own = own_term(at, feat_all, w_self, share)
+    partial_sum, adjacency_t, ids, own = lax.optimization_barrier(
+        (partial_sum, adjacency_t, ids, own)
+    )
     neighbor_mean = scatter_high(low_in, high_in, partial_sum, degrees)
     mean_pieces = swap(neighbor_mean.reshape(feat_size, share, feat_cols), "feat")
-    back_pieces, hidden_pieces, grad_pre = dense(
-        mean_pieces, own, pieces[:, 1], w_neigh, degree_rows
-    )
+    back_pieces, hidden_pieces, grad_pre = dense(at, mean_pieces, own, cot_all, w_neigh, degrees)
     back_rows = swap(back_pieces, "feat").reshape(node_rows, feat_cols)
+    back_rows, grad_pre, hidden_pieces = lax.optimization_barrier(
+        (back_rows, grad_pre, hidden_pieces)
+    )
+    rows_low = gather_rows(0, ids[0], ids[2], back_rows)
+    rows_high = gather_rows(1, ids[1], ids[3], back_rows)
+    back_low = swap(rows_low, graph)
+    back_high = swap(rows_high, graph)
     grad_full = lax.all_gather(grad_pre, "feat", axis=0, tiled=True)
-    back_low = swap(gather_rows(0, ids[0], ids[2], back_rows), graph)
-    back_high = swap(gather_rows(1, ids[1], ids[3], back_rows), graph)
-    hidden_out = swap(hidden_pieces, "feat").reshape(node_rows, feat_cols)
+    grad_full = after(grad_full, rows_low, rows_high)
 
     both = jnp.concatenate([features, neighbor_mean], axis=1)
     weight_part = lax.dot_general(
         both, grad_full, (((0,), (0,)), ((), ())), preferred_element_type=F32
     ).astype(BF16)
-    weight_grads = reduce_over_graph(weight_part)
+    hidden_all = lax.all_gather(after(hidden_pieces, weight_part), "feat", axis=0)
+    hidden_out = lax.dynamic_index_in_dim(hidden_all, feat_at, 1, keepdims=False)
+    hidden_out = hidden_out.reshape(node_rows, feat_cols)
+    grad_self, grad_neigh = reduce_over_graph(weight_part)
     self_grad = lax.dot_general(
         grad_full, self_rows, (((1,), (1,)), ((), ())), preferred_element_type=F32
     )
     grad_features = backward_blocks(
         block_source, block_to_slot, back_low, back_high, adjacency_t, self_grad
     )
-    return hidden_out, grad_features, weight_grads[:feat_cols], weight_grads[feat_cols:]
+    return hidden_out, grad_features, grad_self, grad_neigh
 
 
 def solution(mesh):

time: 317 us -> 285 us (0.90)
  waiting for transfers between devices: 106 us -> 68.1 us
  starting transfers between devices: 43.4 us -> 66 us
  blocking collectives: 70.9 us -> 56.1 us
  Pallas kernels: 44.6 us -> 50.4 us
    all_to_all x9 -> x4, waiting for transfers between devices: 88.2 us -> 31.4 us  [swap(): return lax.all_to_all(value, axis, split_axis=0, concat_axis=0, tiled=True)]
    ppermute x0 -> x20, starting transfers between devices: none -> 43.5 us  [rotate(): lax.ppermute(value, axis, [(i, (i + distance) % size) for i in range(size)])]
    all_to_all x9 -> x4, starting transfers between devices: 43.4 us -> 22.4 us  [swap(): return lax.all_to_all(value, axis, split_axis=0, concat_axis=0, tiled=True)]
    ppermute x0 -> x20, waiting for transfers between devices: none -> 18.1 us  [rotate(): lax.ppermute(value, axis, [(i, (i + distance) % size) for i in range(size)])]
    all_to_all x3 -> x2, blocking collectives: 70.9 us -> 56.1 us  [swap(): return lax.all_to_all(value, axis, split_axis=0, concat_axis=0, tiled=True)]
    pallas_call x2 -> x3, Pallas kernels: 5.6 us -> 10.5 us  [the longest x1 5.91 us: dense(): pl.pallas_call(dense_kernel, grid_spec=pltpu.PrefetchScalarGridSpec(num_s...]
    unnamed x39 -> x48, local copies, waits for them, and re-layouts: 12 us -> 10.6 us
  transfers between devices with their start and end apart: 10 -> 28, of which waited for: 8 -> 9; matrix products, arithmetic and copies ran while one was open for 6% -> 4% of each run, Pallas kernels for 11% -> 16%
where the time goes in v2:
time: 285 us; the launch traced here: 282 us
  waiting for transfers between devices  68.1 us (24%)
  starting transfers between devices  66 us (23%)
  blocking collectives  56.1 us (20%)
  Pallas kernels  50.4 us (18%)
  local copies, waits for them, and re-layouts  20.6 us (7%)
  between operations  14.2 us (5%)
  matrix products  6.93 us (2%)
    all_to_all x2, blocking collectives, swap(): return lax.all_to_all(value, axis, split_axis=0, concat_axis=0, tiled=True)  56.1 us
    ppermute x20, starting transfers between devices, rotate(): lax.ppermute(value, axis, [(i, (i + distance) % size) for i in range(size)])  43.5 us
    all_to_all x4, waiting for transfers between devices, swap(): return lax.all_to_all(value, axis, split_axis=0, concat_axis=0, tiled=True)  31.4 us
    all_to_all x4, starting transfers between devices, swap(): return lax.all_to_all(value, axis, split_axis=0, concat_axis=0, tiled=True)  22.4 us
    ppermute x20, waiting for transfers between devices, rotate(): lax.ppermute(value, axis, [(i, (i + distance) % size) for i in range(size)])  18.1 us
    all_gather x1, waiting for transfers between devices, on_device(): grad_full = lax.all_gather(grad_pre, 'feat', axis=0, tiled=True)  17.2 us
    pallas_call x2, Pallas kernels, gather_rows(): pl.pallas_call(functools.partial(gather_kernel, half), grid=(steps,), in_...  13 us
    unnamed x48, local copies, waits for them, and re-layouts  10.6 us
  transfers between devices with their start and end apart: 28, of which 9 were waited for; matrix products, arithmetic and copies ran while one was open for 4% of the time, Pallas kernels for 16%

profile of v2, /device:TPU:32, one launch (start us, length us, event | category | flops | bytes accessed | tf_op | source)
XLA Modules:
  0.0 282.4 jit_solution(8258056183807622346)
XLA Ops:
  7.2 0.7 all-gather.10.cloned.1.call-update
  7.9 0.7 all-gather.12.cloned.1.call-update
  8.7 1.0 copy-done.7
  9.7 0.8 copy-done.9
  10.5 0.7 copy-done.10
  11.1 0.7 copy-done.12
  11.8 0.7 copy-done.14
  12.4 8.4 %forward_blocks.1 = (bf16[32,144,128]{2,1,0:T(8,128)(2,1)S(1)}, bf16[32,128,128]{2,1,0:T(8,128)(2,1)}) custom-call(s32[128]{0:T(128)S(1)} %copy-done.10, s32[128]{0:T(128)S(1)} %copy-done.12, s32[32]{0:T(128)S(1)} %bitcast.87, s32[32,256]{1,0:T(8,128)S(1)} %bitcast.86, bf16[2048,128]{1,0:T(8,128)(2,1)S(1)} %copy-done.7, bf16[128,128,128]{2,1,0:T(8,128)(2,1)} %adj_ref.1), custom_call_target="tpu_custom_call" | custom-call | tf_op jit(solution)/shard_map/forward_blocks/pallas_call | solution.py:76
  20.8 43.1 %all_to_all.30.payload_ids_ref.rows_ref = bf16[32,144,128]{2,1,0:T(8,128)(2,1)S(1)} all-to-all(bf16[32,144,128]{2,1,0:T(8,128)(2,1)S(1)} %get-tuple-element.21), channel_id=1, replica_groups=mesh['z'=8,'y'=4,'feat'=8] {'z','y'}, dimensions={0} | all-to-all | bytes 2359296 | tf_op jit(solution)/shard_map/all_to_all | solution.py:362
  63.9 4.8 %all-to-all-start.1 = ((bf16[32,128,128]{2,1,0:T(8,128)(2,1)}), bf16[32,128,128]{2,1,0:T(8,128)(2,1)S(1)}, u32[]{:S(2)}, u32[]{:S(2)}) async-start(bf16[32,128,128]{2,1,0:T(8,128)(2,1)} %get-tuple-element.22), calls=%async_computation.1 | async-start | bytes 2097152 | tf_op jit(solution)/shard_map/all_to_all | solution.py:362
  68.8 0.4 copy.28.degree_ref
  69.1 6.4 %copy.25 = bf16[128,128,128]{1,2,0:T(8,128)(2,1)} copy(bf16[128,128,128]{2,1,0:T(8,128)(2,1)} %adj_ref.1) | data formatting | bytes 8388608 | tf_op jit(solution)/shard_map/optimization_barrier | solution.py:366
  75.6 1.2 copy.27
  76.8 5.4 %scatter_low.1.init_ref = f32[2048,128]{1,0:T(8,128)S(1)} custom-call(bf16[32,144,128]{2,1,0:T(8,128)(2,1)S(1)} %all_to_all.30.payload_ids_ref.rows_ref, bf16[32,144,128]{2,1,0:T(8,128)(2,1)S(1)} %all_to_all.30.payload_ids_ref.rows_ref), custom_call_target="tpu_custom_call" | custom-call | tf_op jit(solution)/shard_map/scatter_low/pallas_call | solution.py:137
  82.2 1.0 copy-done
  83.2 1.6 copy-done.4
  84.8 2.6 own_term.1.own_ref
  87.4 1.0 copy-done.2
  88.3 6.8 %all-to-all-done.1.rows_ref = bf16[32,128,128]{2,1,0:T(8,128)(2,1)S(1)} async-done(((bf16[32,128,128]{2,1,0:T(8,128)(2,1)}), bf16[32,128,128]{2,1,0:T(8,128)(2,1)S(1)}, u32[]{:S(2)}, u32[]{:S(2)}) %all-to-all-start.1) | async-done | bytes 1048608 | tf_op jit(solution)/shard_map/all_to_all | solution.py:362
  95.1 1.2 copy-done.1
  96.3 5.7 %scatter_high.1 = bf16[2048,128]{1,0:T(8,128)(2,1)S(1)} custom-call(bf16[32,144,128]{2,1,0:T(8,128)(2,1)S(1)} %all_to_all.30.payload_ids_ref.rows_ref, bf16[32,128,128]{2,1,0:T(8,128)(2,1)S(1)} %all-to-all-done.1.rows_ref, f32[2048,128]{1,0:T(8,128)S(1)} %copy-done.1, f32[2048,1]{1,0:T(8,128)S(1)} %copy.28.degree_ref), custom_call_target="tpu_custom_call" | custom-call | tf_op jit(solution)/shard_map/scatter_high/pallas_call | solution.py:156
  102.0 0.8 copy-done.5
  102.8 4.3 %all-to-all-start.2 = ((bf16[8,256,128]{2,1,0:T(8,128)(2,1)}), bf16[8,256,128]{2,1,0:T(8,128)(2,1)S(1)}, u32[]{:S(2)}, u32[]{:S(2)}) async-start(bf16[8,256,128]{2,1,0:T(8,128)(2,1)} %bitcast.85), calls=%async_computation.2 | async-start | bytes 1048576 | tf_op jit(solution)/shard_map/all_to_all | solution.py:362
  107.2 10.3 %all-to-all-done.2.mean_ref = bf16[8,256,128]{2,1,0:T(8,128)(2,1)S(1)} async-done(((bf16[8,256,128]{2,1,0:T(8,128)(2,1)}), bf16[8,256,128]{2,1,0:T(8,128)(2,1)S(1)}, u32[]{:S(2)}, u32[]{:S(2)}) %all-to-all-start.2) | async-done | bytes 524320 | tf_op jit(solution)/shard_map/all_to_all | solution.py:362
  117.5 1.2 copy-done.3
  118.7 5.9 %dense.1 = (bf16[8,256,128]{2,1,0:T(8,128)(2,1)S(1)}, bf16[8,256,128]{2,1,0:T(8,128)(2,1)}, bf16[256,1024]{1,0:T(8,128)(2,1)}) custom-call(s32[1]{0:T(128)} %bitcast.at_ref, bf16[8,256,128]{2,1,0:T(8,128)(2,1)S(1)} %all-to-all-done.2.mean_ref, f32[256,1024]{1,0:T(8,128)S(1)} %copy-done.3, bf16[8,2048,128]{2,1,0:T(8,128)(2,1)} %bitcast.89, ...), custom_call_target="tpu_custom_call" | custom-call | tf_op jit(solution)/shard_map/dense/pallas_call | solution.py:277
  124.6 12.9 %all_to_all.31 = bf16[8,256,128]{2,1,0:T(8,128)(2,1)S(1)} all-to-all(bf16[8,256,128]{2,1,0:T(8,128)(2,1)S(1)} %get-tuple-element.26), channel_id=1, replica_groups=mesh['z'=8,'y'=4,'feat'=8] {'feat'}, dimensions={0} | all-to-all | bytes 1048576 | tf_op jit(solution)/shard_map/all_to_all | solution.py:362
  137.7 6.5 %gather_rows.3 = bf16[32,128,128]{2,1,0:T(8,128)(2,1)} custom-call(f32[4,128,8]{2,1,0:T(8,128)S(1)} %get-tuple-element.41.fine_ref, f32[4,128,8]{2,1,0:T(8,128)S(1)} %get-tuple-element.40.coarse_ref, bf16[2048,128]{1,0:T(8,128)(2,1)S(1)} %bitcast.83), custom_call_target="tpu_custom_call" | custom-call | tf_op jit(solution)/shard_map/gather_rows/pallas_call | solution.py:194
  144.2 6.5 %gather_rows.2 = bf16[32,128,128]{2,1,0:T(8,128)(2,1)} custom-call(f32[4,128,8]{2,1,0:T(8,128)S(1)} %get-tuple-element.43.fine_ref, f32[4,128,8]{2,1,0:T(8,128)S(1)} %get-tuple-element.42.coarse_ref, bf16[2048,128]{1,0:T(8,128)(2,1)S(1)} %bitcast.84), custom_call_target="tpu_custom_call" | custom-call | tf_op jit(solution)/shard_map/gather_rows/pallas_call | solution.py:194
  150.7 17.2 %all-gather.8.cloned.1.call-done = bf16[2048,1024]{1,0:T(8,128)(2,1)} async-done(((bf16[256,1024]{1,0:T(8,128)(2,1)}), bf16[2048,1024]{1,0:T(8,128)(2,1)}) %all-gather.8.cloned.1.call-update) | async-done | bytes 4194320 | tf_op jit(solution)/shard_map/all_gather | solution.py:489
  167.9 3.5 %convolution_convert_fusion = bf16[256,1024]{1,0:T(8,128)(2,1)S(1)} fusion(bf16[2048,1024]{1,0:T(8,128)(2,1)} %all-gather.8.cloned.1.call-done, bf16[2048,128]{1,0:T(8,128)(2,1)S(1)} %copy-done.6, bf16[2048,128]{1,0:T(8,128)(2,1)S(1)} %copy-done.8), kind=kOutput, calls=%fused_computation | convolution fusion | flops 1076101120 | bytes 5767168 | tf_op jit(solution)/shard_map/dot_general | solution.py:493
  171.5 1.5 collective-permute-start
  173.0 2.7 collective-permute-start.1
  175.7 1.4 collective-permute-start.2
  177.2 1.3 collective-permute-done
  178.4 3.7 %collective-permute-done.1 = bf16[64,1024]{1,0:T(8,128)(2,1)S(1)} collective-permute-done((bf16[64,1024]{1,0:T(8,128)(2,1)S(1)}, bf16[64,1024]{1,0:T(8,128)(2,1)S(1)}, u32[]{:S(2)}, u32[]{:S(2)}) %collective-permute-start.1) | collective-permute-done | bytes 131104 | tf_op jit(solution)/shard_map/ppermute | solution.py:371
  182.2 0.1 fusion.8
  182.3 1.6 collective-permute-start.3
  183.9 3.8 %collective-permute-start.4 = (bf16[8,1024]{1,0:T(8,128)(2,1)S(1)}, bf16[8,1024]{1,0:T(8,128)(2,1)S(1)}, u32[]{:S(2)}, u32[]{:S(2)}) collective-permute-start(bf16[8,1024]{1,0:T(8,128)(2,1)S(1)} %get-tuple-element.53), channel_id=1, source_target_pairs={{0,64},{32,96},{64,128},{96,160},{128,192},{160,224},{192,0},{224,... | collective-permute-start | bytes 49160 | tf_op jit(solution)/shard_map/ppermute | solution.py:371
  187.7 0.8 collective-permute-start.5
  188.5 2.9 %collective-permute-start.6 = (bf16[8,1024]{1,0:T(8,128)(2,1)S(1)}, bf16[8,1024]{1,0:T(8,128)(2,1)S(1)}, u32[]{:S(2)}, u32[]{:S(2)}) collective-permute-start(bf16[8,1024]{1,0:T(8,128)(2,1)S(1)} %get-tuple-element.51), channel_id=1, source_target_pairs={{0,128},{32,160},{64,192},{96,224},{128,0},{160,32},{192,64},{224,... | collective-permute-start | bytes 49160 | tf_op jit(solution)/shard_map/ppermute | solution.py:371
  191.4 1.7 collective-permute-start.7
  193.1 2.7 collective-permute-start.8
  195.8 2.6 collective-permute-start.9
  198.4 5.5 %all-to-all-start.5 = ((bf16[32,128,128]{2,1,0:T(8,128)(2,1)}), bf16[32,128,128]{2,1,0:T(8,128)(2,1)S(1)}, u32[]{:S(2)}, u32[]{:S(2)}) async-start(bf16[32,128,128]{2,1,0:T(8,128)(2,1)} %gather_rows.3), calls=%async_computation.5 | async-start | bytes 2097152 | tf_op jit(solution)/shard_map/all_to_all | solution.py:362
  204.0 0.3 collective-permute-start.10
  204.4 3.9 %collective-permute-start.11 = (bf16[8,1024]{1,0:T(8,128)(2,1)S(1)}, bf16[8,1024]{1,0:T(8,128)(2,1)S(1)}, u32[]{:S(2)}, u32[]{:S(2)}) collective-permute-start(bf16[8,1024]{1,0:T(8,128)(2,1)S(1)} %get-tuple-element.39), channel_id=1, source_target_pairs={{0,192},{32,224},{64,0},{96,32},{128,64},{160,96},{192,128},{224,1... | collective-permute-start | bytes 49160 | tf_op jit(solution)/shard_map/ppermute | solution.py:371
  208.3 2.3 collective-permute-start.12
  210.6 2.7 collective-permute-start.13
  213.4 2.3 collective-permute-start.14
  215.7 10.1 %collective-permute-done.10 = bf16[8,1024]{1,0:T(8,128)(2,1)S(1)} collective-permute-done((bf16[8,1024]{1,0:T(8,128)(2,1)S(1)}, bf16[8,1024]{1,0:T(8,128)(2,1)S(1)}, u32[]{:S(2)}, u32[]{:S(2)}) %collective-permute-start.10) | collective-permute-done | bytes 16416 | tf_op jit(solution)/shard_map/ppermute | solution.py:371
  225.8 4.9 %collective-permute-start.15 = (bf16[8,1024]{1,0:T(8,128)(2,1)S(1)}, bf16[8,1024]{1,0:T(8,128)(2,1)S(1)}, u32[]{:S(2)}, u32[]{:S(2)}) collective-permute-start(bf16[8,1024]{1,0:T(8,128)(2,1)S(1)} %get-tuple-element.39), channel_id=1, source_target_pairs={{0,64},{32,96},{64,128},{96,160},{128,192},{160,224},{192,0},{224,... | collective-permute-start | bytes 49160 | tf_op jit(solution)/shard_map/ppermute | solution.py:371
  230.7 0.7 collective-permute-start.16
  231.5 0.7 collective-permute-done.15
  232.1 2.3 collective-permute-done.16
  234.4 7.7 %all-to-all-start.4 = ((bf16[32,128,128]{2,1,0:T(8,128)(2,1)}), bf16[32,128,128]{2,1,0:T(8,128)(2,1)S(1)}, u32[]{:S(2)}, u32[]{:S(2)}) async-start(bf16[32,128,128]{2,1,0:T(8,128)(2,1)} %gather_rows.2), calls=%async_computation.4 | async-start | bytes 2097152 | tf_op jit(solution)/shard_map/all_to_all | solution.py:362
  242.3 2.8 collective-permute-start.17
  245.0 0.9 collective-permute-start.18
  245.9 0.9 collective-permute-start.19
  246.7 3.5 %fusion.6.self_ref = f32[2048,128]{1,0:T(8,128)S(1)} fusion(bf16[2048,1024]{1,0:T(8,128)(2,1)} %all-gather.8.cloned.1.call-done, bf16[1024,1024]{1,0:T(8,128)(2,1)} %weight_ref.2, s32[]{:T(128)S(6)} %select_n.96), kind=kOutput, calls=%fused_computation.8 | convolution fusion | flops 536870912 | bytes 5505028 | tf_op jit(solution)/shard_map/dot_general | solution.py:500
  250.2 14.4 %all-to-all-done.4.low_ref = bf16[32,128,128]{2,1,0:T(8,128)(2,1)S(1)} async-done(((bf16[32,128,128]{2,1,0:T(8,128)(2,1)}), bf16[32,128,128]{2,1,0:T(8,128)(2,1)S(1)}, u32[]{:S(2)}, u32[]{:S(2)}) %all-to-all-start.4) | async-done | bytes 1048608 | tf_op jit(solution)/shard_map/all_to_all | solution.py:362
  264.6 7.5 %backward_blocks.1 = bf16[2048,128]{1,0:T(8,128)(2,1)} custom-call(s32[128]{0:T(128)S(1)} %copy-done.11, s32[128]{0:T(128)S(1)} %copy-done.13, bf16[32,128,128]{2,1,0:T(8,128)(2,1)S(1)} %all-to-all-done.4.low_ref, bf16[32,128,128]{2,1,0:T(8,128)(2,1)S(1)} %all-to-all-done.5.high_ref, bf16[128,128,128]{2,1,0:T(8,128)(2,1)} %bitcast.88, ...), custom_call_target="tpu_custom_call" | custom-call | tf_op jit(solution)/shard_map/backward_blocks/pallas_call | solution.py:338
  272.0 2.0 assemble.1
  274.0 1.9 constant_dynamic-slice_fusion
  (70 shorter events, 0.5 us)
Async XLA Ops:
  7.2 76.0 %all-gather.10.cloned.1.call-start = ((), (), s32[]{:S(2)}) async-start(), calls=%async_computation.7 | async-start | bytes 4718592 | tf_op jit(solution)/shard_map/all_gather | solution.py:464
  7.9 99.3 %all-gather.12.cloned.1.call-start = ((), (), s32[]{:S(2)}) async-start(), calls=%async_computation.8 | async-start | bytes 4718592 | tf_op jit(solution)/shard_map/all_gather | solution.py:465
  8.6 1.0 copy-start.7
  9.7 0.8 copy-start.9
  10.5 0.7 copy-start.10
  11.1 0.7 copy-start.12
  11.8 0.7 copy-start.14
  12.4 56.3 %copy-start.16 = (s32[2048]{0:T(1024)S(1)}, s32[2048]{0:T(1024)}, u32[]{:S(2)}) copy-start(s32[2048]{0:T(1024)} %param.18) | copy-start | bytes 24580
  63.9 31.2 %all-to-all-start.1 = ((bf16[32,128,128]{2,1,0:T(8,128)(2,1)}), bf16[32,128,128]{2,1,0:T(8,128)(2,1)S(1)}, u32[]{:S(2)}, u32[]{:S(2)}) async-start(bf16[32,128,128]{2,1,0:T(8,128)(2,1)} %get-tuple-element.22), calls=%async_computation.1 | async-start | bytes 2097152 | tf_op jit(solution)/shard_map/all_to_all | solution.py:362
  82.2 1.0 copy-start
  83.2 1.6 copy-start.4
  87.3 1.0 copy-start.2
  95.1 1.2 copy-start.1
  102.0 0.8 copy-start.5
  102.8 14.7 %all-to-all-start.2 = ((bf16[8,256,128]{2,1,0:T(8,128)(2,1)}), bf16[8,256,128]{2,1,0:T(8,128)(2,1)S(1)}, u32[]{:S(2)}, u32[]{:S(2)}) async-start(bf16[8,256,128]{2,1,0:T(8,128)(2,1)} %bitcast.85), calls=%async_computation.2 | async-start | bytes 1048576 | tf_op jit(solution)/shard_map/all_to_all | solution.py:362
  107.1 60.8 %all-gather.8.cloned.1.call-start = ((), (), s32[]{:S(2)}) async-start(), calls=%async_computation.6 | async-start | bytes 4718592 | tf_op jit(solution)/shard_map/all_gather | solution.py:489
  117.5 1.2 copy-start.3
  118.7 18.9 %copy-start.15 = (f32[4,8,4,128]{1,3,0,2:T(8,128)S(1)}, f32[4,8,4,128]{1,3,0,2:T(8,128)}, u32[]{:S(2)}) copy-start(f32[4,8,4,128]{1,3,0,2:T(8,128)} %copy.27) | copy-start | bytes 196612
  124.6 43.3 %copy-start.6 = (bf16[2048,128]{1,0:T(8,128)(2,1)S(1)}, bf16[2048,128]{1,0:T(8,128)(2,1)}, u32[]{:S(2)}) copy-start(bf16[2048,128]{1,0:T(8,128)(2,1)} %copy-done.5) | copy-start | bytes 1572868
  124.6 43.3 %copy-start.8 = (bf16[2048,128]{1,0:T(8,128)(2,1)S(1)}, bf16[2048,128]{1,0:T(8,128)(2,1)}, u32[]{:S(2)}) copy-start(bf16[2048,128]{1,0:T(8,128)(2,1)} %feat_ref.1) | copy-start | bytes 1572868
  137.6 136.5 %all-gather.14.cloned.1.call-start = ((), (), s32[]{:S(2)}) async-start(), calls=%async_computation.9 | async-start | bytes 4718592 | tf_op jit(solution)/shard_map/all_gather | solution.py:496
  171.5 6.9 %collective-permute-start = (bf16[64,1024]{1,0:T(8,128)(2,1)S(1)}, bf16[64,1024]{1,0:T(8,128)(2,1)S(1)}, u32[]{:S(2)}, u32[]{:S(2)}) collective-permute-start(bf16[64,1024]{1,0:T(8,128)(2,1)S(1)} %get-tuple-element.44), channel_id=1, source_target_pairs={{0,8},{8,16},{16,24},{24,0},{1,9},{9,17},{17,25},{25,1},{2,10},{10... | collective-permute-start | bytes 393224 | tf_op jit(solution)/shard_map/ppermute | solution.py:371
  173.0 9.2 %collective-permute-start.1 = (bf16[64,1024]{1,0:T(8,128)(2,1)S(1)}, bf16[64,1024]{1,0:T(8,128)(2,1)S(1)}, u32[]{:S(2)}, u32[]{:S(2)}) collective-permute-start(bf16[64,1024]{1,0:T(8,128)(2,1)S(1)} %get-tuple-element.46), channel_id=1, source_target_pairs={{0,16},{8,24},{16,0},{24,8},{1,17},{9,25},{17,1},{25,9},{2,18},{10... | collective-permute-start | bytes 393224 | tf_op jit(solution)/shard_map/ppermute | solution.py:371
  175.7 6.4 %collective-permute-start.2 = (bf16[64,1024]{1,0:T(8,128)(2,1)S(1)}, bf16[64,1024]{1,0:T(8,128)(2,1)S(1)}, u32[]{:S(2)}, u32[]{:S(2)}) collective-permute-start(bf16[64,1024]{1,0:T(8,128)(2,1)S(1)} %get-tuple-element.45), channel_id=1, source_target_pairs={{0,24},{8,0},{16,8},{24,16},{1,25},{9,1},{17,9},{25,17},{2,26},{10... | collective-permute-start | bytes 393224 | tf_op jit(solution)/shard_map/ppermute | solution.py:371
  182.3 10.8 %collective-permute-start.3 = (bf16[8,1024]{1,0:T(8,128)(2,1)S(1)}, bf16[8,1024]{1,0:T(8,128)(2,1)S(1)}, u32[]{:S(2)}, u32[]{:S(2)}) collective-permute-start(bf16[8,1024]{1,0:T(8,128)(2,1)S(1)} %get-tuple-element.47), channel_id=1, source_target_pairs={{0,32},{32,64},{64,96},{96,128},{128,160},{160,192},{192,224},{224... | collective-permute-start | bytes 49160 | tf_op jit(solution)/shard_map/ppermute | solution.py:371
  183.9 11.9 %collective-permute-start.4 = (bf16[8,1024]{1,0:T(8,128)(2,1)S(1)}, bf16[8,1024]{1,0:T(8,128)(2,1)S(1)}, u32[]{:S(2)}, u32[]{:S(2)}) collective-permute-start(bf16[8,1024]{1,0:T(8,128)(2,1)S(1)} %get-tuple-element.53), channel_id=1, source_target_pairs={{0,64},{32,96},{64,128},{96,160},{128,192},{160,224},{192,0},{224,... | collective-permute-start | bytes 49160 | tf_op jit(solution)/shard_map/ppermute | solution.py:371
  187.7 16.3 %collective-permute-start.5 = (bf16[8,1024]{1,0:T(8,128)(2,1)S(1)}, bf16[8,1024]{1,0:T(8,128)(2,1)S(1)}, u32[]{:S(2)}, u32[]{:S(2)}) collective-permute-start(bf16[8,1024]{1,0:T(8,128)(2,1)S(1)} %get-tuple-element.52), channel_id=1, source_target_pairs={{0,96},{32,128},{64,160},{96,192},{128,224},{160,0},{192,32},{224,... | collective-permute-start | bytes 49160 | tf_op jit(solution)/shard_map/ppermute | solution.py:371
  188.5 15.5 %collective-permute-start.6 = (bf16[8,1024]{1,0:T(8,128)(2,1)S(1)}, bf16[8,1024]{1,0:T(8,128)(2,1)S(1)}, u32[]{:S(2)}, u32[]{:S(2)}) collective-permute-start(bf16[8,1024]{1,0:T(8,128)(2,1)S(1)} %get-tuple-element.51), channel_id=1, source_target_pairs={{0,128},{32,160},{64,192},{96,224},{128,0},{160,32},{192,64},{224,... | collective-permute-start | bytes 49160 | tf_op jit(solution)/shard_map/ppermute | solution.py:371
  191.4 12.6 %collective-permute-start.7 = (bf16[8,1024]{1,0:T(8,128)(2,1)S(1)}, bf16[8,1024]{1,0:T(8,128)(2,1)S(1)}, u32[]{:S(2)}, u32[]{:S(2)}) collective-permute-start(bf16[8,1024]{1,0:T(8,128)(2,1)S(1)} %get-tuple-element.50), channel_id=1, source_target_pairs={{0,160},{32,192},{64,224},{96,0},{128,32},{160,64},{192,96},{224,1... | collective-permute-start | bytes 49160 | tf_op jit(solution)/shard_map/ppermute | solution.py:371
  193.1 10.9 %collective-permute-start.8 = (bf16[8,1024]{1,0:T(8,128)(2,1)S(1)}, bf16[8,1024]{1,0:T(8,128)(2,1)S(1)}, u32[]{:S(2)}, u32[]{:S(2)}) collective-permute-start(bf16[8,1024]{1,0:T(8,128)(2,1)S(1)} %get-tuple-element.49), channel_id=1, source_target_pairs={{0,192},{32,224},{64,0},{96,32},{128,64},{160,96},{192,128},{224,1... | collective-permute-start | bytes 49160 | tf_op jit(solution)/shard_map/ppermute | solution.py:371
  195.8 8.2 %collective-permute-start.9 = (bf16[8,1024]{1,0:T(8,128)(2,1)S(1)}, bf16[8,1024]{1,0:T(8,128)(2,1)S(1)}, u32[]{:S(2)}, u32[]{:S(2)}) collective-permute-start(bf16[8,1024]{1,0:T(8,128)(2,1)S(1)} %get-tuple-element.48), channel_id=1, source_target_pairs={{0,224},{32,0},{64,32},{96,64},{128,96},{160,128},{192,160},{224,1... | collective-permute-start | bytes 49160 | tf_op jit(solution)/shard_map/ppermute | solution.py:371
  198.4 36.0 %all-to-all-start.5 = ((bf16[32,128,128]{2,1,0:T(8,128)(2,1)}), bf16[32,128,128]{2,1,0:T(8,128)(2,1)S(1)}, u32[]{:S(2)}, u32[]{:S(2)}) async-start(bf16[32,128,128]{2,1,0:T(8,128)(2,1)} %gather_rows.3), calls=%async_computation.5 | async-start | bytes 2097152 | tf_op jit(solution)/shard_map/all_to_all | solution.py:362
  204.0 21.7 %collective-permute-start.10 = (bf16[8,1024]{1,0:T(8,128)(2,1)S(1)}, bf16[8,1024]{1,0:T(8,128)(2,1)S(1)}, u32[]{:S(2)}, u32[]{:S(2)}) collective-permute-start(bf16[8,1024]{1,0:T(8,128)(2,1)S(1)} %get-tuple-element.39), channel_id=1, source_target_pairs={{0,224},{32,0},{64,32},{96,64},{128,96},{160,128},{192,160},{224,1... | collective-permute-start | bytes 49160 | tf_op jit(solution)/shard_map/ppermute | solution.py:371
  204.4 26.3 %collective-permute-start.11 = (bf16[8,1024]{1,0:T(8,128)(2,1)S(1)}, bf16[8,1024]{1,0:T(8,128)(2,1)S(1)}, u32[]{:S(2)}, u32[]{:S(2)}) collective-permute-start(bf16[8,1024]{1,0:T(8,128)(2,1)S(1)} %get-tuple-element.39), channel_id=1, source_target_pairs={{0,192},{32,224},{64,0},{96,32},{128,64},{160,96},{192,128},{224,1... | collective-permute-start | bytes 49160 | tf_op jit(solution)/shard_map/ppermute | solution.py:371
  208.3 23.1 %collective-permute-start.12 = (bf16[8,1024]{1,0:T(8,128)(2,1)S(1)}, bf16[8,1024]{1,0:T(8,128)(2,1)S(1)}, u32[]{:S(2)}, u32[]{:S(2)}) collective-permute-start(bf16[8,1024]{1,0:T(8,128)(2,1)S(1)} %get-tuple-element.39), channel_id=1, source_target_pairs={{0,160},{32,192},{64,224},{96,0},{128,32},{160,64},{192,96},{224,1... | collective-permute-start | bytes 49160 | tf_op jit(solution)/shard_map/ppermute | solution.py:371
  210.6 20.8 %collective-permute-start.13 = (bf16[8,1024]{1,0:T(8,128)(2,1)S(1)}, bf16[8,1024]{1,0:T(8,128)(2,1)S(1)}, u32[]{:S(2)}, u32[]{:S(2)}) collective-permute-start(bf16[8,1024]{1,0:T(8,128)(2,1)S(1)} %get-tuple-element.39), channel_id=1, source_target_pairs={{0,128},{32,160},{64,192},{96,224},{128,0},{160,32},{192,64},{224,... | collective-permute-start | bytes 49160 | tf_op jit(solution)/shard_map/ppermute | solution.py:371
  213.4 18.1 %collective-permute-start.14 = (bf16[8,1024]{1,0:T(8,128)(2,1)S(1)}, bf16[8,1024]{1,0:T(8,128)(2,1)S(1)}, u32[]{:S(2)}, u32[]{:S(2)}) collective-permute-start(bf16[8,1024]{1,0:T(8,128)(2,1)S(1)} %get-tuple-element.39), channel_id=1, source_target_pairs={{0,96},{32,128},{64,160},{96,192},{128,224},{160,0},{192,32},{224,... | collective-permute-start | bytes 49160 | tf_op jit(solution)/shard_map/ppermute | solution.py:371
  225.8 6.4 %collective-permute-start.15 = (bf16[8,1024]{1,0:T(8,128)(2,1)S(1)}, bf16[8,1024]{1,0:T(8,128)(2,1)S(1)}, u32[]{:S(2)}, u32[]{:S(2)}) collective-permute-start(bf16[8,1024]{1,0:T(8,128)(2,1)S(1)} %get-tuple-element.39), channel_id=1, source_target_pairs={{0,64},{32,96},{64,128},{96,160},{128,192},{160,224},{192,0},{224,... | collective-permute-start | bytes 49160 | tf_op jit(solution)/shard_map/ppermute | solution.py:371
  230.7 3.7 %collective-permute-start.16 = (bf16[8,1024]{1,0:T(8,128)(2,1)S(1)}, bf16[8,1024]{1,0:T(8,128)(2,1)S(1)}, u32[]{:S(2)}, u32[]{:S(2)}) collective-permute-start(bf16[8,1024]{1,0:T(8,128)(2,1)S(1)} %get-tuple-element.39), channel_id=1, source_target_pairs={{0,32},{32,64},{64,96},{96,128},{128,160},{160,192},{192,224},{224... | collective-permute-start | bytes 49160 | tf_op jit(solution)/shard_map/ppermute | solution.py:371
  234.4 30.1 %copy-start.11 = (s32[128]{0:T(128)S(1)}, s32[128]{0:T(128)}, u32[]{:S(2)}) copy-start(s32[128]{0:T(128)} %source_ref.3) | copy-start | bytes 1540
  234.4 30.1 %copy-start.13 = (s32[128]{0:T(128)S(1)}, s32[128]{0:T(128)}, u32[]{:S(2)}) copy-start(s32[128]{0:T(128)} %slot_ref.3) | copy-start | bytes 1540
  234.4 30.1 %all-to-all-start.4 = ((bf16[32,128,128]{2,1,0:T(8,128)(2,1)}), bf16[32,128,128]{2,1,0:T(8,128)(2,1)S(1)}, u32[]{:S(2)}, u32[]{:S(2)}) async-start(bf16[32,128,128]{2,1,0:T(8,128)(2,1)} %gather_rows.2), calls=%async_computation.4 | async-start | bytes 2097152 | tf_op jit(solution)/shard_map/all_to_all | solution.py:362
  242.3 29.8 %collective-permute-start.17 = (bf16[64,1024]{1,0:T(8,128)(2,1)S(1)}, bf16[64,1024]{1,0:T(8,128)(2,1)S(1)}, u32[]{:S(2)}, u32[]{:S(2)}) collective-permute-start(bf16[64,1024]{1,0:T(8,128)(2,1)S(1)} %dynamic-slice_bitcast_fusion.refs_0_), channel_id=1, source_target_pairs={{0,24},{8,0},{16,8},{24,16},{1,25},{9,1},{17,9},{25,17},{2,26},{10... | collective-permute-start | bytes 393224 | tf_op jit(solution)/shard_map/ppermute | solution.py:371
  245.0 27.0 %collective-permute-start.18 = (bf16[64,1024]{1,0:T(8,128)(2,1)S(1)}, bf16[64,1024]{1,0:T(8,128)(2,1)S(1)}, u32[]{:S(2)}, u32[]{:S(2)}) collective-permute-start(bf16[64,1024]{1,0:T(8,128)(2,1)S(1)} %dynamic-slice_bitcast_fusion.refs_0_), channel_id=1, source_target_pairs={{0,16},{8,24},{16,0},{24,8},{1,17},{9,25},{17,1},{25,9},{2,18},{10... | collective-permute-start | bytes 393224 | tf_op jit(solution)/shard_map/ppermute | solution.py:371
  245.9 26.2 %collective-permute-start.19 = (bf16[64,1024]{1,0:T(8,128)(2,1)S(1)}, bf16[64,1024]{1,0:T(8,128)(2,1)}, u32[]{:S(2)}, u32[]{:S(2)}) collective-permute-start(bf16[64,1024]{1,0:T(8,128)(2,1)S(1)} %dynamic-slice_bitcast_fusion.refs_0_), channel_id=1, source_target_pairs={{0,8},{8,16},{16,24},{24,0},{1,9},{9,17},{17,25},{25,1},{2,10},{10... | collective-permute-start | bytes 393224 | tf_op jit(solution)/shard_map/ppermute | solution.py:371
Sparse Core Ops, SparseCore 0:
  9.9 37.2 all-gather.9
  49.0 34.6 all-gather.11
  137.7 30.1 all-gather.7
  171.5 34.5 all-gather.13

commit v3 on v2

--- a/solution.py
+++ b/solution.py
@@ -386,10 +386,13 @@
     return [piece] + [rotate(piece, axis, size - i) for i in range(1, size)]
 
 
-def unroll_pieces(pieces, axis):
-    size, at = lax.axis_size(axis), lax.axis_index(axis)
-    doubled = jnp.stack(pieces + pieces)
-    return lax.dynamic_slice_in_dim(doubled, (size - at) % size, size, 0)
+def exchange_sum(value, axis):
+    size, distance = lax.axis_size(axis), 1
+    while distance < size:
+        other = lax.ppermute(value, axis, [(i, i ^ distance) for i in range(size)])
+        value = (value.astype(F32) + other.astype(F32)).astype(BF16)
+        distance *= 2
+    return value
 
 
 def assemble_kernel(at_ref, *refs):
@@ -429,11 +432,9 @@
 
 def reduce_over_graph(partial):
     rows, wide = partial.shape
-    over_y, over_z = lax.axis_size("y"), lax.axis_size("z")
-    chunk = rows // over_y
-    part = scatter_sum(partial.reshape(over_y, chunk, wide), "y")
-    part = scatter_sum(part.reshape(over_z, chunk // over_z, wide), "z")
-    part = unroll_pieces(around(part, "z"), "z").reshape(chunk, wide)
+    over_y = lax.axis_size("y")
+    part = scatter_sum(partial.reshape(over_y, rows // over_y, wide), "y")
+    part = exchange_sum(part, "z")
     at = jnp.full((1,), lax.axis_index("y"), jnp.int32)
     return assemble(at, around(part, "y"))
 
@@ -487,7 +488,7 @@
     back_low = swap(rows_low, graph)
     back_high = swap(rows_high, graph)
     grad_full = lax.all_gather(grad_pre, "feat", axis=0, tiled=True)
-    grad_full = after(grad_full, rows_low, rows_high)
+    grad_full = after(grad_full, rows_high, back_low)
 
     both = jnp.concatenate([features, neighbor_mean], axis=1)
     weight_part = lax.dot_general(

time: 285 us -> 259 us (0.909)
  starting transfers between devices: 66 us -> 41.1 us
  waiting for transfers between devices: 68.1 us -> 64.5 us
    ppermute x20 -> x6, starting transfers between devices: 43.5 us -> 10.8 us  [rotate(): lax.ppermute(value, axis, [(i, (i + distance) % size) for i in range(size)])]
    all_gather x1, waiting for transfers between devices: 17.2 us -> 0.01 us  [on_device(): grad_full = lax.all_gather(grad_pre, 'feat', axis=0, tiled=True)]
    ppermute x0 -> x3, waiting for transfers between devices: none -> 16.1 us  [exchange_sum(): other = lax.ppermute(value, axis, [(i, i ^ distance) for i in range(size)])]
    ppermute x20 -> x6, waiting for transfers between devices: 18.1 us -> 9.56 us  [rotate(): lax.ppermute(value, axis, [(i, (i + distance) % size) for i in range(size)])]
    ppermute x0 -> x3, starting transfers between devices: none -> 8.54 us  [exchange_sum(): other = lax.ppermute(value, axis, [(i, i ^ distance) for i in range(size)])]
    all_to_all x4, waiting for transfers between devices: 31.4 us -> 37.4 us  [swap(): return lax.all_to_all(value, axis, split_axis=0, concat_axis=0, tiled=True)]
    unnamed x48 -> x32, local copies, waits for them, and re-layouts: 10.6 us -> 10.6 us
  transfers between devices with their start and end apart: 28 -> 17, of which waited for: 9 -> 9; matrix products, arithmetic and copies ran while one was open for 4% -> 5% of each run, Pallas kernels for 16% -> 17%
where the time goes in v3:
time: 259 us; the launch traced here: 255 us
  waiting for transfers between devices  64.5 us (25%)
  blocking collectives  55.9 us (22%)
  Pallas kernels  50.3 us (19%)
  starting transfers between devices  41.1 us (16%)
  local copies, waits for them, and re-layouts  21.8 us (8%)
  between operations  14 us (5%)
  matrix products  6.93 us (3%)
    all_to_all x2, blocking collectives, swap(): return lax.all_to_all(value, axis, split_axis=0, concat_axis=0, tiled=True)  55.9 us
    all_to_all x4, waiting for transfers between devices, swap(): return lax.all_to_all(value, axis, split_axis=0, concat_axis=0, tiled=True)  37.4 us
    all_to_all x4, starting transfers between devices, swap(): return lax.all_to_all(value, axis, split_axis=0, concat_axis=0, tiled=True)  21.6 us
    ppermute x3, waiting for transfers between devices, exchange_sum(): other = lax.ppermute(value, axis, [(i, i ^ distance) for i in range(size)])  16.1 us
    pallas_call x2, Pallas kernels, gather_rows(): pl.pallas_call(functools.partial(gather_kernel, half), grid=(steps,), in_...  13.1 us
    ppermute x6, starting transfers between devices, rotate(): lax.ppermute(value, axis, [(i, (i + distance) % size) for i in range(size)])  10.8 us
    unnamed x32, local copies, waits for them, and re-layouts  10.6 us
    ppermute x6, waiting for transfers between devices, rotate(): lax.ppermute(value, axis, [(i, (i + distance) % size) for i in range(size)])  9.56 us
  transfers between devices with their start and end apart: 17, of which 9 were waited for; matrix products, arithmetic and copies ran while one was open for 5% of the time, Pallas kernels for 17%

profile of v3, /device:TPU:32, one launch (start us, length us, event | category | flops | bytes accessed | tf_op | source)
XLA Modules:
  0.0 254.9 jit_solution(2511835584469791480)
XLA Ops:
  7.2 0.0 all-gather.10.cloned.1.call-start
  7.2 0.7 all-gather.10.cloned.1.call-update
  7.9 0.0 all-gather.12.cloned.1.call-start
  7.9 0.7 all-gather.12.cloned.1.call-update
  8.6 0.0 copy-start.7
  8.7 1.0 copy-done.7
  9.7 0.8 copy-done.9
  10.5 0.7 copy-done.10
  11.1 0.7 copy-done.12
  11.8 0.7 copy-done.14
  12.4 8.4 %forward_blocks.1 = (bf16[32,144,128]{2,1,0:T(8,128)(2,1)S(1)}, bf16[32,128,128]{2,1,0:T(8,128)(2,1)}) custom-call(s32[128]{0:T(128)S(1)} %copy-done.10, s32[128]{0:T(128)S(1)} %copy-done.12, s32[32]{0:T(128)S(1)} %bitcast.41, s32[32,256]{1,0:T(8,128)S(1)} %bitcast.40, bf16[2048,128]{1,0:T(8,128)(2,1)S(1)} %copy-done.7, bf16[128,128,128]{2,1,0:T(8,128)(2,1)} %adj_ref.1), custom_call_target="tpu_custom_call" | custom-call | tf_op jit(solution)/shard_map/forward_blocks/pallas_call | solution.py:76
  20.8 43.1 %all_to_all.30.payload_ids_ref.rows_ref = bf16[32,144,128]{2,1,0:T(8,128)(2,1)S(1)} all-to-all(bf16[32,144,128]{2,1,0:T(8,128)(2,1)S(1)} %get-tuple-element.21), channel_id=1, replica_groups=mesh['z'=8,'y'=4,'feat'=8] {'z','y'}, dimensions={0} | all-to-all | bytes 2359296 | tf_op jit(solution)/shard_map/all_to_all | solution.py:362
  63.9 4.8 %all-to-all-start.1 = ((bf16[32,128,128]{2,1,0:T(8,128)(2,1)}), bf16[32,128,128]{2,1,0:T(8,128)(2,1)S(1)}, u32[]{:S(2)}, u32[]{:S(2)}) async-start(bf16[32,128,128]{2,1,0:T(8,128)(2,1)} %get-tuple-element.22), calls=%async_computation.1 | async-start | bytes 2097152 | tf_op jit(solution)/shard_map/all_to_all | solution.py:362
  68.8 0.4 copy.28.degree_ref
  69.1 6.4 %copy.25 = bf16[128,128,128]{1,2,0:T(8,128)(2,1)} copy(bf16[128,128,128]{2,1,0:T(8,128)(2,1)} %adj_ref.1) | data formatting | bytes 8388608 | tf_op jit(solution)/shard_map/optimization_barrier | solution.py:366
  75.5 1.2 copy.27
  76.7 5.4 %scatter_low.1.init_ref = f32[2048,128]{1,0:T(8,128)S(1)} custom-call(bf16[32,144,128]{2,1,0:T(8,128)(2,1)S(1)} %all_to_all.30.payload_ids_ref.rows_ref, bf16[32,144,128]{2,1,0:T(8,128)(2,1)S(1)} %all_to_all.30.payload_ids_ref.rows_ref), custom_call_target="tpu_custom_call" | custom-call | tf_op jit(solution)/shard_map/scatter_low/pallas_call | solution.py:137
  82.1 1.0 copy-done
  83.2 1.6 copy-done.4
  84.7 2.6 %own_term.1.own_ref = f32[256,1024]{1,0:T(8,128)S(1)} custom-call(s32[1]{0:T(128)} %bitcast.at_ref, bf16[8,2048,128]{2,1,0:T(8,128)(2,1)} %bitcast.44, bf16[1024,1024]{1,0:T(8,128)(2,1)S(1)} %copy-done.4), custom_call_target="tpu_custom_call" | custom-call | tf_op jit(solution)/shard_map/own_term/pallas_call | solution.py:220
  87.3 1.0 copy-done.2
  88.3 6.8 %all-to-all-done.1.rows_ref = bf16[32,128,128]{2,1,0:T(8,128)(2,1)S(1)} async-done(((bf16[32,128,128]{2,1,0:T(8,128)(2,1)}), bf16[32,128,128]{2,1,0:T(8,128)(2,1)S(1)}, u32[]{:S(2)}, u32[]{:S(2)}) %all-to-all-start.1) | async-done | bytes 1048608 | tf_op jit(solution)/shard_map/all_to_all | solution.py:362
  95.1 1.2 copy-done.1
  96.3 5.7 %scatter_high.1 = bf16[2048,128]{1,0:T(8,128)(2,1)S(1)} custom-call(bf16[32,144,128]{2,1,0:T(8,128)(2,1)S(1)} %all_to_all.30.payload_ids_ref.rows_ref, bf16[32,128,128]{2,1,0:T(8,128)(2,1)S(1)} %all-to-all-done.1.rows_ref, f32[2048,128]{1,0:T(8,128)S(1)} %copy-done.1, f32[2048,1]{1,0:T(8,128)S(1)} %copy.28.degree_ref), custom_call_target="tpu_custom_call" | custom-call | tf_op jit(solution)/shard_map/scatter_high/pallas_call | solution.py:156
  102.0 0.0 copy-start.5
  102.0 0.8 copy-done.5
  102.8 4.3 %all-to-all-start.2 = ((bf16[8,256,128]{2,1,0:T(8,128)(2,1)}), bf16[8,256,128]{2,1,0:T(8,128)(2,1)S(1)}, u32[]{:S(2)}, u32[]{:S(2)}) async-start(bf16[8,256,128]{2,1,0:T(8,128)(2,1)} %bitcast.39), calls=%async_computation.2 | async-start | bytes 1048576 | tf_op jit(solution)/shard_map/all_to_all | solution.py:362
  107.1 0.0 all-gather.8.cloned.1.call-start
  107.2 0.0 all-gather.12.cloned.1.call-done
  107.2 10.3 %all-to-all-done.2.mean_ref = bf16[8,256,128]{2,1,0:T(8,128)(2,1)S(1)} async-done(((bf16[8,256,128]{2,1,0:T(8,128)(2,1)}), bf16[8,256,128]{2,1,0:T(8,128)(2,1)S(1)}, u32[]{:S(2)}, u32[]{:S(2)}) %all-to-all-start.2) | async-done | bytes 524320 | tf_op jit(solution)/shard_map/all_to_all | solution.py:362
  117.5 1.2 copy-done.3
  118.7 5.8 %dense.1 = (bf16[8,256,128]{2,1,0:T(8,128)(2,1)S(1)}, bf16[8,256,128]{2,1,0:T(8,128)(2,1)}, bf16[256,1024]{1,0:T(8,128)(2,1)}) custom-call(s32[1]{0:T(128)} %bitcast.at_ref, bf16[8,256,128]{2,1,0:T(8,128)(2,1)S(1)} %all-to-all-done.2.mean_ref, f32[256,1024]{1,0:T(8,128)S(1)} %copy-done.3, bf16[8,2048,128]{2,1,0:T(8,128)(2,1)} %bitcast.43, ...), custom_call_target="tpu_custom_call" | custom-call | tf_op jit(solution)/shard_map/dense/pallas_call | solution.py:277
  124.5 12.8 %all_to_all.31 = bf16[8,256,128]{2,1,0:T(8,128)(2,1)S(1)} all-to-all(bf16[8,256,128]{2,1,0:T(8,128)(2,1)S(1)} %get-tuple-element.26), channel_id=1, replica_groups=mesh['z'=8,'y'=4,'feat'=8] {'feat'}, dimensions={0} | all-to-all | bytes 1048576 | tf_op jit(solution)/shard_map/all_to_all | solution.py:362
  137.3 0.0 all-gather.8.cloned.1.call-update
  137.3 0.0 copy-start.6
  137.4 1.4 slice_bitcast_fusion
  138.7 6.5 %gather_rows.3 = bf16[32,128,128]{2,1,0:T(8,128)(2,1)} custom-call(f32[4,128,8]{2,1,0:T(8,128)S(1)} %get-tuple-element.39.fine_ref, f32[4,128,8]{2,1,0:T(8,128)S(1)} %get-tuple-element.38.coarse_ref, bf16[2048,128]{1,0:T(8,128)(2,1)S(1)} %bitcast.37), custom_call_target="tpu_custom_call" | custom-call | tf_op jit(solution)/shard_map/gather_rows/pallas_call | solution.py:194
  145.3 6.1 %all-to-all-start.4 = ((bf16[32,128,128]{2,1,0:T(8,128)(2,1)}), bf16[32,128,128]{2,1,0:T(8,128)(2,1)S(1)}, u32[]{:S(2)}, u32[]{:S(2)}) async-start(bf16[32,128,128]{2,1,0:T(8,128)(2,1)} %gather_rows.3), calls=%async_computation.4 | async-start | bytes 2097152 | tf_op jit(solution)/shard_map/all_to_all | solution.py:362
  151.4 0.0 all-gather.14.cloned.1.call-start
  151.4 6.5 %gather_rows.2 = bf16[32,128,128]{2,1,0:T(8,128)(2,1)} custom-call(f32[4,128,8]{2,1,0:T(8,128)S(1)} %get-tuple-element.41.fine_ref, f32[4,128,8]{2,1,0:T(8,128)S(1)} %get-tuple-element.40.coarse_ref, bf16[2048,128]{1,0:T(8,128)(2,1)S(1)} %bitcast.38), custom_call_target="tpu_custom_call" | custom-call | tf_op jit(solution)/shard_map/gather_rows/pallas_call | solution.py:194
  157.9 20.4 %all-to-all-done.4.low_ref = bf16[32,128,128]{2,1,0:T(8,128)(2,1)S(1)} async-done(((bf16[32,128,128]{2,1,0:T(8,128)(2,1)}), bf16[32,128,128]{2,1,0:T(8,128)(2,1)S(1)}, u32[]{:S(2)}, u32[]{:S(2)}) %all-to-all-start.4) | async-done | bytes 1048608 | tf_op jit(solution)/shard_map/all_to_all | solution.py:362
  178.3 3.5 %convolution_convert_fusion = bf16[256,1024]{1,0:T(8,128)(2,1)S(1)} fusion(bf16[2048,1024]{1,0:T(8,128)(2,1)} %all-gather.8.cloned.1.call-done, bf16[2048,128]{1,0:T(8,128)(2,1)S(1)} %copy-done.6, bf16[2048,128]{1,0:T(8,128)(2,1)S(1)} %copy-done.8), kind=kOutput, calls=%fused_computation | convolution fusion | flops 1076101120 | bytes 5767168 | tf_op jit(solution)/shard_map/dot_general | solution.py:494
  181.8 0.0 all-gather.14.cloned.1.call-update
  181.8 6.3 %all-to-all-start.5 = ((bf16[32,128,128]{2,1,0:T(8,128)(2,1)}), bf16[32,128,128]{2,1,0:T(8,128)(2,1)S(1)}, u32[]{:S(2)}, u32[]{:S(2)}) async-start(bf16[32,128,128]{2,1,0:T(8,128)(2,1)} %gather_rows.2), calls=%async_computation.5 | async-start | bytes 2097152 | tf_op jit(solution)/shard_map/all_to_all | solution.py:362
  188.3 1.6 collective-permute-start
  189.8 2.6 %collective-permute-start.1 = (bf16[64,1024]{1,0:T(8,128)(2,1)S(1)}, bf16[64,1024]{1,0:T(8,128)(2,1)S(1)}, u32[]{:S(2)}, u32[]{:S(2)}) collective-permute-start(bf16[64,1024]{1,0:T(8,128)(2,1)S(1)} %get-tuple-element.44), channel_id=1, source_target_pairs={{0,16},{8,24},{16,0},{24,8},{1,17},{9,25},{17,1},{25,9},{2,18},{10... | collective-permute-start | bytes 393224 | tf_op jit(solution)/shard_map/ppermute | solution.py:371
  192.5 1.5 collective-permute-start.2
  194.0 4.8 %collective-permute-done = bf16[64,1024]{1,0:T(8,128)(2,1)S(1)} collective-permute-done((bf16[64,1024]{1,0:T(8,128)(2,1)S(1)}, bf16[64,1024]{1,0:T(8,128)(2,1)S(1)}, u32[]{:S(2)}, u32[]{:S(2)}) %collective-permute-start) | collective-permute-done | bytes 131104 | tf_op jit(solution)/shard_map/ppermute | solution.py:371
  198.7 2.9 %collective-permute-done.1 = bf16[64,1024]{1,0:T(8,128)(2,1)S(1)} collective-permute-done((bf16[64,1024]{1,0:T(8,128)(2,1)S(1)}, bf16[64,1024]{1,0:T(8,128)(2,1)S(1)}, u32[]{:S(2)}, u32[]{:S(2)}) %collective-permute-start.1) | collective-permute-done | bytes 131104 | tf_op jit(solution)/shard_map/ppermute | solution.py:371
  201.6 1.9 collective-permute-done.2
  203.5 0.1 fusion.5
  203.6 0.5 collective-permute-start.3
  204.2 8.4 %collective-permute-done.3 = bf16[64,1024]{1,0:T(8,128)(2,1)S(1)} collective-permute-done((bf16[64,1024]{1,0:T(8,128)(2,1)S(1)}, bf16[64,1024]{1,0:T(8,128)(2,1)S(1)}, u32[]{:S(2)}, u32[]{:S(2)}) %collective-permute-start.3) | collective-permute-done | bytes 131104 | tf_op jit(solution)/shard_map/ppermute | solution.py:392
  212.5 2.8 %collective-permute-start.4 = (bf16[64,1024]{1,0:T(8,128)(2,1)S(1)}, bf16[64,1024]{1,0:T(8,128)(2,1)S(1)}, u32[]{:S(2)}, u32[]{:S(2)}) collective-permute-start(bf16[64,1024]{1,0:T(8,128)(2,1)S(1)} %add_convert_fusion.2), channel_id=1, source_target_pairs={{0,64},{32,96},{64,0},{96,32},{128,192},{160,224},{192,128},{224,1... | collective-permute-start | bytes 393224 | tf_op jit(solution)/shard_map/ppermute | solution.py:392
  215.4 3.9 %collective-permute-done.4 = bf16[64,1024]{1,0:T(8,128)(2,1)S(1)} collective-permute-done((bf16[64,1024]{1,0:T(8,128)(2,1)S(1)}, bf16[64,1024]{1,0:T(8,128)(2,1)S(1)}, u32[]{:S(2)}, u32[]{:S(2)}) %collective-permute-start.4) | collective-permute-done | bytes 131104 | tf_op jit(solution)/shard_map/ppermute | solution.py:392
  219.3 5.2 %collective-permute-start.5 = (bf16[64,1024]{1,0:T(8,128)(2,1)S(1)}, bf16[64,1024]{1,0:T(8,128)(2,1)S(1)}, u32[]{:S(2)}, u32[]{:S(2)}) collective-permute-start(bf16[64,1024]{1,0:T(8,128)(2,1)S(1)} %add_convert_fusion.1), channel_id=1, source_target_pairs={{0,128},{32,160},{64,192},{96,224},{128,0},{160,32},{192,64},{224,... | collective-permute-start | bytes 393224 | tf_op jit(solution)/shard_map/ppermute | solution.py:392
  224.5 3.8 %collective-permute-done.5 = bf16[64,1024]{1,0:T(8,128)(2,1)S(1)} collective-permute-done((bf16[64,1024]{1,0:T(8,128)(2,1)S(1)}, bf16[64,1024]{1,0:T(8,128)(2,1)S(1)}, u32[]{:S(2)}, u32[]{:S(2)}) %collective-permute-start.5) | collective-permute-done | bytes 131104 | tf_op jit(solution)/shard_map/ppermute | solution.py:392
  228.4 3.1 %collective-permute-start.6 = (bf16[64,1024]{1,0:T(8,128)(2,1)S(1)}, bf16[64,1024]{1,0:T(8,128)(2,1)S(1)}, u32[]{:S(2)}, u32[]{:S(2)}) collective-permute-start(bf16[64,1024]{1,0:T(8,128)(2,1)S(1)} %add_convert_fusion.refs_0_), channel_id=1, source_target_pairs={{0,24},{8,0},{16,8},{24,16},{1,25},{9,1},{17,9},{25,17},{2,26},{10... | collective-permute-start | bytes 393224 | tf_op jit(solution)/shard_map/ppermute | solution.py:371
  231.5 0.7 collective-permute-start.7
  232.2 1.3 collective-permute-start.8
  233.5 3.5 %fusion.6.self_ref = f32[2048,128]{1,0:T(8,128)S(1)} fusion(bf16[2048,1024]{1,0:T(8,128)(2,1)} %all-gather.8.cloned.1.call-done, bf16[1024,1024]{1,0:T(8,128)(2,1)} %weight_ref.2, s32[]{:T(128)S(6)} %select_n.36), kind=kOutput, calls=%fused_computation.11 | convolution fusion | flops 536870912 | bytes 5505028 | tf_op jit(solution)/shard_map/dot_general | solution.py:501
  237.0 7.5 %backward_blocks.1 = bf16[2048,128]{1,0:T(8,128)(2,1)} custom-call(s32[128]{0:T(128)S(1)} %copy-done.11, s32[128]{0:T(128)S(1)} %copy-done.13, bf16[32,128,128]{2,1,0:T(8,128)(2,1)S(1)} %all-to-all-done.4.low_ref, bf16[32,128,128]{2,1,0:T(8,128)(2,1)S(1)} %all-to-all-done.5.high_ref, bf16[128,128,128]{2,1,0:T(8,128)(2,1)} %bitcast.42, ...), custom_call_target="tpu_custom_call" | custom-call | tf_op jit(solution)/shard_map/backward_blocks/pallas_call | solution.py:338
  244.5 2.0 assemble.1
  246.5 1.9 constant_dynamic-slice_fusion
  (31 shorter events, 0.2 us)
Async XLA Ops:
  7.2 76.0 %all-gather.10.cloned.1.call-start = ((), (), s32[]{:S(2)}) async-start(), calls=%async_computation.7 | async-start | bytes 4718592 | tf_op jit(solution)/shard_map/all_gather | solution.py:465
  7.9 99.3 %all-gather.12.cloned.1.call-start = ((), (), s32[]{:S(2)}) async-start(), calls=%async_computation.8 | async-start | bytes 4718592 | tf_op jit(solution)/shard_map/all_gather | solution.py:466
  8.6 1.0 copy-start.7
  9.7 0.8 copy-start.9
  10.5 0.7 copy-start.10
  11.1 0.7 copy-start.12
  11.8 0.7 copy-start.14
  12.4 56.3 %copy-start.15 = (s32[2048]{0:T(1024)S(1)}, s32[2048]{0:T(1024)}, u32[]{:S(2)}) copy-start(s32[2048]{0:T(1024)} %param.18) | copy-start | bytes 24580
  63.9 31.2 %all-to-all-start.1 = ((bf16[32,128,128]{2,1,0:T(8,128)(2,1)}), bf16[32,128,128]{2,1,0:T(8,128)(2,1)S(1)}, u32[]{:S(2)}, u32[]{:S(2)}) async-start(bf16[32,128,128]{2,1,0:T(8,128)(2,1)} %get-tuple-element.22), calls=%async_computation.1 | async-start | bytes 2097152 | tf_op jit(solution)/shard_map/all_to_all | solution.py:362
  82.1 1.0 copy-start
  83.1 1.6 copy-start.4
  87.3 1.0 copy-start.2
  95.1 1.2 copy-start.1
  102.0 0.8 copy-start.5
  102.8 14.7 %all-to-all-start.2 = ((bf16[8,256,128]{2,1,0:T(8,128)(2,1)}), bf16[8,256,128]{2,1,0:T(8,128)(2,1)S(1)}, u32[]{:S(2)}, u32[]{:S(2)}) async-start(bf16[8,256,128]{2,1,0:T(8,128)(2,1)} %bitcast.39), calls=%async_computation.2 | async-start | bytes 1048576 | tf_op jit(solution)/shard_map/all_to_all | solution.py:362
  107.1 71.2 %all-gather.8.cloned.1.call-start = ((), (), s32[]{:S(2)}) async-start(), calls=%async_computation.6 | async-start | bytes 4718592 | tf_op jit(solution)/shard_map/all_gather | solution.py:490
  117.5 1.2 copy-start.3
  137.3 41.0 %copy-start.6 = (bf16[2048,128]{1,0:T(8,128)(2,1)S(1)}, bf16[2048,128]{1,0:T(8,128)(2,1)}, u32[]{:S(2)}) copy-start(bf16[2048,128]{1,0:T(8,128)(2,1)} %copy-done.5) | copy-start | bytes 1572868
  137.3 41.0 %copy-start.8 = (bf16[2048,128]{1,0:T(8,128)(2,1)S(1)}, bf16[2048,128]{1,0:T(8,128)(2,1)}, u32[]{:S(2)}) copy-start(bf16[2048,128]{1,0:T(8,128)(2,1)} %feat_ref.1) | copy-start | bytes 1572868
  145.3 33.1 %all-to-all-start.4 = ((bf16[32,128,128]{2,1,0:T(8,128)(2,1)}), bf16[32,128,128]{2,1,0:T(8,128)(2,1)S(1)}, u32[]{:S(2)}, u32[]{:S(2)}) async-start(bf16[32,128,128]{2,1,0:T(8,128)(2,1)} %gather_rows.3), calls=%async_computation.4 | async-start | bytes 2097152 | tf_op jit(solution)/shard_map/all_to_all | solution.py:362
  151.4 95.1 %all-gather.14.cloned.1.call-start = ((), (), s32[]{:S(2)}) async-start(), calls=%async_computation.9 | async-start | bytes 4718592 | tf_op jit(solution)/shard_map/all_gather | solution.py:497
  181.8 55.1 %all-to-all-start.5 = ((bf16[32,128,128]{2,1,0:T(8,128)(2,1)}), bf16[32,128,128]{2,1,0:T(8,128)(2,1)S(1)}, u32[]{:S(2)}, u32[]{:S(2)}) async-start(bf16[32,128,128]{2,1,0:T(8,128)(2,1)} %gather_rows.2), calls=%async_computation.5 | async-start | bytes 2097152 | tf_op jit(solution)/shard_map/all_to_all | solution.py:362
  188.3 10.5 %collective-permute-start = (bf16[64,1024]{1,0:T(8,128)(2,1)S(1)}, bf16[64,1024]{1,0:T(8,128)(2,1)S(1)}, u32[]{:S(2)}, u32[]{:S(2)}) collective-permute-start(bf16[64,1024]{1,0:T(8,128)(2,1)S(1)} %get-tuple-element.42), channel_id=1, source_target_pairs={{0,8},{8,16},{16,24},{24,0},{1,9},{9,17},{17,25},{25,1},{2,10},{10... | collective-permute-start | bytes 393224 | tf_op jit(solution)/shard_map/ppermute | solution.py:371
  189.8 11.8 %collective-permute-start.1 = (bf16[64,1024]{1,0:T(8,128)(2,1)S(1)}, bf16[64,1024]{1,0:T(8,128)(2,1)S(1)}, u32[]{:S(2)}, u32[]{:S(2)}) collective-permute-start(bf16[64,1024]{1,0:T(8,128)(2,1)S(1)} %get-tuple-element.44), channel_id=1, source_target_pairs={{0,16},{8,24},{16,0},{24,8},{1,17},{9,25},{17,1},{25,9},{2,18},{10... | collective-permute-start | bytes 393224 | tf_op jit(solution)/shard_map/ppermute | solution.py:371
  192.5 11.1 %collective-permute-start.2 = (bf16[64,1024]{1,0:T(8,128)(2,1)S(1)}, bf16[64,1024]{1,0:T(8,128)(2,1)S(1)}, u32[]{:S(2)}, u32[]{:S(2)}) collective-permute-start(bf16[64,1024]{1,0:T(8,128)(2,1)S(1)} %get-tuple-element.43), channel_id=1, source_target_pairs={{0,24},{8,0},{16,8},{24,16},{1,25},{9,1},{17,9},{25,17},{2,26},{10... | collective-permute-start | bytes 393224 | tf_op jit(solution)/shard_map/ppermute | solution.py:371
  194.0 43.0 %copy-start.11 = (s32[128]{0:T(128)S(1)}, s32[128]{0:T(128)}, u32[]{:S(2)}) copy-start(s32[128]{0:T(128)} %source_ref.3) | copy-start | bytes 1540
  194.0 43.0 %copy-start.13 = (s32[128]{0:T(128)S(1)}, s32[128]{0:T(128)}, u32[]{:S(2)}) copy-start(s32[128]{0:T(128)} %slot_ref.3) | copy-start | bytes 1540
  203.6 8.9 %collective-permute-start.3 = (bf16[64,1024]{1,0:T(8,128)(2,1)S(1)}, bf16[64,1024]{1,0:T(8,128)(2,1)S(1)}, u32[]{:S(2)}, u32[]{:S(2)}) collective-permute-start(bf16[64,1024]{1,0:T(8,128)(2,1)S(1)} %fusion.5), channel_id=1, source_target_pairs={{0,32},{32,0},{64,96},{96,64},{128,160},{160,128},{192,224},{224,1... | collective-permute-start | bytes 393224 | tf_op jit(solution)/shard_map/ppermute | solution.py:392
  212.5 6.7 %collective-permute-start.4 = (bf16[64,1024]{1,0:T(8,128)(2,1)S(1)}, bf16[64,1024]{1,0:T(8,128)(2,1)S(1)}, u32[]{:S(2)}, u32[]{:S(2)}) collective-permute-start(bf16[64,1024]{1,0:T(8,128)(2,1)S(1)} %add_convert_fusion.2), channel_id=1, source_target_pairs={{0,64},{32,96},{64,0},{96,32},{128,192},{160,224},{192,128},{224,1... | collective-permute-start | bytes 393224 | tf_op jit(solution)/shard_map/ppermute | solution.py:392
  219.3 9.0 %collective-permute-start.5 = (bf16[64,1024]{1,0:T(8,128)(2,1)S(1)}, bf16[64,1024]{1,0:T(8,128)(2,1)S(1)}, u32[]{:S(2)}, u32[]{:S(2)}) collective-permute-start(bf16[64,1024]{1,0:T(8,128)(2,1)S(1)} %add_convert_fusion.1), channel_id=1, source_target_pairs={{0,128},{32,160},{64,192},{96,224},{128,0},{160,32},{192,64},{224,... | collective-permute-start | bytes 393224 | tf_op jit(solution)/shard_map/ppermute | solution.py:392
  228.4 16.1 %collective-permute-start.6 = (bf16[64,1024]{1,0:T(8,128)(2,1)S(1)}, bf16[64,1024]{1,0:T(8,128)(2,1)S(1)}, u32[]{:S(2)}, u32[]{:S(2)}) collective-permute-start(bf16[64,1024]{1,0:T(8,128)(2,1)S(1)} %add_convert_fusion.refs_0_), channel_id=1, source_target_pairs={{0,24},{8,0},{16,8},{24,16},{1,25},{9,1},{17,9},{25,17},{2,26},{10... | collective-permute-start | bytes 393224 | tf_op jit(solution)/shard_map/ppermute | solution.py:371
  231.5 13.0 %collective-permute-start.7 = (bf16[64,1024]{1,0:T(8,128)(2,1)S(1)}, bf16[64,1024]{1,0:T(8,128)(2,1)S(1)}, u32[]{:S(2)}, u32[]{:S(2)}) collective-permute-start(bf16[64,1024]{1,0:T(8,128)(2,1)S(1)} %add_convert_fusion.refs_0_), channel_id=1, source_target_pairs={{0,16},{8,24},{16,0},{24,8},{1,17},{9,25},{17,1},{25,9},{2,18},{10... | collective-permute-start | bytes 393224 | tf_op jit(solution)/shard_map/ppermute | solution.py:371
  232.2 12.2 %collective-permute-start.8 = (bf16[64,1024]{1,0:T(8,128)(2,1)S(1)}, bf16[64,1024]{1,0:T(8,128)(2,1)}, u32[]{:S(2)}, u32[]{:S(2)}) collective-permute-start(bf16[64,1024]{1,0:T(8,128)(2,1)S(1)} %add_convert_fusion.refs_0_), channel_id=1, source_target_pairs={{0,8},{8,16},{16,24},{24,0},{1,9},{9,17},{17,25},{25,1},{2,10},{10... | collective-permute-start | bytes 393224 | tf_op jit(solution)/shard_map/ppermute | solution.py:371
Sparse Core Ops, SparseCore 0:
  9.9 37.2 all-gather.9
  49.0 34.6 all-gather.11
  137.5 30.1 all-gather.7
  182.0 30.3 all-gather.13

commit v4 on v3

--- a/solution.py
+++ b/solution.py
@@ -10,6 +10,7 @@
 BF16 = jnp.bfloat16
 F32 = jnp.float32
 VMEM_BYTES = 48 * 1024 * 1024
+ID_ROWS = 8
 
 
 def params(axes=0):
@@ -46,7 +47,7 @@
     def _():
         slot_row = lax.broadcasted_iota(jnp.int32, (blk, cols), 0)
         lane = lax.broadcasted_iota(jnp.int32, (1, 2 * blk), 1)
-        tile_row = lax.broadcasted_iota(jnp.int32, (16, blk), 0)
+        tile_row = lax.broadcasted_iota(jnp.int32, (ID_ROWS, blk), 0)
 
         def emit(part, carry):
             count = count_ref[part]
@@ -62,7 +63,7 @@
             tile = jnp.where(tile_row == 1, fine[:, blk:], tile)
             tile = jnp.where(tile_row == 2, coarse[:, :blk], tile)
             tile = jnp.where(tile_row == 3, coarse[:, blk:], tile)
-            low_ref[part, blk : blk + 16, :] = tile.astype(BF16)
+            low_ref[part, blk : blk + ID_ROWS, :] = tile.astype(BF16)
             return carry
 
         lax.fori_loop(0, parts, emit, 0)
@@ -83,11 +84,11 @@
                 full_spec((nodes, cols)),
                 pl.BlockSpec((chunk, blk, blk), lambda i, *unused: (i, 0, 0)),
             ],
-            out_specs=[full_spec((parts, blk + 16, cols)), full_spec((parts, blk, cols))],
+            out_specs=[full_spec((parts, blk + ID_ROWS, cols)), full_spec((parts, blk, cols))],
             scratch_shapes=[pltpu.VMEM((parts * cap // blk, blk, cols), F32)],
         ),
         out_shape=[
-            jax.ShapeDtypeStruct((parts, blk + 16, cols), BF16),
+            jax.ShapeDtypeStruct((parts, blk + ID_ROWS, cols), BF16),
             jax.ShapeDtypeStruct((parts, blk, cols), BF16),
         ],
         compiler_params=params(1),
@@ -119,16 +120,41 @@
     scatter_body(0, payload_ids_ref, rows_ref, hot_ref, sum_ref, rows_ref.shape[0])
 
 
-def scatter_high_kernel(payload_ids_ref, rows_ref, init_ref, degree_ref, mean_ref, hot_ref, acc_ref):
-    @pl.when(pl.program_id(0) == 0)
-    def _():
-        acc_ref[...] = init_ref[...]
-
-    scatter_body(1, payload_ids_ref, rows_ref, hot_ref, acc_ref, rows_ref.shape[0])
-
-    @pl.when(pl.program_id(0) == pl.num_programs(0) - 1)
-    def _():
-        mean_ref[...] = (acc_ref[...] / degree_ref[...]).astype(BF16)
+def scatter_high_kernel(
+    ids_ref, rows_ref, coarse_ref, init_ref, degree_ref, mean_ref, hot_ref, both_ref, acc_ref
+):
+    step = pl.program_id(0)
+    group, blk, cols = rows_ref.shape
+    half_nodes = acc_ref.shape[0]
+    half_blocks = half_nodes // blk
+
+    @pl.when(step == 0)
+    def _():
+        acc_ref[:, :cols] = init_ref[:half_nodes]
+        acc_ref[:, cols:] = init_ref[half_nodes:]
+
+    node_row = lax.broadcasted_iota(jnp.int32, (blk, blk), 0).astype(F32)
+    for part in range(group):
+        tile = ids_ref[part].astype(F32)
+        fine = tile[1:2, :]
+        coarse = tile[3:4, :]
+        coarse = jnp.where(coarse >= half_blocks, coarse - half_blocks, coarse)
+        hot = jnp.where(node_row == fine, 1.0, 0.0).astype(BF16)
+        here = slice(part * blk, (part + 1) * blk)
+        for block in range(half_blocks):
+            keep = jnp.where(coarse == float(block), 1.0, 0.0).astype(BF16)
+            hot_ref[block * blk : (block + 1) * blk, here] = hot * keep
+        column = jnp.broadcast_to(coarse_ref[0, 0, :, part : part + 1], (blk, cols))
+        upper = jnp.where(column >= half_blocks, 1.0, 0.0).astype(BF16)
+        rows = rows_ref[part]
+        both_ref[here, cols:] = rows * upper
+        both_ref[here, :cols] = rows * (1.0 - upper)
+    acc_ref[...] += jnp.dot(hot_ref[...], both_ref[...], preferred_element_type=F32)
+
+    @pl.when(step == pl.num_programs(0) - 1)
+    def _():
+        mean_ref[:half_nodes] = (acc_ref[:, :cols] / degree_ref[:half_nodes]).astype(BF16)
+        mean_ref[half_nodes:] = (acc_ref[:, cols:] / degree_ref[half_nodes:]).astype(BF16)
 
 
 def scatter_low(low, nodes):
@@ -138,7 +164,7 @@
         scatter_low_kernel,
         grid=(parts // group,),
         in_specs=[
-            pl.BlockSpec((group, 16, cols), lambda i: (i, blk // 16, 0)),
+            pl.BlockSpec((group, ID_ROWS, cols), lambda i: (i, blk // ID_ROWS, 0)),
             pl.BlockSpec((group, blk, cols), lambda i: (i, 0, 0)),
         ],
         out_specs=full_spec((nodes, cols)),
@@ -149,62 +175,71 @@
     )(low, low)
 
 
-def scatter_high(low, high, partial_sum, degrees):
+def scatter_high(low, high, columns, partial_sum, degrees):
     parts, blk, cols = high.shape
     nodes = partial_sum.shape[0]
-    group = 8
+    group = columns.shape[3]
     return pl.pallas_call(
         scatter_high_kernel,
         grid=(parts // group,),
         in_specs=[
-            pl.BlockSpec((group, 16, cols), lambda i: (i, blk // 16, 0)),
+            pl.BlockSpec((group, ID_ROWS, cols), lambda i: (i, blk // ID_ROWS, 0)),
             pl.BlockSpec((group, blk, cols), lambda i: (i, 0, 0)),
+            pl.BlockSpec((1, 1, blk, group), lambda i: (3, i, 0, 0)),
             full_spec((nodes, cols)),
             full_spec((nodes, 1)),
         ],
         out_specs=full_spec((nodes, cols)),
         out_shape=jax.ShapeDtypeStruct((nodes, cols), BF16),
         scratch_shapes=[
-            pltpu.VMEM((nodes, group * blk), BF16),
-            pltpu.VMEM((nodes, cols), F32),
+            pltpu.VMEM((nodes // 2, group * blk), BF16),
+            pltpu.VMEM((group * blk, 2 * cols), BF16),
+            pltpu.VMEM((nodes // 2, 2 * cols), F32),
         ],
         compiler_params=params(1),
         name="scatter_high",
-    )(low, high, partial_sum, degrees)
-
-
-def gather_kernel(half, fine_ref, coarse_ref, back_ref, out_ref, hot_ref):
+    )(low, high, columns, partial_sum, degrees)
+
+
+def gather_kernel(fine_ref, coarse_ref, back_ref, out_ref, hot_ref):
     group, blk, cols = out_ref.shape
-    nodes = back_ref.shape[0]
+    half_nodes = back_ref.shape[0] // 2
+    half_blocks = half_nodes // blk
     lane = lax.broadcasted_iota(jnp.int32, (blk, blk), 1).astype(F32)
     for part in range(group):
-        fine = jnp.broadcast_to(fine_ref[0, :, part : part + 1], (blk, blk))
-        coarse = jnp.broadcast_to(coarse_ref[0, :, part : part + 1], (blk, blk))
+        fine = jnp.broadcast_to(fine_ref[0, 0, :, part : part + 1], (blk, blk))
+        coarse = jnp.broadcast_to(coarse_ref[0, 0, :, part : part + 1], (blk, blk))
+        coarse = jnp.where(coarse >= half_blocks, coarse - half_blocks, coarse)
         hot = jnp.where(lane == fine, 1.0, 0.0)
-        for block in range(nodes // blk):
+        for block in range(half_blocks):
             value = jnp.where(coarse == float(block), hot, 0.0).astype(BF16)
             hot_ref[part * blk : (part + 1) * blk, block * blk : (block + 1) * blk] = value
-    picked = jnp.dot(hot_ref[...], back_ref[...], preferred_element_type=F32)
-    out_ref[...] = picked.astype(BF16).reshape(group, blk, cols)
-
-
-def gather_rows(half, fine, coarse, back):
-    steps, blk, group = fine.shape
+    both = jnp.concatenate([back_ref[:half_nodes], back_ref[half_nodes:]], axis=1)
+    picked = jnp.dot(hot_ref[...], both, preferred_element_type=F32)
+    for part in range(group):
+        coarse = jnp.broadcast_to(coarse_ref[0, 0, :, part : part + 1], (blk, cols))
+        here = slice(part * blk, (part + 1) * blk)
+        rows = jnp.where(coarse >= half_blocks, picked[here, cols:], picked[here, :cols])
+        out_ref[part] = rows.astype(BF16)
+
+
+def gather_rows(half, columns, back):
+    _, steps, blk, group = columns.shape
     nodes, cols = back.shape
     return pl.pallas_call(
-        functools.partial(gather_kernel, half),
+        gather_kernel,
         grid=(steps,),
         in_specs=[
-            pl.BlockSpec((1, blk, group), lambda i: (i, 0, 0)),
-            pl.BlockSpec((1, blk, group), lambda i: (i, 0, 0)),
+            pl.BlockSpec((1, 1, blk, group), lambda i: (half, i, 0, 0)),
+            pl.BlockSpec((1, 1, blk, group), lambda i: (2 + half, i, 0, 0)),
             full_spec((nodes, cols)),
         ],
         out_specs=pl.BlockSpec((group, blk, cols), lambda i: (i, 0, 0)),
         out_shape=jax.ShapeDtypeStruct((steps * group, blk, cols), BF16),
-        scratch_shapes=[pltpu.VMEM((group * blk, nodes), BF16)],
+        scratch_shapes=[pltpu.VMEM((group * blk, nodes // 2), BF16)],
         compiler_params=params(1),
         name="gather_rows",
-    )(fine, coarse, back)
+    )(columns, columns, back)
 
 
 def own_term_kernel(at_ref, feat_ref, weight_ref, out_ref):
@@ -386,13 +421,11 @@
     return [piece] + [rotate(piece, axis, size - i) for i in range(1, size)]
 
 
-def exchange_sum(value, axis):
-    size, distance = lax.axis_size(axis), 1
-    while distance < size:
-        other = lax.ppermute(value, axis, [(i, i ^ distance) for i in range(size)])
-        value = (value.astype(F32) + other.astype(F32)).astype(BF16)
-        distance *= 2
-    return value
+def exchange_sum(value, axis, distance, *beside):
+    size = lax.axis_size(axis)
+    other = lax.ppermute(value, axis, [(i, i ^ distance) for i in range(size)])
+    other = after(other, *beside)
+    return (value.astype(F32) + other.astype(F32)).astype(BF16)
 
 
 def assemble_kernel(at_ref, *refs):
@@ -428,15 +461,6 @@
         name="assemble",
     )(at, *pieces)
     return first.reshape(half * rows, wide), second.reshape(half * rows, wide)
-
-
-def reduce_over_graph(partial):
-    rows, wide = partial.shape
-    over_y = lax.axis_size("y")
-    part = scatter_sum(partial.reshape(over_y, rows // over_y, wide), "y")
-    part = exchange_sum(part, "z")
-    at = jnp.full((1,), lax.axis_index("y"), jnp.int32)
-    return assemble(at, around(part, "y"))
 
 
 def on_device(
@@ -476,15 +500,15 @@
     partial_sum, adjacency_t, ids, own = lax.optimization_barrier(
         (partial_sum, adjacency_t, ids, own)
     )
-    neighbor_mean = scatter_high(low_in, high_in, partial_sum, degrees)
+    neighbor_mean = scatter_high(low_in, high_in, ids, partial_sum, degrees)
     mean_pieces = swap(neighbor_mean.reshape(feat_size, share, feat_cols), "feat")
     back_pieces, hidden_pieces, grad_pre = dense(at, mean_pieces, own, cot_all, w_neigh, degrees)
     back_rows = swap(back_pieces, "feat").reshape(node_rows, feat_cols)
     back_rows, grad_pre, hidden_pieces = lax.optimization_barrier(
         (back_rows, grad_pre, hidden_pieces)
     )
-    rows_low = gather_rows(0, ids[0], ids[2], back_rows)
-    rows_high = gather_rows(1, ids[1], ids[3], back_rows)
+    rows_low = gather_rows(0, ids, back_rows)
+    rows_high = gather_rows(1, ids, back_rows)
     back_low = swap(rows_low, graph)
     back_high = swap(rows_high, graph)
     grad_full = lax.all_gather(grad_pre, "feat", axis=0, tiled=True)
@@ -497,12 +521,21 @@
     hidden_all = lax.all_gather(after(hidden_pieces, weight_part), "feat", axis=0)
     hidden_out = lax.dynamic_index_in_dim(hidden_all, feat_at, 1, keepdims=False)
     hidden_out = hidden_out.reshape(node_rows, feat_cols)
-    grad_self, grad_neigh = reduce_over_graph(weight_part)
     self_grad = lax.dot_general(
         grad_full, self_rows, (((1,), (1,)), ((), ())), preferred_element_type=F32
     )
+    over_y = lax.axis_size("y")
+    part = weight_part.reshape(over_y, 2 * feat_cols // over_y, weight_part.shape[1])
+    part = after(scatter_sum(part, "y"), self_grad)
+    part = exchange_sum(part, "z", 4)
+    part = exchange_sum(part, "z", 2)
+    part = after(part, back_high)
+    part = exchange_sum(part, "z", 1, hidden_out)
     grad_features = backward_blocks(
         block_source, block_to_slot, back_low, back_high, adjacency_t, self_grad
+    )
+    grad_self, grad_neigh = assemble(
+        jnp.full((1,), lax.axis_index("y"), jnp.int32), around(part, "y")
     )
     return hidden_out, grad_features, grad_self, grad_neigh
 

time: 259 us -> 251 us (0.969)
  starting transfers between devices: 41.1 us -> 36.2 us
  Pallas kernels: 50.3 us -> 45.8 us
  waiting for transfers between devices: 64.5 us -> 68.4 us
    ppermute x3, waiting for transfers between devices: 16.1 us -> 21.4 us  [exchange_sum(): other = lax.ppermute(value, axis, [(i, i ^ distance) for i in range(size)])]
    ppermute x3, starting transfers between devices: 8.54 us -> 4.08 us  [exchange_sum(): other = lax.ppermute(value, axis, [(i, i ^ distance) for i in range(size)])]
    pallas_call x2, Pallas kernels: 13.1 us -> 9.42 us  [gather_rows(): pl.pallas_call(gather_kernel, grid=(steps,), in_specs=[pl.BlockSpec((1, 1...]
    ppermute x6, waiting for transfers between devices: 9.56 us -> 6.06 us  [rotate(): lax.ppermute(value, axis, [(i, (i + distance) % size) for i in range(size)])]
    unnamed x32 -> x34, local copies, waits for them, and re-layouts: 10.6 us -> 11.5 us
  transfers between devices with their start and end apart: 17 -> 17, of which waited for: 9 -> 9; matrix products, arithmetic and copies ran while one was open for 5% -> 5% of each run, Pallas kernels for 17% -> 16%
where the time goes in v4:
time: 251 us; the launch traced here: 248 us
  waiting for transfers between devices  68.4 us (27%)
  blocking collectives  54.7 us (22%)
  Pallas kernels  45.8 us (18%)
  starting transfers between devices  36.2 us (14%)
  local copies, waits for them, and re-layouts  20.6 us (8%)
  between operations  14.1 us (6%)
  matrix products  7.09 us (3%)
    all_to_all x2, blocking collectives, swap(): return lax.all_to_all(value, axis, split_axis=0, concat_axis=0, tiled=True)  54.7 us
    all_to_all x4, waiting for transfers between devices, swap(): return lax.all_to_all(value, axis, split_axis=0, concat_axis=0, tiled=True)  39.4 us
    all_to_all x4, starting transfers between devices, swap(): return lax.all_to_all(value, axis, split_axis=0, concat_axis=0, tiled=True)  22.3 us
    ppermute x3, waiting for transfers between devices, exchange_sum(): other = lax.ppermute(value, axis, [(i, i ^ distance) for i in range(size)])  21.4 us
    unnamed x34, local copies, waits for them, and re-layouts  11.5 us
    ppermute x6, starting transfers between devices, rotate(): lax.ppermute(value, axis, [(i, (i + distance) % size) for i in range(size)])  9.76 us
    pallas_call x2, Pallas kernels, gather_rows(): pl.pallas_call(gather_kernel, grid=(steps,), in_specs=[pl.BlockSpec((1, 1...  9.42 us
    pallas_call x1, Pallas kernels, forward_blocks(): pl.pallas_call(forward_blocks_kernel, grid_spec=pltpu.PrefetchScalarGridS...  8.38 us
  transfers between devices with their start and end apart: 17, of which 9 were waited for; matrix products, arithmetic and copies ran while one was open for 5% of the time, Pallas kernels for 16%

profile of v4, /device:TPU:32, one launch (start us, length us, event | category | flops | bytes accessed | tf_op | source)
XLA Modules:
  0.0 247.9 jit_solution(8518336531683531098)
XLA Ops:
  7.2 0.0 all-gather.10.cloned.1.call-start
  7.2 0.7 all-gather.10.cloned.1.call-update
  7.9 0.0 all-gather.12.cloned.1.call-start
  7.9 0.7 all-gather.12.cloned.1.call-update
  8.7 1.0 copy-done.8
  9.7 0.8 copy-done.9
  10.5 0.7 copy-done.10
  11.1 0.7 copy-done.12
  11.8 0.7 copy-done.14
  12.4 8.4 %forward_blocks.1 = (bf16[32,136,128]{2,1,0:T(8,128)(2,1)S(1)}, bf16[32,128,128]{2,1,0:T(8,128)(2,1)}) custom-call(s32[128]{0:T(128)S(1)} %copy-done.10, s32[128]{0:T(128)S(1)} %copy-done.12, s32[32]{0:T(128)S(1)} %bitcast.38, s32[32,256]{1,0:T(8,128)S(1)} %bitcast.37, bf16[2048,128]{1,0:T(8,128)(2,1)S(1)} %copy-done.8, bf16[128,128,128]{2,1,0:T(8,128)(2,1)} %adj_ref.1), custom_call_target="tpu_custom_call" | custom-call | tf_op jit(solution)/shard_map/forward_blocks/pallas_call | solution.py:77
  20.8 41.9 %all_to_all.30.payload_ids_ref.rows_ref.ids_ref = bf16[32,136,128]{2,1,0:T(8,128)(2,1)S(1)} all-to-all(bf16[32,136,128]{2,1,0:T(8,128)(2,1)S(1)} %get-tuple-element.24), channel_id=1, replica_groups=mesh['z'=8,'y'=4,'feat'=8] {'z','y'}, dimensions={0} | all-to-all | bytes 2228224 | tf_op jit(solution)/shard_map/all_to_all | solution.py:397
  62.7 5.5 %all-to-all-start.1 = ((bf16[32,128,128]{2,1,0:T(8,128)(2,1)}), bf16[32,128,128]{2,1,0:T(8,128)(2,1)}, u32[]{:S(2)}, u32[]{:S(2)}) async-start(bf16[32,128,128]{2,1,0:T(8,128)(2,1)} %get-tuple-element.25), calls=%async_computation.1 | async-start | bytes 2097152 | tf_op jit(solution)/shard_map/all_to_all | solution.py:397
  68.2 0.4 copy.28.degree_ref
  68.6 6.5 %copy.25 = bf16[128,128,128]{1,2,0:T(8,128)(2,1)} copy(bf16[128,128,128]{2,1,0:T(8,128)(2,1)} %adj_ref.1) | data formatting | bytes 8388608 | tf_op jit(solution)/shard_map/optimization_barrier | solution.py:401
  75.1 0.2 copy.27
  75.3 5.4 %scatter_low.1.init_ref = f32[2048,128]{1,0:T(8,128)S(1)} custom-call(bf16[32,136,128]{2,1,0:T(8,128)(2,1)S(1)} %all_to_all.30.payload_ids_ref.rows_ref.ids_ref, bf16[32,136,128]{2,1,0:T(8,128)(2,1)S(1)} %all_to_all.30.payload_ids_ref.rows_ref.ids_ref), custom_call_target="tpu_custom_call" | custom-call | tf_op jit(solution)/shard_map/scatter_low/pallas_call | solution.py:163
  80.7 1.0 copy-done.1
  81.7 1.6 copy-done.5
  83.3 2.6 %own_term.1.own_ref = f32[256,1024]{1,0:T(8,128)S(1)} custom-call(s32[1]{0:T(128)} %bitcast.at_ref, bf16[8,2048,128]{2,1,0:T(8,128)(2,1)} %bitcast.41, bf16[1024,1024]{1,0:T(8,128)(2,1)S(1)} %copy-done.5), custom_call_target="tpu_custom_call" | custom-call | tf_op jit(solution)/shard_map/own_term/pallas_call | solution.py:255
  85.9 1.0 copy-done.3
  86.9 7.3 %all-to-all-done.1.rows_ref = bf16[32,128,128]{2,1,0:T(8,128)(2,1)} async-done(((bf16[32,128,128]{2,1,0:T(8,128)(2,1)}), bf16[32,128,128]{2,1,0:T(8,128)(2,1)}, u32[]{:S(2)}, u32[]{:S(2)}) %all-to-all-start.1) | async-done | bytes 1048608 | tf_op jit(solution)/shard_map/all_to_all | solution.py:397
  94.2 1.2 copy-done.2
  95.4 5.3 %scatter_high.1 = bf16[2048,128]{1,0:T(8,128)(2,1)S(1)} custom-call(bf16[32,136,128]{2,1,0:T(8,128)(2,1)S(1)} %all_to_all.30.payload_ids_ref.rows_ref.ids_ref, bf16[32,128,128]{2,1,0:T(8,128)(2,1)} %all-to-all-done.1.rows_ref, f32[4,4,128,8]{3,2,1,0:T(8,128)S(1)} %bitcast.29, f32[2048,128]{1,0:T(8,128)S(1)} %copy-done.2, f32[2048,1]{1,0:T(8,128)S(1)} %copy.28.degree_ref), custom_call_target="tpu_custom_call" | custom-call | tf_op jit(solution)/shard_map/scatter_high/pallas_call | solution.py:182
  100.7 0.0 copy-start.6
  100.7 0.8 copy-done.6
  101.5 4.3 %all-to-all-start.2 = ((bf16[8,256,128]{2,1,0:T(8,128)(2,1)}), bf16[8,256,128]{2,1,0:T(8,128)(2,1)S(1)}, u32[]{:S(2)}, u32[]{:S(2)}) async-start(bf16[8,256,128]{2,1,0:T(8,128)(2,1)} %bitcast.36), calls=%async_computation.2 | async-start | bytes 1048576 | tf_op jit(solution)/shard_map/all_to_all | solution.py:397
  105.8 0.0 all-gather.8.cloned.1.call-start
  105.9 0.0 all-gather.12.cloned.1.call-done
  105.9 10.3 %all-to-all-done.2.mean_ref = bf16[8,256,128]{2,1,0:T(8,128)(2,1)S(1)} async-done(((bf16[8,256,128]{2,1,0:T(8,128)(2,1)}), bf16[8,256,128]{2,1,0:T(8,128)(2,1)S(1)}, u32[]{:S(2)}, u32[]{:S(2)}) %all-to-all-start.2) | async-done | bytes 524320 | tf_op jit(solution)/shard_map/all_to_all | solution.py:397
  116.2 1.2 copy-done.4
  117.4 5.8 %dense.1 = (bf16[8,256,128]{2,1,0:T(8,128)(2,1)S(1)}, bf16[8,256,128]{2,1,0:T(8,128)(2,1)}, bf16[256,1024]{1,0:T(8,128)(2,1)}) custom-call(s32[1]{0:T(128)} %bitcast.at_ref, bf16[8,256,128]{2,1,0:T(8,128)(2,1)S(1)} %all-to-all-done.2.mean_ref, f32[256,1024]{1,0:T(8,128)S(1)} %copy-done.4, bf16[8,2048,128]{2,1,0:T(8,128)(2,1)} %bitcast.40, ...), custom_call_target="tpu_custom_call" | custom-call | tf_op jit(solution)/shard_map/dense/pallas_call | solution.py:312
  123.2 12.8 %all_to_all.31 = bf16[8,256,128]{2,1,0:T(8,128)(2,1)S(1)} all-to-all(bf16[8,256,128]{2,1,0:T(8,128)(2,1)S(1)} %get-tuple-element.30), channel_id=1, replica_groups=mesh['z'=8,'y'=4,'feat'=8] {'feat'}, dimensions={0} | all-to-all | bytes 1048576 | tf_op jit(solution)/shard_map/all_to_all | solution.py:397
  136.0 0.0 all-gather.8.cloned.1.call-update
  136.1 0.0 copy-start.7
  136.1 4.4 %gather_rows.3 = bf16[32,128,128]{2,1,0:T(8,128)(2,1)S(1)} custom-call(f32[4,4,128,8]{3,2,1,0:T(8,128)S(1)} %bitcast.30, f32[4,4,128,8]{3,2,1,0:T(8,128)S(1)} %bitcast.31, bf16[2048,128]{1,0:T(8,128)(2,1)S(1)} %bitcast.34), custom_call_target="tpu_custom_call" | custom-call | tf_op jit(solution)/shard_map/gather_rows/pallas_call | solution.py:229
  140.4 1.0 copy-done
  141.4 6.1 %all-to-all-start.4 = ((bf16[32,128,128]{2,1,0:T(8,128)(2,1)}), bf16[32,128,128]{2,1,0:T(8,128)(2,1)S(1)}, u32[]{:S(2)}, u32[]{:S(2)}) async-start(bf16[32,128,128]{2,1,0:T(8,128)(2,1)} %copy-done), calls=%async_computation.4 | async-start | bytes 2097152 | tf_op jit(solution)/shard_map/all_to_all | solution.py:397
  147.5 0.0 all-gather.14.cloned.1.call-start
  147.5 5.1 %gather_rows.2 = bf16[32,128,128]{2,1,0:T(8,128)(2,1)} custom-call(f32[4,4,128,8]{3,2,1,0:T(8,128)S(1)} %bitcast.32, f32[4,4,128,8]{3,2,1,0:T(8,128)S(1)} %bitcast.33, bf16[2048,128]{1,0:T(8,128)(2,1)S(1)} %bitcast.35), custom_call_target="tpu_custom_call" | custom-call | tf_op jit(solution)/shard_map/gather_rows/pallas_call | solution.py:229
  152.6 21.8 %all-to-all-done.4.low_ref = bf16[32,128,128]{2,1,0:T(8,128)(2,1)S(1)} async-done(((bf16[32,128,128]{2,1,0:T(8,128)(2,1)}), bf16[32,128,128]{2,1,0:T(8,128)(2,1)S(1)}, u32[]{:S(2)}, u32[]{:S(2)}) %all-to-all-start.4) | async-done | bytes 1048608 | tf_op jit(solution)/shard_map/all_to_all | solution.py:397
  174.5 3.6 %convolution_convert_fusion = bf16[256,1024]{1,0:T(8,128)(2,1)S(1)} fusion(bf16[2048,1024]{1,0:T(8,128)(2,1)} %all-gather.8.cloned.1.call-done, bf16[2048,128]{1,0:T(8,128)(2,1)S(1)} %copy-done.7, bf16[2048,128]{1,0:T(8,128)(2,1)} %feat_ref.1), kind=kOutput, calls=%fused_computation | convolution fusion | flops 1076101120 | bytes 5767168 | tf_op jit(solution)/shard_map/dot_general | solution.py:518
  178.1 0.0 all-gather.14.cloned.1.call-update
  178.1 6.4 %all-to-all-start.5 = ((bf16[32,128,128]{2,1,0:T(8,128)(2,1)}), bf16[32,128,128]{2,1,0:T(8,128)(2,1)}, u32[]{:S(2)}, u32[]{:S(2)}) async-start(bf16[32,128,128]{2,1,0:T(8,128)(2,1)} %gather_rows.2), calls=%async_computation.5 | async-start | bytes 2097152 | tf_op jit(solution)/shard_map/all_to_all | solution.py:397
  184.6 1.6 collective-permute-start
  186.2 2.6 %collective-permute-start.1 = (bf16[64,1024]{1,0:T(8,128)(2,1)S(1)}, bf16[64,1024]{1,0:T(8,128)(2,1)S(1)}, u32[]{:S(2)}, u32[]{:S(2)}) collective-permute-start(bf16[64,1024]{1,0:T(8,128)(2,1)S(1)} %get-tuple-element.46), channel_id=1, source_target_pairs={{0,16},{8,24},{16,0},{24,8},{1,17},{9,25},{17,1},{25,9},{2,18},{10... | collective-permute-start | bytes 393224 | tf_op jit(solution)/shard_map/ppermute | solution.py:406
  188.8 1.5 collective-permute-start.2
  190.3 3.5 %fusion.6.self_ref = f32[2048,128]{1,0:T(8,128)S(1)} fusion(bf16[2048,1024]{1,0:T(8,128)(2,1)} %all-gather.8.cloned.1.call-done, bf16[1024,1024]{1,0:T(8,128)(2,1)} %weight_ref.2, s32[]{:T(128)S(6)} %select_n.36), kind=kOutput, calls=%fused_computation.11 | convolution fusion | flops 536870912 | bytes 5505028 | tf_op jit(solution)/shard_map/dot_general | solution.py:524
  193.8 1.2 collective-permute-done
  195.0 2.9 %collective-permute-done.1 = bf16[64,1024]{1,0:T(8,128)(2,1)S(1)} collective-permute-done((bf16[64,1024]{1,0:T(8,128)(2,1)S(1)}, bf16[64,1024]{1,0:T(8,128)(2,1)S(1)}, u32[]{:S(2)}, u32[]{:S(2)}) %collective-permute-start.1) | collective-permute-done | bytes 131104 | tf_op jit(solution)/shard_map/ppermute | solution.py:406
  197.9 1.9 collective-permute-done.2
  199.9 1.0 fusion.5
  200.8 3.9 %collective-permute-start.3 = (bf16[64,1024]{1,0:T(8,128)(2,1)S(1)}, bf16[64,1024]{1,0:T(8,128)(2,1)S(1)}, u32[]{:S(2)}, u32[]{:S(2)}) collective-permute-start(bf16[64,1024]{1,0:T(8,128)(2,1)S(1)} %fusion.5), channel_id=1, source_target_pairs={{0,128},{32,160},{64,192},{96,224},{128,0},{160,32},{192,64},{224,... | collective-permute-start | bytes 393224 | tf_op jit(solution)/shard_map/ppermute | solution.py:426
  204.7 11.2 %collective-permute-done.3 = bf16[64,1024]{1,0:T(8,128)(2,1)S(1)} collective-permute-done((bf16[64,1024]{1,0:T(8,128)(2,1)S(1)}, bf16[64,1024]{1,0:T(8,128)(2,1)S(1)}, u32[]{:S(2)}, u32[]{:S(2)}) %collective-permute-start.3) | collective-permute-done | bytes 131104 | tf_op jit(solution)/shard_map/ppermute | solution.py:426
  216.0 0.1 collective-permute-start.4
  216.1 7.2 %collective-permute-done.4 = bf16[64,1024]{1,0:T(8,128)(2,1)S(1)} collective-permute-done((bf16[64,1024]{1,0:T(8,128)(2,1)S(1)}, bf16[64,1024]{1,0:T(8,128)(2,1)S(1)}, u32[]{:S(2)}, u32[]{:S(2)}) %collective-permute-start.4) | collective-permute-done | bytes 131104 | tf_op jit(solution)/shard_map/ppermute | solution.py:426
  223.3 0.1 collective-permute-start.5
  223.4 0.0 all-gather.14.cloned.1.call-done
  223.4 1.9 constant_dynamic-slice_fusion
  225.3 3.0 %collective-permute-done.5 = bf16[64,1024]{1,0:T(8,128)(2,1)S(1)} collective-permute-done((bf16[64,1024]{1,0:T(8,128)(2,1)S(1)}, bf16[64,1024]{1,0:T(8,128)(2,1)S(1)}, u32[]{:S(2)}, u32[]{:S(2)}) %collective-permute-start.5) | collective-permute-done | bytes 131104 | tf_op jit(solution)/shard_map/ppermute | solution.py:426
  228.4 2.3 collective-permute-start.6
  230.7 1.1 collective-permute-start.7
  231.8 0.7 collective-permute-start.8
  232.4 7.8 %backward_blocks.1 = bf16[2048,128]{1,0:T(8,128)(2,1)} custom-call(s32[128]{0:T(128)S(1)} %copy-done.11, s32[128]{0:T(128)S(1)} %copy-done.13, bf16[32,128,128]{2,1,0:T(8,128)(2,1)S(1)} %all-to-all-done.4.low_ref, bf16[32,128,128]{2,1,0:T(8,128)(2,1)} %all-to-all-done.5.high_ref, bf16[128,128,128]{2,1,0:T(8,128)(2,1)} %bitcast.39, ...), custom_call_target="tpu_custom_call" | custom-call | tf_op jit(solution)/shard_map/backward_blocks/pallas_call | solution.py:373
  240.3 1.1 assemble.1
  (32 shorter events, 0.2 us)
Async XLA Ops:
  7.2 74.6 %all-gather.10.cloned.1.call-start = ((), (), s32[]{:S(2)}) async-start(), calls=%async_computation.7 | async-start | bytes 4718592 | tf_op jit(solution)/shard_map/all_gather | solution.py:489
  7.9 98.0 %all-gather.12.cloned.1.call-start = ((), (), s32[]{:S(2)}) async-start(), calls=%async_computation.8 | async-start | bytes 4718592 | tf_op jit(solution)/shard_map/all_gather | solution.py:490
  8.6 1.0 copy-start.8
  9.7 0.8 copy-start.9
  10.5 0.7 copy-start.10
  11.1 0.7 copy-start.12
  11.8 0.7 copy-start.14
  12.4 55.7 %copy-start.16 = (s32[2048]{0:T(1024)S(1)}, s32[2048]{0:T(1024)}, u32[]{:S(2)}) copy-start(s32[2048]{0:T(1024)} %param.18) | copy-start | bytes 24580
  62.7 31.5 %all-to-all-start.1 = ((bf16[32,128,128]{2,1,0:T(8,128)(2,1)}), bf16[32,128,128]{2,1,0:T(8,128)(2,1)}, u32[]{:S(2)}, u32[]{:S(2)}) async-start(bf16[32,128,128]{2,1,0:T(8,128)(2,1)} %get-tuple-element.25), calls=%async_computation.1 | async-start | bytes 2097152 | tf_op jit(solution)/shard_map/all_to_all | solution.py:397
  80.7 1.0 copy-start.1
  81.7 1.6 copy-start.5
  85.9 1.0 copy-start.3
  94.2 1.2 copy-start.2
  100.7 0.8 copy-start.6
  101.5 14.7 %all-to-all-start.2 = ((bf16[8,256,128]{2,1,0:T(8,128)(2,1)}), bf16[8,256,128]{2,1,0:T(8,128)(2,1)S(1)}, u32[]{:S(2)}, u32[]{:S(2)}) async-start(bf16[8,256,128]{2,1,0:T(8,128)(2,1)} %bitcast.36), calls=%async_computation.2 | async-start | bytes 1048576 | tf_op jit(solution)/shard_map/all_to_all | solution.py:397
  105.8 68.6 %all-gather.8.cloned.1.call-start = ((), (), s32[]{:S(2)}) async-start(), calls=%async_computation.6 | async-start | bytes 4718592 | tf_op jit(solution)/shard_map/all_gather | solution.py:514
  116.2 1.2 copy-start.4
  136.1 38.4 %copy-start.7 = (bf16[2048,128]{1,0:T(8,128)(2,1)S(1)}, bf16[2048,128]{1,0:T(8,128)(2,1)}, u32[]{:S(2)}) copy-start(bf16[2048,128]{1,0:T(8,128)(2,1)} %copy-done.6) | copy-start | bytes 1572868
  140.4 1.0 copy-start
  141.4 33.1 %all-to-all-start.4 = ((bf16[32,128,128]{2,1,0:T(8,128)(2,1)}), bf16[32,128,128]{2,1,0:T(8,128)(2,1)S(1)}, u32[]{:S(2)}, u32[]{:S(2)}) async-start(bf16[32,128,128]{2,1,0:T(8,128)(2,1)} %copy-done), calls=%async_computation.4 | async-start | bytes 2097152 | tf_op jit(solution)/shard_map/all_to_all | solution.py:397
  147.5 75.9 %all-gather.14.cloned.1.call-start = ((), (), s32[]{:S(2)}) async-start(), calls=%async_computation.9 | async-start | bytes 4718592 | tf_op jit(solution)/shard_map/all_gather | solution.py:521
  178.1 10.7 %copy-start.15 = (bf16[256,1024]{1,0:T(8,128)(2,1)}, bf16[256,1024]{1,0:T(8,128)(2,1)S(1)}, u32[]{:S(2)}) copy-start(bf16[256,1024]{1,0:T(8,128)(2,1)S(1)} %convolution_convert_fusion) | copy-start | bytes 1572868
  178.1 45.1 %all-to-all-start.5 = ((bf16[32,128,128]{2,1,0:T(8,128)(2,1)}), bf16[32,128,128]{2,1,0:T(8,128)(2,1)}, u32[]{:S(2)}, u32[]{:S(2)}) async-start(bf16[32,128,128]{2,1,0:T(8,128)(2,1)} %gather_rows.2), calls=%async_computation.5 | async-start | bytes 2097152 | tf_op jit(solution)/shard_map/all_to_all | solution.py:397
  184.6 10.4 %collective-permute-start = (bf16[64,1024]{1,0:T(8,128)(2,1)S(1)}, bf16[64,1024]{1,0:T(8,128)(2,1)S(1)}, u32[]{:S(2)}, u32[]{:S(2)}) collective-permute-start(bf16[64,1024]{1,0:T(8,128)(2,1)S(1)} %get-tuple-element.44), channel_id=1, source_target_pairs={{0,8},{8,16},{16,24},{24,0},{1,9},{9,17},{17,25},{25,1},{2,10},{10... | collective-permute-start | bytes 393224 | tf_op jit(solution)/shard_map/ppermute | solution.py:406
  186.2 11.8 %collective-permute-start.1 = (bf16[64,1024]{1,0:T(8,128)(2,1)S(1)}, bf16[64,1024]{1,0:T(8,128)(2,1)S(1)}, u32[]{:S(2)}, u32[]{:S(2)}) collective-permute-start(bf16[64,1024]{1,0:T(8,128)(2,1)S(1)} %get-tuple-element.46), channel_id=1, source_target_pairs={{0,16},{8,24},{16,0},{24,8},{1,17},{9,25},{17,1},{25,9},{2,18},{10... | collective-permute-start | bytes 393224 | tf_op jit(solution)/shard_map/ppermute | solution.py:406
  188.8 43.6 %copy-start.11 = (s32[128]{0:T(128)S(1)}, s32[128]{0:T(128)}, u32[]{:S(2)}) copy-start(s32[128]{0:T(128)} %source_ref.3) | copy-start | bytes 1540
  188.8 43.6 %copy-start.13 = (s32[128]{0:T(128)S(1)}, s32[128]{0:T(128)}, u32[]{:S(2)}) copy-start(s32[128]{0:T(128)} %slot_ref.3) | copy-start | bytes 1540
  188.8 11.0 %collective-permute-start.2 = (bf16[64,1024]{1,0:T(8,128)(2,1)S(1)}, bf16[64,1024]{1,0:T(8,128)(2,1)S(1)}, u32[]{:S(2)}, u32[]{:S(2)}) collective-permute-start(bf16[64,1024]{1,0:T(8,128)(2,1)S(1)} %get-tuple-element.45), channel_id=1, source_target_pairs={{0,24},{8,0},{16,8},{24,16},{1,25},{9,1},{17,9},{25,17},{2,26},{10... | collective-permute-start | bytes 393224 | tf_op jit(solution)/shard_map/ppermute | solution.py:406
  200.8 15.1 %collective-permute-start.3 = (bf16[64,1024]{1,0:T(8,128)(2,1)S(1)}, bf16[64,1024]{1,0:T(8,128)(2,1)S(1)}, u32[]{:S(2)}, u32[]{:S(2)}) collective-permute-start(bf16[64,1024]{1,0:T(8,128)(2,1)S(1)} %fusion.5), channel_id=1, source_target_pairs={{0,128},{32,160},{64,192},{96,224},{128,0},{160,32},{192,64},{224,... | collective-permute-start | bytes 393224 | tf_op jit(solution)/shard_map/ppermute | solution.py:426
  216.0 7.3 %collective-permute-start.4 = (bf16[64,1024]{1,0:T(8,128)(2,1)S(1)}, bf16[64,1024]{1,0:T(8,128)(2,1)S(1)}, u32[]{:S(2)}, u32[]{:S(2)}) collective-permute-start(bf16[64,1024]{1,0:T(8,128)(2,1)S(1)} %add_convert_fusion.2), channel_id=1, source_target_pairs={{0,64},{32,96},{64,0},{96,32},{128,192},{160,224},{192,128},{224,1... | collective-permute-start | bytes 393224 | tf_op jit(solution)/shard_map/ppermute | solution.py:426
  223.3 5.1 %collective-permute-start.5 = (bf16[64,1024]{1,0:T(8,128)(2,1)S(1)}, bf16[64,1024]{1,0:T(8,128)(2,1)S(1)}, u32[]{:S(2)}, u32[]{:S(2)}) collective-permute-start(bf16[64,1024]{1,0:T(8,128)(2,1)S(1)} %add_convert_fusion.1), channel_id=1, source_target_pairs={{0,32},{32,0},{64,96},{96,64},{128,160},{160,128},{192,224},{224,1... | collective-permute-start | bytes 393224 | tf_op jit(solution)/shard_map/ppermute | solution.py:426
  228.4 11.9 %collective-permute-start.6 = (bf16[64,1024]{1,0:T(8,128)(2,1)S(1)}, bf16[64,1024]{1,0:T(8,128)(2,1)S(1)}, u32[]{:S(2)}, u32[]{:S(2)}) collective-permute-start(bf16[64,1024]{1,0:T(8,128)(2,1)S(1)} %add_convert_fusion.refs_0_), channel_id=1, source_target_pairs={{0,24},{8,0},{16,8},{24,16},{1,25},{9,1},{17,9},{25,17},{2,26},{10... | collective-permute-start | bytes 393224 | tf_op jit(solution)/shard_map/ppermute | solution.py:406
  230.7 9.6 %collective-permute-start.7 = (bf16[64,1024]{1,0:T(8,128)(2,1)S(1)}, bf16[64,1024]{1,0:T(8,128)(2,1)S(1)}, u32[]{:S(2)}, u32[]{:S(2)}) collective-permute-start(bf16[64,1024]{1,0:T(8,128)(2,1)S(1)} %add_convert_fusion.refs_0_), channel_id=1, source_target_pairs={{0,16},{8,24},{16,0},{24,8},{1,17},{9,25},{17,1},{25,9},{2,18},{10... | collective-permute-start | bytes 393224 | tf_op jit(solution)/shard_map/ppermute | solution.py:406
  231.8 8.5 %collective-permute-start.8 = (bf16[64,1024]{1,0:T(8,128)(2,1)S(1)}, bf16[64,1024]{1,0:T(8,128)(2,1)S(1)}, u32[]{:S(2)}, u32[]{:S(2)}) collective-permute-start(bf16[64,1024]{1,0:T(8,128)(2,1)S(1)} %add_convert_fusion.refs_0_), channel_id=1, source_target_pairs={{0,8},{8,16},{16,24},{24,0},{1,9},{9,17},{17,25},{25,1},{2,10},{10... | collective-permute-start | bytes 393224 | tf_op jit(solution)/shard_map/ppermute | solution.py:406
Sparse Core Ops, SparseCore 0:
  9.9 37.2 all-gather.9
  49.0 34.6 all-gather.11
  136.2 30.0 all-gather.7
  178.3 30.3 all-gather.13

commit v5 on v4

--- a/solution.py
+++ b/solution.py
@@ -9,7 +9,7 @@
 
 BF16 = jnp.bfloat16
 F32 = jnp.float32
-VMEM_BYTES = 48 * 1024 * 1024
+VMEM_BYTES = 20 * 1024 * 1024
 ID_ROWS = 8
 
 
@@ -190,7 +190,7 @@
             full_spec((nodes, 1)),
         ],
         out_specs=full_spec((nodes, cols)),
-        out_shape=jax.ShapeDtypeStruct((nodes, cols), BF16),
+        out_shape=pltpu.HBM((nodes, cols), BF16),
         scratch_shapes=[
             pltpu.VMEM((nodes // 2, group * blk), BF16),
             pltpu.VMEM((group * blk, 2 * cols), BF16),
@@ -235,7 +235,7 @@
             full_spec((nodes, cols)),
         ],
         out_specs=pl.BlockSpec((group, blk, cols), lambda i: (i, 0, 0)),
-        out_shape=jax.ShapeDtypeStruct((steps * group, blk, cols), BF16),
+        out_shape=pltpu.HBM((steps * group, blk, cols), BF16),
         scratch_shapes=[pltpu.VMEM((group * blk, nodes // 2), BF16)],
         compiler_params=params(1),
         name="gather_rows",
@@ -393,6 +393,10 @@
     )(block_source, block_to_slot, low, high, adjacency_t, self_grad)
 
 
+def in_hbm(value):
+    return pltpu.with_memory_space_constraint(value, pltpu.HBM)
+
+
 def swap(value, axis):
     return lax.all_to_all(value, axis, split_axis=0, concat_axis=0, tiled=True)
 
@@ -482,27 +486,32 @@
     share = node_rows // feat_size
     graph = ("z", "y")
     low, high = forward_blocks(
-        block_source, block_to_slot, send_counts[0], send_rows[0], features, adjacency
+        block_source,
+        block_to_slot,
+        send_counts[0],
+        in_hbm(send_rows[0]),
+        in_hbm(features),
+        in_hbm(adjacency),
     )
     low_in = swap(low, graph)
     high_in = swap(high, graph)
     feat_all = lax.all_gather(features, "feat", axis=0)
     cot_all = lax.all_gather(cotangent, "feat", axis=0)
     degrees = degree.astype(F32)[:, None]
-    adjacency_t = after(adjacency, low_in).swapaxes(1, 2)
+    adjacency_t = in_hbm(after(adjacency, low_in).swapaxes(1, 2))
     self_rows = lax.dynamic_slice_in_dim(w_self, feat_at * feat_cols, feat_cols, 0)
 
     partial_sum = scatter_low(low_in, node_rows)
     blk = adjacency.shape[1]
     parts = low.shape[0]
     ids = low_in[:, blk : blk + 4, :].astype(F32).reshape(parts // 8, 8, 4, blk).transpose(2, 0, 3, 1)
-    own = own_term(at, feat_all, w_self, share)
+    own = own_term(at, in_hbm(feat_all), w_self, share)
     partial_sum, adjacency_t, ids, own = lax.optimization_barrier(
         (partial_sum, adjacency_t, ids, own)
     )
     neighbor_mean = scatter_high(low_in, high_in, ids, partial_sum, degrees)
     mean_pieces = swap(neighbor_mean.reshape(feat_size, share, feat_cols), "feat")
-    back_pieces, hidden_pieces, grad_pre = dense(at, mean_pieces, own, cot_all, w_neigh, degrees)
+    back_pieces, hidden_pieces, grad_pre = dense(at, mean_pieces, own, in_hbm(cot_all), w_neigh, degrees)
     back_rows = swap(back_pieces, "feat").reshape(node_rows, feat_cols)
     back_rows, grad_pre, hidden_pieces = lax.optimization_barrier(
         (back_rows, grad_pre, hidden_pieces)
@@ -510,32 +519,31 @@
     rows_low = gather_rows(0, ids, back_rows)
     rows_high = gather_rows(1, ids, back_rows)
     back_low = swap(rows_low, graph)
-    back_high = swap(rows_high, graph)
     grad_full = lax.all_gather(grad_pre, "feat", axis=0, tiled=True)
-    grad_full = after(grad_full, rows_high, back_low)
-
+    grad_full = after(grad_full, rows_high)
     both = jnp.concatenate([features, neighbor_mean], axis=1)
     weight_part = lax.dot_general(
         both, grad_full, (((0,), (0,)), ((), ())), preferred_element_type=F32
     ).astype(BF16)
-    hidden_all = lax.all_gather(after(hidden_pieces, weight_part), "feat", axis=0)
+    over_y = lax.axis_size("y")
+    part = weight_part.reshape(over_y, 2 * feat_cols // over_y, weight_part.shape[1])
+    part = scatter_sum(part, "y")
+    back_high = swap(after(rows_high, part, back_low), graph)
+
+    hidden_all = lax.all_gather(after(hidden_pieces, rows_low), "feat", axis=0)
     hidden_out = lax.dynamic_index_in_dim(hidden_all, feat_at, 1, keepdims=False)
     hidden_out = hidden_out.reshape(node_rows, feat_cols)
     self_grad = lax.dot_general(
         grad_full, self_rows, (((1,), (1,)), ((), ())), preferred_element_type=F32
     )
-    over_y = lax.axis_size("y")
-    part = weight_part.reshape(over_y, 2 * feat_cols // over_y, weight_part.shape[1])
-    part = after(scatter_sum(part, "y"), self_grad)
-    part = exchange_sum(part, "z", 4)
+    part = exchange_sum(part, "z", 4, self_grad)
     part = exchange_sum(part, "z", 2)
-    part = after(part, back_high)
     part = exchange_sum(part, "z", 1, hidden_out)
     grad_features = backward_blocks(
         block_source, block_to_slot, back_low, back_high, adjacency_t, self_grad
     )
     grad_self, grad_neigh = assemble(
-        jnp.full((1,), lax.axis_index("y"), jnp.int32), around(part, "y")
+        jnp.full((1,), lax.axis_index("y"), jnp.int32), around(after(part, back_high), "y")
     )
     return hidden_out, grad_features, grad_self, grad_neigh
 

time: 251 us -> 258 us (1.028)
  starting transfers between devices: 36.2 us -> 40.7 us
  waiting for transfers between devices: 68.4 us -> 71.8 us
    all_to_all x4, waiting for transfers between devices: 39.4 us -> 17.7 us  [swap(): return lax.all_to_all(value, axis, split_axis=0, concat_axis=0, tiled=True)]
    all_gather x1, waiting for transfers between devices: 0.01 us -> 13.9 us  [on_device(): grad_full = lax.all_gather(grad_pre, 'feat', axis=0, tiled=True)]
    ppermute x3, waiting for transfers between devices: 21.4 us -> 33.5 us  [exchange_sum(): other = lax.ppermute(value, axis, [(i, i ^ distance) for i in range(size)])]
    all_to_all x4, starting transfers between devices: 22.3 us -> 25.4 us  [swap(): return lax.all_to_all(value, axis, split_axis=0, concat_axis=0, tiled=True)]
    unnamed x34 -> x26, local copies, waits for them, and re-layouts: 11.5 us -> 9.59 us
  transfers between devices with their start and end apart: 17 -> 17, of which waited for: 9 -> 8; matrix products, arithmetic and copies ran while one was open for 5% -> 6% of each run, Pallas kernels for 16% -> 16%
where the time goes in v5:
time: 258 us; the launch traced here: 254 us
  waiting for transfers between devices  71.8 us (28%)
  blocking collectives  54.6 us (21%)
  Pallas kernels  47.2 us (18%)
  starting transfers between devices  40.7 us (16%)
  local copies, waits for them, and re-layouts  18.5 us (7%)
  between operations  14 us (5%)
  matrix products  7.19 us (3%)
    all_to_all x2, blocking collectives, swap(): return lax.all_to_all(value, axis, split_axis=0, concat_axis=0, tiled=True)  54.6 us
    ppermute x3, waiting for transfers between devices, exchange_sum(): other = lax.ppermute(value, axis, [(i, i ^ distance) for i in range(size)])  33.5 us
    all_to_all x4, starting transfers between devices, swap(): return lax.all_to_all(value, axis, split_axis=0, concat_axis=0, tiled=True)  25.4 us
    all_to_all x4, waiting for transfers between devices, swap(): return lax.all_to_all(value, axis, split_axis=0, concat_axis=0, tiled=True)  17.7 us
    all_gather x1, waiting for transfers between devices, on_device(): grad_full = lax.all_gather(grad_pre, 'feat', axis=0, tiled=True)  13.9 us
    ppermute x6, starting transfers between devices, rotate(): lax.ppermute(value, axis, [(i, (i + distance) % size) for i in range(size)])  10.4 us
    pallas_call x2, Pallas kernels, gather_rows(): pl.pallas_call(gather_kernel, grid=(steps,), in_specs=[pl.BlockSpec((1, 1...  10.1 us
    unnamed x26, local copies, waits for them, and re-layouts  9.59 us
  transfers between devices with their start and end apart: 17, of which 8 were waited for; matrix products, arithmetic and copies ran while one was open for 6% of the time, Pallas kernels for 16%

profile of v5, /device:TPU:32, one launch (start us, length us, event | category | flops | bytes accessed | tf_op | source)
XLA Modules:
  0.0 254.3 jit_solution(2423258164871149895)
XLA Ops:
  7.2 0.0 all-gather.10.cloned.1.call-start
  7.2 0.7 all-gather.10.cloned.1.call-update
  7.9 0.0 all-gather.12.cloned.1.call-start
  7.9 0.7 all-gather.12.cloned.1.call-update
  8.6 0.0 copy-start.6
  8.7 0.6 copy-done.6
  9.3 0.7 copy-done.8
  10.0 0.7 copy-done.10
  10.6 8.6 %forward_blocks.1 = (bf16[32,136,128]{2,1,0:T(8,128)(2,1)S(1)}, bf16[32,128,128]{2,1,0:T(8,128)(2,1)}) custom-call(s32[128]{0:T(128)S(1)} %copy-done.6, s32[128]{0:T(128)S(1)} %copy-done.8, s32[32]{0:T(128)S(1)} %bitcast.36, s32[32,256]{1,0:T(8,128)} %bitcast.46, bf16[2048,128]{1,0:T(8,128)(2,1)} %feat_ref.1, bf16[128,128,128]{2,1,0:T(8,128)(2,1)} %adj_ref.1), custom_call_target="tpu_custom_call" | custom-call | tf_op jit(solution)/shard_map/forward_blocks/pallas_call | solution.py:77
  19.2 41.9 %all_to_all.30.payload_ids_ref.rows_ref.ids_ref = bf16[32,136,128]{2,1,0:T(8,128)(2,1)S(1)} all-to-all(bf16[32,136,128]{2,1,0:T(8,128)(2,1)S(1)} %get-tuple-element.25), channel_id=1, replica_groups=mesh['z'=8,'y'=4,'feat'=8] {'z','y'}, dimensions={0} | all-to-all | bytes 2228224 | tf_op jit(solution)/shard_map/all_to_all | solution.py:401
  61.1 5.5 %all-to-all-start.1 = ((bf16[32,128,128]{2,1,0:T(8,128)(2,1)}), bf16[32,128,128]{2,1,0:T(8,128)(2,1)}, u32[]{:S(2)}, u32[]{:S(2)}) async-start(bf16[32,128,128]{2,1,0:T(8,128)(2,1)} %get-tuple-element.26), calls=%async_computation.1 | async-start | bytes 2097152 | tf_op jit(solution)/shard_map/all_to_all | solution.py:401
  66.6 0.4 copy.28.degree_ref
  66.9 6.4 %copy.25 = bf16[128,128,128]{1,2,0:T(8,128)(2,1)} copy(bf16[128,128,128]{2,1,0:T(8,128)(2,1)} %adj_ref.1) | data formatting | bytes 8388608 | tf_op jit(solution)/shard_map/optimization_barrier | solution.py:405
  73.4 0.2 copy.27
  73.6 5.4 %scatter_low.1.init_ref = f32[2048,128]{1,0:T(8,128)S(1)} custom-call(bf16[32,136,128]{2,1,0:T(8,128)(2,1)S(1)} %all_to_all.30.payload_ids_ref.rows_ref.ids_ref, bf16[32,136,128]{2,1,0:T(8,128)(2,1)S(1)} %all_to_all.30.payload_ids_ref.rows_ref.ids_ref), custom_call_target="tpu_custom_call" | custom-call | tf_op jit(solution)/shard_map/scatter_low/pallas_call | solution.py:163
  79.0 1.0 copy-done
  80.0 1.6 copy-done.4
  81.6 2.6 %own_term.1.own_ref = f32[256,1024]{1,0:T(8,128)S(1)} custom-call(s32[1]{0:T(128)} %bitcast.at_ref, bf16[8,2048,128]{2,1,0:T(8,128)(2,1)} %bitcast.39, bf16[1024,1024]{1,0:T(8,128)(2,1)S(1)} %copy-done.4), custom_call_target="tpu_custom_call" | custom-call | tf_op jit(solution)/shard_map/own_term/pallas_call | solution.py:255
  84.2 1.0 copy-done.2
  85.2 7.4 %all-to-all-done.1.rows_ref = bf16[32,128,128]{2,1,0:T(8,128)(2,1)} async-done(((bf16[32,128,128]{2,1,0:T(8,128)(2,1)}), bf16[32,128,128]{2,1,0:T(8,128)(2,1)}, u32[]{:S(2)}, u32[]{:S(2)}) %all-to-all-start.1) | async-done | bytes 1048608 | tf_op jit(solution)/shard_map/all_to_all | solution.py:401
  92.6 1.2 copy-done.1
  93.8 6.1 %scatter_high.1 = bf16[2048,128]{1,0:T(8,128)(2,1)} custom-call(bf16[32,136,128]{2,1,0:T(8,128)(2,1)S(1)} %all_to_all.30.payload_ids_ref.rows_ref.ids_ref, bf16[32,128,128]{2,1,0:T(8,128)(2,1)} %all-to-all-done.1.rows_ref, f32[4,4,128,8]{3,2,1,0:T(8,128)S(1)} %bitcast.29, f32[2048,128]{1,0:T(8,128)S(1)} %copy-done.1, f32[2048,1]{1,0:T(8,128)S(1)} %copy.28.degree_ref), custom_call_target="tpu_custom_call" | custom-call | tf_op jit(solution)/shard_map/scatter_high/pallas_call | solution.py:182
  99.9 4.3 %all-to-all-start.2 = ((bf16[8,256,128]{2,1,0:T(8,128)(2,1)}), bf16[8,256,128]{2,1,0:T(8,128)(2,1)S(1)}, u32[]{:S(2)}, u32[]{:S(2)}) async-start(bf16[8,256,128]{2,1,0:T(8,128)(2,1)} %bitcast.40), calls=%async_computation.2 | async-start | bytes 1048576 | tf_op jit(solution)/shard_map/all_to_all | solution.py:401
  104.2 0.0 all-gather.8.cloned.1.call-start
  104.2 0.0 all-gather.12.cloned.1.call-done
  104.2 10.3 %all-to-all-done.2.mean_ref = bf16[8,256,128]{2,1,0:T(8,128)(2,1)S(1)} async-done(((bf16[8,256,128]{2,1,0:T(8,128)(2,1)}), bf16[8,256,128]{2,1,0:T(8,128)(2,1)S(1)}, u32[]{:S(2)}, u32[]{:S(2)}) %all-to-all-start.2) | async-done | bytes 524320 | tf_op jit(solution)/shard_map/all_to_all | solution.py:401
  114.5 1.2 copy-done.3
  115.8 1.6 copy-done.5
  117.3 5.5 %dense.1 = (bf16[8,256,128]{2,1,0:T(8,128)(2,1)S(1)}, bf16[8,256,128]{2,1,0:T(8,128)(2,1)}, bf16[256,1024]{1,0:T(8,128)(2,1)}) custom-call(s32[1]{0:T(128)} %bitcast.at_ref, bf16[8,256,128]{2,1,0:T(8,128)(2,1)S(1)} %all-to-all-done.2.mean_ref, f32[256,1024]{1,0:T(8,128)S(1)} %copy-done.3, bf16[8,2048,128]{2,1,0:T(8,128)(2,1)} %bitcast.38, ...), custom_call_target="tpu_custom_call" | custom-call | tf_op jit(solution)/shard_map/dense/pallas_call | solution.py:312
  122.8 12.8 %all_to_all.31 = bf16[8,256,128]{2,1,0:T(8,128)(2,1)S(1)} all-to-all(bf16[8,256,128]{2,1,0:T(8,128)(2,1)S(1)} %get-tuple-element.31), channel_id=1, replica_groups=mesh['z'=8,'y'=4,'feat'=8] {'feat'}, dimensions={0} | all-to-all | bytes 1048576 | tf_op jit(solution)/shard_map/all_to_all | solution.py:401
  135.6 0.0 all-gather.8.cloned.1.call-update
  135.7 0.0 copy-start.11
  135.7 0.0 all-gather.14.cloned.1.call-start
  135.7 5.0 %gather_rows.2 = bf16[32,128,128]{2,1,0:T(8,128)(2,1)} custom-call(f32[4,4,128,8]{3,2,1,0:T(8,128)S(1)} %bitcast.30, f32[4,4,128,8]{3,2,1,0:T(8,128)S(1)} %bitcast.31, bf16[2048,128]{1,0:T(8,128)(2,1)S(1)} %bitcast.34), custom_call_target="tpu_custom_call" | custom-call | tf_op jit(solution)/shard_map/gather_rows/pallas_call | solution.py:229
  140.8 0.0 all-gather.14.cloned.1.call-update
  140.8 6.1 %all-to-all-start.4 = ((bf16[32,128,128]{2,1,0:T(8,128)(2,1)}), bf16[32,128,128]{2,1,0:T(8,128)(2,1)S(1)}, u32[]{:S(2)}, u32[]{:S(2)}) async-start(bf16[32,128,128]{2,1,0:T(8,128)(2,1)} %gather_rows.2), calls=%async_computation.4 | async-start | bytes 2097152 | tf_op jit(solution)/shard_map/all_to_all | solution.py:401
  146.9 5.0 %gather_rows.3 = bf16[32,128,128]{2,1,0:T(8,128)(2,1)} custom-call(f32[4,4,128,8]{3,2,1,0:T(8,128)S(1)} %bitcast.32, f32[4,4,128,8]{3,2,1,0:T(8,128)S(1)} %bitcast.33, bf16[2048,128]{1,0:T(8,128)(2,1)S(1)} %bitcast.35), custom_call_target="tpu_custom_call" | custom-call | tf_op jit(solution)/shard_map/gather_rows/pallas_call | solution.py:229
  152.0 13.9 %all-gather.8.cloned.1.call-done = bf16[2048,1024]{1,0:T(8,128)(2,1)} async-done(((bf16[256,1024]{1,0:T(8,128)(2,1)}), bf16[2048,1024]{1,0:T(8,128)(2,1)}) %all-gather.8.cloned.1.call-update) | async-done | bytes 4194320 | tf_op jit(solution)/shard_map/all_gather | solution.py:522
  165.9 3.6 %convolution_convert_fusion = bf16[256,1024]{1,0:T(8,128)(2,1)S(1)} fusion(bf16[2048,1024]{1,0:T(8,128)(2,1)} %all-gather.8.cloned.1.call-done, bf16[2048,128]{1,0:T(8,128)(2,1)S(1)} %copy-done.11, bf16[2048,128]{1,0:T(8,128)(2,1)} %feat_ref.1), kind=kOutput, calls=%fused_computation | convolution fusion | flops 1076101120 | bytes 5767168 | tf_op jit(solution)/shard_map/dot_general | solution.py:525
  169.6 1.6 collective-permute-start
  171.2 2.7 %collective-permute-start.1 = (bf16[64,1024]{1,0:T(8,128)(2,1)S(1)}, bf16[64,1024]{1,0:T(8,128)(2,1)S(1)}, u32[]{:S(2)}, u32[]{:S(2)}) collective-permute-start(bf16[64,1024]{1,0:T(8,128)(2,1)S(1)} %get-tuple-element.48), channel_id=1, source_target_pairs={{0,16},{8,24},{16,0},{24,8},{1,17},{9,25},{17,1},{25,9},{2,18},{10... | collective-permute-start | bytes 393224 | tf_op jit(solution)/shard_map/ppermute | solution.py:410
  173.9 1.4 collective-permute-start.2
  175.3 1.2 collective-permute-done
  176.6 4.0 %collective-permute-done.1 = bf16[64,1024]{1,0:T(8,128)(2,1)S(1)} collective-permute-done((bf16[64,1024]{1,0:T(8,128)(2,1)S(1)}, bf16[64,1024]{1,0:T(8,128)(2,1)S(1)}, u32[]{:S(2)}, u32[]{:S(2)}) %collective-permute-start.1) | collective-permute-done | bytes 131104 | tf_op jit(solution)/shard_map/ppermute | solution.py:410
  180.6 0.1 fusion.5
  180.6 0.0 all-to-all-done.4.low_ref
  180.7 9.6 %all-to-all-start.5 = ((bf16[32,128,128]{2,1,0:T(8,128)(2,1)}), bf16[32,128,128]{2,1,0:T(8,128)(2,1)}, u32[]{:S(2)}, u32[]{:S(2)}) async-start(bf16[32,128,128]{2,1,0:T(8,128)(2,1)} %gather_rows.3), calls=%async_computation.5 | async-start | bytes 2097152 | tf_op jit(solution)/shard_map/all_to_all | solution.py:401
  190.2 0.0 copy-start.7
  190.2 0.0 copy-start.9
  190.3 4.6 %collective-permute-start.3 = (bf16[64,1024]{1,0:T(8,128)(2,1)S(1)}, bf16[64,1024]{1,0:T(8,128)(2,1)S(1)}, u32[]{:S(2)}, u32[]{:S(2)}) collective-permute-start(bf16[64,1024]{1,0:T(8,128)(2,1)S(1)} %fusion.5), channel_id=1, source_target_pairs={{0,128},{32,160},{64,192},{96,224},{128,0},{160,32},{192,64},{224,... | collective-permute-start | bytes 393224 | tf_op jit(solution)/shard_map/ppermute | solution.py:430
  194.8 3.6 %fusion.6.self_ref = f32[2048,128]{1,0:T(8,128)S(1)} fusion(bf16[2048,1024]{1,0:T(8,128)(2,1)} %all-gather.8.cloned.1.call-done, bf16[1024,1024]{1,0:T(8,128)(2,1)} %weight_ref.2, s32[]{:T(128)S(6)} %select_n.43), kind=kOutput, calls=%fused_computation.11 | convolution fusion | flops 536870912 | bytes 5505028 | tf_op jit(solution)/shard_map/dot_general | solution.py:536
  198.4 23.9 %collective-permute-done.3 = bf16[64,1024]{1,0:T(8,128)(2,1)S(1)} collective-permute-done((bf16[64,1024]{1,0:T(8,128)(2,1)S(1)}, bf16[64,1024]{1,0:T(8,128)(2,1)S(1)}, u32[]{:S(2)}, u32[]{:S(2)}) %collective-permute-start.3) | collective-permute-done | bytes 131104 | tf_op jit(solution)/shard_map/ppermute | solution.py:430
  222.3 0.1 collective-permute-start.4
  222.4 6.6 %collective-permute-done.4 = bf16[64,1024]{1,0:T(8,128)(2,1)S(1)} collective-permute-done((bf16[64,1024]{1,0:T(8,128)(2,1)S(1)}, bf16[64,1024]{1,0:T(8,128)(2,1)S(1)}, u32[]{:S(2)}, u32[]{:S(2)}) %collective-permute-start.4) | collective-permute-done | bytes 131104 | tf_op jit(solution)/shard_map/ppermute | solution.py:430
  229.1 0.1 collective-permute-start.5
  229.2 0.0 all-gather.14.cloned.1.call-done
  229.2 1.9 constant_dynamic-slice_fusion
  231.1 3.0 %collective-permute-done.5 = bf16[64,1024]{1,0:T(8,128)(2,1)S(1)} collective-permute-done((bf16[64,1024]{1,0:T(8,128)(2,1)S(1)}, bf16[64,1024]{1,0:T(8,128)(2,1)S(1)}, u32[]{:S(2)}, u32[]{:S(2)}) %collective-permute-start.5) | collective-permute-done | bytes 131104 | tf_op jit(solution)/shard_map/ppermute | solution.py:430
  234.2 0.0 all-to-all-done.5.high_ref
  234.2 3.0 %collective-permute-start.6 = (bf16[64,1024]{1,0:T(8,128)(2,1)S(1)}, bf16[64,1024]{1,0:T(8,128)(2,1)S(1)}, u32[]{:S(2)}, u32[]{:S(2)}) collective-permute-start(bf16[64,1024]{1,0:T(8,128)(2,1)S(1)} %add_convert_fusion.refs_0_), channel_id=1, source_target_pairs={{0,24},{8,0},{16,8},{24,16},{1,25},{9,1},{17,9},{25,17},{2,26},{10... | collective-permute-start | bytes 393224 | tf_op jit(solution)/shard_map/ppermute | solution.py:410
  237.1 0.6 collective-permute-start.7
  237.7 1.1 collective-permute-start.8
  238.8 7.8 %backward_blocks.1 = bf16[2048,128]{1,0:T(8,128)(2,1)} custom-call(s32[128]{0:T(128)S(1)} %copy-done.7, s32[128]{0:T(128)S(1)} %copy-done.9, bf16[32,128,128]{2,1,0:T(8,128)(2,1)S(1)} %all-to-all-done.4.low_ref, bf16[32,128,128]{2,1,0:T(8,128)(2,1)} %all-to-all-done.5.high_ref, bf16[128,128,128]{2,1,0:T(8,128)(2,1)} %bitcast.37, f32[2048,128]{1,0:T(8,128)S(1)} %fusion.6.self_ref), custom_call_target="tpu_custom_call" | custom-call | tf_op jit(solution)/shard_map/backward_blocks/pallas_call | solution.py:373
  246.7 1.1 assemble.1
  (24 shorter events, 0.2 us)
Async XLA Ops:
  7.2 72.8 %all-gather.10.cloned.1.call-start = ((), (), s32[]{:S(2)}) async-start(), calls=%async_computation.7 | async-start | bytes 4718592 | tf_op jit(solution)/shard_map/all_gather | solution.py:498
  7.9 96.3 %all-gather.12.cloned.1.call-start = ((), (), s32[]{:S(2)}) async-start(), calls=%async_computation.8 | async-start | bytes 4718592 | tf_op jit(solution)/shard_map/all_gather | solution.py:499
  8.6 0.7 copy-start.6
  9.3 0.7 copy-start.8
  10.0 0.7 copy-start.10
  10.6 55.9 %copy-start.12 = (s32[2048]{0:T(1024)S(1)}, s32[2048]{0:T(1024)}, u32[]{:S(2)}) copy-start(s32[2048]{0:T(1024)} %param.18) | copy-start | bytes 24580
  61.1 31.5 %all-to-all-start.1 = ((bf16[32,128,128]{2,1,0:T(8,128)(2,1)}), bf16[32,128,128]{2,1,0:T(8,128)(2,1)}, u32[]{:S(2)}, u32[]{:S(2)}) async-start(bf16[32,128,128]{2,1,0:T(8,128)(2,1)} %get-tuple-element.26), calls=%async_computation.1 | async-start | bytes 2097152 | tf_op jit(solution)/shard_map/all_to_all | solution.py:401
  79.0 1.0 copy-start
  80.0 1.6 copy-start.4
  84.2 1.0 copy-start.2
  92.6 1.2 copy-start.1
  99.9 14.6 %all-to-all-start.2 = ((bf16[8,256,128]{2,1,0:T(8,128)(2,1)}), bf16[8,256,128]{2,1,0:T(8,128)(2,1)S(1)}, u32[]{:S(2)}, u32[]{:S(2)}) async-start(bf16[8,256,128]{2,1,0:T(8,128)(2,1)} %bitcast.40), calls=%async_computation.2 | async-start | bytes 1048576 | tf_op jit(solution)/shard_map/all_to_all | solution.py:401
  104.2 61.7 %all-gather.8.cloned.1.call-start = ((), (), s32[]{:S(2)}) async-start(), calls=%async_computation.6 | async-start | bytes 4718592 | tf_op jit(solution)/shard_map/all_gather | solution.py:522
  114.5 1.2 copy-start.3
  115.8 1.6 copy-start.5
  135.7 30.3 %copy-start.11 = (bf16[2048,128]{1,0:T(8,128)(2,1)S(1)}, bf16[2048,128]{1,0:T(8,128)(2,1)}, u32[]{:S(2)}) copy-start(bf16[2048,128]{1,0:T(8,128)(2,1)} %scatter_high.1) | copy-start | bytes 1572868
  135.7 93.5 %all-gather.14.cloned.1.call-start = ((), (), s32[]{:S(2)}) async-start(), calls=%async_computation.9 | async-start | bytes 4718592 | tf_op jit(solution)/shard_map/all_gather | solution.py:533
  140.8 39.9 %all-to-all-start.4 = ((bf16[32,128,128]{2,1,0:T(8,128)(2,1)}), bf16[32,128,128]{2,1,0:T(8,128)(2,1)S(1)}, u32[]{:S(2)}, u32[]{:S(2)}) async-start(bf16[32,128,128]{2,1,0:T(8,128)(2,1)} %gather_rows.2), calls=%async_computation.4 | async-start | bytes 2097152 | tf_op jit(solution)/shard_map/all_to_all | solution.py:401
  169.6 6.9 %collective-permute-start = (bf16[64,1024]{1,0:T(8,128)(2,1)S(1)}, bf16[64,1024]{1,0:T(8,128)(2,1)S(1)}, u32[]{:S(2)}, u32[]{:S(2)}) collective-permute-start(bf16[64,1024]{1,0:T(8,128)(2,1)S(1)} %get-tuple-element.46), channel_id=1, source_target_pairs={{0,8},{8,16},{16,24},{24,0},{1,9},{9,17},{17,25},{25,1},{2,10},{10... | collective-permute-start | bytes 393224 | tf_op jit(solution)/shard_map/ppermute | solution.py:410
  171.2 9.4 %collective-permute-start.1 = (bf16[64,1024]{1,0:T(8,128)(2,1)S(1)}, bf16[64,1024]{1,0:T(8,128)(2,1)S(1)}, u32[]{:S(2)}, u32[]{:S(2)}) collective-permute-start(bf16[64,1024]{1,0:T(8,128)(2,1)S(1)} %get-tuple-element.48), channel_id=1, source_target_pairs={{0,16},{8,24},{16,0},{24,8},{1,17},{9,25},{17,1},{25,9},{2,18},{10... | collective-permute-start | bytes 393224 | tf_op jit(solution)/shard_map/ppermute | solution.py:410
  173.9 6.7 %collective-permute-start.2 = (bf16[64,1024]{1,0:T(8,128)(2,1)S(1)}, bf16[64,1024]{1,0:T(8,128)(2,1)S(1)}, u32[]{:S(2)}, u32[]{:S(2)}) collective-permute-start(bf16[64,1024]{1,0:T(8,128)(2,1)S(1)} %get-tuple-element.47), channel_id=1, source_target_pairs={{0,24},{8,0},{16,8},{24,16},{1,25},{9,1},{17,9},{25,17},{2,26},{10... | collective-permute-start | bytes 393224 | tf_op jit(solution)/shard_map/ppermute | solution.py:410
  180.7 53.5 %all-to-all-start.5 = ((bf16[32,128,128]{2,1,0:T(8,128)(2,1)}), bf16[32,128,128]{2,1,0:T(8,128)(2,1)}, u32[]{:S(2)}, u32[]{:S(2)}) async-start(bf16[32,128,128]{2,1,0:T(8,128)(2,1)} %gather_rows.3), calls=%async_computation.5 | async-start | bytes 2097152 | tf_op jit(solution)/shard_map/all_to_all | solution.py:401
  190.2 48.6 %copy-start.7 = (s32[128]{0:T(128)S(1)}, s32[128]{0:T(128)}, u32[]{:S(2)}) copy-start(s32[128]{0:T(128)} %source_ref.3) | copy-start | bytes 1540
  190.2 48.6 %copy-start.9 = (s32[128]{0:T(128)S(1)}, s32[128]{0:T(128)}, u32[]{:S(2)}) copy-start(s32[128]{0:T(128)} %slot_ref.3) | copy-start | bytes 1540
  190.3 32.0 %collective-permute-start.3 = (bf16[64,1024]{1,0:T(8,128)(2,1)S(1)}, bf16[64,1024]{1,0:T(8,128)(2,1)S(1)}, u32[]{:S(2)}, u32[]{:S(2)}) collective-permute-start(bf16[64,1024]{1,0:T(8,128)(2,1)S(1)} %fusion.5), channel_id=1, source_target_pairs={{0,128},{32,160},{64,192},{96,224},{128,0},{160,32},{192,64},{224,... | collective-permute-start | bytes 393224 | tf_op jit(solution)/shard_map/ppermute | solution.py:430
  222.3 6.7 %collective-permute-start.4 = (bf16[64,1024]{1,0:T(8,128)(2,1)S(1)}, bf16[64,1024]{1,0:T(8,128)(2,1)S(1)}, u32[]{:S(2)}, u32[]{:S(2)}) collective-permute-start(bf16[64,1024]{1,0:T(8,128)(2,1)S(1)} %add_convert_fusion.2), channel_id=1, source_target_pairs={{0,64},{32,96},{64,0},{96,32},{128,192},{160,224},{192,128},{224,1... | collective-permute-start | bytes 393224 | tf_op jit(solution)/shard_map/ppermute | solution.py:430
  229.1 5.1 %collective-permute-start.5 = (bf16[64,1024]{1,0:T(8,128)(2,1)S(1)}, bf16[64,1024]{1,0:T(8,128)(2,1)S(1)}, u32[]{:S(2)}, u32[]{:S(2)}) collective-permute-start(bf16[64,1024]{1,0:T(8,128)(2,1)S(1)} %add_convert_fusion.1), channel_id=1, source_target_pairs={{0,32},{32,0},{64,96},{96,64},{128,160},{160,128},{192,224},{224,1... | collective-permute-start | bytes 393224 | tf_op jit(solution)/shard_map/ppermute | solution.py:430
  234.2 12.5 %collective-permute-start.6 = (bf16[64,1024]{1,0:T(8,128)(2,1)S(1)}, bf16[64,1024]{1,0:T(8,128)(2,1)S(1)}, u32[]{:S(2)}, u32[]{:S(2)}) collective-permute-start(bf16[64,1024]{1,0:T(8,128)(2,1)S(1)} %add_convert_fusion.refs_0_), channel_id=1, source_target_pairs={{0,24},{8,0},{16,8},{24,16},{1,25},{9,1},{17,9},{25,17},{2,26},{10... | collective-permute-start | bytes 393224 | tf_op jit(solution)/shard_map/ppermute | solution.py:410
  237.1 9.6 %collective-permute-start.7 = (bf16[64,1024]{1,0:T(8,128)(2,1)S(1)}, bf16[64,1024]{1,0:T(8,128)(2,1)S(1)}, u32[]{:S(2)}, u32[]{:S(2)}) collective-permute-start(bf16[64,1024]{1,0:T(8,128)(2,1)S(1)} %add_convert_fusion.refs_0_), channel_id=1, source_target_pairs={{0,16},{8,24},{16,0},{24,8},{1,17},{9,25},{17,1},{25,9},{2,18},{10... | collective-permute-start | bytes 393224 | tf_op jit(solution)/shard_map/ppermute | solution.py:410
  237.7 8.9 %collective-permute-start.8 = (bf16[64,1024]{1,0:T(8,128)(2,1)S(1)}, bf16[64,1024]{1,0:T(8,128)(2,1)S(1)}, u32[]{:S(2)}, u32[]{:S(2)}) collective-permute-start(bf16[64,1024]{1,0:T(8,128)(2,1)S(1)} %add_convert_fusion.refs_0_), channel_id=1, source_target_pairs={{0,8},{8,16},{16,24},{24,0},{1,9},{9,17},{17,25},{25,1},{2,10},{10... | collective-permute-start | bytes 393224 | tf_op jit(solution)/shard_map/ppermute | solution.py:410
Sparse Core Ops, SparseCore 0:
  9.9 37.2 all-gather.9
  49.0 34.6 all-gather.11
  135.8 30.0 all-gather.7
  168.2 34.6 all-gather.13

commit v6 on v5

--- a/solution.py
+++ b/solution.py
@@ -168,7 +168,7 @@
             pl.BlockSpec((group, blk, cols), lambda i: (i, 0, 0)),
         ],
         out_specs=full_spec((nodes, cols)),
-        out_shape=jax.ShapeDtypeStruct((nodes, cols), F32),
+        out_shape=pltpu.HBM((nodes, cols), F32),
         scratch_shapes=[pltpu.VMEM((nodes, group * blk), BF16)],
         compiler_params=params(1),
         name="scatter_low",
@@ -263,7 +263,7 @@
             ],
             out_specs=pl.BlockSpec((share, tile), lambda i, at: (0, i)),
         ),
-        out_shape=jax.ShapeDtypeStruct((share, wide), F32),
+        out_shape=pltpu.HBM((share, wide), F32),
         compiler_params=params(1),
         name="own_term",
     )(at, feat_all, w_self)
@@ -420,6 +420,15 @@
     return total.astype(BF16)
 
 
+def quad_sum(value, axis):
+    size = lax.axis_size(axis)
+    one, two, three = (
+        lax.ppermute(value, axis, [(i, i ^ d) for i in range(size)]).astype(F32)
+        for d in (1, 2, 3)
+    )
+    return ((value.astype(F32) + one) + (two + three)).astype(BF16)
+
+
 def around(piece, axis):
     size = lax.axis_size(axis)
     return [piece] + [rotate(piece, axis, size - i) for i in range(1, size)]
@@ -486,9 +495,9 @@
     share = node_rows // feat_size
     graph = ("z", "y")
     low, high = forward_blocks(
-        block_source,
-        block_to_slot,
-        send_counts[0],
+        in_hbm(block_source),
+        in_hbm(block_to_slot),
+        in_hbm(send_counts[0]),
         in_hbm(send_rows[0]),
         in_hbm(features),
         in_hbm(adjacency),
@@ -496,7 +505,7 @@
     low_in = swap(low, graph)
     high_in = swap(high, graph)
     feat_all = lax.all_gather(features, "feat", axis=0)
-    cot_all = lax.all_gather(cotangent, "feat", axis=0)
+    cot_all = lax.all_gather(after(cotangent, low_in), "feat", axis=0)
     degrees = degree.astype(F32)[:, None]
     adjacency_t = in_hbm(after(adjacency, low_in).swapaxes(1, 2))
     self_rows = lax.dynamic_slice_in_dim(w_self, feat_at * feat_cols, feat_cols, 0)
@@ -509,9 +518,11 @@
     partial_sum, adjacency_t, ids, own = lax.optimization_barrier(
         (partial_sum, adjacency_t, ids, own)
     )
-    neighbor_mean = scatter_high(low_in, high_in, ids, partial_sum, degrees)
+    neighbor_mean = scatter_high(low_in, high_in, ids, in_hbm(partial_sum), degrees)
     mean_pieces = swap(neighbor_mean.reshape(feat_size, share, feat_cols), "feat")
-    back_pieces, hidden_pieces, grad_pre = dense(at, mean_pieces, own, in_hbm(cot_all), w_neigh, degrees)
+    back_pieces, hidden_pieces, grad_pre = dense(
+        at, mean_pieces, in_hbm(own), in_hbm(cot_all), in_hbm(w_neigh), degrees
+    )
     back_rows = swap(back_pieces, "feat").reshape(node_rows, feat_cols)
     back_rows, grad_pre, hidden_pieces = lax.optimization_barrier(
         (back_rows, grad_pre, hidden_pieces)
@@ -528,7 +539,7 @@
     over_y = lax.axis_size("y")
     part = weight_part.reshape(over_y, 2 * feat_cols // over_y, weight_part.shape[1])
     part = scatter_sum(part, "y")
-    back_high = swap(after(rows_high, part, back_low), graph)
+    back_high = swap(after(rows_high, weight_part, back_low), graph)
 
     hidden_all = lax.all_gather(after(hidden_pieces, rows_low), "feat", axis=0)
     hidden_out = lax.dynamic_index_in_dim(hidden_all, feat_at, 1, keepdims=False)
@@ -536,11 +547,15 @@
     self_grad = lax.dot_general(
         grad_full, self_rows, (((1,), (1,)), ((), ())), preferred_element_type=F32
     )
-    part = exchange_sum(part, "z", 4, self_grad)
-    part = exchange_sum(part, "z", 2)
-    part = exchange_sum(part, "z", 1, hidden_out)
+    part = after(quad_sum(part, "z"), self_grad)
+    part = exchange_sum(part, "z", 4, hidden_out)
     grad_features = backward_blocks(
-        block_source, block_to_slot, back_low, back_high, adjacency_t, self_grad
+        in_hbm(block_source),
+        in_hbm(block_to_slot),
+        back_low,
+        back_high,
+        adjacency_t,
+        self_grad,
     )
     grad_self, grad_neigh = assemble(
         jnp.full((1,), lax.axis_index("y"), jnp.int32), around(after(part, back_high), "y")

time: 258 us -> 242 us (0.938)
  waiting for transfers between devices: 71.8 us -> 52.9 us
  blocking collectives: 54.6 us -> 69.4 us
  local copies, waits for them, and re-layouts: 18.5 us -> 10.6 us
  starting transfers between devices: 40.7 us -> 35.1 us
  Pallas kernels: 47.2 us -> 50.4 us
    ppermute x3 -> x1, waiting for transfers between devices: 33.5 us -> 4.29 us  [exchange_sum(): other = lax.ppermute(value, axis, [(i, i ^ distance) for i in range(size)])]
    all_to_all x2 -> x3, blocking collectives: 54.6 us -> 69.4 us  [swap(): return lax.all_to_all(value, axis, split_axis=0, concat_axis=0, tiled=True)]
    ppermute x0 -> x3, waiting for transfers between devices: none -> 12.5 us  [quad_sum(): lax.ppermute(value, axis, [(i, i ^ d) for i in range(size)]).astype(F32)]
    unnamed x26 -> x6, local copies, waits for them, and re-layouts: 9.59 us -> 1.66 us
    all_to_all x4 -> x3, starting transfers between devices: 25.4 us -> 18 us  [swap(): return lax.all_to_all(value, axis, split_axis=0, concat_axis=0, tiled=True)]
    all_to_all x4 -> x3, waiting for transfers between devices: 17.7 us -> 11.6 us  [swap(): return lax.all_to_all(value, axis, split_axis=0, concat_axis=0, tiled=True)]
    ppermute x6, waiting for transfers between devices: 5.25 us -> 9.84 us  [rotate(): lax.ppermute(value, axis, [(i, (i + distance) % size) for i in range(size)])]
    ppermute x0 -> x3, starting transfers between devices: none -> 3.58 us  [quad_sum(): lax.ppermute(value, axis, [(i, i ^ d) for i in range(size)]).astype(F32)]
  transfers between devices with their start and end apart: 17 -> 17, of which waited for: 8 -> 9; matrix products, arithmetic and copies ran while one was open for 6% -> 7% of each run, Pallas kernels for 16% -> 18%
where the time goes in v6:
time: 242 us; the launch traced here: 240 us
  blocking collectives  69.4 us (29%)
  waiting for transfers between devices  52.9 us (22%)
  Pallas kernels  50.4 us (21%)
  starting transfers between devices  35.1 us (15%)
  between operations  13.9 us (6%)
  local copies, waits for them, and re-layouts  10.6 us (4%)
  matrix products  7.14 us (3%)
    all_to_all x3, blocking collectives, swap(): return lax.all_to_all(value, axis, split_axis=0, concat_axis=0, tiled=True)  69.4 us
    all_to_all x3, starting transfers between devices, swap(): return lax.all_to_all(value, axis, split_axis=0, concat_axis=0, tiled=True)  18 us
    all_gather x1, waiting for transfers between devices, on_device(): grad_full = lax.all_gather(grad_pre, 'feat', axis=0, tiled=True)  14 us
    ppermute x3, waiting for transfers between devices, quad_sum(): lax.ppermute(value, axis, [(i, i ^ d) for i in range(size)]).astype(F32)  12.5 us
    all_to_all x3, waiting for transfers between devices, swap(): return lax.all_to_all(value, axis, split_axis=0, concat_axis=0, tiled=True)  11.6 us
    pallas_call x2, Pallas kernels, gather_rows(): pl.pallas_call(gather_kernel, grid=(steps,), in_specs=[pl.BlockSpec((1, 1...  10.1 us
    ppermute x6, waiting for transfers between devices, rotate(): lax.ppermute(value, axis, [(i, (i + distance) % size) for i in range(size)])  9.84 us
    ppermute x6, starting transfers between devices, rotate(): lax.ppermute(value, axis, [(i, (i + distance) % size) for i in range(size)])  9.7 us
  transfers between devices with their start and end apart: 17, of which 9 were waited for; matrix products, arithmetic and copies ran while one was open for 7% of the time, Pallas kernels for 18%

profile of v6, /device:TPU:32, one launch (start us, length us, event | category | flops | bytes accessed | tf_op | source)
XLA Modules:
  0.0 239.7 jit_solution(15159274558203948882)
XLA Ops:
  7.2 0.0 all-gather.10.cloned.1.call-start
  7.2 0.7 all-gather.10.cloned.1.call-update
  7.9 0.0 all-gather.12.cloned.1.call-start
  7.9 0.0 copy-start.2
  8.0 8.8 %forward_blocks.1 = (bf16[32,136,128]{2,1,0:T(8,128)(2,1)S(1)}, bf16[32,128,128]{2,1,0:T(8,128)(2,1)}) custom-call(s32[128]{0:T(128)} %source_ref.3, s32[128]{0:T(128)} %slot_ref.3, s32[32]{0:T(128)} %bitcast.47, s32[32,256]{1,0:T(8,128)} %bitcast.45, bf16[2048,128]{1,0:T(8,128)(2,1)} %feat_ref.1, bf16[128,128,128]{2,1,0:T(8,128)(2,1)} %adj_ref.1), custom_call_target="tpu_custom_call" | custom-call | tf_op jit(solution)/shard_map/forward_blocks/pallas_call | solution.py:77
  16.8 41.9 %all_to_all.30.payload_ids_ref.rows_ref.ids_ref = bf16[32,136,128]{2,1,0:T(8,128)(2,1)S(1)} all-to-all(bf16[32,136,128]{2,1,0:T(8,128)(2,1)S(1)} %get-tuple-element.26), channel_id=1, replica_groups=mesh['z'=8,'y'=4,'feat'=8] {'z','y'}, dimensions={0} | all-to-all | bytes 2228224 | tf_op jit(solution)/shard_map/all_to_all | solution.py:401
  58.7 0.0 all-gather.12.cloned.1.call-update
  58.7 5.5 %all-to-all-start.1 = ((bf16[32,128,128]{2,1,0:T(8,128)(2,1)}), bf16[32,128,128]{2,1,0:T(8,128)(2,1)}, u32[]{:S(2)}, u32[]{:S(2)}) async-start(bf16[32,128,128]{2,1,0:T(8,128)(2,1)} %get-tuple-element.27), calls=%async_computation.1 | async-start | bytes 2097152 | tf_op jit(solution)/shard_map/all_to_all | solution.py:401
  64.3 0.0 all-gather.8.cloned.1.call-start
  64.3 0.0 copy-done.2
  64.3 0.4 copy.28.degree_ref
  64.7 6.4 %copy.25 = bf16[128,128,128]{1,2,0:T(8,128)(2,1)} copy(bf16[128,128,128]{2,1,0:T(8,128)(2,1)} %adj_ref.1) | data formatting | bytes 8388608 | tf_op jit(solution)/shard_map/optimization_barrier | solution.py:405
  71.1 0.2 copy.27
  71.4 6.3 %scatter_low.1.init_ref = f32[2048,128]{1,0:T(8,128)} custom-call(bf16[32,136,128]{2,1,0:T(8,128)(2,1)S(1)} %all_to_all.30.payload_ids_ref.rows_ref.ids_ref, bf16[32,136,128]{2,1,0:T(8,128)(2,1)S(1)} %all_to_all.30.payload_ids_ref.rows_ref.ids_ref), custom_call_target="tpu_custom_call" | custom-call | tf_op jit(solution)/shard_map/scatter_low/pallas_call | solution.py:163
  77.7 0.0 all-gather.10.cloned.1.call-done
  77.7 0.0 copy-start
  77.7 1.6 copy-done
  79.4 3.6 %own_term.1.own_ref = f32[256,1024]{1,0:T(8,128)} custom-call(s32[1]{0:T(128)} %bitcast.at_ref, bf16[8,2048,128]{2,1,0:T(8,128)(2,1)} %bitcast.38, bf16[1024,1024]{1,0:T(8,128)(2,1)S(1)} %copy-done), custom_call_target="tpu_custom_call" | custom-call | tf_op jit(solution)/shard_map/own_term/pallas_call | solution.py:255
  83.0 7.3 %all-to-all-done.1.rows_ref = bf16[32,128,128]{2,1,0:T(8,128)(2,1)} async-done(((bf16[32,128,128]{2,1,0:T(8,128)(2,1)}), bf16[32,128,128]{2,1,0:T(8,128)(2,1)}, u32[]{:S(2)}, u32[]{:S(2)}) %all-to-all-start.1) | async-done | bytes 1048608 | tf_op jit(solution)/shard_map/all_to_all | solution.py:401
  90.3 6.4 %scatter_high.1 = bf16[2048,128]{1,0:T(8,128)(2,1)} custom-call(bf16[32,136,128]{2,1,0:T(8,128)(2,1)S(1)} %all_to_all.30.payload_ids_ref.rows_ref.ids_ref, bf16[32,128,128]{2,1,0:T(8,128)(2,1)} %all-to-all-done.1.rows_ref, f32[4,4,128,8]{3,2,1,0:T(8,128)S(1)} %bitcast.29, f32[2048,128]{1,0:T(8,128)} %scatter_low.1.init_ref, f32[2048,1]{1,0:T(8,128)S(1)} %copy.28.degree_ref), custom_call_target="tpu_custom_call" | custom-call | tf_op jit(solution)/shard_map/scatter_high/pallas_call | solution.py:182
  96.7 14.7 %all_to_all.31.mean_ref = bf16[8,256,128]{2,1,0:T(8,128)(2,1)S(1)} all-to-all(bf16[8,256,128]{2,1,0:T(8,128)(2,1)} %bitcast.39), channel_id=1, replica_groups=mesh['z'=8,'y'=4,'feat'=8] {'feat'}, dimensions={0} | all-to-all | bytes 1048576 | tf_op jit(solution)/shard_map/all_to_all | solution.py:401
  111.4 0.0 all-gather.12.cloned.1.call-done
  111.4 6.0 %dense.1 = (bf16[8,256,128]{2,1,0:T(8,128)(2,1)S(1)}, bf16[8,256,128]{2,1,0:T(8,128)(2,1)}, bf16[256,1024]{1,0:T(8,128)(2,1)}) custom-call(s32[1]{0:T(128)} %bitcast.at_ref, bf16[8,256,128]{2,1,0:T(8,128)(2,1)S(1)} %all_to_all.31.mean_ref, f32[256,1024]{1,0:T(8,128)} %own_term.1.own_ref, bf16[8,2048,128]{2,1,0:T(8,128)(2,1)} %bitcast.37, ...), custom_call_target="tpu_custom_call" | custom-call | tf_op jit(solution)/shard_map/dense/pallas_call | solution.py:312
  117.4 12.8 %all_to_all.32 = bf16[8,256,128]{2,1,0:T(8,128)(2,1)S(1)} all-to-all(bf16[8,256,128]{2,1,0:T(8,128)(2,1)S(1)} %get-tuple-element.33), channel_id=1, replica_groups=mesh['z'=8,'y'=4,'feat'=8] {'feat'}, dimensions={0} | all-to-all | bytes 1048576 | tf_op jit(solution)/shard_map/all_to_all | solution.py:401
  130.2 0.0 all-gather.8.cloned.1.call-update
  130.2 0.0 copy-start.1
  130.2 0.0 all-gather.14.cloned.1.call-start
  130.3 5.0 %gather_rows.2 = bf16[32,128,128]{2,1,0:T(8,128)(2,1)} custom-call(f32[4,4,128,8]{3,2,1,0:T(8,128)S(1)} %bitcast.30, f32[4,4,128,8]{3,2,1,0:T(8,128)S(1)} %bitcast.31, bf16[2048,128]{1,0:T(8,128)(2,1)S(1)} %bitcast.34), custom_call_target="tpu_custom_call" | custom-call | tf_op jit(solution)/shard_map/gather_rows/pallas_call | solution.py:229
  135.3 0.0 all-gather.14.cloned.1.call-update
  135.3 6.1 %all-to-all-start.4 = ((bf16[32,128,128]{2,1,0:T(8,128)(2,1)}), bf16[32,128,128]{2,1,0:T(8,128)(2,1)S(1)}, u32[]{:S(2)}, u32[]{:S(2)}) async-start(bf16[32,128,128]{2,1,0:T(8,128)(2,1)} %gather_rows.2), calls=%async_computation.4 | async-start | bytes 2097152 | tf_op jit(solution)/shard_map/all_to_all | solution.py:401
  141.4 5.1 %gather_rows.3 = bf16[32,128,128]{2,1,0:T(8,128)(2,1)} custom-call(f32[4,4,128,8]{3,2,1,0:T(8,128)S(1)} %bitcast.32, f32[4,4,128,8]{3,2,1,0:T(8,128)S(1)} %bitcast.33, bf16[2048,128]{1,0:T(8,128)(2,1)S(1)} %bitcast.35), custom_call_target="tpu_custom_call" | custom-call | tf_op jit(solution)/shard_map/gather_rows/pallas_call | solution.py:229
  146.5 14.0 %all-gather.8.cloned.1.call-done = bf16[2048,1024]{1,0:T(8,128)(2,1)} async-done(((bf16[256,1024]{1,0:T(8,128)(2,1)}), bf16[2048,1024]{1,0:T(8,128)(2,1)}) %all-gather.8.cloned.1.call-update) | async-done | bytes 4194320 | tf_op jit(solution)/shard_map/all_gather | solution.py:533
  160.5 0.0 copy-done.1
  160.5 3.6 %convolution_convert_fusion = bf16[256,1024]{1,0:T(8,128)(2,1)S(1)} fusion(bf16[2048,1024]{1,0:T(8,128)(2,1)} %all-gather.8.cloned.1.call-done, bf16[2048,128]{1,0:T(8,128)(2,1)S(1)} %copy-done.1, bf16[2048,128]{1,0:T(8,128)(2,1)} %feat_ref.1), kind=kOutput, calls=%fused_computation | convolution fusion | flops 1076101120 | bytes 5767168 | tf_op jit(solution)/shard_map/dot_general | solution.py:536
  164.1 4.3 %all-to-all-done.4.low_ref = bf16[32,128,128]{2,1,0:T(8,128)(2,1)S(1)} async-done(((bf16[32,128,128]{2,1,0:T(8,128)(2,1)}), bf16[32,128,128]{2,1,0:T(8,128)(2,1)S(1)}, u32[]{:S(2)}, u32[]{:S(2)}) %all-to-all-start.4) | async-done | bytes 1048608 | tf_op jit(solution)/shard_map/all_to_all | solution.py:401
  168.4 6.4 %all-to-all-start.5 = ((bf16[32,128,128]{2,1,0:T(8,128)(2,1)}), bf16[32,128,128]{2,1,0:T(8,128)(2,1)}, u32[]{:S(2)}, u32[]{:S(2)}) async-start(bf16[32,128,128]{2,1,0:T(8,128)(2,1)} %gather_rows.3), calls=%async_computation.5 | async-start | bytes 2097152 | tf_op jit(solution)/shard_map/all_to_all | solution.py:401
  174.9 1.5 collective-permute-start
  176.4 2.7 %collective-permute-start.1 = (bf16[64,1024]{1,0:T(8,128)(2,1)S(1)}, bf16[64,1024]{1,0:T(8,128)(2,1)S(1)}, u32[]{:S(2)}, u32[]{:S(2)}) collective-permute-start(bf16[64,1024]{1,0:T(8,128)(2,1)S(1)} %get-tuple-element.50), channel_id=1, source_target_pairs={{0,16},{8,24},{16,0},{24,8},{1,17},{9,25},{17,1},{25,9},{2,18},{10... | collective-permute-start | bytes 393224 | tf_op jit(solution)/shard_map/ppermute | solution.py:410
  179.1 1.5 collective-permute-start.2
  180.5 2.5 %collective-permute-done = bf16[64,1024]{1,0:T(8,128)(2,1)S(1)} collective-permute-done((bf16[64,1024]{1,0:T(8,128)(2,1)S(1)}, bf16[64,1024]{1,0:T(8,128)(2,1)S(1)}, u32[]{:S(2)}, u32[]{:S(2)}) %collective-permute-start) | collective-permute-done | bytes 131104 | tf_op jit(solution)/shard_map/ppermute | solution.py:410
  183.1 7.3 %collective-permute-done.1 = bf16[64,1024]{1,0:T(8,128)(2,1)S(1)} collective-permute-done((bf16[64,1024]{1,0:T(8,128)(2,1)S(1)}, bf16[64,1024]{1,0:T(8,128)(2,1)S(1)}, u32[]{:S(2)}, u32[]{:S(2)}) %collective-permute-start.1) | collective-permute-done | bytes 131104 | tf_op jit(solution)/shard_map/ppermute | solution.py:410
  190.3 0.0 collective-permute-done.2
  190.3 0.1 fusion.5
  190.4 0.5 collective-permute-start.3
  190.9 2.6 %collective-permute-start.4 = (bf16[64,1024]{1,0:T(8,128)(2,1)S(1)}, bf16[64,1024]{1,0:T(8,128)(2,1)S(1)}, u32[]{:S(2)}, u32[]{:S(2)}) collective-permute-start(bf16[64,1024]{1,0:T(8,128)(2,1)S(1)} %fusion.5), channel_id=1, source_target_pairs={{0,64},{32,96},{64,0},{96,32},{128,192},{160,224},{192,128},{224,1... | collective-permute-start | bytes 393224 | tf_op jit(solution)/shard_map/ppermute | solution.py:426
  193.5 0.5 collective-permute-start.5
  194.0 3.5 %fusion.6.self_ref = f32[2048,128]{1,0:T(8,128)S(1)} fusion(bf16[2048,1024]{1,0:T(8,128)(2,1)} %all-gather.8.cloned.1.call-done, bf16[1024,1024]{1,0:T(8,128)(2,1)} %weight_ref.2, s32[]{:T(128)S(6)} %select_n.36), kind=kOutput, calls=%fused_computation.10 | convolution fusion | flops 536870912 | bytes 5505028 | tf_op jit(solution)/shard_map/dot_general | solution.py:547
  197.5 4.7 %collective-permute-done.3 = bf16[64,1024]{1,0:T(8,128)(2,1)S(1)} collective-permute-done((bf16[64,1024]{1,0:T(8,128)(2,1)S(1)}, bf16[64,1024]{1,0:T(8,128)(2,1)S(1)}, u32[]{:S(2)}, u32[]{:S(2)}) %collective-permute-start.3) | collective-permute-done | bytes 131104 | tf_op jit(solution)/shard_map/ppermute | solution.py:426
  202.2 4.5 %collective-permute-done.4 = bf16[64,1024]{1,0:T(8,128)(2,1)S(1)} collective-permute-done((bf16[64,1024]{1,0:T(8,128)(2,1)S(1)}, bf16[64,1024]{1,0:T(8,128)(2,1)S(1)}, u32[]{:S(2)}, u32[]{:S(2)}) %collective-permute-start.4) | collective-permute-done | bytes 131104 | tf_op jit(solution)/shard_map/ppermute | solution.py:426
  206.8 3.3 %collective-permute-done.5 = bf16[64,1024]{1,0:T(8,128)(2,1)S(1)} collective-permute-done((bf16[64,1024]{1,0:T(8,128)(2,1)S(1)}, bf16[64,1024]{1,0:T(8,128)(2,1)S(1)}, u32[]{:S(2)}, u32[]{:S(2)}) %collective-permute-start.5) | collective-permute-done | bytes 131104 | tf_op jit(solution)/shard_map/ppermute | solution.py:426
  210.0 0.1 add_convert_fusion.1
  210.1 3.7 %collective-permute-start.6 = (bf16[64,1024]{1,0:T(8,128)(2,1)S(1)}, bf16[64,1024]{1,0:T(8,128)(2,1)S(1)}, u32[]{:S(2)}, u32[]{:S(2)}) collective-permute-start(bf16[64,1024]{1,0:T(8,128)(2,1)S(1)} %add_convert_fusion.1), channel_id=1, source_target_pairs={{0,128},{32,160},{64,192},{96,224},{128,0},{160,32},{192,64},{224,... | collective-permute-start | bytes 393224 | tf_op jit(solution)/shard_map/ppermute | solution.py:439
  213.8 0.0 all-gather.14.cloned.1.call-done
  213.8 1.9 constant_dynamic-slice_fusion
  215.7 4.3 %collective-permute-done.6 = bf16[64,1024]{1,0:T(8,128)(2,1)S(1)} collective-permute-done((bf16[64,1024]{1,0:T(8,128)(2,1)S(1)}, bf16[64,1024]{1,0:T(8,128)(2,1)S(1)}, u32[]{:S(2)}, u32[]{:S(2)}) %collective-permute-start.6) | collective-permute-done | bytes 131104 | tf_op jit(solution)/shard_map/ppermute | solution.py:439
  220.0 0.0 all-to-all-done.5.high_ref
  220.0 3.0 %collective-permute-start.7 = (bf16[64,1024]{1,0:T(8,128)(2,1)S(1)}, bf16[64,1024]{1,0:T(8,128)(2,1)S(1)}, u32[]{:S(2)}, u32[]{:S(2)}) collective-permute-start(bf16[64,1024]{1,0:T(8,128)(2,1)S(1)} %add_convert_fusion.refs_0_), channel_id=1, source_target_pairs={{0,24},{8,0},{16,8},{24,16},{1,25},{9,1},{17,9},{25,17},{2,26},{10... | collective-permute-start | bytes 393224 | tf_op jit(solution)/shard_map/ppermute | solution.py:410
  223.0 0.5 collective-permute-start.8
  223.6 0.5 collective-permute-start.9
  224.1 8.0 %backward_blocks.1 = bf16[2048,128]{1,0:T(8,128)(2,1)} custom-call(s32[128]{0:T(128)} %source_ref.3, s32[128]{0:T(128)} %slot_ref.3, bf16[32,128,128]{2,1,0:T(8,128)(2,1)S(1)} %all-to-all-done.4.low_ref, bf16[32,128,128]{2,1,0:T(8,128)(2,1)} %all-to-all-done.5.high_ref, bf16[128,128,128]{2,1,0:T(8,128)(2,1)} %bitcast.36, f32[2048,128]{1,0:T(8,128)S(1)} %fusion.6.self_ref), custom_call_target="tpu_custom_call" | custom-call | tf_op jit(solution)/shard_map/backward_blocks/pallas_call | solution.py:373
  232.0 0.0 collective-permute-done.7.refs_1_
  232.0 0.0 collective-permute-done.8.refs_2_
  232.0 0.0 collective-permute-done.9.refs_3_
  232.0 1.1 assemble.1
  (4 shorter events, 0.1 us)
Async XLA Ops:
  7.2 70.6 %all-gather.10.cloned.1.call-start = ((), (), s32[]{:S(2)}) async-start(), calls=%async_computation.7 | async-start | bytes 4718592 | tf_op jit(solution)/shard_map/all_gather | solution.py:507
  7.9 103.5 %all-gather.12.cloned.1.call-start = ((), (), s32[]{:S(2)}) async-start(), calls=%async_computation.8 | async-start | bytes 4718592 | tf_op jit(solution)/shard_map/all_gather | solution.py:508
  7.9 56.4 %copy-start.2 = (s32[2048]{0:T(1024)S(1)}, s32[2048]{0:T(1024)}, u32[]{:S(2)}) copy-start(s32[2048]{0:T(1024)} %param.18) | copy-start | bytes 24580
  58.7 31.5 %all-to-all-start.1 = ((bf16[32,128,128]{2,1,0:T(8,128)(2,1)}), bf16[32,128,128]{2,1,0:T(8,128)(2,1)}, u32[]{:S(2)}, u32[]{:S(2)}) async-start(bf16[32,128,128]{2,1,0:T(8,128)(2,1)} %get-tuple-element.27), calls=%async_computation.1 | async-start | bytes 2097152 | tf_op jit(solution)/shard_map/all_to_all | solution.py:401
  64.3 96.2 %all-gather.8.cloned.1.call-start = ((), (), s32[]{:S(2)}) async-start(), calls=%async_computation.6 | async-start | bytes 4718592 | tf_op jit(solution)/shard_map/all_gather | solution.py:533
  77.7 1.7 copy-start
  130.2 30.3 %copy-start.1 = (bf16[2048,128]{1,0:T(8,128)(2,1)S(1)}, bf16[2048,128]{1,0:T(8,128)(2,1)}, u32[]{:S(2)}) copy-start(bf16[2048,128]{1,0:T(8,128)(2,1)} %scatter_high.1) | copy-start | bytes 1572868
  130.2 83.6 %all-gather.14.cloned.1.call-start = ((), (), s32[]{:S(2)}) async-start(), calls=%async_computation.9 | async-start | bytes 4718592 | tf_op jit(solution)/shard_map/all_gather | solution.py:544
  135.3 33.1 %all-to-all-start.4 = ((bf16[32,128,128]{2,1,0:T(8,128)(2,1)}), bf16[32,128,128]{2,1,0:T(8,128)(2,1)S(1)}, u32[]{:S(2)}, u32[]{:S(2)}) async-start(bf16[32,128,128]{2,1,0:T(8,128)(2,1)} %gather_rows.2), calls=%async_computation.4 | async-start | bytes 2097152 | tf_op jit(solution)/shard_map/all_to_all | solution.py:401
  168.4 51.6 %all-to-all-start.5 = ((bf16[32,128,128]{2,1,0:T(8,128)(2,1)}), bf16[32,128,128]{2,1,0:T(8,128)(2,1)}, u32[]{:S(2)}, u32[]{:S(2)}) async-start(bf16[32,128,128]{2,1,0:T(8,128)(2,1)} %gather_rows.3), calls=%async_computation.5 | async-start | bytes 2097152 | tf_op jit(solution)/shard_map/all_to_all | solution.py:401
  174.9 8.2 %collective-permute-start = (bf16[64,1024]{1,0:T(8,128)(2,1)S(1)}, bf16[64,1024]{1,0:T(8,128)(2,1)S(1)}, u32[]{:S(2)}, u32[]{:S(2)}) collective-permute-start(bf16[64,1024]{1,0:T(8,128)(2,1)S(1)} %get-tuple-element.48), channel_id=1, source_target_pairs={{0,8},{8,16},{16,24},{24,0},{1,9},{9,17},{17,25},{25,1},{2,10},{10... | collective-permute-start | bytes 393224 | tf_op jit(solution)/shard_map/ppermute | solution.py:410
  176.4 13.9 %collective-permute-start.1 = (bf16[64,1024]{1,0:T(8,128)(2,1)S(1)}, bf16[64,1024]{1,0:T(8,128)(2,1)S(1)}, u32[]{:S(2)}, u32[]{:S(2)}) collective-permute-start(bf16[64,1024]{1,0:T(8,128)(2,1)S(1)} %get-tuple-element.50), channel_id=1, source_target_pairs={{0,16},{8,24},{16,0},{24,8},{1,17},{9,25},{17,1},{25,9},{2,18},{10... | collective-permute-start | bytes 393224 | tf_op jit(solution)/shard_map/ppermute | solution.py:410
  179.1 11.3 %collective-permute-start.2 = (bf16[64,1024]{1,0:T(8,128)(2,1)S(1)}, bf16[64,1024]{1,0:T(8,128)(2,1)S(1)}, u32[]{:S(2)}, u32[]{:S(2)}) collective-permute-start(bf16[64,1024]{1,0:T(8,128)(2,1)S(1)} %get-tuple-element.49), channel_id=1, source_target_pairs={{0,24},{8,0},{16,8},{24,16},{1,25},{9,1},{17,9},{25,17},{2,26},{10... | collective-permute-start | bytes 393224 | tf_op jit(solution)/shard_map/ppermute | solution.py:410
  190.4 11.8 %collective-permute-start.3 = (bf16[64,1024]{1,0:T(8,128)(2,1)S(1)}, bf16[64,1024]{1,0:T(8,128)(2,1)S(1)}, u32[]{:S(2)}, u32[]{:S(2)}) collective-permute-start(bf16[64,1024]{1,0:T(8,128)(2,1)S(1)} %fusion.5), channel_id=1, source_target_pairs={{0,32},{32,0},{64,96},{96,64},{128,160},{160,128},{192,224},{224,1... | collective-permute-start | bytes 393224 | tf_op jit(solution)/shard_map/ppermute | solution.py:426
  190.9 15.9 %collective-permute-start.4 = (bf16[64,1024]{1,0:T(8,128)(2,1)S(1)}, bf16[64,1024]{1,0:T(8,128)(2,1)S(1)}, u32[]{:S(2)}, u32[]{:S(2)}) collective-permute-start(bf16[64,1024]{1,0:T(8,128)(2,1)S(1)} %fusion.5), channel_id=1, source_target_pairs={{0,64},{32,96},{64,0},{96,32},{128,192},{160,224},{192,128},{224,1... | collective-permute-start | bytes 393224 | tf_op jit(solution)/shard_map/ppermute | solution.py:426
  193.5 16.5 %collective-permute-start.5 = (bf16[64,1024]{1,0:T(8,128)(2,1)S(1)}, bf16[64,1024]{1,0:T(8,128)(2,1)S(1)}, u32[]{:S(2)}, u32[]{:S(2)}) collective-permute-start(bf16[64,1024]{1,0:T(8,128)(2,1)S(1)} %fusion.5), channel_id=1, source_target_pairs={{0,96},{32,64},{64,32},{96,0},{128,224},{160,192},{192,160},{224,1... | collective-permute-start | bytes 393224 | tf_op jit(solution)/shard_map/ppermute | solution.py:426
  210.1 9.9 %collective-permute-start.6 = (bf16[64,1024]{1,0:T(8,128)(2,1)S(1)}, bf16[64,1024]{1,0:T(8,128)(2,1)S(1)}, u32[]{:S(2)}, u32[]{:S(2)}) collective-permute-start(bf16[64,1024]{1,0:T(8,128)(2,1)S(1)} %add_convert_fusion.1), channel_id=1, source_target_pairs={{0,128},{32,160},{64,192},{96,224},{128,0},{160,32},{192,64},{224,... | collective-permute-start | bytes 393224 | tf_op jit(solution)/shard_map/ppermute | solution.py:439
  220.0 12.0 %collective-permute-start.7 = (bf16[64,1024]{1,0:T(8,128)(2,1)S(1)}, bf16[64,1024]{1,0:T(8,128)(2,1)S(1)}, u32[]{:S(2)}, u32[]{:S(2)}) collective-permute-start(bf16[64,1024]{1,0:T(8,128)(2,1)S(1)} %add_convert_fusion.refs_0_), channel_id=1, source_target_pairs={{0,24},{8,0},{16,8},{24,16},{1,25},{9,1},{17,9},{25,17},{2,26},{10... | collective-permute-start | bytes 393224 | tf_op jit(solution)/shard_map/ppermute | solution.py:410
  223.0 9.0 %collective-permute-start.8 = (bf16[64,1024]{1,0:T(8,128)(2,1)S(1)}, bf16[64,1024]{1,0:T(8,128)(2,1)S(1)}, u32[]{:S(2)}, u32[]{:S(2)}) collective-permute-start(bf16[64,1024]{1,0:T(8,128)(2,1)S(1)} %add_convert_fusion.refs_0_), channel_id=1, source_target_pairs={{0,16},{8,24},{16,0},{24,8},{1,17},{9,25},{17,1},{25,9},{2,18},{10... | collective-permute-start | bytes 393224 | tf_op jit(solution)/shard_map/ppermute | solution.py:410
  223.6 8.5 %collective-permute-start.9 = (bf16[64,1024]{1,0:T(8,128)(2,1)S(1)}, bf16[64,1024]{1,0:T(8,128)(2,1)S(1)}, u32[]{:S(2)}, u32[]{:S(2)}) collective-permute-start(bf16[64,1024]{1,0:T(8,128)(2,1)S(1)} %add_convert_fusion.refs_0_), channel_id=1, source_target_pairs={{0,8},{8,16},{16,24},{24,0},{1,9},{9,17},{17,25},{25,1},{2,10},{10... | collective-permute-start | bytes 393224 | tf_op jit(solution)/shard_map/ppermute | solution.py:410
Sparse Core Ops, SparseCore 0:
  9.9 37.2 all-gather.9
  58.9 30.1 all-gather.11
  130.3 30.1 all-gather.7
  162.8 34.6 all-gather.13

commit v7 on v6

--- a/solution.py
+++ b/solution.py
@@ -66,14 +66,14 @@
             low_ref[part, blk : blk + ID_ROWS, :] = tile.astype(BF16)
             return carry
 
-        lax.fori_loop(0, parts, emit, 0)
+        lax.fori_loop(0, parts, emit, 0, unroll=4)
 
 
 def forward_blocks(block_source, block_to_slot, counts, rows, features, adjacency):
     blocks, blk, _ = adjacency.shape
     nodes, cols = features.shape
     parts, cap = rows.shape
-    chunk = 16
+    chunk = 32
     return pl.pallas_call(
         forward_blocks_kernel,
         grid_spec=pltpu.PrefetchScalarGridSpec(
@@ -210,9 +210,10 @@
         fine = jnp.broadcast_to(fine_ref[0, 0, :, part : part + 1], (blk, blk))
         coarse = jnp.broadcast_to(coarse_ref[0, 0, :, part : part + 1], (blk, blk))
         coarse = jnp.where(coarse >= half_blocks, coarse - half_blocks, coarse)
-        hot = jnp.where(lane == fine, 1.0, 0.0)
+        hot = jnp.where(lane == fine, 1.0, 0.0).astype(BF16)
+        coarse = coarse.astype(BF16)
         for block in range(half_blocks):
-            value = jnp.where(coarse == float(block), hot, 0.0).astype(BF16)
+            value = jnp.where(coarse == BF16(block), hot, BF16(0))
             hot_ref[part * blk : (part + 1) * blk, block * blk : (block + 1) * blk] = value
     both = jnp.concatenate([back_ref[:half_nodes], back_ref[half_nodes:]], axis=1)
     picked = jnp.dot(hot_ref[...], both, preferred_element_type=F32)
@@ -369,7 +370,7 @@
     blocks, blk, _ = adjacency_t.shape
     nodes, cols = self_grad.shape
     parts = low.shape[0]
-    chunk = 16
+    chunk = 32
     return pl.pallas_call(
         backward_blocks_kernel,
         grid_spec=pltpu.PrefetchScalarGridSpec(
@@ -548,7 +549,6 @@
         grad_full, self_rows, (((1,), (1,)), ((), ())), preferred_element_type=F32
     )
     part = after(quad_sum(part, "z"), self_grad)
-    part = exchange_sum(part, "z", 4, hidden_out)
     grad_features = backward_blocks(
         in_hbm(block_source),
         in_hbm(block_to_slot),
@@ -557,9 +557,9 @@
         adjacency_t,
         self_grad,
     )
-    grad_self, grad_neigh = assemble(
-        jnp.full((1,), lax.axis_index("y"), jnp.int32), around(after(part, back_high), "y")
-    )
+    part = exchange_sum(part, "z", 4, grad_features)
+    at = after(jnp.full((1,), lax.axis_index("y"), jnp.int32), hidden_out)
+    grad_self, grad_neigh = assemble(at, around(part, "y"))
     return hidden_out, grad_features, grad_self, grad_neigh
 
 

time: 242 us -> 239 us (0.988)
  Pallas kernels: 50.4 us -> 45.3 us
    ppermute x6, waiting for transfers between devices: 9.84 us -> 16 us  [rotate(): lax.ppermute(value, axis, [(i, (i + distance) % size) for i in range(size)])]
    ppermute x1, waiting for transfers between devices: 4.29 us -> 0.13 us  [exchange_sum(): other = lax.ppermute(value, axis, [(i, i ^ distance) for i in range(size)])]
  transfers between devices with their start and end apart: 17 -> 17, of which waited for: 9 -> 12; matrix products, arithmetic and copies ran while one was open for 7% -> 7% of each run, Pallas kernels for 18% -> 16%
where the time goes in v7:
time: 239 us; the launch traced here: 237 us
  blocking collectives  69.4 us (29%)
  waiting for transfers between devices  55 us (23%)
  Pallas kernels  45.3 us (19%)
  starting transfers between devices  35.8 us (15%)
  between operations  13.9 us (6%)
  local copies, waits for them, and re-layouts  10.6 us (4%)
  matrix products  7.14 us (3%)
    all_to_all x3, blocking collectives, swap(): return lax.all_to_all(value, axis, split_axis=0, concat_axis=0, tiled=True)  69.4 us
    all_to_all x3, starting transfers between devices, swap(): return lax.all_to_all(value, axis, split_axis=0, concat_axis=0, tiled=True)  18 us
    ppermute x6, waiting for transfers between devices, rotate(): lax.ppermute(value, axis, [(i, (i + distance) % size) for i in range(size)])  16 us
    all_gather x1, waiting for transfers between devices, on_device(): grad_full = lax.all_gather(grad_pre, 'feat', axis=0, tiled=True)  15 us
    ppermute x3, waiting for transfers between devices, quad_sum(): lax.ppermute(value, axis, [(i, i ^ d) for i in range(size)]).astype(F32)  12.2 us
    all_to_all x3, waiting for transfers between devices, swap(): return lax.all_to_all(value, axis, split_axis=0, concat_axis=0, tiled=True)  11.1 us
    ppermute x6, starting transfers between devices, rotate(): lax.ppermute(value, axis, [(i, (i + distance) % size) for i in range(size)])  10.3 us
    pallas_call x2, Pallas kernels, gather_rows(): pl.pallas_call(gather_kernel, grid=(steps,), in_specs=[pl.BlockSpec((1, 1...  9.09 us
  transfers between devices with their start and end apart: 17, of which 12 were waited for; matrix products, arithmetic and copies ran while one was open for 7% of the time, Pallas kernels for 16%

profile of v7, /device:TPU:32, one launch (start us, length us, event | category | flops | bytes accessed | tf_op | source)
XLA Modules:
  0.0 237.4 jit_solution(8990338924472748245)
XLA Ops:
  7.2 0.0 all-gather.10.cloned.1.call-start
  7.2 0.7 all-gather.10.cloned.1.call-update
  7.9 0.0 all-gather.12.cloned.1.call-start
  7.9 0.0 copy-start.2
  8.0 6.7 %forward_blocks.1 = (bf16[32,136,128]{2,1,0:T(8,128)(2,1)S(1)}, bf16[32,128,128]{2,1,0:T(8,128)(2,1)}) custom-call(s32[128]{0:T(128)} %source_ref.3, s32[128]{0:T(128)} %slot_ref.3, s32[32]{0:T(128)} %bitcast.47, s32[32,256]{1,0:T(8,128)} %bitcast.45, bf16[2048,128]{1,0:T(8,128)(2,1)} %feat_ref.1, bf16[128,128,128]{2,1,0:T(8,128)(2,1)} %adj_ref.1), custom_call_target="tpu_custom_call" | custom-call | tf_op jit(solution)/shard_map/forward_blocks/pallas_call | solution.py:77
  14.7 41.9 %all_to_all.30.payload_ids_ref.rows_ref.ids_ref = bf16[32,136,128]{2,1,0:T(8,128)(2,1)S(1)} all-to-all(bf16[32,136,128]{2,1,0:T(8,128)(2,1)S(1)} %get-tuple-element.26), channel_id=1, replica_groups=mesh['z'=8,'y'=4,'feat'=8] {'z','y'}, dimensions={0} | all-to-all | bytes 2228224 | tf_op jit(solution)/shard_map/all_to_all | solution.py:402
  56.6 0.0 all-gather.12.cloned.1.call-update
  56.6 5.5 %all-to-all-start.1 = ((bf16[32,128,128]{2,1,0:T(8,128)(2,1)}), bf16[32,128,128]{2,1,0:T(8,128)(2,1)}, u32[]{:S(2)}, u32[]{:S(2)}) async-start(bf16[32,128,128]{2,1,0:T(8,128)(2,1)} %get-tuple-element.27), calls=%async_computation.1 | async-start | bytes 2097152 | tf_op jit(solution)/shard_map/all_to_all | solution.py:402
  62.1 0.0 all-gather.8.cloned.1.call-start
  62.2 0.0 copy-done.2
  62.2 0.4 copy.28.degree_ref
  62.6 6.4 %copy.25 = bf16[128,128,128]{1,2,0:T(8,128)(2,1)} copy(bf16[128,128,128]{2,1,0:T(8,128)(2,1)} %adj_ref.1) | data formatting | bytes 8388608 | tf_op jit(solution)/shard_map/optimization_barrier | solution.py:406
  69.0 0.2 copy.27
  69.2 6.3 %scatter_low.1.init_ref = f32[2048,128]{1,0:T(8,128)} custom-call(bf16[32,136,128]{2,1,0:T(8,128)(2,1)S(1)} %all_to_all.30.payload_ids_ref.rows_ref.ids_ref, bf16[32,136,128]{2,1,0:T(8,128)(2,1)S(1)} %all_to_all.30.payload_ids_ref.rows_ref.ids_ref), custom_call_target="tpu_custom_call" | custom-call | tf_op jit(solution)/shard_map/scatter_low/pallas_call | solution.py:163
  75.6 0.0 all-gather.10.cloned.1.call-done
  75.6 0.0 copy-start
  75.6 1.6 copy-done
  77.2 3.6 %own_term.1.own_ref = f32[256,1024]{1,0:T(8,128)} custom-call(s32[1]{0:T(128)} %bitcast.at_ref, bf16[8,2048,128]{2,1,0:T(8,128)(2,1)} %bitcast.38, bf16[1024,1024]{1,0:T(8,128)(2,1)S(1)} %copy-done), custom_call_target="tpu_custom_call" | custom-call | tf_op jit(solution)/shard_map/own_term/pallas_call | solution.py:256
  80.9 7.3 %all-to-all-done.1.rows_ref = bf16[32,128,128]{2,1,0:T(8,128)(2,1)} async-done(((bf16[32,128,128]{2,1,0:T(8,128)(2,1)}), bf16[32,128,128]{2,1,0:T(8,128)(2,1)}, u32[]{:S(2)}, u32[]{:S(2)}) %all-to-all-start.1) | async-done | bytes 1048608 | tf_op jit(solution)/shard_map/all_to_all | solution.py:402
  88.1 6.4 %scatter_high.1 = bf16[2048,128]{1,0:T(8,128)(2,1)} custom-call(bf16[32,136,128]{2,1,0:T(8,128)(2,1)S(1)} %all_to_all.30.payload_ids_ref.rows_ref.ids_ref, bf16[32,128,128]{2,1,0:T(8,128)(2,1)} %all-to-all-done.1.rows_ref, f32[4,4,128,8]{3,2,1,0:T(8,128)S(1)} %bitcast.29, f32[2048,128]{1,0:T(8,128)} %scatter_low.1.init_ref, f32[2048,1]{1,0:T(8,128)S(1)} %copy.28.degree_ref), custom_call_target="tpu_custom_call" | custom-call | tf_op jit(solution)/shard_map/scatter_high/pallas_call | solution.py:182
  94.6 14.7 %all_to_all.31.mean_ref = bf16[8,256,128]{2,1,0:T(8,128)(2,1)S(1)} all-to-all(bf16[8,256,128]{2,1,0:T(8,128)(2,1)} %bitcast.39), channel_id=1, replica_groups=mesh['z'=8,'y'=4,'feat'=8] {'feat'}, dimensions={0} | all-to-all | bytes 1048576 | tf_op jit(solution)/shard_map/all_to_all | solution.py:402
  109.3 0.0 all-gather.12.cloned.1.call-done
  109.3 6.0 %dense.1 = (bf16[8,256,128]{2,1,0:T(8,128)(2,1)S(1)}, bf16[8,256,128]{2,1,0:T(8,128)(2,1)}, bf16[256,1024]{1,0:T(8,128)(2,1)}) custom-call(s32[1]{0:T(128)} %bitcast.at_ref, bf16[8,256,128]{2,1,0:T(8,128)(2,1)S(1)} %all_to_all.31.mean_ref, f32[256,1024]{1,0:T(8,128)} %own_term.1.own_ref, bf16[8,2048,128]{2,1,0:T(8,128)(2,1)} %bitcast.37, ...), custom_call_target="tpu_custom_call" | custom-call | tf_op jit(solution)/shard_map/dense/pallas_call | solution.py:313
  115.3 12.8 %all_to_all.32 = bf16[8,256,128]{2,1,0:T(8,128)(2,1)S(1)} all-to-all(bf16[8,256,128]{2,1,0:T(8,128)(2,1)S(1)} %get-tuple-element.33), channel_id=1, replica_groups=mesh['z'=8,'y'=4,'feat'=8] {'feat'}, dimensions={0} | all-to-all | bytes 1048576 | tf_op jit(solution)/shard_map/all_to_all | solution.py:402
  128.0 0.0 all-gather.8.cloned.1.call-update
  128.1 0.0 copy-start.1
  128.1 0.0 all-gather.14.cloned.1.call-start
  128.1 4.5 %gather_rows.2 = bf16[32,128,128]{2,1,0:T(8,128)(2,1)} custom-call(f32[4,4,128,8]{3,2,1,0:T(8,128)S(1)} %bitcast.30, f32[4,4,128,8]{3,2,1,0:T(8,128)S(1)} %bitcast.31, bf16[2048,128]{1,0:T(8,128)(2,1)S(1)} %bitcast.34), custom_call_target="tpu_custom_call" | custom-call | tf_op jit(solution)/shard_map/gather_rows/pallas_call | solution.py:230
  132.7 0.0 all-gather.14.cloned.1.call-update
  132.7 6.1 %all-to-all-start.4 = ((bf16[32,128,128]{2,1,0:T(8,128)(2,1)}), bf16[32,128,128]{2,1,0:T(8,128)(2,1)S(1)}, u32[]{:S(2)}, u32[]{:S(2)}) async-start(bf16[32,128,128]{2,1,0:T(8,128)(2,1)} %gather_rows.2), calls=%async_computation.4 | async-start | bytes 2097152 | tf_op jit(solution)/shard_map/all_to_all | solution.py:402
  138.8 4.6 %gather_rows.3 = bf16[32,128,128]{2,1,0:T(8,128)(2,1)} custom-call(f32[4,4,128,8]{3,2,1,0:T(8,128)S(1)} %bitcast.32, f32[4,4,128,8]{3,2,1,0:T(8,128)S(1)} %bitcast.33, bf16[2048,128]{1,0:T(8,128)(2,1)S(1)} %bitcast.35), custom_call_target="tpu_custom_call" | custom-call | tf_op jit(solution)/shard_map/gather_rows/pallas_call | solution.py:230
  143.4 15.0 %all-gather.8.cloned.1.call-done = bf16[2048,1024]{1,0:T(8,128)(2,1)} async-done(((bf16[256,1024]{1,0:T(8,128)(2,1)}), bf16[2048,1024]{1,0:T(8,128)(2,1)}) %all-gather.8.cloned.1.call-update) | async-done | bytes 4194320 | tf_op jit(solution)/shard_map/all_gather | solution.py:534
  158.4 0.0 copy-done.1
  158.4 3.6 %convolution_convert_fusion = bf16[256,1024]{1,0:T(8,128)(2,1)S(1)} fusion(bf16[2048,1024]{1,0:T(8,128)(2,1)} %all-gather.8.cloned.1.call-done, bf16[2048,128]{1,0:T(8,128)(2,1)S(1)} %copy-done.1, bf16[2048,128]{1,0:T(8,128)(2,1)} %feat_ref.1), kind=kOutput, calls=%fused_computation | convolution fusion | flops 1076101120 | bytes 5767168 | tf_op jit(solution)/shard_map/dot_general | solution.py:537
  162.0 3.8 %all-to-all-done.4.low_ref = bf16[32,128,128]{2,1,0:T(8,128)(2,1)S(1)} async-done(((bf16[32,128,128]{2,1,0:T(8,128)(2,1)}), bf16[32,128,128]{2,1,0:T(8,128)(2,1)S(1)}, u32[]{:S(2)}, u32[]{:S(2)}) %all-to-all-start.4) | async-done | bytes 1048608 | tf_op jit(solution)/shard_map/all_to_all | solution.py:402
  165.8 6.4 %all-to-all-start.5 = ((bf16[32,128,128]{2,1,0:T(8,128)(2,1)}), bf16[32,128,128]{2,1,0:T(8,128)(2,1)}, u32[]{:S(2)}, u32[]{:S(2)}) async-start(bf16[32,128,128]{2,1,0:T(8,128)(2,1)} %gather_rows.3), calls=%async_computation.5 | async-start | bytes 2097152 | tf_op jit(solution)/shard_map/all_to_all | solution.py:402
  172.3 1.5 collective-permute-start
  173.8 2.7 %collective-permute-start.1 = (bf16[64,1024]{1,0:T(8,128)(2,1)S(1)}, bf16[64,1024]{1,0:T(8,128)(2,1)S(1)}, u32[]{:S(2)}, u32[]{:S(2)}) collective-permute-start(bf16[64,1024]{1,0:T(8,128)(2,1)S(1)} %get-tuple-element.50), channel_id=1, source_target_pairs={{0,16},{8,24},{16,0},{24,8},{1,17},{9,25},{17,1},{25,9},{2,18},{10... | collective-permute-start | bytes 393224 | tf_op jit(solution)/shard_map/ppermute | solution.py:411
  176.5 1.5 collective-permute-start.2
  177.9 3.0 %collective-permute-done = bf16[64,1024]{1,0:T(8,128)(2,1)S(1)} collective-permute-done((bf16[64,1024]{1,0:T(8,128)(2,1)S(1)}, bf16[64,1024]{1,0:T(8,128)(2,1)S(1)}, u32[]{:S(2)}, u32[]{:S(2)}) %collective-permute-start) | collective-permute-done | bytes 131104 | tf_op jit(solution)/shard_map/ppermute | solution.py:411
  181.0 7.6 %collective-permute-done.1 = bf16[64,1024]{1,0:T(8,128)(2,1)S(1)} collective-permute-done((bf16[64,1024]{1,0:T(8,128)(2,1)S(1)}, bf16[64,1024]{1,0:T(8,128)(2,1)S(1)}, u32[]{:S(2)}, u32[]{:S(2)}) %collective-permute-start.1) | collective-permute-done | bytes 131104 | tf_op jit(solution)/shard_map/ppermute | solution.py:411
  188.6 0.0 collective-permute-done.2
  188.6 0.1 fusion.5
  188.7 0.1 collective-permute-start.3
  188.8 2.5 %collective-permute-start.4 = (bf16[64,1024]{1,0:T(8,128)(2,1)S(1)}, bf16[64,1024]{1,0:T(8,128)(2,1)S(1)}, u32[]{:S(2)}, u32[]{:S(2)}) collective-permute-start(bf16[64,1024]{1,0:T(8,128)(2,1)S(1)} %fusion.5), channel_id=1, source_target_pairs={{0,64},{32,96},{64,0},{96,32},{128,192},{160,224},{192,128},{224,1... | collective-permute-start | bytes 393224 | tf_op jit(solution)/shard_map/ppermute | solution.py:427
  191.3 1.0 collective-permute-start.5
  192.2 3.5 %fusion.6.self_ref = f32[2048,128]{1,0:T(8,128)S(1)} fusion(bf16[2048,1024]{1,0:T(8,128)(2,1)} %all-gather.8.cloned.1.call-done, bf16[1024,1024]{1,0:T(8,128)(2,1)} %weight_ref.2, s32[]{:T(128)S(6)} %select_n.36), kind=kOutput, calls=%fused_computation.10 | convolution fusion | flops 536870912 | bytes 5505028 | tf_op jit(solution)/shard_map/dot_general | solution.py:548
  195.8 4.6 %collective-permute-done.3 = bf16[64,1024]{1,0:T(8,128)(2,1)S(1)} collective-permute-done((bf16[64,1024]{1,0:T(8,128)(2,1)S(1)}, bf16[64,1024]{1,0:T(8,128)(2,1)S(1)}, u32[]{:S(2)}, u32[]{:S(2)}) %collective-permute-start.3) | collective-permute-done | bytes 131104 | tf_op jit(solution)/shard_map/ppermute | solution.py:427
  200.4 3.9 %collective-permute-done.4 = bf16[64,1024]{1,0:T(8,128)(2,1)S(1)} collective-permute-done((bf16[64,1024]{1,0:T(8,128)(2,1)S(1)}, bf16[64,1024]{1,0:T(8,128)(2,1)S(1)}, u32[]{:S(2)}, u32[]{:S(2)}) %collective-permute-start.4) | collective-permute-done | bytes 131104 | tf_op jit(solution)/shard_map/ppermute | solution.py:427
  204.3 3.6 %collective-permute-done.5 = bf16[64,1024]{1,0:T(8,128)(2,1)S(1)} collective-permute-done((bf16[64,1024]{1,0:T(8,128)(2,1)S(1)}, bf16[64,1024]{1,0:T(8,128)(2,1)S(1)}, u32[]{:S(2)}, u32[]{:S(2)}) %collective-permute-start.5) | collective-permute-done | bytes 131104 | tf_op jit(solution)/shard_map/ppermute | solution.py:427
  207.9 0.1 add_convert_fusion.1
  208.0 3.7 %collective-permute-start.6 = (bf16[64,1024]{1,0:T(8,128)(2,1)S(1)}, bf16[64,1024]{1,0:T(8,128)(2,1)S(1)}, u32[]{:S(2)}, u32[]{:S(2)}) collective-permute-start(bf16[64,1024]{1,0:T(8,128)(2,1)S(1)} %add_convert_fusion.1), channel_id=1, source_target_pairs={{0,128},{32,160},{64,192},{96,224},{128,0},{160,32},{192,64},{224,... | collective-permute-start | bytes 393224 | tf_op jit(solution)/shard_map/ppermute | solution.py:440
  211.7 0.0 all-to-all-done.5.high_ref
  211.7 6.0 %backward_blocks.1 = bf16[2048,128]{1,0:T(8,128)(2,1)} custom-call(s32[128]{0:T(128)} %source_ref.3, s32[128]{0:T(128)} %slot_ref.3, bf16[32,128,128]{2,1,0:T(8,128)(2,1)S(1)} %all-to-all-done.4.low_ref, bf16[32,128,128]{2,1,0:T(8,128)(2,1)} %all-to-all-done.5.high_ref, bf16[128,128,128]{2,1,0:T(8,128)(2,1)} %bitcast.36, f32[2048,128]{1,0:T(8,128)S(1)} %fusion.6.self_ref), custom_call_target="tpu_custom_call" | custom-call | tf_op jit(solution)/shard_map/backward_blocks/pallas_call | solution.py:374
  217.8 0.1 collective-permute-done.6
  217.9 2.9 %collective-permute-start.7 = (bf16[64,1024]{1,0:T(8,128)(2,1)S(1)}, bf16[64,1024]{1,0:T(8,128)(2,1)S(1)}, u32[]{:S(2)}, u32[]{:S(2)}) collective-permute-start(bf16[64,1024]{1,0:T(8,128)(2,1)S(1)} %add_convert_fusion.refs_0_), channel_id=1, source_target_pairs={{0,24},{8,0},{16,8},{24,16},{1,25},{9,1},{17,9},{25,17},{2,26},{10... | collective-permute-start | bytes 393224 | tf_op jit(solution)/shard_map/ppermute | solution.py:411
  220.8 0.7 collective-permute-start.8
  221.6 1.0 collective-permute-start.9
  222.6 0.0 all-gather.14.cloned.1.call-done
  222.6 1.9 constant_dynamic-slice_fusion
  224.4 1.6 collective-permute-done.7.refs_1_
  226.1 2.3 collective-permute-done.8.refs_2_
  228.4 1.4 collective-permute-done.9.refs_3_
  229.8 1.1 assemble.1
  (4 shorter events, 0.1 us)
Async XLA Ops:
  7.2 68.4 %all-gather.10.cloned.1.call-start = ((), (), s32[]{:S(2)}) async-start(), calls=%async_computation.7 | async-start | bytes 4718592 | tf_op jit(solution)/shard_map/all_gather | solution.py:508
  7.9 101.4 %all-gather.12.cloned.1.call-start = ((), (), s32[]{:S(2)}) async-start(), calls=%async_computation.8 | async-start | bytes 4718592 | tf_op jit(solution)/shard_map/all_gather | solution.py:509
  7.9 54.2 %copy-start.2 = (s32[2048]{0:T(1024)S(1)}, s32[2048]{0:T(1024)}, u32[]{:S(2)}) copy-start(s32[2048]{0:T(1024)} %param.18) | copy-start | bytes 24580
  56.6 31.5 %all-to-all-start.1 = ((bf16[32,128,128]{2,1,0:T(8,128)(2,1)}), bf16[32,128,128]{2,1,0:T(8,128)(2,1)}, u32[]{:S(2)}, u32[]{:S(2)}) async-start(bf16[32,128,128]{2,1,0:T(8,128)(2,1)} %get-tuple-element.27), calls=%async_computation.1 | async-start | bytes 2097152 | tf_op jit(solution)/shard_map/all_to_all | solution.py:402
  62.1 96.2 %all-gather.8.cloned.1.call-start = ((), (), s32[]{:S(2)}) async-start(), calls=%async_computation.6 | async-start | bytes 4718592 | tf_op jit(solution)/shard_map/all_gather | solution.py:534
  75.6 1.6 copy-start
  128.1 30.3 %copy-start.1 = (bf16[2048,128]{1,0:T(8,128)(2,1)S(1)}, bf16[2048,128]{1,0:T(8,128)(2,1)}, u32[]{:S(2)}) copy-start(bf16[2048,128]{1,0:T(8,128)(2,1)} %scatter_high.1) | copy-start | bytes 1572868
  128.1 94.5 %all-gather.14.cloned.1.call-start = ((), (), s32[]{:S(2)}) async-start(), calls=%async_computation.9 | async-start | bytes 4718592 | tf_op jit(solution)/shard_map/all_gather | solution.py:545
  132.7 33.1 %all-to-all-start.4 = ((bf16[32,128,128]{2,1,0:T(8,128)(2,1)}), bf16[32,128,128]{2,1,0:T(8,128)(2,1)S(1)}, u32[]{:S(2)}, u32[]{:S(2)}) async-start(bf16[32,128,128]{2,1,0:T(8,128)(2,1)} %gather_rows.2), calls=%async_computation.4 | async-start | bytes 2097152 | tf_op jit(solution)/shard_map/all_to_all | solution.py:402
  165.8 46.0 %all-to-all-start.5 = ((bf16[32,128,128]{2,1,0:T(8,128)(2,1)}), bf16[32,128,128]{2,1,0:T(8,128)(2,1)}, u32[]{:S(2)}, u32[]{:S(2)}) async-start(bf16[32,128,128]{2,1,0:T(8,128)(2,1)} %gather_rows.3), calls=%async_computation.5 | async-start | bytes 2097152 | tf_op jit(solution)/shard_map/all_to_all | solution.py:402
  172.3 8.7 %collective-permute-start = (bf16[64,1024]{1,0:T(8,128)(2,1)S(1)}, bf16[64,1024]{1,0:T(8,128)(2,1)S(1)}, u32[]{:S(2)}, u32[]{:S(2)}) collective-permute-start(bf16[64,1024]{1,0:T(8,128)(2,1)S(1)} %get-tuple-element.48), channel_id=1, source_target_pairs={{0,8},{8,16},{16,24},{24,0},{1,9},{9,17},{17,25},{25,1},{2,10},{10... | collective-permute-start | bytes 393224 | tf_op jit(solution)/shard_map/ppermute | solution.py:411
  173.8 14.8 %collective-permute-start.1 = (bf16[64,1024]{1,0:T(8,128)(2,1)S(1)}, bf16[64,1024]{1,0:T(8,128)(2,1)S(1)}, u32[]{:S(2)}, u32[]{:S(2)}) collective-permute-start(bf16[64,1024]{1,0:T(8,128)(2,1)S(1)} %get-tuple-element.50), channel_id=1, source_target_pairs={{0,16},{8,24},{16,0},{24,8},{1,17},{9,25},{17,1},{25,9},{2,18},{10... | collective-permute-start | bytes 393224 | tf_op jit(solution)/shard_map/ppermute | solution.py:411
  176.5 12.1 %collective-permute-start.2 = (bf16[64,1024]{1,0:T(8,128)(2,1)S(1)}, bf16[64,1024]{1,0:T(8,128)(2,1)S(1)}, u32[]{:S(2)}, u32[]{:S(2)}) collective-permute-start(bf16[64,1024]{1,0:T(8,128)(2,1)S(1)} %get-tuple-element.49), channel_id=1, source_target_pairs={{0,24},{8,0},{16,8},{24,16},{1,25},{9,1},{17,9},{25,17},{2,26},{10... | collective-permute-start | bytes 393224 | tf_op jit(solution)/shard_map/ppermute | solution.py:411
  188.7 11.7 %collective-permute-start.3 = (bf16[64,1024]{1,0:T(8,128)(2,1)S(1)}, bf16[64,1024]{1,0:T(8,128)(2,1)S(1)}, u32[]{:S(2)}, u32[]{:S(2)}) collective-permute-start(bf16[64,1024]{1,0:T(8,128)(2,1)S(1)} %fusion.5), channel_id=1, source_target_pairs={{0,32},{32,0},{64,96},{96,64},{128,160},{160,128},{192,224},{224,1... | collective-permute-start | bytes 393224 | tf_op jit(solution)/shard_map/ppermute | solution.py:427
  188.8 15.5 %collective-permute-start.4 = (bf16[64,1024]{1,0:T(8,128)(2,1)S(1)}, bf16[64,1024]{1,0:T(8,128)(2,1)S(1)}, u32[]{:S(2)}, u32[]{:S(2)}) collective-permute-start(bf16[64,1024]{1,0:T(8,128)(2,1)S(1)} %fusion.5), channel_id=1, source_target_pairs={{0,64},{32,96},{64,0},{96,32},{128,192},{160,224},{192,128},{224,1... | collective-permute-start | bytes 393224 | tf_op jit(solution)/shard_map/ppermute | solution.py:427
  191.3 16.6 %collective-permute-start.5 = (bf16[64,1024]{1,0:T(8,128)(2,1)S(1)}, bf16[64,1024]{1,0:T(8,128)(2,1)S(1)}, u32[]{:S(2)}, u32[]{:S(2)}) collective-permute-start(bf16[64,1024]{1,0:T(8,128)(2,1)S(1)} %fusion.5), channel_id=1, source_target_pairs={{0,96},{32,64},{64,32},{96,0},{128,224},{160,192},{192,160},{224,1... | collective-permute-start | bytes 393224 | tf_op jit(solution)/shard_map/ppermute | solution.py:427
  208.0 9.9 %collective-permute-start.6 = (bf16[64,1024]{1,0:T(8,128)(2,1)S(1)}, bf16[64,1024]{1,0:T(8,128)(2,1)S(1)}, u32[]{:S(2)}, u32[]{:S(2)}) collective-permute-start(bf16[64,1024]{1,0:T(8,128)(2,1)S(1)} %add_convert_fusion.1), channel_id=1, source_target_pairs={{0,128},{32,160},{64,192},{96,224},{128,0},{160,32},{192,64},{224,... | collective-permute-start | bytes 393224 | tf_op jit(solution)/shard_map/ppermute | solution.py:440
  217.9 8.1 %collective-permute-start.7 = (bf16[64,1024]{1,0:T(8,128)(2,1)S(1)}, bf16[64,1024]{1,0:T(8,128)(2,1)S(1)}, u32[]{:S(2)}, u32[]{:S(2)}) collective-permute-start(bf16[64,1024]{1,0:T(8,128)(2,1)S(1)} %add_convert_fusion.refs_0_), channel_id=1, source_target_pairs={{0,24},{8,0},{16,8},{24,16},{1,25},{9,1},{17,9},{25,17},{2,26},{10... | collective-permute-start | bytes 393224 | tf_op jit(solution)/shard_map/ppermute | solution.py:411
  220.8 7.6 %collective-permute-start.8 = (bf16[64,1024]{1,0:T(8,128)(2,1)S(1)}, bf16[64,1024]{1,0:T(8,128)(2,1)S(1)}, u32[]{:S(2)}, u32[]{:S(2)}) collective-permute-start(bf16[64,1024]{1,0:T(8,128)(2,1)S(1)} %add_convert_fusion.refs_0_), channel_id=1, source_target_pairs={{0,16},{8,24},{16,0},{24,8},{1,17},{9,25},{17,1},{25,9},{2,18},{10... | collective-permute-start | bytes 393224 | tf_op jit(solution)/shard_map/ppermute | solution.py:411
  221.6 8.2 %collective-permute-start.9 = (bf16[64,1024]{1,0:T(8,128)(2,1)S(1)}, bf16[64,1024]{1,0:T(8,128)(2,1)S(1)}, u32[]{:S(2)}, u32[]{:S(2)}) collective-permute-start(bf16[64,1024]{1,0:T(8,128)(2,1)S(1)} %add_convert_fusion.refs_0_), channel_id=1, source_target_pairs={{0,8},{8,16},{16,24},{24,0},{1,9},{9,17},{17,25},{25,1},{2,10},{10... | collective-permute-start | bytes 393224 | tf_op jit(solution)/shard_map/ppermute | solution.py:411
Sparse Core Ops, SparseCore 0:
  9.9 37.2 all-gather.9
  56.7 30.1 all-gather.11
  128.2 30.1 all-gather.7
  160.7 34.6 all-gather.13

commit v8 on v7

--- a/solution.py
+++ b/solution.py
@@ -121,40 +121,46 @@
 
 
 def scatter_high_kernel(
-    ids_ref, rows_ref, coarse_ref, init_ref, degree_ref, mean_ref, hot_ref, both_ref, acc_ref
+    ids_ref,
+    rows_ref,
+    coarse_ref,
+    init_ref,
+    degree_ref,
+    mean_ref,
+    hot_a_ref,
+    hot_b_ref,
+    both_a_ref,
+    both_b_ref,
+    acc_ref,
 ):
-    step = pl.program_id(0)
-    group, blk, cols = rows_ref.shape
+    blk, cols = rows_ref.shape[1:]
+    groups, group = coarse_ref.shape[1], coarse_ref.shape[3]
     half_nodes = acc_ref.shape[0]
     half_blocks = half_nodes // blk
-
-    @pl.when(step == 0)
-    def _():
-        acc_ref[:, :cols] = init_ref[:half_nodes]
-        acc_ref[:, cols:] = init_ref[half_nodes:]
-
+    acc_ref[:, :cols] = init_ref[:half_nodes]
+    acc_ref[:, cols:] = init_ref[half_nodes:]
     node_row = lax.broadcasted_iota(jnp.int32, (blk, blk), 0).astype(F32)
-    for part in range(group):
-        tile = ids_ref[part].astype(F32)
-        fine = tile[1:2, :]
-        coarse = tile[3:4, :]
-        coarse = jnp.where(coarse >= half_blocks, coarse - half_blocks, coarse)
-        hot = jnp.where(node_row == fine, 1.0, 0.0).astype(BF16)
-        here = slice(part * blk, (part + 1) * blk)
-        for block in range(half_blocks):
-            keep = jnp.where(coarse == float(block), 1.0, 0.0).astype(BF16)
-            hot_ref[block * blk : (block + 1) * blk, here] = hot * keep
-        column = jnp.broadcast_to(coarse_ref[0, 0, :, part : part + 1], (blk, cols))
-        upper = jnp.where(column >= half_blocks, 1.0, 0.0).astype(BF16)
-        rows = rows_ref[part]
-        both_ref[here, cols:] = rows * upper
-        both_ref[here, :cols] = rows * (1.0 - upper)
-    acc_ref[...] += jnp.dot(hot_ref[...], both_ref[...], preferred_element_type=F32)
-
-    @pl.when(step == pl.num_programs(0) - 1)
-    def _():
-        mean_ref[:half_nodes] = (acc_ref[:, :cols] / degree_ref[:half_nodes]).astype(BF16)
-        mean_ref[half_nodes:] = (acc_ref[:, cols:] / degree_ref[half_nodes:]).astype(BF16)
+    for at in range(groups):
+        hot_ref = hot_b_ref if at % 2 else hot_a_ref
+        both_ref = both_b_ref if at % 2 else both_a_ref
+        for part in range(group):
+            tile = ids_ref[at * group + part].astype(F32)
+            fine = tile[1:2, :]
+            coarse = tile[3:4, :]
+            coarse = jnp.where(coarse >= half_blocks, coarse - half_blocks, coarse)
+            hot = jnp.where(node_row == fine, 1.0, 0.0).astype(BF16)
+            here = slice(part * blk, (part + 1) * blk)
+            for block in range(half_blocks):
+                keep = jnp.where(coarse == float(block), 1.0, 0.0).astype(BF16)
+                hot_ref[block * blk : (block + 1) * blk, here] = hot * keep
+            column = jnp.broadcast_to(coarse_ref[0, at, :, part : part + 1], (blk, cols))
+            upper = jnp.where(column >= half_blocks, 1.0, 0.0).astype(BF16)
+            rows = rows_ref[at * group + part]
+            both_ref[here, cols:] = rows * upper
+            both_ref[here, :cols] = rows * (1.0 - upper)
+        acc_ref[...] += jnp.dot(hot_ref[...], both_ref[...], preferred_element_type=F32)
+    mean_ref[:half_nodes] = (acc_ref[:, :cols] / degree_ref[:half_nodes]).astype(BF16)
+    mean_ref[half_nodes:] = (acc_ref[:, cols:] / degree_ref[half_nodes:]).astype(BF16)
 
 
 def scatter_low(low, nodes):
@@ -178,14 +184,14 @@
 def scatter_high(low, high, columns, partial_sum, degrees):
     parts, blk, cols = high.shape
     nodes = partial_sum.shape[0]
-    group = columns.shape[3]
+    groups, group = columns.shape[1], columns.shape[3]
     return pl.pallas_call(
         scatter_high_kernel,
-        grid=(parts // group,),
+        grid=(1,),
         in_specs=[
-            pl.BlockSpec((group, ID_ROWS, cols), lambda i: (i, blk // ID_ROWS, 0)),
-            pl.BlockSpec((group, blk, cols), lambda i: (i, 0, 0)),
-            pl.BlockSpec((1, 1, blk, group), lambda i: (3, i, 0, 0)),
+            pl.BlockSpec((parts, ID_ROWS, cols), lambda i: (0, blk // ID_ROWS, 0)),
+            full_spec((parts, blk, cols)),
+            pl.BlockSpec((1, groups, blk, group), lambda i: (3, 0, 0, 0)),
             full_spec((nodes, cols)),
             full_spec((nodes, 1)),
         ],
@@ -193,6 +199,8 @@
         out_shape=pltpu.HBM((nodes, cols), BF16),
         scratch_shapes=[
             pltpu.VMEM((nodes // 2, group * blk), BF16),
+            pltpu.VMEM((nodes // 2, group * blk), BF16),
+            pltpu.VMEM((group * blk, 2 * cols), BF16),
             pltpu.VMEM((group * blk, 2 * cols), BF16),
             pltpu.VMEM((nodes // 2, 2 * cols), F32),
         ],
@@ -201,43 +209,49 @@
     )(low, high, columns, partial_sum, degrees)
 
 
-def gather_kernel(fine_ref, coarse_ref, back_ref, out_ref, hot_ref):
-    group, blk, cols = out_ref.shape
+def gather_kernel(fine_ref, coarse_ref, back_ref, out_ref, hot_a_ref, hot_b_ref):
+    blk, cols = out_ref.shape[1:]
+    groups, group = fine_ref.shape[1], fine_ref.shape[3]
     half_nodes = back_ref.shape[0] // 2
     half_blocks = half_nodes // blk
     lane = lax.broadcasted_iota(jnp.int32, (blk, blk), 1).astype(F32)
-    for part in range(group):
-        fine = jnp.broadcast_to(fine_ref[0, 0, :, part : part + 1], (blk, blk))
-        coarse = jnp.broadcast_to(coarse_ref[0, 0, :, part : part + 1], (blk, blk))
-        coarse = jnp.where(coarse >= half_blocks, coarse - half_blocks, coarse)
-        hot = jnp.where(lane == fine, 1.0, 0.0).astype(BF16)
-        coarse = coarse.astype(BF16)
-        for block in range(half_blocks):
-            value = jnp.where(coarse == BF16(block), hot, BF16(0))
-            hot_ref[part * blk : (part + 1) * blk, block * blk : (block + 1) * blk] = value
     both = jnp.concatenate([back_ref[:half_nodes], back_ref[half_nodes:]], axis=1)
-    picked = jnp.dot(hot_ref[...], both, preferred_element_type=F32)
-    for part in range(group):
-        coarse = jnp.broadcast_to(coarse_ref[0, 0, :, part : part + 1], (blk, cols))
-        here = slice(part * blk, (part + 1) * blk)
-        rows = jnp.where(coarse >= half_blocks, picked[here, cols:], picked[here, :cols])
-        out_ref[part] = rows.astype(BF16)
+    for at in range(groups):
+        hot_ref = hot_b_ref if at % 2 else hot_a_ref
+        for part in range(group):
+            fine = jnp.broadcast_to(fine_ref[0, at, :, part : part + 1], (blk, blk))
+            coarse = jnp.broadcast_to(coarse_ref[0, at, :, part : part + 1], (blk, blk))
+            coarse = jnp.where(coarse >= half_blocks, coarse - half_blocks, coarse)
+            hot = jnp.where(lane == fine, 1.0, 0.0).astype(BF16)
+            coarse = coarse.astype(BF16)
+            for block in range(half_blocks):
+                value = jnp.where(coarse == BF16(block), hot, BF16(0))
+                hot_ref[part * blk : (part + 1) * blk, block * blk : (block + 1) * blk] = value
+        picked = jnp.dot(hot_ref[...], both, preferred_element_type=F32)
+        for part in range(group):
+            coarse = jnp.broadcast_to(coarse_ref[0, at, :, part : part + 1], (blk, cols))
+            here = slice(part * blk, (part + 1) * blk)
+            rows = jnp.where(coarse >= half_blocks, picked[here, cols:], picked[here, :cols])
+            out_ref[at * group + part] = rows.astype(BF16)
 
 
 def gather_rows(half, columns, back):
-    _, steps, blk, group = columns.shape
+    _, groups, blk, group = columns.shape
     nodes, cols = back.shape
     return pl.pallas_call(
         gather_kernel,
-        grid=(steps,),
+        grid=(1,),
         in_specs=[
-            pl.BlockSpec((1, 1, blk, group), lambda i: (half, i, 0, 0)),
-            pl.BlockSpec((1, 1, blk, group), lambda i: (2 + half, i, 0, 0)),
+            pl.BlockSpec((1, groups, blk, group), lambda i: (half, 0, 0, 0)),
+            pl.BlockSpec((1, groups, blk, group), lambda i: (2 + half, 0, 0, 0)),
             full_spec((nodes, cols)),
         ],
-        out_specs=pl.BlockSpec((group, blk, cols), lambda i: (i, 0, 0)),
-        out_shape=pltpu.HBM((steps * group, blk, cols), BF16),
-        scratch_shapes=[pltpu.VMEM((group * blk, nodes // 2), BF16)],
+        out_specs=full_spec((groups * group, blk, cols)),
+        out_shape=pltpu.HBM((groups * group, blk, cols), BF16),
+        scratch_shapes=[
+            pltpu.VMEM((group * blk, nodes // 2), BF16),
+            pltpu.VMEM((group * blk, nodes // 2), BF16),
+        ],
         compiler_params=params(1),
         name="gather_rows",
     )(columns, columns, back)

time: 239 us -> 238 us (level)
  no operation moved by 1% of the time
where the time goes in v8:
time: 238 us; the launch traced here: 237 us
  blocking collectives  69.4 us (29%)
  waiting for transfers between devices  54.9 us (23%)
  Pallas kernels  45.1 us (19%)
  starting transfers between devices  35.6 us (15%)
  between operations  13.9 us (6%)
  local copies, waits for them, and re-layouts  10.6 us (4%)
  matrix products  7.14 us (3%)
    all_to_all x3, blocking collectives, swap(): return lax.all_to_all(value, axis, split_axis=0, concat_axis=0, tiled=True)  69.4 us
    all_to_all x3, starting transfers between devices, swap(): return lax.all_to_all(value, axis, split_axis=0, concat_axis=0, tiled=True)  18.2 us
    ppermute x6, waiting for transfers between devices, rotate(): lax.ppermute(value, axis, [(i, (i + distance) % size) for i in range(size)])  15.7 us
    all_gather x1, waiting for transfers between devices, on_device(): grad_full = lax.all_gather(grad_pre, 'feat', axis=0, tiled=True)  14.5 us
    ppermute x3, waiting for transfers between devices, quad_sum(): lax.ppermute(value, axis, [(i, i ^ d) for i in range(size)]).astype(F32)  12.4 us
    all_to_all x3, waiting for transfers between devices, swap(): return lax.all_to_all(value, axis, split_axis=0, concat_axis=0, tiled=True)  11.4 us
    ppermute x6, starting transfers between devices, rotate(): lax.ppermute(value, axis, [(i, (i + distance) % size) for i in range(size)])  10 us
    pallas_call x2, Pallas kernels, gather_rows(): pl.pallas_call(gather_kernel, grid=(1,), in_specs=[pl.BlockSpec((1, group...  9.42 us
  transfers between devices with their start and end apart: 17, of which 12 were waited for; matrix products, arithmetic and copies ran while one was open for 7% of the time, Pallas kernels for 16%

profile of v8, /device:TPU:32, one launch (start us, length us, event | category | flops | bytes accessed | tf_op | source)
XLA Modules:
  0.0 236.8 jit_solution(1188083399714028121)
XLA Ops:
  7.2 0.0 all-gather.10.cloned.1.call-start
  7.2 0.7 all-gather.10.cloned.1.call-update
  7.9 0.0 all-gather.12.cloned.1.call-start
  7.9 0.0 copy-start.2
  8.0 6.7 %forward_blocks.1 = (bf16[32,136,128]{2,1,0:T(8,128)(2,1)S(1)}, bf16[32,128,128]{2,1,0:T(8,128)(2,1)}) custom-call(s32[128]{0:T(128)} %source_ref.3, s32[128]{0:T(128)} %slot_ref.3, s32[32]{0:T(128)} %bitcast.47, s32[32,256]{1,0:T(8,128)} %bitcast.45, bf16[2048,128]{1,0:T(8,128)(2,1)} %feat_ref.1, bf16[128,128,128]{2,1,0:T(8,128)(2,1)} %adj_ref.1), custom_call_target="tpu_custom_call" | custom-call | tf_op jit(solution)/shard_map/forward_blocks/pallas_call | solution.py:77
  14.7 41.9 %all_to_all.30.payload_ids_ref.rows_ref.ids_ref = bf16[32,136,128]{2,1,0:T(8,128)(2,1)S(1)} all-to-all(bf16[32,136,128]{2,1,0:T(8,128)(2,1)S(1)} %get-tuple-element.26), channel_id=1, replica_groups=mesh['z'=8,'y'=4,'feat'=8] {'z','y'}, dimensions={0} | all-to-all | bytes 2228224 | tf_op jit(solution)/shard_map/all_to_all | solution.py:416
  56.6 0.0 all-gather.12.cloned.1.call-update
  56.6 5.5 %all-to-all-start.1 = ((bf16[32,128,128]{2,1,0:T(8,128)(2,1)}), bf16[32,128,128]{2,1,0:T(8,128)(2,1)}, u32[]{:S(2)}, u32[]{:S(2)}) async-start(bf16[32,128,128]{2,1,0:T(8,128)(2,1)} %get-tuple-element.27), calls=%async_computation.1 | async-start | bytes 2097152 | tf_op jit(solution)/shard_map/all_to_all | solution.py:416
  62.1 0.0 all-gather.8.cloned.1.call-start
  62.2 0.0 copy-done.2
  62.2 0.4 copy.28.degree_ref
  62.6 6.4 %copy.25 = bf16[128,128,128]{1,2,0:T(8,128)(2,1)} copy(bf16[128,128,128]{2,1,0:T(8,128)(2,1)} %adj_ref.1) | data formatting | bytes 8388608 | tf_op jit(solution)/shard_map/optimization_barrier | solution.py:420
  69.0 0.2 copy.27
  69.2 6.3 %scatter_low.1.init_ref = f32[2048,128]{1,0:T(8,128)} custom-call(bf16[32,136,128]{2,1,0:T(8,128)(2,1)S(1)} %all_to_all.30.payload_ids_ref.rows_ref.ids_ref, bf16[32,136,128]{2,1,0:T(8,128)(2,1)S(1)} %all_to_all.30.payload_ids_ref.rows_ref.ids_ref), custom_call_target="tpu_custom_call" | custom-call | tf_op jit(solution)/shard_map/scatter_low/pallas_call | solution.py:169
  75.6 0.0 all-gather.10.cloned.1.call-done
  75.6 0.0 copy-start
  75.6 1.6 copy-done
  77.2 3.6 %own_term.1.own_ref = f32[256,1024]{1,0:T(8,128)} custom-call(s32[1]{0:T(128)} %bitcast.at_ref, bf16[8,2048,128]{2,1,0:T(8,128)(2,1)} %bitcast.38, bf16[1024,1024]{1,0:T(8,128)(2,1)S(1)} %copy-done), custom_call_target="tpu_custom_call" | custom-call | tf_op jit(solution)/shard_map/own_term/pallas_call | solution.py:270
  80.9 7.3 %all-to-all-done.1.rows_ref = bf16[32,128,128]{2,1,0:T(8,128)(2,1)} async-done(((bf16[32,128,128]{2,1,0:T(8,128)(2,1)}), bf16[32,128,128]{2,1,0:T(8,128)(2,1)}, u32[]{:S(2)}, u32[]{:S(2)}) %all-to-all-start.1) | async-done | bytes 1048608 | tf_op jit(solution)/shard_map/all_to_all | solution.py:416
  88.1 5.8 %scatter_high.1 = bf16[2048,128]{1,0:T(8,128)(2,1)} custom-call(bf16[32,136,128]{2,1,0:T(8,128)(2,1)S(1)} %all_to_all.30.payload_ids_ref.rows_ref.ids_ref, bf16[32,128,128]{2,1,0:T(8,128)(2,1)} %all-to-all-done.1.rows_ref, f32[4,4,128,8]{3,2,1,0:T(8,128)S(1)} %bitcast.29, f32[2048,128]{1,0:T(8,128)} %scatter_low.1.init_ref, f32[2048,1]{1,0:T(8,128)S(1)} %copy.28.degree_ref), custom_call_target="tpu_custom_call" | custom-call | tf_op jit(solution)/shard_map/scatter_high/pallas_call | solution.py:188
  94.0 14.7 %all_to_all.31.mean_ref = bf16[8,256,128]{2,1,0:T(8,128)(2,1)S(1)} all-to-all(bf16[8,256,128]{2,1,0:T(8,128)(2,1)} %bitcast.39), channel_id=1, replica_groups=mesh['z'=8,'y'=4,'feat'=8] {'feat'}, dimensions={0} | all-to-all | bytes 1048576 | tf_op jit(solution)/shard_map/all_to_all | solution.py:416
  108.7 0.0 all-gather.12.cloned.1.call-done
  108.7 6.0 %dense.1 = (bf16[8,256,128]{2,1,0:T(8,128)(2,1)S(1)}, bf16[8,256,128]{2,1,0:T(8,128)(2,1)}, bf16[256,1024]{1,0:T(8,128)(2,1)}) custom-call(s32[1]{0:T(128)} %bitcast.at_ref, bf16[8,256,128]{2,1,0:T(8,128)(2,1)S(1)} %all_to_all.31.mean_ref, f32[256,1024]{1,0:T(8,128)} %own_term.1.own_ref, bf16[8,2048,128]{2,1,0:T(8,128)(2,1)} %bitcast.37, ...), custom_call_target="tpu_custom_call" | custom-call | tf_op jit(solution)/shard_map/dense/pallas_call | solution.py:327
  114.7 12.8 %all_to_all.32 = bf16[8,256,128]{2,1,0:T(8,128)(2,1)S(1)} all-to-all(bf16[8,256,128]{2,1,0:T(8,128)(2,1)S(1)} %get-tuple-element.33), channel_id=1, replica_groups=mesh['z'=8,'y'=4,'feat'=8] {'feat'}, dimensions={0} | all-to-all | bytes 1048576 | tf_op jit(solution)/shard_map/all_to_all | solution.py:416
  127.4 0.0 all-gather.8.cloned.1.call-update
  127.5 0.0 copy-start.1
  127.5 0.0 all-gather.14.cloned.1.call-start
  127.5 4.7 %gather_rows.2 = bf16[32,128,128]{2,1,0:T(8,128)(2,1)} custom-call(f32[4,4,128,8]{3,2,1,0:T(8,128)S(1)} %bitcast.30, f32[4,4,128,8]{3,2,1,0:T(8,128)S(1)} %bitcast.31, bf16[2048,128]{1,0:T(8,128)(2,1)S(1)} %bitcast.34), custom_call_target="tpu_custom_call" | custom-call | tf_op jit(solution)/shard_map/gather_rows/pallas_call | solution.py:241
  132.3 0.0 all-gather.14.cloned.1.call-update
  132.3 6.3 %all-to-all-start.4 = ((bf16[32,128,128]{2,1,0:T(8,128)(2,1)}), bf16[32,128,128]{2,1,0:T(8,128)(2,1)S(1)}, u32[]{:S(2)}, u32[]{:S(2)}) async-start(bf16[32,128,128]{2,1,0:T(8,128)(2,1)} %gather_rows.2), calls=%async_computation.4 | async-start | bytes 2097152 | tf_op jit(solution)/shard_map/all_to_all | solution.py:416
  138.6 4.7 %gather_rows.3 = bf16[32,128,128]{2,1,0:T(8,128)(2,1)} custom-call(f32[4,4,128,8]{3,2,1,0:T(8,128)S(1)} %bitcast.32, f32[4,4,128,8]{3,2,1,0:T(8,128)S(1)} %bitcast.33, bf16[2048,128]{1,0:T(8,128)(2,1)S(1)} %bitcast.35), custom_call_target="tpu_custom_call" | custom-call | tf_op jit(solution)/shard_map/gather_rows/pallas_call | solution.py:241
  143.3 14.5 %all-gather.8.cloned.1.call-done = bf16[2048,1024]{1,0:T(8,128)(2,1)} async-done(((bf16[256,1024]{1,0:T(8,128)(2,1)}), bf16[2048,1024]{1,0:T(8,128)(2,1)}) %all-gather.8.cloned.1.call-update) | async-done | bytes 4194320 | tf_op jit(solution)/shard_map/all_gather | solution.py:548
  157.8 0.0 copy-done.1
  157.8 3.6 %convolution_convert_fusion = bf16[256,1024]{1,0:T(8,128)(2,1)S(1)} fusion(bf16[2048,1024]{1,0:T(8,128)(2,1)} %all-gather.8.cloned.1.call-done, bf16[2048,128]{1,0:T(8,128)(2,1)S(1)} %copy-done.1, bf16[2048,128]{1,0:T(8,128)(2,1)} %feat_ref.1), kind=kOutput, calls=%fused_computation | convolution fusion | flops 1076101120 | bytes 5767168 | tf_op jit(solution)/shard_map/dot_general | solution.py:551
  161.4 4.1 %all-to-all-done.4.low_ref = bf16[32,128,128]{2,1,0:T(8,128)(2,1)S(1)} async-done(((bf16[32,128,128]{2,1,0:T(8,128)(2,1)}), bf16[32,128,128]{2,1,0:T(8,128)(2,1)S(1)}, u32[]{:S(2)}, u32[]{:S(2)}) %all-to-all-start.4) | async-done | bytes 1048608 | tf_op jit(solution)/shard_map/all_to_all | solution.py:416
  165.5 6.4 %all-to-all-start.5 = ((bf16[32,128,128]{2,1,0:T(8,128)(2,1)}), bf16[32,128,128]{2,1,0:T(8,128)(2,1)}, u32[]{:S(2)}, u32[]{:S(2)}) async-start(bf16[32,128,128]{2,1,0:T(8,128)(2,1)} %gather_rows.3), calls=%async_computation.5 | async-start | bytes 2097152 | tf_op jit(solution)/shard_map/all_to_all | solution.py:416
  172.0 1.5 collective-permute-start
  173.5 2.7 %collective-permute-start.1 = (bf16[64,1024]{1,0:T(8,128)(2,1)S(1)}, bf16[64,1024]{1,0:T(8,128)(2,1)S(1)}, u32[]{:S(2)}, u32[]{:S(2)}) collective-permute-start(bf16[64,1024]{1,0:T(8,128)(2,1)S(1)} %get-tuple-element.50), channel_id=1, source_target_pairs={{0,16},{8,24},{16,0},{24,8},{1,17},{9,25},{17,1},{25,9},{2,18},{10... | collective-permute-start | bytes 393224 | tf_op jit(solution)/shard_map/ppermute | solution.py:425
  176.2 1.5 collective-permute-start.2
  177.7 2.8 %collective-permute-done = bf16[64,1024]{1,0:T(8,128)(2,1)S(1)} collective-permute-done((bf16[64,1024]{1,0:T(8,128)(2,1)S(1)}, bf16[64,1024]{1,0:T(8,128)(2,1)S(1)}, u32[]{:S(2)}, u32[]{:S(2)}) %collective-permute-start) | collective-permute-done | bytes 131104 | tf_op jit(solution)/shard_map/ppermute | solution.py:425
  180.4 7.3 %collective-permute-done.1 = bf16[64,1024]{1,0:T(8,128)(2,1)S(1)} collective-permute-done((bf16[64,1024]{1,0:T(8,128)(2,1)S(1)}, bf16[64,1024]{1,0:T(8,128)(2,1)S(1)}, u32[]{:S(2)}, u32[]{:S(2)}) %collective-permute-start.1) | collective-permute-done | bytes 131104 | tf_op jit(solution)/shard_map/ppermute | solution.py:425
  187.8 0.0 collective-permute-done.2
  187.8 0.1 fusion.5
  187.8 0.1 collective-permute-start.3
  187.9 2.8 %collective-permute-start.4 = (bf16[64,1024]{1,0:T(8,128)(2,1)S(1)}, bf16[64,1024]{1,0:T(8,128)(2,1)S(1)}, u32[]{:S(2)}, u32[]{:S(2)}) collective-permute-start(bf16[64,1024]{1,0:T(8,128)(2,1)S(1)} %fusion.5), channel_id=1, source_target_pairs={{0,64},{32,96},{64,0},{96,32},{128,192},{160,224},{192,128},{224,1... | collective-permute-start | bytes 393224 | tf_op jit(solution)/shard_map/ppermute | solution.py:441
  190.8 0.7 collective-permute-start.5
  191.4 3.5 %fusion.6.self_ref = f32[2048,128]{1,0:T(8,128)S(1)} fusion(bf16[2048,1024]{1,0:T(8,128)(2,1)} %all-gather.8.cloned.1.call-done, bf16[1024,1024]{1,0:T(8,128)(2,1)} %weight_ref.2, s32[]{:T(128)S(6)} %select_n.36), kind=kOutput, calls=%fused_computation.10 | convolution fusion | flops 536870912 | bytes 5505028 | tf_op jit(solution)/shard_map/dot_general | solution.py:562
  194.9 4.7 %collective-permute-done.3 = bf16[64,1024]{1,0:T(8,128)(2,1)S(1)} collective-permute-done((bf16[64,1024]{1,0:T(8,128)(2,1)S(1)}, bf16[64,1024]{1,0:T(8,128)(2,1)S(1)}, u32[]{:S(2)}, u32[]{:S(2)}) %collective-permute-start.3) | collective-permute-done | bytes 131104 | tf_op jit(solution)/shard_map/ppermute | solution.py:441
  199.6 4.4 %collective-permute-done.4 = bf16[64,1024]{1,0:T(8,128)(2,1)S(1)} collective-permute-done((bf16[64,1024]{1,0:T(8,128)(2,1)S(1)}, bf16[64,1024]{1,0:T(8,128)(2,1)S(1)}, u32[]{:S(2)}, u32[]{:S(2)}) %collective-permute-start.4) | collective-permute-done | bytes 131104 | tf_op jit(solution)/shard_map/ppermute | solution.py:441
  204.0 3.3 %collective-permute-done.5 = bf16[64,1024]{1,0:T(8,128)(2,1)S(1)} collective-permute-done((bf16[64,1024]{1,0:T(8,128)(2,1)S(1)}, bf16[64,1024]{1,0:T(8,128)(2,1)S(1)}, u32[]{:S(2)}, u32[]{:S(2)}) %collective-permute-start.5) | collective-permute-done | bytes 131104 | tf_op jit(solution)/shard_map/ppermute | solution.py:441
  207.3 0.1 add_convert_fusion.1
  207.4 3.7 %collective-permute-start.6 = (bf16[64,1024]{1,0:T(8,128)(2,1)S(1)}, bf16[64,1024]{1,0:T(8,128)(2,1)S(1)}, u32[]{:S(2)}, u32[]{:S(2)}) collective-permute-start(bf16[64,1024]{1,0:T(8,128)(2,1)S(1)} %add_convert_fusion.1), channel_id=1, source_target_pairs={{0,128},{32,160},{64,192},{96,224},{128,0},{160,32},{192,64},{224,... | collective-permute-start | bytes 393224 | tf_op jit(solution)/shard_map/ppermute | solution.py:454
  211.1 0.0 all-to-all-done.5.high_ref
  211.1 6.0 %backward_blocks.1 = bf16[2048,128]{1,0:T(8,128)(2,1)} custom-call(s32[128]{0:T(128)} %source_ref.3, s32[128]{0:T(128)} %slot_ref.3, bf16[32,128,128]{2,1,0:T(8,128)(2,1)S(1)} %all-to-all-done.4.low_ref, bf16[32,128,128]{2,1,0:T(8,128)(2,1)} %all-to-all-done.5.high_ref, bf16[128,128,128]{2,1,0:T(8,128)(2,1)} %bitcast.36, f32[2048,128]{1,0:T(8,128)S(1)} %fusion.6.self_ref), custom_call_target="tpu_custom_call" | custom-call | tf_op jit(solution)/shard_map/backward_blocks/pallas_call | solution.py:388
  217.1 0.1 collective-permute-done.6
  217.3 2.9 %collective-permute-start.7 = (bf16[64,1024]{1,0:T(8,128)(2,1)S(1)}, bf16[64,1024]{1,0:T(8,128)(2,1)S(1)}, u32[]{:S(2)}, u32[]{:S(2)}) collective-permute-start(bf16[64,1024]{1,0:T(8,128)(2,1)S(1)} %add_convert_fusion.refs_0_), channel_id=1, source_target_pairs={{0,24},{8,0},{16,8},{24,16},{1,25},{9,1},{17,9},{25,17},{2,26},{10... | collective-permute-start | bytes 393224 | tf_op jit(solution)/shard_map/ppermute | solution.py:425
  220.2 0.6 collective-permute-start.8
  220.8 0.9 collective-permute-start.9
  221.7 0.0 all-gather.14.cloned.1.call-done
  221.7 1.9 constant_dynamic-slice_fusion
  223.5 2.2 collective-permute-done.7.refs_1_
  225.8 2.4 collective-permute-done.8.refs_2_
  228.1 1.1 collective-permute-done.9.refs_3_
  229.2 1.1 assemble.1
  (4 shorter events, 0.1 us)
Async XLA Ops:
  7.2 68.4 %all-gather.10.cloned.1.call-start = ((), (), s32[]{:S(2)}) async-start(), calls=%async_computation.7 | async-start | bytes 4718592 | tf_op jit(solution)/shard_map/all_gather | solution.py:522
  7.9 100.8 %all-gather.12.cloned.1.call-start = ((), (), s32[]{:S(2)}) async-start(), calls=%async_computation.8 | async-start | bytes 4718592 | tf_op jit(solution)/shard_map/all_gather | solution.py:523
  7.9 54.2 %copy-start.2 = (s32[2048]{0:T(1024)S(1)}, s32[2048]{0:T(1024)}, u32[]{:S(2)}) copy-start(s32[2048]{0:T(1024)} %param.18) | copy-start | bytes 24580
  56.6 31.5 %all-to-all-start.1 = ((bf16[32,128,128]{2,1,0:T(8,128)(2,1)}), bf16[32,128,128]{2,1,0:T(8,128)(2,1)}, u32[]{:S(2)}, u32[]{:S(2)}) async-start(bf16[32,128,128]{2,1,0:T(8,128)(2,1)} %get-tuple-element.27), calls=%async_computation.1 | async-start | bytes 2097152 | tf_op jit(solution)/shard_map/all_to_all | solution.py:416
  62.1 95.6 %all-gather.8.cloned.1.call-start = ((), (), s32[]{:S(2)}) async-start(), calls=%async_computation.6 | async-start | bytes 4718592 | tf_op jit(solution)/shard_map/all_gather | solution.py:548
  75.6 1.6 copy-start
  127.5 30.3 %copy-start.1 = (bf16[2048,128]{1,0:T(8,128)(2,1)S(1)}, bf16[2048,128]{1,0:T(8,128)(2,1)}, u32[]{:S(2)}) copy-start(bf16[2048,128]{1,0:T(8,128)(2,1)} %scatter_high.1) | copy-start | bytes 1572868
  127.5 94.2 %all-gather.14.cloned.1.call-start = ((), (), s32[]{:S(2)}) async-start(), calls=%async_computation.9 | async-start | bytes 4718592 | tf_op jit(solution)/shard_map/all_gather | solution.py:559
  132.3 33.3 %all-to-all-start.4 = ((bf16[32,128,128]{2,1,0:T(8,128)(2,1)}), bf16[32,128,128]{2,1,0:T(8,128)(2,1)S(1)}, u32[]{:S(2)}, u32[]{:S(2)}) async-start(bf16[32,128,128]{2,1,0:T(8,128)(2,1)} %gather_rows.2), calls=%async_computation.4 | async-start | bytes 2097152 | tf_op jit(solution)/shard_map/all_to_all | solution.py:416
  165.5 45.6 %all-to-all-start.5 = ((bf16[32,128,128]{2,1,0:T(8,128)(2,1)}), bf16[32,128,128]{2,1,0:T(8,128)(2,1)}, u32[]{:S(2)}, u32[]{:S(2)}) async-start(bf16[32,128,128]{2,1,0:T(8,128)(2,1)} %gather_rows.3), calls=%async_computation.5 | async-start | bytes 2097152 | tf_op jit(solution)/shard_map/all_to_all | solution.py:416
  172.0 8.4 %collective-permute-start = (bf16[64,1024]{1,0:T(8,128)(2,1)S(1)}, bf16[64,1024]{1,0:T(8,128)(2,1)S(1)}, u32[]{:S(2)}, u32[]{:S(2)}) collective-permute-start(bf16[64,1024]{1,0:T(8,128)(2,1)S(1)} %get-tuple-element.48), channel_id=1, source_target_pairs={{0,8},{8,16},{16,24},{24,0},{1,9},{9,17},{17,25},{25,1},{2,10},{10... | collective-permute-start | bytes 393224 | tf_op jit(solution)/shard_map/ppermute | solution.py:425
  173.5 14.2 %collective-permute-start.1 = (bf16[64,1024]{1,0:T(8,128)(2,1)S(1)}, bf16[64,1024]{1,0:T(8,128)(2,1)S(1)}, u32[]{:S(2)}, u32[]{:S(2)}) collective-permute-start(bf16[64,1024]{1,0:T(8,128)(2,1)S(1)} %get-tuple-element.50), channel_id=1, source_target_pairs={{0,16},{8,24},{16,0},{24,8},{1,17},{9,25},{17,1},{25,9},{2,18},{10... | collective-permute-start | bytes 393224 | tf_op jit(solution)/shard_map/ppermute | solution.py:425
  176.2 11.5 %collective-permute-start.2 = (bf16[64,1024]{1,0:T(8,128)(2,1)S(1)}, bf16[64,1024]{1,0:T(8,128)(2,1)S(1)}, u32[]{:S(2)}, u32[]{:S(2)}) collective-permute-start(bf16[64,1024]{1,0:T(8,128)(2,1)S(1)} %get-tuple-element.49), channel_id=1, source_target_pairs={{0,24},{8,0},{16,8},{24,16},{1,25},{9,1},{17,9},{25,17},{2,26},{10... | collective-permute-start | bytes 393224 | tf_op jit(solution)/shard_map/ppermute | solution.py:425
  187.8 11.8 %collective-permute-start.3 = (bf16[64,1024]{1,0:T(8,128)(2,1)S(1)}, bf16[64,1024]{1,0:T(8,128)(2,1)S(1)}, u32[]{:S(2)}, u32[]{:S(2)}) collective-permute-start(bf16[64,1024]{1,0:T(8,128)(2,1)S(1)} %fusion.5), channel_id=1, source_target_pairs={{0,32},{32,0},{64,96},{96,64},{128,160},{160,128},{192,224},{224,1... | collective-permute-start | bytes 393224 | tf_op jit(solution)/shard_map/ppermute | solution.py:441
  187.9 16.1 %collective-permute-start.4 = (bf16[64,1024]{1,0:T(8,128)(2,1)S(1)}, bf16[64,1024]{1,0:T(8,128)(2,1)S(1)}, u32[]{:S(2)}, u32[]{:S(2)}) collective-permute-start(bf16[64,1024]{1,0:T(8,128)(2,1)S(1)} %fusion.5), channel_id=1, source_target_pairs={{0,64},{32,96},{64,0},{96,32},{128,192},{160,224},{192,128},{224,1... | collective-permute-start | bytes 393224 | tf_op jit(solution)/shard_map/ppermute | solution.py:441
  190.8 16.6 %collective-permute-start.5 = (bf16[64,1024]{1,0:T(8,128)(2,1)S(1)}, bf16[64,1024]{1,0:T(8,128)(2,1)S(1)}, u32[]{:S(2)}, u32[]{:S(2)}) collective-permute-start(bf16[64,1024]{1,0:T(8,128)(2,1)S(1)} %fusion.5), channel_id=1, source_target_pairs={{0,96},{32,64},{64,32},{96,0},{128,224},{160,192},{192,160},{224,1... | collective-permute-start | bytes 393224 | tf_op jit(solution)/shard_map/ppermute | solution.py:441
  207.4 9.9 %collective-permute-start.6 = (bf16[64,1024]{1,0:T(8,128)(2,1)S(1)}, bf16[64,1024]{1,0:T(8,128)(2,1)S(1)}, u32[]{:S(2)}, u32[]{:S(2)}) collective-permute-start(bf16[64,1024]{1,0:T(8,128)(2,1)S(1)} %add_convert_fusion.1), channel_id=1, source_target_pairs={{0,128},{32,160},{64,192},{96,224},{128,0},{160,32},{192,64},{224,... | collective-permute-start | bytes 393224 | tf_op jit(solution)/shard_map/ppermute | solution.py:454
  217.3 8.5 %collective-permute-start.7 = (bf16[64,1024]{1,0:T(8,128)(2,1)S(1)}, bf16[64,1024]{1,0:T(8,128)(2,1)S(1)}, u32[]{:S(2)}, u32[]{:S(2)}) collective-permute-start(bf16[64,1024]{1,0:T(8,128)(2,1)S(1)} %add_convert_fusion.refs_0_), channel_id=1, source_target_pairs={{0,24},{8,0},{16,8},{24,16},{1,25},{9,1},{17,9},{25,17},{2,26},{10... | collective-permute-start | bytes 393224 | tf_op jit(solution)/shard_map/ppermute | solution.py:425
  220.2 7.9 %collective-permute-start.8 = (bf16[64,1024]{1,0:T(8,128)(2,1)S(1)}, bf16[64,1024]{1,0:T(8,128)(2,1)S(1)}, u32[]{:S(2)}, u32[]{:S(2)}) collective-permute-start(bf16[64,1024]{1,0:T(8,128)(2,1)S(1)} %add_convert_fusion.refs_0_), channel_id=1, source_target_pairs={{0,16},{8,24},{16,0},{24,8},{1,17},{9,25},{17,1},{25,9},{2,18},{10... | collective-permute-start | bytes 393224 | tf_op jit(solution)/shard_map/ppermute | solution.py:425
  220.8 8.4 %collective-permute-start.9 = (bf16[64,1024]{1,0:T(8,128)(2,1)S(1)}, bf16[64,1024]{1,0:T(8,128)(2,1)S(1)}, u32[]{:S(2)}, u32[]{:S(2)}) collective-permute-start(bf16[64,1024]{1,0:T(8,128)(2,1)S(1)} %add_convert_fusion.refs_0_), channel_id=1, source_target_pairs={{0,8},{8,16},{16,24},{24,0},{1,9},{9,17},{17,25},{25,1},{2,10},{10... | collective-permute-start | bytes 393224 | tf_op jit(solution)/shard_map/ppermute | solution.py:425
Sparse Core Ops, SparseCore 0:
  9.9 37.2 all-gather.9
  56.7 30.1 all-gather.11
  127.6 30.1 all-gather.7
  160.0 34.6 all-gather.13

commit v9 on v8

--- a/solution.py
+++ b/solution.py
@@ -73,7 +73,7 @@
     blocks, blk, _ = adjacency.shape
     nodes, cols = features.shape
     parts, cap = rows.shape
-    chunk = 32
+    chunk = 64
     return pl.pallas_call(
         forward_blocks_kernel,
         grid_spec=pltpu.PrefetchScalarGridSpec(
@@ -285,7 +285,17 @@
 
 
 def dense_kernel(
-    at_ref, mean_ref, own_ref, cot_ref, weight_ref, degree_ref, back_ref, hidden_ref, grad_ref, acc_ref
+    at_ref,
+    mean_ref,
+    own_ref,
+    cot_ref,
+    weight_ref,
+    turned_ref,
+    degree_ref,
+    back_ref,
+    hidden_ref,
+    grad_ref,
+    acc_ref,
 ):
     step = pl.program_id(0)
     pieces, rows, cols = mean_ref.shape
@@ -300,9 +310,7 @@
     grad_ref[...] = grad
     for piece in range(tile // cols):
         hidden_ref[piece] = hidden[:, piece * cols : (piece + 1) * cols]
-    update = lax.dot_general(
-        grad, weight_ref[...], (((1,), (1,)), ((), ())), preferred_element_type=F32
-    )
+    update = jnp.dot(grad, turned_ref[...], preferred_element_type=F32)
 
     @pl.when(step == 0)
     def _():
@@ -319,7 +327,7 @@
             back_ref[piece] = back[:, piece * cols : (piece + 1) * cols]
 
 
-def dense(at, mean_pieces, own, cot_all, w_neigh, degrees):
+def dense(at, mean_pieces, own, cot_all, w_neigh, w_neigh_t, degrees):
     pieces, rows, cols = mean_pieces.shape
     wide = w_neigh.shape[1]
     tile = 256
@@ -334,6 +342,7 @@
                 pl.BlockSpec((rows, tile), lambda i, at: (0, i)),
                 pl.BlockSpec((per, rows, cols), lambda i, at: (i, at[0], 0)),
                 pl.BlockSpec((pieces * cols, tile), lambda i, at: (0, i)),
+                pl.BlockSpec((tile, pieces * cols), lambda i, at: (i, 0)),
                 pl.BlockSpec((rows, 1), lambda i, at: (at[0], 0)),
             ],
             out_specs=[
@@ -350,7 +359,7 @@
         ],
         compiler_params=params(1),
         name="dense",
-    )(at, mean_pieces, own, cot_all, w_neigh, degrees)
+    )(at, mean_pieces, own, cot_all, w_neigh, w_neigh_t, degrees)
 
 
 def backward_blocks_kernel(
@@ -384,7 +393,7 @@
     blocks, blk, _ = adjacency_t.shape
     nodes, cols = self_grad.shape
     parts = low.shape[0]
-    chunk = 32
+    chunk = 64
     return pl.pallas_call(
         backward_blocks_kernel,
         grid_spec=pltpu.PrefetchScalarGridSpec(
@@ -530,13 +539,14 @@
     parts = low.shape[0]
     ids = low_in[:, blk : blk + 4, :].astype(F32).reshape(parts // 8, 8, 4, blk).transpose(2, 0, 3, 1)
     own = own_term(at, in_hbm(feat_all), w_self, share)
-    partial_sum, adjacency_t, ids, own = lax.optimization_barrier(
-        (partial_sum, adjacency_t, ids, own)
+    w_neigh_t = in_hbm(after(w_neigh, low_in).T)
+    partial_sum, adjacency_t, ids, own, w_neigh_t = lax.optimization_barrier(
+        (partial_sum, adjacency_t, ids, own, w_neigh_t)
     )
     neighbor_mean = scatter_high(low_in, high_in, ids, in_hbm(partial_sum), degrees)
     mean_pieces = swap(neighbor_mean.reshape(feat_size, share, feat_cols), "feat")
     back_pieces, hidden_pieces, grad_pre = dense(
-        at, mean_pieces, in_hbm(own), in_hbm(cot_all), in_hbm(w_neigh), degrees
+        at, mean_pieces, in_hbm(own), in_hbm(cot_all), in_hbm(w_neigh), w_neigh_t, degrees
     )
     back_rows = swap(back_pieces, "feat").reshape(node_rows, feat_cols)
     back_rows, grad_pre, hidden_pieces = lax.optimization_barrier(

time: 238 us -> 238 us (level)
  local copies, waits for them, and re-layouts: 10.6 us -> 14.5 us
  waiting for transfers between devices: 54.9 us -> 51.8 us
    optimization_barrier x1 -> x2, local copies, waits for them, and re-layouts: 6.42 us -> 10.4 us  [after(): return lax.optimization_barrier((value, *others))[0]]
    all_to_all x3, waiting for transfers between devices: 11.4 us -> 7.53 us  [swap(): return lax.all_to_all(value, axis, split_axis=0, concat_axis=0, tiled=True)]
  transfers between devices with their start and end apart: 17 -> 17, of which waited for: 12 -> 12; matrix products, arithmetic and copies ran while one was open for 7% -> 9% of each run, Pallas kernels for 16% -> 15%
where the time goes in v9:
time: 238 us; the launch traced here: 237 us
  blocking collectives  69.4 us (29%)
  waiting for transfers between devices  51.8 us (22%)
  Pallas kernels  44 us (18%)
  starting transfers between devices  35.9 us (15%)
  local copies, waits for them, and re-layouts  14.5 us (6%)
  between operations  13.9 us (6%)
  matrix products  7.14 us (3%)
    all_to_all x3, blocking collectives, swap(): return lax.all_to_all(value, axis, split_axis=0, concat_axis=0, tiled=True)  69.4 us
    all_to_all x3, starting transfers between devices, swap(): return lax.all_to_all(value, axis, split_axis=0, concat_axis=0, tiled=True)  18.4 us
    ppermute x6, waiting for transfers between devices, rotate(): lax.ppermute(value, axis, [(i, (i + distance) % size) for i in range(size)])  15.8 us
    all_gather x1, waiting for transfers between devices, on_device(): grad_full = lax.all_gather(grad_pre, 'feat', axis=0, tiled=True)  14.5 us
    ppermute x3, waiting for transfers between devices, quad_sum(): lax.ppermute(value, axis, [(i, i ^ d) for i in range(size)]).astype(F32)  12.4 us
    optimization_barrier x2, local copies, waits for them, and re-layouts, after(): return lax.optimization_barrier((value, *others))[0]  10.4 us
    ppermute x6, starting transfers between devices, rotate(): lax.ppermute(value, axis, [(i, (i + distance) % size) for i in range(size)])  9.97 us
    pallas_call x2, Pallas kernels, gather_rows(): pl.pallas_call(gather_kernel, grid=(1,), in_specs=[pl.BlockSpec((1, group...  9.42 us
  transfers between devices with their start and end apart: 17, of which 12 were waited for; matrix products, arithmetic and copies ran while one was open for 9% of the time, Pallas kernels for 15%

profile of v9, /device:TPU:32, one launch (start us, length us, event | category | flops | bytes accessed | tf_op | source)
XLA Modules:
  0.0 236.8 jit_solution(1711306115084603826)
XLA Ops:
  7.2 0.0 all-gather.10.cloned.1.call-start
  7.2 0.7 all-gather.10.cloned.1.call-update
  7.9 0.0 all-gather.12.cloned.1.call-start
  7.9 0.0 copy-start.2
  8.0 6.0 %forward_blocks.1 = (bf16[32,136,128]{2,1,0:T(8,128)(2,1)S(1)}, bf16[32,128,128]{2,1,0:T(8,128)(2,1)}) custom-call(s32[128]{0:T(128)} %source_ref.3, s32[128]{0:T(128)} %slot_ref.3, s32[32]{0:T(128)} %bitcast.49, s32[32,256]{1,0:T(8,128)} %bitcast.47, bf16[2048,128]{1,0:T(8,128)(2,1)} %feat_ref.1, bf16[128,128,128]{2,1,0:T(8,128)(2,1)} %adj_ref.1), custom_call_target="tpu_custom_call" | custom-call | tf_op jit(solution)/shard_map/forward_blocks/pallas_call | solution.py:77
  13.9 41.9 %all_to_all.30.payload_ids_ref.rows_ref.ids_ref = bf16[32,136,128]{2,1,0:T(8,128)(2,1)S(1)} all-to-all(bf16[32,136,128]{2,1,0:T(8,128)(2,1)S(1)} %get-tuple-element.28), channel_id=1, replica_groups=mesh['z'=8,'y'=4,'feat'=8] {'z','y'}, dimensions={0} | all-to-all | bytes 2228224 | tf_op jit(solution)/shard_map/all_to_all | solution.py:425
  55.8 0.0 all-gather.12.cloned.1.call-update
  55.8 5.5 %all-to-all-start.1 = ((bf16[32,128,128]{2,1,0:T(8,128)(2,1)}), bf16[32,128,128]{2,1,0:T(8,128)(2,1)}, u32[]{:S(2)}, u32[]{:S(2)}) async-start(bf16[32,128,128]{2,1,0:T(8,128)(2,1)} %get-tuple-element.29), calls=%async_computation.1 | async-start | bytes 2097152 | tf_op jit(solution)/shard_map/all_to_all | solution.py:425
  61.3 0.0 all-gather.8.cloned.1.call-start
  61.4 0.0 copy-done.2
  61.4 0.4 copy.32.degree_ref
  61.8 6.4 %copy.28 = bf16[128,128,128]{1,2,0:T(8,128)(2,1)} copy(bf16[128,128,128]{2,1,0:T(8,128)(2,1)} %adj_ref.1) | data formatting | bytes 8388608 | tf_op jit(solution)/shard_map/optimization_barrier | solution.py:429
  68.2 4.0 %copy.31 = bf16[1024,1024]{0,1:T(8,128)(2,1)} copy(bf16[1024,1024]{1,0:T(8,128)(2,1)} %weight_ref.3) | data formatting | bytes 4194304 | tf_op jit(solution)/shard_map/optimization_barrier | solution.py:429
  72.2 0.2 copy.30
  72.4 6.3 %scatter_low.1.init_ref = f32[2048,128]{1,0:T(8,128)} custom-call(bf16[32,136,128]{2,1,0:T(8,128)(2,1)S(1)} %all_to_all.30.payload_ids_ref.rows_ref.ids_ref, bf16[32,136,128]{2,1,0:T(8,128)(2,1)S(1)} %all_to_all.30.payload_ids_ref.rows_ref.ids_ref), custom_call_target="tpu_custom_call" | custom-call | tf_op jit(solution)/shard_map/scatter_low/pallas_call | solution.py:169
  78.7 0.0 all-gather.10.cloned.1.call-done
  78.7 0.0 copy-start
  78.7 1.6 copy-done
  80.3 3.6 %own_term.1.own_ref = f32[256,1024]{1,0:T(8,128)} custom-call(s32[1]{0:T(128)} %bitcast.at_ref, bf16[8,2048,128]{2,1,0:T(8,128)(2,1)} %bitcast.40, bf16[1024,1024]{1,0:T(8,128)(2,1)S(1)} %copy-done), custom_call_target="tpu_custom_call" | custom-call | tf_op jit(solution)/shard_map/own_term/pallas_call | solution.py:270
  84.0 3.4 %all-to-all-done.1.rows_ref = bf16[32,128,128]{2,1,0:T(8,128)(2,1)} async-done(((bf16[32,128,128]{2,1,0:T(8,128)(2,1)}), bf16[32,128,128]{2,1,0:T(8,128)(2,1)}, u32[]{:S(2)}, u32[]{:S(2)}) %all-to-all-start.1) | async-done | bytes 1048608 | tf_op jit(solution)/shard_map/all_to_all | solution.py:425
  87.4 5.8 %scatter_high.1 = bf16[2048,128]{1,0:T(8,128)(2,1)} custom-call(bf16[32,136,128]{2,1,0:T(8,128)(2,1)S(1)} %all_to_all.30.payload_ids_ref.rows_ref.ids_ref, bf16[32,128,128]{2,1,0:T(8,128)(2,1)} %all-to-all-done.1.rows_ref, f32[4,4,128,8]{3,2,1,0:T(8,128)S(1)} %bitcast.30, f32[2048,128]{1,0:T(8,128)} %scatter_low.1.init_ref, f32[2048,1]{1,0:T(8,128)S(1)} %copy.32.degree_ref), custom_call_target="tpu_custom_call" | custom-call | tf_op jit(solution)/shard_map/scatter_high/pallas_call | solution.py:188
  93.2 14.7 %all_to_all.31.mean_ref = bf16[8,256,128]{2,1,0:T(8,128)(2,1)S(1)} all-to-all(bf16[8,256,128]{2,1,0:T(8,128)(2,1)} %bitcast.41), channel_id=1, replica_groups=mesh['z'=8,'y'=4,'feat'=8] {'feat'}, dimensions={0} | all-to-all | bytes 1048576 | tf_op jit(solution)/shard_map/all_to_all | solution.py:425
  107.9 0.0 all-gather.12.cloned.1.call-done
  107.9 6.4 %dense.1 = (bf16[8,256,128]{2,1,0:T(8,128)(2,1)S(1)}, bf16[8,256,128]{2,1,0:T(8,128)(2,1)}, bf16[256,1024]{1,0:T(8,128)(2,1)}) custom-call(s32[1]{0:T(128)} %bitcast.at_ref, bf16[8,256,128]{2,1,0:T(8,128)(2,1)S(1)} %all_to_all.31.mean_ref, f32[256,1024]{1,0:T(8,128)} %own_term.1.own_ref, bf16[8,2048,128]{2,1,0:T(8,128)(2,1)} %bitcast.39, ...), custom_call_target="tpu_custom_call" | custom-call | tf_op jit(solution)/shard_map/dense/pallas_call | solution.py:335
  114.3 12.8 %all_to_all.32 = bf16[8,256,128]{2,1,0:T(8,128)(2,1)S(1)} all-to-all(bf16[8,256,128]{2,1,0:T(8,128)(2,1)S(1)} %get-tuple-element.37), channel_id=1, replica_groups=mesh['z'=8,'y'=4,'feat'=8] {'feat'}, dimensions={0} | all-to-all | bytes 1048576 | tf_op jit(solution)/shard_map/all_to_all | solution.py:425
  127.1 0.0 all-gather.8.cloned.1.call-update
  127.1 0.0 copy-start.1
  127.1 0.2 all-gather.14.cloned.1.call-start
  127.4 4.7 %gather_rows.2 = bf16[32,128,128]{2,1,0:T(8,128)(2,1)} custom-call(f32[4,4,128,8]{3,2,1,0:T(8,128)S(1)} %bitcast.31, f32[4,4,128,8]{3,2,1,0:T(8,128)S(1)} %bitcast.32, bf16[2048,128]{1,0:T(8,128)(2,1)S(1)} %bitcast.35), custom_call_target="tpu_custom_call" | custom-call | tf_op jit(solution)/shard_map/gather_rows/pallas_call | solution.py:241
  132.1 0.0 all-gather.14.cloned.1.call-update
  132.1 6.5 %all-to-all-start.4 = ((bf16[32,128,128]{2,1,0:T(8,128)(2,1)}), bf16[32,128,128]{2,1,0:T(8,128)(2,1)S(1)}, u32[]{:S(2)}, u32[]{:S(2)}) async-start(bf16[32,128,128]{2,1,0:T(8,128)(2,1)} %gather_rows.2), calls=%async_computation.4 | async-start | bytes 2097152 | tf_op jit(solution)/shard_map/all_to_all | solution.py:425
  138.6 4.7 %gather_rows.3 = bf16[32,128,128]{2,1,0:T(8,128)(2,1)} custom-call(f32[4,4,128,8]{3,2,1,0:T(8,128)S(1)} %bitcast.33, f32[4,4,128,8]{3,2,1,0:T(8,128)S(1)} %bitcast.34, bf16[2048,128]{1,0:T(8,128)(2,1)S(1)} %bitcast.36), custom_call_target="tpu_custom_call" | custom-call | tf_op jit(solution)/shard_map/gather_rows/pallas_call | solution.py:241
  143.3 14.5 %all-gather.8.cloned.1.call-done = bf16[2048,1024]{1,0:T(8,128)(2,1)} async-done(((bf16[256,1024]{1,0:T(8,128)(2,1)}), bf16[2048,1024]{1,0:T(8,128)(2,1)}) %all-gather.8.cloned.1.call-update) | async-done | bytes 4194320 | tf_op jit(solution)/shard_map/all_gather | solution.py:558
  157.8 0.0 copy-done.1
  157.8 3.6 %convolution_convert_fusion = bf16[256,1024]{1,0:T(8,128)(2,1)S(1)} fusion(bf16[2048,1024]{1,0:T(8,128)(2,1)} %all-gather.8.cloned.1.call-done, bf16[2048,128]{1,0:T(8,128)(2,1)S(1)} %copy-done.1, bf16[2048,128]{1,0:T(8,128)(2,1)} %feat_ref.1), kind=kOutput, calls=%fused_computation | convolution fusion | flops 1076101120 | bytes 5767168 | tf_op jit(solution)/shard_map/dot_general | solution.py:561
  161.4 4.1 %all-to-all-done.4.low_ref = bf16[32,128,128]{2,1,0:T(8,128)(2,1)S(1)} async-done(((bf16[32,128,128]{2,1,0:T(8,128)(2,1)}), bf16[32,128,128]{2,1,0:T(8,128)(2,1)S(1)}, u32[]{:S(2)}, u32[]{:S(2)}) %all-to-all-start.4) | async-done | bytes 1048608 | tf_op jit(solution)/shard_map/all_to_all | solution.py:425
  165.6 6.4 %all-to-all-start.5 = ((bf16[32,128,128]{2,1,0:T(8,128)(2,1)}), bf16[32,128,128]{2,1,0:T(8,128)(2,1)}, u32[]{:S(2)}, u32[]{:S(2)}) async-start(bf16[32,128,128]{2,1,0:T(8,128)(2,1)} %gather_rows.3), calls=%async_computation.5 | async-start | bytes 2097152 | tf_op jit(solution)/shard_map/all_to_all | solution.py:425
  172.0 1.5 collective-permute-start
  173.6 2.7 %collective-permute-start.1 = (bf16[64,1024]{1,0:T(8,128)(2,1)S(1)}, bf16[64,1024]{1,0:T(8,128)(2,1)S(1)}, u32[]{:S(2)}, u32[]{:S(2)}) collective-permute-start(bf16[64,1024]{1,0:T(8,128)(2,1)S(1)} %get-tuple-element.54), channel_id=1, source_target_pairs={{0,16},{8,24},{16,0},{24,8},{1,17},{9,25},{17,1},{25,9},{2,18},{10... | collective-permute-start | bytes 393224 | tf_op jit(solution)/shard_map/ppermute | solution.py:434
  176.3 1.5 collective-permute-start.2
  177.7 2.8 %collective-permute-done = bf16[64,1024]{1,0:T(8,128)(2,1)S(1)} collective-permute-done((bf16[64,1024]{1,0:T(8,128)(2,1)S(1)}, bf16[64,1024]{1,0:T(8,128)(2,1)S(1)}, u32[]{:S(2)}, u32[]{:S(2)}) %collective-permute-start) | collective-permute-done | bytes 131104 | tf_op jit(solution)/shard_map/ppermute | solution.py:434
  180.5 7.3 %collective-permute-done.1 = bf16[64,1024]{1,0:T(8,128)(2,1)S(1)} collective-permute-done((bf16[64,1024]{1,0:T(8,128)(2,1)S(1)}, bf16[64,1024]{1,0:T(8,128)(2,1)S(1)}, u32[]{:S(2)}, u32[]{:S(2)}) %collective-permute-start.1) | collective-permute-done | bytes 131104 | tf_op jit(solution)/shard_map/ppermute | solution.py:434
  187.8 0.0 collective-permute-done.2
  187.8 0.1 fusion.5
  187.9 0.1 collective-permute-start.3
  188.0 2.8 %collective-permute-start.4 = (bf16[64,1024]{1,0:T(8,128)(2,1)S(1)}, bf16[64,1024]{1,0:T(8,128)(2,1)S(1)}, u32[]{:S(2)}, u32[]{:S(2)}) collective-permute-start(bf16[64,1024]{1,0:T(8,128)(2,1)S(1)} %fusion.5), channel_id=1, source_target_pairs={{0,64},{32,96},{64,0},{96,32},{128,192},{160,224},{192,128},{224,1... | collective-permute-start | bytes 393224 | tf_op jit(solution)/shard_map/ppermute | solution.py:450
  190.8 0.7 collective-permute-start.5
  191.5 3.5 %fusion.6.self_ref = f32[2048,128]{1,0:T(8,128)S(1)} fusion(bf16[2048,1024]{1,0:T(8,128)(2,1)} %all-gather.8.cloned.1.call-done, bf16[1024,1024]{1,0:T(8,128)(2,1)} %weight_ref.2, s32[]{:T(128)S(6)} %select_n.36), kind=kOutput, calls=%fused_computation.10 | convolution fusion | flops 536870912 | bytes 5505028 | tf_op jit(solution)/shard_map/dot_general | solution.py:572
  195.0 4.7 %collective-permute-done.3 = bf16[64,1024]{1,0:T(8,128)(2,1)S(1)} collective-permute-done((bf16[64,1024]{1,0:T(8,128)(2,1)S(1)}, bf16[64,1024]{1,0:T(8,128)(2,1)S(1)}, u32[]{:S(2)}, u32[]{:S(2)}) %collective-permute-start.3) | collective-permute-done | bytes 131104 | tf_op jit(solution)/shard_map/ppermute | solution.py:450
  199.7 4.4 %collective-permute-done.4 = bf16[64,1024]{1,0:T(8,128)(2,1)S(1)} collective-permute-done((bf16[64,1024]{1,0:T(8,128)(2,1)S(1)}, bf16[64,1024]{1,0:T(8,128)(2,1)S(1)}, u32[]{:S(2)}, u32[]{:S(2)}) %collective-permute-start.4) | collective-permute-done | bytes 131104 | tf_op jit(solution)/shard_map/ppermute | solution.py:450
  204.1 3.3 %collective-permute-done.5 = bf16[64,1024]{1,0:T(8,128)(2,1)S(1)} collective-permute-done((bf16[64,1024]{1,0:T(8,128)(2,1)S(1)}, bf16[64,1024]{1,0:T(8,128)(2,1)S(1)}, u32[]{:S(2)}, u32[]{:S(2)}) %collective-permute-start.5) | collective-permute-done | bytes 131104 | tf_op jit(solution)/shard_map/ppermute | solution.py:450
  207.4 0.1 add_convert_fusion.1
  207.4 3.7 %collective-permute-start.6 = (bf16[64,1024]{1,0:T(8,128)(2,1)S(1)}, bf16[64,1024]{1,0:T(8,128)(2,1)S(1)}, u32[]{:S(2)}, u32[]{:S(2)}) collective-permute-start(bf16[64,1024]{1,0:T(8,128)(2,1)S(1)} %add_convert_fusion.1), channel_id=1, source_target_pairs={{0,128},{32,160},{64,192},{96,224},{128,0},{160,32},{192,64},{224,... | collective-permute-start | bytes 393224 | tf_op jit(solution)/shard_map/ppermute | solution.py:463
  211.2 0.0 all-to-all-done.5.high_ref
  211.2 5.3 %backward_blocks.1 = bf16[2048,128]{1,0:T(8,128)(2,1)} custom-call(s32[128]{0:T(128)} %source_ref.3, s32[128]{0:T(128)} %slot_ref.3, bf16[32,128,128]{2,1,0:T(8,128)(2,1)S(1)} %all-to-all-done.4.low_ref, bf16[32,128,128]{2,1,0:T(8,128)(2,1)} %all-to-all-done.5.high_ref, bf16[128,128,128]{2,1,0:T(8,128)(2,1)} %bitcast.37, f32[2048,128]{1,0:T(8,128)S(1)} %fusion.6.self_ref), custom_call_target="tpu_custom_call" | custom-call | tf_op jit(solution)/shard_map/backward_blocks/pallas_call | solution.py:397
  216.4 0.9 collective-permute-done.6
  217.4 2.9 %collective-permute-start.7 = (bf16[64,1024]{1,0:T(8,128)(2,1)S(1)}, bf16[64,1024]{1,0:T(8,128)(2,1)S(1)}, u32[]{:S(2)}, u32[]{:S(2)}) collective-permute-start(bf16[64,1024]{1,0:T(8,128)(2,1)S(1)} %add_convert_fusion.refs_0_), channel_id=1, source_target_pairs={{0,24},{8,0},{16,8},{24,16},{1,25},{9,1},{17,9},{25,17},{2,26},{10... | collective-permute-start | bytes 393224 | tf_op jit(solution)/shard_map/ppermute | solution.py:434
  220.3 0.5 collective-permute-start.8
  220.8 0.8 collective-permute-start.9
  221.6 1.9 constant_dynamic-slice_fusion
  223.5 2.3 collective-permute-done.7.refs_1_
  225.8 2.4 collective-permute-done.8.refs_2_
  228.1 1.1 collective-permute-done.9.refs_3_
  229.2 1.1 assemble.1
  (5 shorter events, 0.1 us)
Async XLA Ops:
  7.2 71.6 %all-gather.10.cloned.1.call-start = ((), (), s32[]{:S(2)}) async-start(), calls=%async_computation.7 | async-start | bytes 4718592 | tf_op jit(solution)/shard_map/all_gather | solution.py:531
  7.9 100.0 %all-gather.12.cloned.1.call-start = ((), (), s32[]{:S(2)}) async-start(), calls=%async_computation.8 | async-start | bytes 4718592 | tf_op jit(solution)/shard_map/all_gather | solution.py:532
  7.9 53.4 %copy-start.2 = (s32[2048]{0:T(1024)S(1)}, s32[2048]{0:T(1024)}, u32[]{:S(2)}) copy-start(s32[2048]{0:T(1024)} %param.18) | copy-start | bytes 24580
  55.8 31.5 %all-to-all-start.1 = ((bf16[32,128,128]{2,1,0:T(8,128)(2,1)}), bf16[32,128,128]{2,1,0:T(8,128)(2,1)}, u32[]{:S(2)}, u32[]{:S(2)}) async-start(bf16[32,128,128]{2,1,0:T(8,128)(2,1)} %get-tuple-element.29), calls=%async_computation.1 | async-start | bytes 2097152 | tf_op jit(solution)/shard_map/all_to_all | solution.py:425
  61.3 96.5 %all-gather.8.cloned.1.call-start = ((), (), s32[]{:S(2)}) async-start(), calls=%async_computation.6 | async-start | bytes 4718592 | tf_op jit(solution)/shard_map/all_gather | solution.py:558
  78.7 1.6 copy-start
  127.1 30.7 %copy-start.1 = (bf16[2048,128]{1,0:T(8,128)(2,1)S(1)}, bf16[2048,128]{1,0:T(8,128)(2,1)}, u32[]{:S(2)}) copy-start(bf16[2048,128]{1,0:T(8,128)(2,1)} %scatter_high.1) | copy-start | bytes 1572868
  127.1 94.5 %all-gather.14.cloned.1.call-start = ((), (), s32[]{:S(2)}) async-start(), calls=%async_computation.9 | async-start | bytes 4718592 | tf_op jit(solution)/shard_map/all_gather | solution.py:569
  132.1 33.5 %all-to-all-start.4 = ((bf16[32,128,128]{2,1,0:T(8,128)(2,1)}), bf16[32,128,128]{2,1,0:T(8,128)(2,1)S(1)}, u32[]{:S(2)}, u32[]{:S(2)}) async-start(bf16[32,128,128]{2,1,0:T(8,128)(2,1)} %gather_rows.2), calls=%async_computation.4 | async-start | bytes 2097152 | tf_op jit(solution)/shard_map/all_to_all | solution.py:425
  165.6 45.6 %all-to-all-start.5 = ((bf16[32,128,128]{2,1,0:T(8,128)(2,1)}), bf16[32,128,128]{2,1,0:T(8,128)(2,1)}, u32[]{:S(2)}, u32[]{:S(2)}) async-start(bf16[32,128,128]{2,1,0:T(8,128)(2,1)} %gather_rows.3), calls=%async_computation.5 | async-start | bytes 2097152 | tf_op jit(solution)/shard_map/all_to_all | solution.py:425
  172.0 8.5 %collective-permute-start = (bf16[64,1024]{1,0:T(8,128)(2,1)S(1)}, bf16[64,1024]{1,0:T(8,128)(2,1)S(1)}, u32[]{:S(2)}, u32[]{:S(2)}) collective-permute-start(bf16[64,1024]{1,0:T(8,128)(2,1)S(1)} %get-tuple-element.52), channel_id=1, source_target_pairs={{0,8},{8,16},{16,24},{24,0},{1,9},{9,17},{17,25},{25,1},{2,10},{10... | collective-permute-start | bytes 393224 | tf_op jit(solution)/shard_map/ppermute | solution.py:434
  173.6 14.2 %collective-permute-start.1 = (bf16[64,1024]{1,0:T(8,128)(2,1)S(1)}, bf16[64,1024]{1,0:T(8,128)(2,1)S(1)}, u32[]{:S(2)}, u32[]{:S(2)}) collective-permute-start(bf16[64,1024]{1,0:T(8,128)(2,1)S(1)} %get-tuple-element.54), channel_id=1, source_target_pairs={{0,16},{8,24},{16,0},{24,8},{1,17},{9,25},{17,1},{25,9},{2,18},{10... | collective-permute-start | bytes 393224 | tf_op jit(solution)/shard_map/ppermute | solution.py:434
  176.3 11.6 %collective-permute-start.2 = (bf16[64,1024]{1,0:T(8,128)(2,1)S(1)}, bf16[64,1024]{1,0:T(8,128)(2,1)S(1)}, u32[]{:S(2)}, u32[]{:S(2)}) collective-permute-start(bf16[64,1024]{1,0:T(8,128)(2,1)S(1)} %get-tuple-element.53), channel_id=1, source_target_pairs={{0,24},{8,0},{16,8},{24,16},{1,25},{9,1},{17,9},{25,17},{2,26},{10... | collective-permute-start | bytes 393224 | tf_op jit(solution)/shard_map/ppermute | solution.py:434
  187.9 11.8 %collective-permute-start.3 = (bf16[64,1024]{1,0:T(8,128)(2,1)S(1)}, bf16[64,1024]{1,0:T(8,128)(2,1)S(1)}, u32[]{:S(2)}, u32[]{:S(2)}) collective-permute-start(bf16[64,1024]{1,0:T(8,128)(2,1)S(1)} %fusion.5), channel_id=1, source_target_pairs={{0,32},{32,0},{64,96},{96,64},{128,160},{160,128},{192,224},{224,1... | collective-permute-start | bytes 393224 | tf_op jit(solution)/shard_map/ppermute | solution.py:450
  188.0 16.1 %collective-permute-start.4 = (bf16[64,1024]{1,0:T(8,128)(2,1)S(1)}, bf16[64,1024]{1,0:T(8,128)(2,1)S(1)}, u32[]{:S(2)}, u32[]{:S(2)}) collective-permute-start(bf16[64,1024]{1,0:T(8,128)(2,1)S(1)} %fusion.5), channel_id=1, source_target_pairs={{0,64},{32,96},{64,0},{96,32},{128,192},{160,224},{192,128},{224,1... | collective-permute-start | bytes 393224 | tf_op jit(solution)/shard_map/ppermute | solution.py:450
  190.8 16.6 %collective-permute-start.5 = (bf16[64,1024]{1,0:T(8,128)(2,1)S(1)}, bf16[64,1024]{1,0:T(8,128)(2,1)S(1)}, u32[]{:S(2)}, u32[]{:S(2)}) collective-permute-start(bf16[64,1024]{1,0:T(8,128)(2,1)S(1)} %fusion.5), channel_id=1, source_target_pairs={{0,96},{32,64},{64,32},{96,0},{128,224},{160,192},{192,160},{224,1... | collective-permute-start | bytes 393224 | tf_op jit(solution)/shard_map/ppermute | solution.py:450
  207.4 9.9 %collective-permute-start.6 = (bf16[64,1024]{1,0:T(8,128)(2,1)S(1)}, bf16[64,1024]{1,0:T(8,128)(2,1)S(1)}, u32[]{:S(2)}, u32[]{:S(2)}) collective-permute-start(bf16[64,1024]{1,0:T(8,128)(2,1)S(1)} %add_convert_fusion.1), channel_id=1, source_target_pairs={{0,128},{32,160},{64,192},{96,224},{128,0},{160,32},{192,64},{224,... | collective-permute-start | bytes 393224 | tf_op jit(solution)/shard_map/ppermute | solution.py:463
  217.4 8.4 %collective-permute-start.7 = (bf16[64,1024]{1,0:T(8,128)(2,1)S(1)}, bf16[64,1024]{1,0:T(8,128)(2,1)S(1)}, u32[]{:S(2)}, u32[]{:S(2)}) collective-permute-start(bf16[64,1024]{1,0:T(8,128)(2,1)S(1)} %add_convert_fusion.refs_0_), channel_id=1, source_target_pairs={{0,24},{8,0},{16,8},{24,16},{1,25},{9,1},{17,9},{25,17},{2,26},{10... | collective-permute-start | bytes 393224 | tf_op jit(solution)/shard_map/ppermute | solution.py:434
  220.3 7.9 %collective-permute-start.8 = (bf16[64,1024]{1,0:T(8,128)(2,1)S(1)}, bf16[64,1024]{1,0:T(8,128)(2,1)S(1)}, u32[]{:S(2)}, u32[]{:S(2)}) collective-permute-start(bf16[64,1024]{1,0:T(8,128)(2,1)S(1)} %add_convert_fusion.refs_0_), channel_id=1, source_target_pairs={{0,16},{8,24},{16,0},{24,8},{1,17},{9,25},{17,1},{25,9},{2,18},{10... | collective-permute-start | bytes 393224 | tf_op jit(solution)/shard_map/ppermute | solution.py:434
  220.8 8.4 %collective-permute-start.9 = (bf16[64,1024]{1,0:T(8,128)(2,1)S(1)}, bf16[64,1024]{1,0:T(8,128)(2,1)S(1)}, u32[]{:S(2)}, u32[]{:S(2)}) collective-permute-start(bf16[64,1024]{1,0:T(8,128)(2,1)S(1)} %add_convert_fusion.refs_0_), channel_id=1, source_target_pairs={{0,8},{8,16},{16,24},{24,0},{1,9},{9,17},{17,25},{25,1},{2,10},{10... | collective-permute-start | bytes 393224 | tf_op jit(solution)/shard_map/ppermute | solution.py:434
Sparse Core Ops, SparseCore 0:
  9.9 37.2 all-gather.9
  55.9 30.1 all-gather.11
  127.2 30.5 all-gather.7
  160.1 34.6 all-gather.13

commit v10 on v8

--- a/solution.py
+++ b/solution.py
@@ -73,7 +73,7 @@
     blocks, blk, _ = adjacency.shape
     nodes, cols = features.shape
     parts, cap = rows.shape
-    chunk = 32
+    chunk = 64
     return pl.pallas_call(
         forward_blocks_kernel,
         grid_spec=pltpu.PrefetchScalarGridSpec(
@@ -384,7 +384,7 @@
     blocks, blk, _ = adjacency_t.shape
     nodes, cols = self_grad.shape
     parts = low.shape[0]
-    chunk = 32
+    chunk = 64
     return pl.pallas_call(
         backward_blocks_kernel,
         grid_spec=pltpu.PrefetchScalarGridSpec(
@@ -444,6 +444,15 @@
     return ((value.astype(F32) + one) + (two + three)).astype(BF16)
 
 
+def quad_sum(value, axis):
+    size = lax.axis_size(axis)
+    one, two, three = (
+        lax.ppermute(value, axis, [(i, i ^ d) for i in range(size)]).astype(F32)
+        for d in (1, 2, 3)
+    )
+    return ((value.astype(F32) + one) + (two + three)).astype(BF16)
+
+
 def around(piece, axis):
     size = lax.axis_size(axis)
     return [piece] + [rotate(piece, axis, size - i) for i in range(1, size)]
@@ -454,41 +463,6 @@
     other = lax.ppermute(value, axis, [(i, i ^ distance) for i in range(size)])
     other = after(other, *beside)
     return (value.astype(F32) + other.astype(F32)).astype(BF16)
-
-
-def assemble_kernel(at_ref, *refs):
-    *piece_refs, first_ref, second_ref = refs
-    size = len(piece_refs)
-    half = size // 2
-    for i, piece_ref in enumerate(piece_refs):
-        place = (at_ref[0] + i) % size
-        value = piece_ref[...].astype(F32)
-
-        @pl.when(place < half)
-        def _():
-            first_ref[place] = value
-
-        @pl.when(place >= half)
-        def _():
-            second_ref[place - half] = value
-
-
-def assemble(at, pieces):
-    rows, wide = pieces[0].shape
-    half = len(pieces) // 2
-    first, second = pl.pallas_call(
-        assemble_kernel,
-        grid_spec=pltpu.PrefetchScalarGridSpec(
-            num_scalar_prefetch=1,
-            grid=(1,),
-            in_specs=[full_spec((rows, wide))] * len(pieces),
-            out_specs=[full_spec((half, rows, wide))] * 2,
-        ),
-        out_shape=[jax.ShapeDtypeStruct((half, rows, wide), F32)] * 2,
-        compiler_params=params(1),
-        name="assemble",
-    )(at, *pieces)
-    return first.reshape(half * rows, wide), second.reshape(half * rows, wide)
 
 
 def on_device(
@@ -572,8 +546,9 @@
         self_grad,
     )
     part = exchange_sum(part, "z", 4, grad_features)
-    at = after(jnp.full((1,), lax.axis_index("y"), jnp.int32), hidden_out)
-    grad_self, grad_neigh = assemble(at, around(part, "y"))
+    spread = after(swap(jnp.broadcast_to(part[None], (over_y, *part.shape)), "y"), hidden_out)
+    weight_grads = spread.reshape(2 * feat_cols, part.shape[1]).astype(F32)
+    grad_self, grad_neigh = weight_grads[:feat_cols], weight_grads[feat_cols:]
     return hidden_out, grad_features, grad_self, grad_neigh
 
 

time: 238 us -> 240 us (level)
  waiting for transfers between devices: 54.9 us -> 57.6 us
  Pallas kernels: 45.1 us -> 42.5 us
    all_to_all x3 -> x4, waiting for transfers between devices: 11.4 us -> 19 us  [swap(): return lax.all_to_all(value, axis, split_axis=0, concat_axis=0, tiled=True)]
    ppermute x6 -> x3, waiting for transfers between devices: 15.7 us -> 10.1 us  [rotate(): lax.ppermute(value, axis, [(i, (i + distance) % size) for i in range(size)])]
    ppermute x6 -> x3, starting transfers between devices: 10 us -> 5.68 us  [rotate(): lax.ppermute(value, axis, [(i, (i + distance) % size) for i in range(size)])]
    all_to_all x3 -> x4, starting transfers between devices: 18.2 us -> 22.1 us  [swap(): return lax.all_to_all(value, axis, split_axis=0, concat_axis=0, tiled=True)]
  transfers between devices with their start and end apart: 17 -> 15, of which waited for: 12 -> 10; matrix products, arithmetic and copies ran while one was open for 7% -> 7% of each run, Pallas kernels for 16% -> 15%
where the time goes in v10:
time: 240 us; the launch traced here: 239 us
  blocking collectives  69.4 us (29%)
  waiting for transfers between devices  57.6 us (24%)
  Pallas kernels  42.5 us (18%)
  starting transfers between devices  35.4 us (15%)
  between operations  13.9 us (6%)
  local copies, waits for them, and re-layouts  12.5 us (5%)
  matrix products  7.14 us (3%)
    all_to_all x3, blocking collectives, swap(): return lax.all_to_all(value, axis, split_axis=0, concat_axis=0, tiled=True)  69.4 us
    all_to_all x4, starting transfers between devices, swap(): return lax.all_to_all(value, axis, split_axis=0, concat_axis=0, tiled=True)  22.1 us
    all_to_all x4, waiting for transfers between devices, swap(): return lax.all_to_all(value, axis, split_axis=0, concat_axis=0, tiled=True)  19 us
    all_gather x1, waiting for transfers between devices, on_device(): grad_full = lax.all_gather(grad_pre, 'feat', axis=0, tiled=True)  14.5 us
    ppermute x3, waiting for transfers between devices, quad_sum(): lax.ppermute(value, axis, [(i, i ^ d) for i in range(size)]).astype(F32)  12.4 us
    ppermute x3, waiting for transfers between devices, rotate(): lax.ppermute(value, axis, [(i, (i + distance) % size) for i in range(size)])  10.1 us
    pallas_call x2, Pallas kernels, gather_rows(): pl.pallas_call(gather_kernel, grid=(1,), in_specs=[pl.BlockSpec((1, group...  9.41 us
    optimization_barrier x1, local copies, waits for them, and re-layouts, after(): return lax.optimization_barrier((value, *others))[0]  6.42 us
  transfers between devices with their start and end apart: 15, of which 10 were waited for; matrix products, arithmetic and copies ran while one was open for 7% of the time, Pallas kernels for 15%

profile of v10, /device:TPU:32, one launch (start us, length us, event | category | flops | bytes accessed | tf_op | source)
XLA Modules:
  0.0 238.5 jit_solution(12928183995748985257)
XLA Ops:
  7.2 0.0 all-gather.10.cloned.1.call-start
  7.2 0.7 all-gather.10.cloned.1.call-update
  7.9 0.0 all-gather.12.cloned.1.call-start
  7.9 0.0 copy-start.2
  8.0 6.0 %forward_blocks.1 = (bf16[32,136,128]{2,1,0:T(8,128)(2,1)S(1)}, bf16[32,128,128]{2,1,0:T(8,128)(2,1)}) custom-call(s32[128]{0:T(128)} %source_ref.3, s32[128]{0:T(128)} %slot_ref.3, s32[32]{0:T(128)} %bitcast.48, s32[32,256]{1,0:T(8,128)} %bitcast.46, bf16[2048,128]{1,0:T(8,128)(2,1)} %feat_ref.1, bf16[128,128,128]{2,1,0:T(8,128)(2,1)} %adj_ref.1), custom_call_target="tpu_custom_call" | custom-call | tf_op jit(solution)/shard_map/forward_blocks/pallas_call | solution.py:77
  13.9 41.9 %all_to_all.35.payload_ids_ref.rows_ref.ids_ref = bf16[32,136,128]{2,1,0:T(8,128)(2,1)S(1)} all-to-all(bf16[32,136,128]{2,1,0:T(8,128)(2,1)S(1)} %get-tuple-element.24), channel_id=1, replica_groups=mesh['z'=8,'y'=4,'feat'=8] {'z','y'}, dimensions={0} | all-to-all | bytes 2228224 | tf_op jit(solution)/shard_map/all_to_all | solution.py:416
  55.8 0.0 all-gather.12.cloned.1.call-update
  55.8 5.5 %all-to-all-start.1 = ((bf16[32,128,128]{2,1,0:T(8,128)(2,1)}), bf16[32,128,128]{2,1,0:T(8,128)(2,1)}, u32[]{:S(2)}, u32[]{:S(2)}) async-start(bf16[32,128,128]{2,1,0:T(8,128)(2,1)} %get-tuple-element.25), calls=%async_computation.1 | async-start | bytes 2097152 | tf_op jit(solution)/shard_map/all_to_all | solution.py:416
  61.3 0.0 all-gather.8.cloned.1.call-start
  61.4 0.0 copy-done.2
  61.4 0.4 copy.28.degree_ref
  61.8 6.4 %copy.25 = bf16[128,128,128]{1,2,0:T(8,128)(2,1)} copy(bf16[128,128,128]{2,1,0:T(8,128)(2,1)} %adj_ref.1) | data formatting | bytes 8388608 | tf_op jit(solution)/shard_map/optimization_barrier | solution.py:420
  68.2 0.2 copy.27
  68.4 6.3 %scatter_low.1.init_ref = f32[2048,128]{1,0:T(8,128)} custom-call(bf16[32,136,128]{2,1,0:T(8,128)(2,1)S(1)} %all_to_all.35.payload_ids_ref.rows_ref.ids_ref, bf16[32,136,128]{2,1,0:T(8,128)(2,1)S(1)} %all_to_all.35.payload_ids_ref.rows_ref.ids_ref), custom_call_target="tpu_custom_call" | custom-call | tf_op jit(solution)/shard_map/scatter_low/pallas_call | solution.py:169
  74.8 0.0 all-gather.10.cloned.1.call-done
  74.8 0.0 copy-start
  74.8 1.6 copy-done
  76.4 3.6 %own_term.1.own_ref = f32[256,1024]{1,0:T(8,128)} custom-call(s32[1]{0:T(128)} %bitcast.at_ref, bf16[8,2048,128]{2,1,0:T(8,128)(2,1)} %bitcast.37, bf16[1024,1024]{1,0:T(8,128)(2,1)S(1)} %copy-done), custom_call_target="tpu_custom_call" | custom-call | tf_op jit(solution)/shard_map/own_term/pallas_call | solution.py:270
  80.1 7.3 %all-to-all-done.1.rows_ref = bf16[32,128,128]{2,1,0:T(8,128)(2,1)} async-done(((bf16[32,128,128]{2,1,0:T(8,128)(2,1)}), bf16[32,128,128]{2,1,0:T(8,128)(2,1)}, u32[]{:S(2)}, u32[]{:S(2)}) %all-to-all-start.1) | async-done | bytes 1048608 | tf_op jit(solution)/shard_map/all_to_all | solution.py:416
  87.4 5.8 %scatter_high.1 = bf16[2048,128]{1,0:T(8,128)(2,1)} custom-call(bf16[32,136,128]{2,1,0:T(8,128)(2,1)S(1)} %all_to_all.35.payload_ids_ref.rows_ref.ids_ref, bf16[32,128,128]{2,1,0:T(8,128)(2,1)} %all-to-all-done.1.rows_ref, f32[4,4,128,8]{3,2,1,0:T(8,128)S(1)} %bitcast.28, f32[2048,128]{1,0:T(8,128)} %scatter_low.1.init_ref, f32[2048,1]{1,0:T(8,128)S(1)} %copy.28.degree_ref), custom_call_target="tpu_custom_call" | custom-call | tf_op jit(solution)/shard_map/scatter_high/pallas_call | solution.py:188
  93.2 14.7 %all_to_all.36.mean_ref = bf16[8,256,128]{2,1,0:T(8,128)(2,1)S(1)} all-to-all(bf16[8,256,128]{2,1,0:T(8,128)(2,1)} %bitcast.38), channel_id=1, replica_groups=mesh['z'=8,'y'=4,'feat'=8] {'feat'}, dimensions={0} | all-to-all | bytes 1048576 | tf_op jit(solution)/shard_map/all_to_all | solution.py:416
  107.9 0.0 all-gather.12.cloned.1.call-done
  107.9 6.0 %dense.1 = (bf16[8,256,128]{2,1,0:T(8,128)(2,1)S(1)}, bf16[8,256,128]{2,1,0:T(8,128)(2,1)}, bf16[256,1024]{1,0:T(8,128)(2,1)}) custom-call(s32[1]{0:T(128)} %bitcast.at_ref, bf16[8,256,128]{2,1,0:T(8,128)(2,1)S(1)} %all_to_all.36.mean_ref, f32[256,1024]{1,0:T(8,128)} %own_term.1.own_ref, bf16[8,2048,128]{2,1,0:T(8,128)(2,1)} %bitcast.36, ...), custom_call_target="tpu_custom_call" | custom-call | tf_op jit(solution)/shard_map/dense/pallas_call | solution.py:327
  113.9 12.8 %all_to_all.37 = bf16[8,256,128]{2,1,0:T(8,128)(2,1)S(1)} all-to-all(bf16[8,256,128]{2,1,0:T(8,128)(2,1)S(1)} %get-tuple-element.31), channel_id=1, replica_groups=mesh['z'=8,'y'=4,'feat'=8] {'feat'}, dimensions={0} | all-to-all | bytes 1048576 | tf_op jit(solution)/shard_map/all_to_all | solution.py:416
  126.7 0.0 all-gather.8.cloned.1.call-update
  126.7 0.0 copy-start.1
  126.7 0.2 all-gather.14.cloned.1.call-start
  126.9 4.7 %gather_rows.2 = bf16[32,128,128]{2,1,0:T(8,128)(2,1)} custom-call(f32[4,4,128,8]{3,2,1,0:T(8,128)S(1)} %bitcast.29, f32[4,4,128,8]{3,2,1,0:T(8,128)S(1)} %bitcast.30, bf16[2048,128]{1,0:T(8,128)(2,1)S(1)} %bitcast.33), custom_call_target="tpu_custom_call" | custom-call | tf_op jit(solution)/shard_map/gather_rows/pallas_call | solution.py:241
  131.7 0.0 all-gather.14.cloned.1.call-update
  131.7 6.1 %all-to-all-start.4 = ((bf16[32,128,128]{2,1,0:T(8,128)(2,1)}), bf16[32,128,128]{2,1,0:T(8,128)(2,1)S(1)}, u32[]{:S(2)}, u32[]{:S(2)}) async-start(bf16[32,128,128]{2,1,0:T(8,128)(2,1)} %gather_rows.2), calls=%async_computation.4 | async-start | bytes 2097152 | tf_op jit(solution)/shard_map/all_to_all | solution.py:416
  137.8 4.7 %gather_rows.3 = bf16[32,128,128]{2,1,0:T(8,128)(2,1)} custom-call(f32[4,4,128,8]{3,2,1,0:T(8,128)S(1)} %bitcast.31, f32[4,4,128,8]{3,2,1,0:T(8,128)S(1)} %bitcast.32, bf16[2048,128]{1,0:T(8,128)(2,1)S(1)} %bitcast.34), custom_call_target="tpu_custom_call" | custom-call | tf_op jit(solution)/shard_map/gather_rows/pallas_call | solution.py:241
  142.5 14.5 %all-gather.8.cloned.1.call-done = bf16[2048,1024]{1,0:T(8,128)(2,1)} async-done(((bf16[256,1024]{1,0:T(8,128)(2,1)}), bf16[2048,1024]{1,0:T(8,128)(2,1)}) %all-gather.8.cloned.1.call-update) | async-done | bytes 4194320 | tf_op jit(solution)/shard_map/all_gather | solution.py:522
  157.0 0.0 copy-done.1
  157.0 3.6 %convolution_convert_fusion = bf16[256,1024]{1,0:T(8,128)(2,1)S(1)} fusion(bf16[2048,1024]{1,0:T(8,128)(2,1)} %all-gather.8.cloned.1.call-done, bf16[2048,128]{1,0:T(8,128)(2,1)S(1)} %copy-done.1, bf16[2048,128]{1,0:T(8,128)(2,1)} %feat_ref.1), kind=kOutput, calls=%fused_computation | convolution fusion | flops 1076101120 | bytes 5767168 | tf_op jit(solution)/shard_map/dot_general | solution.py:525
  160.6 4.1 %all-to-all-done.4.low_ref = bf16[32,128,128]{2,1,0:T(8,128)(2,1)S(1)} async-done(((bf16[32,128,128]{2,1,0:T(8,128)(2,1)}), bf16[32,128,128]{2,1,0:T(8,128)(2,1)S(1)}, u32[]{:S(2)}, u32[]{:S(2)}) %all-to-all-start.4) | async-done | bytes 1048608 | tf_op jit(solution)/shard_map/all_to_all | solution.py:416
  164.8 6.4 %all-to-all-start.5 = ((bf16[32,128,128]{2,1,0:T(8,128)(2,1)}), bf16[32,128,128]{2,1,0:T(8,128)(2,1)}, u32[]{:S(2)}, u32[]{:S(2)}) async-start(bf16[32,128,128]{2,1,0:T(8,128)(2,1)} %gather_rows.3), calls=%async_computation.5 | async-start | bytes 2097152 | tf_op jit(solution)/shard_map/all_to_all | solution.py:416
  171.2 1.5 collective-permute-start
  172.8 2.7 %collective-permute-start.1 = (bf16[64,1024]{1,0:T(8,128)(2,1)S(1)}, bf16[64,1024]{1,0:T(8,128)(2,1)S(1)}, u32[]{:S(2)}, u32[]{:S(2)}) collective-permute-start(bf16[64,1024]{1,0:T(8,128)(2,1)S(1)} %get-tuple-element.48), channel_id=1, source_target_pairs={{0,16},{8,24},{16,0},{24,8},{1,17},{9,25},{17,1},{25,9},{2,18},{10... | collective-permute-start | bytes 393224 | tf_op jit(solution)/shard_map/ppermute | solution.py:425
  175.4 1.5 collective-permute-start.2
  176.9 2.8 %collective-permute-done = bf16[64,1024]{1,0:T(8,128)(2,1)S(1)} collective-permute-done((bf16[64,1024]{1,0:T(8,128)(2,1)S(1)}, bf16[64,1024]{1,0:T(8,128)(2,1)S(1)}, u32[]{:S(2)}, u32[]{:S(2)}) %collective-permute-start) | collective-permute-done | bytes 131104 | tf_op jit(solution)/shard_map/ppermute | solution.py:425
  179.7 7.3 %collective-permute-done.1 = bf16[64,1024]{1,0:T(8,128)(2,1)S(1)} collective-permute-done((bf16[64,1024]{1,0:T(8,128)(2,1)S(1)}, bf16[64,1024]{1,0:T(8,128)(2,1)S(1)}, u32[]{:S(2)}, u32[]{:S(2)}) %collective-permute-start.1) | collective-permute-done | bytes 131104 | tf_op jit(solution)/shard_map/ppermute | solution.py:425
  187.0 0.0 collective-permute-done.2
  187.0 0.1 fusion.5
  187.1 0.1 collective-permute-start.3
  187.2 2.8 %collective-permute-start.4 = (bf16[64,1024]{1,0:T(8,128)(2,1)S(1)}, bf16[64,1024]{1,0:T(8,128)(2,1)S(1)}, u32[]{:S(2)}, u32[]{:S(2)}) collective-permute-start(bf16[64,1024]{1,0:T(8,128)(2,1)S(1)} %fusion.5), channel_id=1, source_target_pairs={{0,64},{32,96},{64,0},{96,32},{128,192},{160,224},{192,128},{224,1... | collective-permute-start | bytes 393224 | tf_op jit(solution)/shard_map/ppermute | solution.py:450
  190.0 0.7 collective-permute-start.5
  190.7 3.5 %fusion.6.self_ref = f32[2048,128]{1,0:T(8,128)S(1)} fusion(bf16[2048,1024]{1,0:T(8,128)(2,1)} %all-gather.8.cloned.1.call-done, bf16[1024,1024]{1,0:T(8,128)(2,1)} %weight_ref.2, s32[]{:T(128)S(6)} %select_n.36), kind=kOutput, calls=%fused_computation.10 | convolution fusion | flops 536870912 | bytes 5505028 | tf_op jit(solution)/shard_map/dot_general | solution.py:536
  194.2 4.7 %collective-permute-done.3 = bf16[64,1024]{1,0:T(8,128)(2,1)S(1)} collective-permute-done((bf16[64,1024]{1,0:T(8,128)(2,1)S(1)}, bf16[64,1024]{1,0:T(8,128)(2,1)S(1)}, u32[]{:S(2)}, u32[]{:S(2)}) %collective-permute-start.3) | collective-permute-done | bytes 131104 | tf_op jit(solution)/shard_map/ppermute | solution.py:450
  198.8 4.4 %collective-permute-done.4 = bf16[64,1024]{1,0:T(8,128)(2,1)S(1)} collective-permute-done((bf16[64,1024]{1,0:T(8,128)(2,1)S(1)}, bf16[64,1024]{1,0:T(8,128)(2,1)S(1)}, u32[]{:S(2)}, u32[]{:S(2)}) %collective-permute-start.4) | collective-permute-done | bytes 131104 | tf_op jit(solution)/shard_map/ppermute | solution.py:450
  203.3 3.3 %collective-permute-done.5 = bf16[64,1024]{1,0:T(8,128)(2,1)S(1)} collective-permute-done((bf16[64,1024]{1,0:T(8,128)(2,1)S(1)}, bf16[64,1024]{1,0:T(8,128)(2,1)S(1)}, u32[]{:S(2)}, u32[]{:S(2)}) %collective-permute-start.5) | collective-permute-done | bytes 131104 | tf_op jit(solution)/shard_map/ppermute | solution.py:450
  206.6 0.1 add_convert_fusion.1
  206.6 3.7 %collective-permute-start.6 = (bf16[64,1024]{1,0:T(8,128)(2,1)S(1)}, bf16[64,1024]{1,0:T(8,128)(2,1)S(1)}, u32[]{:S(2)}, u32[]{:S(2)}) collective-permute-start(bf16[64,1024]{1,0:T(8,128)(2,1)S(1)} %add_convert_fusion.1), channel_id=1, source_target_pairs={{0,128},{32,160},{64,192},{96,224},{128,0},{160,32},{192,64},{224,... | collective-permute-start | bytes 393224 | tf_op jit(solution)/shard_map/ppermute | solution.py:463
  210.3 0.0 all-to-all-done.5.high_ref
  210.3 5.3 %backward_blocks.1 = bf16[2048,128]{1,0:T(8,128)(2,1)} custom-call(s32[128]{0:T(128)} %source_ref.3, s32[128]{0:T(128)} %slot_ref.3, bf16[32,128,128]{2,1,0:T(8,128)(2,1)S(1)} %all-to-all-done.4.low_ref, bf16[32,128,128]{2,1,0:T(8,128)(2,1)} %all-to-all-done.5.high_ref, bf16[128,128,128]{2,1,0:T(8,128)(2,1)} %bitcast.35, f32[2048,128]{1,0:T(8,128)S(1)} %fusion.6.self_ref), custom_call_target="tpu_custom_call" | custom-call | tf_op jit(solution)/shard_map/backward_blocks/pallas_call | solution.py:388
  215.6 0.9 collective-permute-done.6
  216.5 0.9 broadcast_in_dim.14
  217.4 4.1 %all-to-all-start.6 = ((bf16[4,64,1024]{2,1,0:T(8,128)(2,1)}), bf16[4,64,1024]{2,1,0:T(8,128)(2,1)S(1)}, u32[]{:S(2)}, u32[]{:S(2)}) async-start(bf16[4,64,1024]{2,1,0:T(8,128)(2,1)} %broadcast_in_dim.14), calls=%async_computation.6 | async-start | bytes 1048576 | tf_op jit(solution)/shard_map/all_to_all | solution.py:416
  221.5 0.0 all-gather.14.cloned.1.call-done
  221.5 1.9 constant_dynamic-slice_fusion
  223.4 7.5 %all-to-all-done.6 = bf16[4,64,1024]{2,1,0:T(8,128)(2,1)S(1)} async-done(((bf16[4,64,1024]{2,1,0:T(8,128)(2,1)}), bf16[4,64,1024]{2,1,0:T(8,128)(2,1)S(1)}, u32[]{:S(2)}, u32[]{:S(2)}) %all-to-all-start.6) | async-done | bytes 524320 | tf_op jit(solution)/shard_map/all_to_all | solution.py:416
  230.9 1.1 fusion.10
  (4 shorter events, 0.1 us)
Async XLA Ops:
  7.2 67.6 %all-gather.10.cloned.1.call-start = ((), (), s32[]{:S(2)}) async-start(), calls=%async_computation.8 | async-start | bytes 4718592 | tf_op jit(solution)/shard_map/all_gather | solution.py:496
  7.9 100.0 %all-gather.12.cloned.1.call-start = ((), (), s32[]{:S(2)}) async-start(), calls=%async_computation.9 | async-start | bytes 4718592 | tf_op jit(solution)/shard_map/all_gather | solution.py:497
  7.9 53.4 %copy-start.2 = (s32[2048]{0:T(1024)S(1)}, s32[2048]{0:T(1024)}, u32[]{:S(2)}) copy-start(s32[2048]{0:T(1024)} %param.18) | copy-start | bytes 24580
  55.8 31.5 %all-to-all-start.1 = ((bf16[32,128,128]{2,1,0:T(8,128)(2,1)}), bf16[32,128,128]{2,1,0:T(8,128)(2,1)}, u32[]{:S(2)}, u32[]{:S(2)}) async-start(bf16[32,128,128]{2,1,0:T(8,128)(2,1)} %get-tuple-element.25), calls=%async_computation.1 | async-start | bytes 2097152 | tf_op jit(solution)/shard_map/all_to_all | solution.py:416
  61.3 95.7 %all-gather.8.cloned.1.call-start = ((), (), s32[]{:S(2)}) async-start(), calls=%async_computation.7 | async-start | bytes 4718592 | tf_op jit(solution)/shard_map/all_gather | solution.py:522
  74.8 1.6 copy-start
  126.7 30.3 %copy-start.1 = (bf16[2048,128]{1,0:T(8,128)(2,1)S(1)}, bf16[2048,128]{1,0:T(8,128)(2,1)}, u32[]{:S(2)}) copy-start(bf16[2048,128]{1,0:T(8,128)(2,1)} %scatter_high.1) | copy-start | bytes 1572868
  126.7 94.8 %all-gather.14.cloned.1.call-start = ((), (), s32[]{:S(2)}) async-start(), calls=%async_computation.10 | async-start | bytes 4718592 | tf_op jit(solution)/shard_map/all_gather | solution.py:533
  131.7 33.1 %all-to-all-start.4 = ((bf16[32,128,128]{2,1,0:T(8,128)(2,1)}), bf16[32,128,128]{2,1,0:T(8,128)(2,1)S(1)}, u32[]{:S(2)}, u32[]{:S(2)}) async-start(bf16[32,128,128]{2,1,0:T(8,128)(2,1)} %gather_rows.2), calls=%async_computation.4 | async-start | bytes 2097152 | tf_op jit(solution)/shard_map/all_to_all | solution.py:416
  164.8 45.6 %all-to-all-start.5 = ((bf16[32,128,128]{2,1,0:T(8,128)(2,1)}), bf16[32,128,128]{2,1,0:T(8,128)(2,1)}, u32[]{:S(2)}, u32[]{:S(2)}) async-start(bf16[32,128,128]{2,1,0:T(8,128)(2,1)} %gather_rows.3), calls=%async_computation.5 | async-start | bytes 2097152 | tf_op jit(solution)/shard_map/all_to_all | solution.py:416
  171.2 8.5 %collective-permute-start = (bf16[64,1024]{1,0:T(8,128)(2,1)S(1)}, bf16[64,1024]{1,0:T(8,128)(2,1)S(1)}, u32[]{:S(2)}, u32[]{:S(2)}) collective-permute-start(bf16[64,1024]{1,0:T(8,128)(2,1)S(1)} %get-tuple-element.46), channel_id=1, source_target_pairs={{0,8},{8,16},{16,24},{24,0},{1,9},{9,17},{17,25},{25,1},{2,10},{10... | collective-permute-start | bytes 393224 | tf_op jit(solution)/shard_map/ppermute | solution.py:425
  172.8 14.3 %collective-permute-start.1 = (bf16[64,1024]{1,0:T(8,128)(2,1)S(1)}, bf16[64,1024]{1,0:T(8,128)(2,1)S(1)}, u32[]{:S(2)}, u32[]{:S(2)}) collective-permute-start(bf16[64,1024]{1,0:T(8,128)(2,1)S(1)} %get-tuple-element.48), channel_id=1, source_target_pairs={{0,16},{8,24},{16,0},{24,8},{1,17},{9,25},{17,1},{25,9},{2,18},{10... | collective-permute-start | bytes 393224 | tf_op jit(solution)/shard_map/ppermute | solution.py:425
  175.4 11.6 %collective-permute-start.2 = (bf16[64,1024]{1,0:T(8,128)(2,1)S(1)}, bf16[64,1024]{1,0:T(8,128)(2,1)S(1)}, u32[]{:S(2)}, u32[]{:S(2)}) collective-permute-start(bf16[64,1024]{1,0:T(8,128)(2,1)S(1)} %get-tuple-element.47), channel_id=1, source_target_pairs={{0,24},{8,0},{16,8},{24,16},{1,25},{9,1},{17,9},{25,17},{2,26},{10... | collective-permute-start | bytes 393224 | tf_op jit(solution)/shard_map/ppermute | solution.py:425
  187.1 11.7 %collective-permute-start.3 = (bf16[64,1024]{1,0:T(8,128)(2,1)S(1)}, bf16[64,1024]{1,0:T(8,128)(2,1)S(1)}, u32[]{:S(2)}, u32[]{:S(2)}) collective-permute-start(bf16[64,1024]{1,0:T(8,128)(2,1)S(1)} %fusion.5), channel_id=1, source_target_pairs={{0,32},{32,0},{64,96},{96,64},{128,160},{160,128},{192,224},{224,1... | collective-permute-start | bytes 393224 | tf_op jit(solution)/shard_map/ppermute | solution.py:450
  187.2 16.1 %collective-permute-start.4 = (bf16[64,1024]{1,0:T(8,128)(2,1)S(1)}, bf16[64,1024]{1,0:T(8,128)(2,1)S(1)}, u32[]{:S(2)}, u32[]{:S(2)}) collective-permute-start(bf16[64,1024]{1,0:T(8,128)(2,1)S(1)} %fusion.5), channel_id=1, source_target_pairs={{0,64},{32,96},{64,0},{96,32},{128,192},{160,224},{192,128},{224,1... | collective-permute-start | bytes 393224 | tf_op jit(solution)/shard_map/ppermute | solution.py:450
  190.0 16.6 %collective-permute-start.5 = (bf16[64,1024]{1,0:T(8,128)(2,1)S(1)}, bf16[64,1024]{1,0:T(8,128)(2,1)S(1)}, u32[]{:S(2)}, u32[]{:S(2)}) collective-permute-start(bf16[64,1024]{1,0:T(8,128)(2,1)S(1)} %fusion.5), channel_id=1, source_target_pairs={{0,96},{32,64},{64,32},{96,0},{128,224},{160,192},{192,160},{224,1... | collective-permute-start | bytes 393224 | tf_op jit(solution)/shard_map/ppermute | solution.py:450
  206.6 9.9 %collective-permute-start.6 = (bf16[64,1024]{1,0:T(8,128)(2,1)S(1)}, bf16[64,1024]{1,0:T(8,128)(2,1)S(1)}, u32[]{:S(2)}, u32[]{:S(2)}) collective-permute-start(bf16[64,1024]{1,0:T(8,128)(2,1)S(1)} %add_convert_fusion.1), channel_id=1, source_target_pairs={{0,128},{32,160},{64,192},{96,224},{128,0},{160,32},{192,64},{224,... | collective-permute-start | bytes 393224 | tf_op jit(solution)/shard_map/ppermute | solution.py:463
  217.4 13.5 %all-to-all-start.6 = ((bf16[4,64,1024]{2,1,0:T(8,128)(2,1)}), bf16[4,64,1024]{2,1,0:T(8,128)(2,1)S(1)}, u32[]{:S(2)}, u32[]{:S(2)}) async-start(bf16[4,64,1024]{2,1,0:T(8,128)(2,1)} %broadcast_in_dim.14), calls=%async_computation.6 | async-start | bytes 1048576 | tf_op jit(solution)/shard_map/all_to_all | solution.py:416
Sparse Core Ops, SparseCore 0:
  9.9 37.2 all-gather.9
  55.9 30.1 all-gather.11
  126.8 30.1 all-gather.7
  159.3 34.6 all-gather.13
